TPU v7x, 256 devices: a whole 4x4x8 slice. The times are simulated.
256 devices in a mesh: gx: 16 (over z_hi, y, core), gy: 16 (over z_lo, x).
Axes of the slice: x: 4, y: 4, z: 8 (z_hi: 2, z_lo: 4; z = z_hi * 4 + z_lo), core: 2. Of those that a mesh axis runs over, the one named last changes fastest.
Arguments:
- skip_input: bfloat16 [32, 64, 4096], P(None, 'gx', 'gy'), may hold values from -6 to 6
- w_encoder: bfloat16 [64, 864], replicated, may hold values from -0.625 to 0.625
- w_bottom: bfloat16 [128, 1728], P('gx'), may hold values from -0.3125 to 0.3125
- w_middle: bfloat16 [64, 5184], replicated, may hold values from -0.15625 to 0.15625
- w_upper: bfloat16 [32, 2592], replicated, may hold values from -0.21875 to 0.21875
- cotangent: bfloat16 [32, 64, 4096], P(None, 'gx', 'gy'), may hold values from -6 to 6
Outputs:
- features: bfloat16 [32, 64, 4096], P(None, 'gx', 'gy')
- grad_skip: bfloat16 [32, 64, 4096], P(None, 'gx', 'gy')
- grad_encoder: float32 [64, 864], replicated
- grad_bottom: float32 [128, 1728], P('gx')
- grad_middle: float32 [64, 5184], replicated
- grad_upper: float32 [32, 2592], replicated
All inputs are finite; a program needn't handle non-finite values.
Results may differ from a plain program's by a relative error of at most 0.017.
Values may be sent and summed in bfloat16 or wider, within the bound.
No kernel may reach another device: no remote copies, remote signals or barrier semaphores. Data moves between devices by JAX's collectives and lax.ppermute only.
A program may use at most 64 MiB of HBM per device.

v0:
```python
import math

import jax
import jax.numpy as jnp
from jax import lax
from jax.sharding import PartitionSpec as P

Z = 16


def extended_2(cells, sides, width):
    for axis, dim in sides:
        count = lax.axis_size(axis)
        ends = count - 1
        head = lax.slice_in_dim(cells, 0, width, axis=dim)
        tail = lax.slice_in_dim(cells, cells.shape[dim] - width, cells.shape[dim], axis=dim)
        cells = jnp.concatenate(
            [
                lax.ppermute(tail, axis, [(i, (i + 1) % count) for i in range(ends)]),
                cells,
                lax.ppermute(head, axis, [((i + 1) % count, i) for i in range(ends)]),
            ],
            axis=dim,
        )
    return cells


def z_shift(extended, z_step, z_depth):
    length = extended.shape[2]
    padded = jnp.pad(extended, ((0, 0), (0, 0), (1, 1)))
    shifted = padded[:, :, 1 + z_step : 1 + z_step + length]
    z_index = lax.broadcasted_iota(jnp.int32, (1, 1, length), 2) % z_depth + z_step
    inside = (z_index >= 0) & (z_index < z_depth)
    return jnp.where(inside, shifted, jnp.zeros_like(shifted))


def tap_piece(shifted_set, a, b, c, row_count, col_count, z_depth, flipped):
    x_off, y_off, z_off = (2 - a, 2 - b, 2 - c) if flipped else (a, b, c)
    source = shifted_set[z_off]
    tap_slice = source[
        :, x_off : x_off + row_count, y_off * z_depth : (y_off + col_count) * z_depth
    ]
    return tap_slice.reshape(source.shape[0], row_count * col_count * z_depth)


def conv_forward(extended, weight, row_count, col_count, z_depth):
    in_chan = extended.shape[0]
    shifted_set = [z_shift(extended, z_step, z_depth) for z_step in (-1, 0, 1)]
    total_sum = jnp.zeros((weight.shape[0], row_count * col_count * z_depth), jnp.float32)
    for a in range(3):
        for b in range(3):
            for c in range(3):
                tap_number = 9 * a + 3 * b + c
                total_sum = total_sum + jnp.dot(
                    weight[:, tap_number * in_chan : (tap_number + 1) * in_chan],
                    tap_piece(shifted_set, a, b, c, row_count, col_count, z_depth, False),
                    preferred_element_type=jnp.float32,
                )
    return total_sum


def conv_backward(extended, weight, row_count, col_count, z_depth):
    in_chan = weight.shape[1] // 27
    shifted_set = [z_shift(extended, z_step, z_depth) for z_step in (-1, 0, 1)]
    total_sum = jnp.zeros((in_chan, row_count * col_count * z_depth), jnp.float32)
    for a in range(3):
        for b in range(3):
            for c in range(3):
                tap_number = 9 * a + 3 * b + c
                total_sum = total_sum + lax.dot_general(
                    weight[:, tap_number * in_chan : (tap_number + 1) * in_chan],
                    tap_piece(shifted_set, a, b, c, row_count, col_count, z_depth, True),
                    (((0,), (0,)), ((), ())),
                    preferred_element_type=jnp.float32,
                )
    return total_sum


def weight_grad(extended, error_flat, row_count, col_count, z_depth):
    shifted_set = [z_shift(extended, z_step, z_depth) for z_step in (-1, 0, 1)]
    blocks = []
    for a in range(3):
        for b in range(3):
            for c in range(3):
                blocks.append(
                    lax.dot_general(
                        error_flat,
                        tap_piece(shifted_set, a, b, c, row_count, col_count, z_depth, False),
                        (((1,), (1,)), ((), ())),
                        preferred_element_type=jnp.float32,
                    )
                )
    return jnp.concatenate(blocks, axis=1)


def pool_mean(values, z_depth):
    channels, row_count, length = values.shape
    col_count = length // z_depth
    shaped = values.astype(jnp.float32).reshape(
        channels, row_count // 2, 2, col_count // 2, 2, z_depth // 2, 2
    )
    return shaped.mean(axis=(2, 4, 6)).reshape(
        channels, row_count // 2, col_count // 2 * (z_depth // 2)
    )


def block_sum(values, z_depth):
    channels, row_count, length = values.shape
    col_count = length // z_depth
    shaped = values.reshape(channels, row_count // 2, 2, col_count // 2, 2, z_depth // 2, 2)
    return shaped.sum(axis=(2, 4, 6)).reshape(
        channels, row_count // 2, col_count // 2 * (z_depth // 2)
    )


def upsample(values, z_depth):
    channels, row_count, length = values.shape
    col_count = length // z_depth
    shaped = values.reshape(channels, row_count, 1, col_count, 1, z_depth, 1)
    shaped = jnp.broadcast_to(shaped, (channels, row_count, 2, col_count, 2, z_depth, 2))
    return shaped.reshape(channels, 2 * row_count, 4 * col_count * z_depth)


def silu_slope(values):
    s_value = jax.nn.sigmoid(values)
    return s_value * (1.0 + values * (1.0 - s_value))


def spatial_halo(values, z_depth):
    widened = extended_2(values, (("gx", 1),), 1)
    return extended_2(widened, (("gy", 2),), z_depth)


def per_device(skip_input, w_encoder, w_bottom, w_middle, w_upper, cotangent):
    top_chan = skip_input.shape[0]
    rows_fine = skip_input.shape[1]
    cols_fine = skip_input.shape[2] // Z
    rows_mid, cols_mid, depth_mid = (rows_fine // 2, cols_fine // 2, Z // 2)
    rows_low, cols_low, depth_low = (rows_fine // 4, cols_fine // 4, Z // 4)
    cells_fine = rows_fine * cols_fine * Z * lax.axis_size("gx") * lax.axis_size("gy")
    scale_fine = 1.0 / math.sqrt(cells_fine)
    scale_mid = 1.0 / math.sqrt(cells_fine // 8)
    scale_low = 1.0 / math.sqrt(cells_fine // 64)
    pool_top = pool_mean(skip_input, Z).astype(jnp.bfloat16)
    ext_pool = spatial_halo(pool_top, depth_mid)
    pre_one = conv_forward(ext_pool, w_encoder, rows_mid, cols_mid, depth_mid)
    act_one = jax.nn.silu(pre_one).astype(jnp.bfloat16).reshape(-1, rows_mid, cols_mid * depth_mid)
    pool_mid = pool_mean(act_one, depth_mid).astype(jnp.bfloat16)
    col_ext = extended_2(pool_mid, (("gy", 2),), depth_low)
    whole_rows = lax.all_gather(col_ext, "gx", axis=1, tiled=True)
    ext_low = jnp.pad(whole_rows, ((0, 0), (1, 1), (0, 0)))
    rows_all = whole_rows.shape[1]
    pre_two = conv_forward(ext_low, w_bottom, rows_all, cols_low, depth_low)
    act_block = (
        jax.nn.silu(pre_two).astype(jnp.bfloat16).reshape(-1, rows_all, cols_low * depth_low)
    )
    act_two = lax.all_to_all(act_block, "gx", split_axis=1, concat_axis=0, tiled=True)
    cat_mid = jnp.concatenate([upsample(act_two, depth_low), act_one], axis=0)
    ext_mid = spatial_halo(cat_mid, depth_mid)
    pre_three = conv_forward(ext_mid, w_middle, rows_mid, cols_mid, depth_mid)
    act_three = (
        jax.nn.silu(pre_three).astype(jnp.bfloat16).reshape(-1, rows_mid, cols_mid * depth_mid)
    )
    cat_top = jnp.concatenate([upsample(act_three, depth_mid), skip_input], axis=0)
    ext_top = spatial_halo(cat_top, Z)
    pre_four = conv_forward(ext_top, w_upper, rows_fine, cols_fine, Z)
    features = (
        jax.nn.silu(pre_four).astype(jnp.bfloat16).reshape(top_chan, rows_fine, cols_fine * Z)
    )
    err_four = (cotangent.reshape(top_chan, -1).astype(jnp.float32) * silu_slope(pre_four)).astype(
        jnp.bfloat16
    )
    local_upper = weight_grad(ext_top, err_four, rows_fine, cols_fine, Z) * scale_fine
    grad_upper = lax.psum(local_upper, ("gx", "gy"))
    dcat_top = conv_backward(
        spatial_halo(err_four.reshape(top_chan, rows_fine, cols_fine * Z), Z),
        w_upper,
        rows_fine,
        cols_fine,
        Z,
    ).reshape(-1, rows_fine, cols_fine * Z)
    mid_chan = act_three.shape[0]
    err_three = (
        block_sum(dcat_top[:mid_chan], Z).reshape(mid_chan, -1) * silu_slope(pre_three)
    ).astype(jnp.bfloat16)
    local_middle = weight_grad(ext_mid, err_three, rows_mid, cols_mid, depth_mid) * scale_mid
    grad_middle = lax.psum(local_middle, ("gx", "gy"))
    dcat_mid = conv_backward(
        spatial_halo(err_three.reshape(mid_chan, rows_mid, cols_mid * depth_mid), depth_mid),
        w_middle,
        rows_mid,
        cols_mid,
        depth_mid,
    ).reshape(-1, rows_mid, cols_mid * depth_mid)
    low_chan = act_two.shape[0]
    dact_two = block_sum(dcat_mid[:low_chan], depth_mid)
    dact_block = lax.all_to_all(dact_two, "gx", split_axis=0, concat_axis=1, tiled=True)
    block_chan = dact_block.shape[0]
    err_two = (dact_block.reshape(block_chan, -1) * silu_slope(pre_two)).astype(jnp.bfloat16)
    part_bottom = weight_grad(ext_low, err_two, rows_all, cols_low, depth_low)
    err_grid = err_two.reshape(block_chan, rows_all, cols_low * depth_low)
    err_cols = extended_2(err_grid, (("gy", 2),), depth_low)
    err_ext = jnp.pad(err_cols, ((0, 0), (1, 1), (0, 0)))
    partial_sum = conv_backward(err_ext, w_bottom, rows_all, cols_low, depth_low).reshape(
        -1, rows_all, cols_low * depth_low
    )
    dpool_mid = lax.psum_scatter(
        partial_sum.astype(jnp.bfloat16), "gx", scatter_dimension=1, tiled=True
    ).astype(jnp.float32)
    grad_bottom = lax.psum((part_bottom * scale_low).astype(jnp.bfloat16), "gy").astype(jnp.float32)
    dact_one = dcat_mid[low_chan:] + upsample(dpool_mid, depth_low) / 8.0
    err_one = (dact_one.reshape(mid_chan, -1) * silu_slope(pre_one)).astype(jnp.bfloat16)
    local_encoder = weight_grad(ext_pool, err_one, rows_mid, cols_mid, depth_mid) * scale_mid
    grad_encoder = lax.psum(local_encoder, ("gx", "gy"))
    dpool_top = conv_backward(
        spatial_halo(err_one.reshape(mid_chan, rows_mid, cols_mid * depth_mid), depth_mid),
        w_encoder,
        rows_mid,
        cols_mid,
        depth_mid,
    ).reshape(-1, rows_mid, cols_mid * depth_mid)
    grad_skip = (dcat_top[mid_chan:] + upsample(dpool_top, depth_mid) / 8.0).astype(jnp.bfloat16)
    return (features, grad_skip, grad_encoder, grad_bottom, grad_middle, grad_upper)


def solution(mesh):
    in_specs = (P(None, "gx", "gy"), P(), P("gx", None), P(), P(), P(None, "gx", "gy"))
    out_specs = (P(None, "gx", "gy"), P(None, "gx", "gy"), P(), P("gx", None), P(), P())
    return jax.shard_map(
        per_device, mesh=mesh, in_specs=in_specs, out_specs=out_specs, check_vma=False
    )
```

profile of v0, /device:TPU:1, one launch (start us, length us, event | category | flops | bytes accessed | tf_op | source)
XLA Modules:
  0.0 700.5 jit_solution(12189707919216640930)
XLA Ops:
  8.6 4.6 collective-permute-start
  13.2 1.9 collective-permute-start.1
  16.3 2.0 collective-permute-done.1
  18.3 3.1 collective-permute-start.2
  21.4 1.3 collective-permute-start.3
  23.4 2.4 collective-permute-done.3
  36.4 3.1 collective-permute-start.4
  39.5 1.3 collective-permute-start.5
  40.9 3.0 collective-permute-done.5
  43.9 35.2 %all_gather.3 = bf16[64,16,24]{0,2,1:T(8,128)(2,1)S(1)} all-gather(bf16[64,1,24]{0,2,1:T(8,128)(2,1)S(1)} %pad_maximum_fusion.21), channel_id=1, replica_groups=mesh['gx'=16,'gy'=16] {'gx'}, dimensions={1}, use_global_device_ids=true | all-gather | bytes 52224 | tf_op jit(solution)/shard_map/all_gather | solution.py:150
  86.1 6.5 all-to-all-start
  92.7 9.6 %all-to-all-done = bf16[8,16,16]{2,0,1:T(8,128)(2,1)S(1)} async-done(((bf16[8,16,16]{2,0,1:T(8,128)(2,1)}), bf16[8,16,16]{2,0,1:T(8,128)(2,1)S(1)}, u32[]{:S(2)}, u32[]{:S(2)}) %all-to-all-start) | async-done | bytes 4128 | tf_op jit(solution)/shard_map/all_to_all | solution.py:157
  102.7 2.5 collective-permute-start.6
  105.1 1.9 collective-permute-start.7
  107.1 3.3 collective-permute-done.7
  110.4 4.0 collective-permute-start.8
  114.4 1.3 collective-permute-start.9
  115.7 3.3 collective-permute-done.9
  121.0 1.3 copy-done.1
  128.2 3.2 collective-permute-start.10
  131.4 1.9 collective-permute-start.11
  133.4 3.6 collective-permute-done.11
  137.1 3.8 collective-permute-start.12
  140.9 1.5 collective-permute-start.13
  142.4 3.3 collective-permute-done.13
  159.2 3.0 collective-permute-start.14
  162.3 1.9 collective-permute-start.15
  164.6 2.9 collective-permute-done.15
  167.7 3.8 collective-permute-start.16
  171.5 1.3 collective-permute-start.17
  174.2 2.5 collective-permute-done.17
  189.6 1.7 fusion.424
  192.0 1.6 fusion.422
  210.7 3.1 collective-permute-start.18
  213.8 2.1 collective-permute-start.19
  216.7 4.1 collective-permute-done.19
  221.6 4.7 collective-permute-start.20
  227.8 1.7 concatenate.78
  229.4 2.2 collective-permute-done.21
  234.6 1.4 reshape.1182
  236.0 1.4 reshape.1179
  237.5 1.4 reshape.1176
  238.9 1.4 reshape.1173
  244.7 1.4 reshape.1181
  246.2 1.4 reshape.1178
  247.6 1.4 reshape.1175
  249.1 1.4 reshape.1172
  254.9 1.5 reshape.1180
  256.4 1.4 reshape.1177
  273.5 26.1 %all-to-all-start.1 = ((f32[16,1,128]{2,1,0:T(1,128)}), f32[16,1,128]{2,1,0:T(1,128)S(1)}, u32[]{:S(2)}, u32[]{:S(2)}) async-start(f32[16,1,128]{2,1,0:T(1,128)} %reshape.1246), calls=%async_computation.1 | async-start | bytes 16384 | tf_op jit(solution)/shard_map/all_to_all | solution.py:197
  301.2 7.7 %all-to-all-done.1 = f32[16,1,128]{2,1,0:T(1,128)S(1)} async-done(((f32[16,1,128]{2,1,0:T(1,128)}), f32[16,1,128]{2,1,0:T(1,128)S(1)}, u32[]{:S(2)}, u32[]{:S(2)}) %all-to-all-start.1) | async-done | bytes 8224 | tf_op jit(solution)/shard_map/all_to_all | solution.py:197
  314.3 3.4 collective-permute-start.22
  317.7 1.3 collective-permute-start.23
  319.3 3.1 collective-permute-done.23
  333.3 62.8 %psum.29 = bf16[8,1728]{1,0:T(8,128)(2,1)S(1)} all-reduce(bf16[8,1728]{1,0:T(8,128)(2,1)S(1)} %multiply_convert_fusion.3), channel_id=1, replica_groups=mesh['gx'=16,'gy'=16] {'gy'}, use_global_device_ids=true, to_apply=%region_6.7 | all-reduce | flops 13824 | bytes 55296 | tf_op jit(solution)/shard_map/psum | solution.py:210
  396.7 5.3 reduce-scatter.2.cloned.1.call-done
  403.9 12.3 %collective-permute-start.24 = (bf16[64,1,64]{2,1,0:T(2,128)(2,1)S(1)}, bf16[64,1,64]{2,1,0:T(2,128)(2,1)S(1)}, u32[]{:S(2)}, u32[]{:S(2)}) collective-permute-start(bf16[64,1,64]{2,1,0:T(2,128)(2,1)S(1)} %get-tuple-element.272), channel_id=1, source_target_pairs={{0,16},{16,32},{32,48},{48,64},{64,80},{80,96},{96,112},{112,128},... | collective-permute-start | bytes 24584 | tf_op jit(solution)/shard_map/ppermute | solution.py:19
  416.2 1.9 collective-permute-start.25
  422.0 1.3 collective-permute-start.26
  423.3 1.6 collective-permute-start.27
  425.7 2.6 collective-permute-done.27
  441.2 247.3 %all-reduce.13.cloned.1.call-done = (f32[64,864]{0,1:T(8,128)}, f32[64,5184]{1,0:T(8,128)}, f32[32,2592]{1,0:T(8,128)}) async-done(((f32[64,864]{0,1:T(8,128)}, f32[64,5184]{1,0:T(8,128)}, f32[32,2592]{1,0:T(8,128)}), (f32[64,864]{0,1:T(8,128)}, f32[64,5184]{1,0:T(8,128)}, f32[32,2592]{1,0:T(8,128)})) %all-reduce.13.cloned.1.call-update) | async-done | bytes 1880080 | tf_op jit(solution)/shard_map/psum | solution.py:214
  688.5 1.9 copy.98
  690.4 2.5 copy.159
  (970 shorter events, 141.5 us)
Async XLA Ops:
  8.6 7.6 %collective-permute-start = (bf16[32,1,64]{0,2,1:T(8,128)(2,1)S(1)}, bf16[32,1,64]{0,2,1:T(8,128)(2,1)S(1)}, u32[]{:S(2)}, u32[]{:S(2)}) collective-permute-start(bf16[32,1,64]{0,2,1:T(8,128)(2,1)S(1)} %get-tuple-element.307), channel_id=1, source_target_pairs={{0,16},{16,32},{32,48},{48,64},{64,80},{80,96},{96,112},{112,128},... | collective-permute-start | bytes 12296 | tf_op jit(solution)/shard_map/ppermute | solution.py:19
  13.2 5.1 collective-permute-start.1
  15.7 63.5 %copy-start.164 = (pred[24]{0:T(512)(128)(4,1)}, pred[24]{0:T(512)(128)(4,1)S(1)}, u32[]{:S(2)}) copy-start(pred[24]{0:T(512)(128)(4,1)S(1)} %get-tuple-element.326) | copy-start | bytes 76
  15.7 63.5 %copy-start.166 = (pred[24]{0:T(512)(128)(4,1)}, pred[24]{0:T(512)(128)(4,1)S(1)}, u32[]{:S(2)}) copy-start(pred[24]{0:T(512)(128)(4,1)S(1)} %get-tuple-element.327) | copy-start | bytes 76
  18.3 7.6 %collective-permute-start.2 = (bf16[32,4,8]{0,2,1:T(8,128)(2,1)S(1)}, bf16[32,4,8]{0,2,1:T(8,128)(2,1)S(1)}, u32[]{:S(2)}, u32[]{:S(2)}) collective-permute-start(bf16[32,4,8]{0,2,1:T(8,128)(2,1)S(1)} %get-tuple-element.241), channel_id=1, source_target_pairs={{0,1},{1,2},{2,3},{3,4},{4,5},{5,6},{6,7},{7,8},{8,9},{9,10},{10,1... | collective-permute-start | bytes 6152 | tf_op jit(solution)/shard_map/ppermute | solution.py:19
  21.4 4.4 collective-permute-start.3
  36.4 4.5 collective-permute-start.4
  39.5 4.3 collective-permute-start.5
  40.9 38.4 %copy-start.168 = (pred[24]{0:T(512)(128)(4,1)}, pred[24]{0:T(512)(128)(4,1)S(1)}, u32[]{:S(2)}) copy-start(pred[24]{0:T(512)(128)(4,1)S(1)} %compare_and_fusion.2) | copy-start | bytes 76
  86.1 16.2 %all-to-all-start = ((bf16[8,16,16]{2,0,1:T(8,128)(2,1)}), bf16[8,16,16]{2,0,1:T(8,128)(2,1)S(1)}, u32[]{:S(2)}, u32[]{:S(2)}) async-start(bf16[8,16,16]{2,0,1:T(8,128)(2,1)} %copy.83), calls=%async_computation | async-start | bytes 65536 | tf_op jit(solution)/shard_map/all_to_all | solution.py:157
  102.7 4.4 collective-permute-start.6
  105.1 5.2 collective-permute-start.7
  110.4 5.3 collective-permute-start.8
  114.4 4.6 collective-permute-start.9
  128.2 5.2 collective-permute-start.10
  131.4 5.6 collective-permute-start.11
  137.1 5.3 collective-permute-start.12
  140.9 4.9 collective-permute-start.13
  159.2 5.4 collective-permute-start.14
  162.3 5.2 collective-permute-start.15
  167.7 6.5 collective-permute-start.16
  171.5 5.3 collective-permute-start.17
  200.6 27.0 %copy-start.36 = (bf16[192,2,64]{0,2,1:T(8,128)(2,1)S(1)}, bf16[192,2,64]{0,2,1:T(8,128)(2,1)}, u32[]{:S(2)}) copy-start(bf16[192,2,64]{0,2,1:T(8,128)(2,1)} %copy-done.35) | copy-start | bytes 147460
  210.7 6.0 collective-permute-start.18
  213.8 7.0 collective-permute-start.19
  221.6 7.8 %collective-permute-start.20 = (bf16[64,4,8]{2,1,0:T(4,128)(2,1)}, bf16[64,4,8]{2,1,0:T(4,128)(2,1)}, u32[]{:S(2)}, u32[]{:S(2)}) collective-permute-start(bf16[64,4,8]{2,1,0:T(4,128)(2,1)} %get-tuple-element.235), channel_id=1, source_target_pairs={{0,1},{1,2},{2,3},{3,4},{4,5},{5,6},{6,7},{7,8},{8,9},{9,10},{10,1... | collective-permute-start | bytes 12296 | tf_op jit(solution)/shard_map/ppermute | solution.py:19
  226.3 5.3 collective-permute-start.21
  271.4 28.3 %copy-start.86 = (f32[192,128]{1,0:T(8,128)}, f32[192,128]{1,0:T(8,128)S(1)}, u32[]{:S(2)}) copy-start(f32[192,128]{1,0:T(8,128)S(1)} %fusion.22) | copy-start | bytes 294916
  273.5 35.4 %all-to-all-start.1 = ((f32[16,1,128]{2,1,0:T(1,128)}), f32[16,1,128]{2,1,0:T(1,128)S(1)}, u32[]{:S(2)}, u32[]{:S(2)}) async-start(f32[16,1,128]{2,1,0:T(1,128)} %reshape.1246), calls=%async_computation.1 | async-start | bytes 16384 | tf_op jit(solution)/shard_map/all_to_all | solution.py:197
  299.6 102.5 %reduce-scatter.2.cloned.1.call-start = ((), (), s32[]{:S(2)}) async-start(), calls=%async_computation.3 | async-start | bytes 69632 | tf_op jit(solution)/shard_map/reduce_scatter | solution.py:207
  314.3 5.0 collective-permute-start.22
  317.7 4.7 collective-permute-start.23
  328.4 74.4 %copy-start.160 = (f32[64,128]{1,0:T(8,128)S(1)}, f32[64,128]{1,0:T(8,128)}, u32[]{:S(2)}) copy-start(f32[64,128]{1,0:T(8,128)} %get-tuple-element.312) | copy-start | bytes 98308
  329.2 89.0 %copy-start.116 = (bf16[32,128]{1,0:T(8,128)(2,1)S(1)}, bf16[32,128]{1,0:T(8,128)(2,1)}, u32[]{:S(2)}) copy-start(bf16[32,128]{1,0:T(8,128)(2,1)} %copy-done.115) | copy-start | bytes 24580
  329.2 89.1 %copy-start.138 = (bf16[32,128]{1,0:T(8,128)(2,1)S(1)}, bf16[32,128]{1,0:T(8,128)(2,1)}, u32[]{:S(2)}) copy-start(bf16[32,128]{1,0:T(8,128)(2,1)} %copy-done.137) | copy-start | bytes 24580
  329.4 89.0 %copy-start.142 = (bf16[32,128]{1,0:T(8,128)(2,1)S(1)}, bf16[32,128]{1,0:T(8,128)(2,1)}, u32[]{:S(2)}) copy-start(bf16[32,128]{1,0:T(8,128)(2,1)} %copy-done.141) | copy-start | bytes 24580
  329.4 89.2 %copy-start.112 = (bf16[32,128]{1,0:T(8,128)(2,1)S(1)}, bf16[32,128]{1,0:T(8,128)(2,1)}, u32[]{:S(2)}) copy-start(bf16[32,128]{1,0:T(8,128)(2,1)} %copy-done.111) | copy-start | bytes 24580
  329.4 89.3 %copy-start.132 = (bf16[32,128]{1,0:T(8,128)(2,1)S(1)}, bf16[32,128]{1,0:T(8,128)(2,1)}, u32[]{:S(2)}) copy-start(bf16[32,128]{1,0:T(8,128)(2,1)} %copy-done.131) | copy-start | bytes 24580
  329.4 89.4 %copy-start.140 = (bf16[32,128]{1,0:T(8,128)(2,1)S(1)}, bf16[32,128]{1,0:T(8,128)(2,1)}, u32[]{:S(2)}) copy-start(bf16[32,128]{1,0:T(8,128)(2,1)} %copy-done.139) | copy-start | bytes 24580
  329.7 89.3 %copy-start.108 = (bf16[32,128]{1,0:T(8,128)(2,1)S(1)}, bf16[32,128]{1,0:T(8,128)(2,1)}, u32[]{:S(2)}) copy-start(bf16[32,128]{1,0:T(8,128)(2,1)} %copy-done.107) | copy-start | bytes 24580
  329.7 89.4 %copy-start.124 = (bf16[32,128]{1,0:T(8,128)(2,1)S(1)}, bf16[32,128]{1,0:T(8,128)(2,1)}, u32[]{:S(2)}) copy-start(bf16[32,128]{1,0:T(8,128)(2,1)} %copy-done.123) | copy-start | bytes 24580
  329.7 89.5 %copy-start.136 = (bf16[32,128]{1,0:T(8,128)(2,1)S(1)}, bf16[32,128]{1,0:T(8,128)(2,1)}, u32[]{:S(2)}) copy-start(bf16[32,128]{1,0:T(8,128)(2,1)} %copy-done.135) | copy-start | bytes 24580
  329.9 89.4 %copy-start.104 = (bf16[32,128]{1,0:T(8,128)(2,1)S(1)}, bf16[32,128]{1,0:T(8,128)(2,1)}, u32[]{:S(2)}) copy-start(bf16[32,128]{1,0:T(8,128)(2,1)} %copy-done.103) | copy-start | bytes 24580
  329.9 89.6 %copy-start.120 = (bf16[32,128]{1,0:T(8,128)(2,1)S(1)}, bf16[32,128]{1,0:T(8,128)(2,1)}, u32[]{:S(2)}) copy-start(bf16[32,128]{1,0:T(8,128)(2,1)} %copy-done.119) | copy-start | bytes 24580
  330.0 89.7 %copy-start.134 = (bf16[32,128]{1,0:T(8,128)(2,1)S(1)}, bf16[32,128]{1,0:T(8,128)(2,1)}, u32[]{:S(2)}) copy-start(bf16[32,128]{1,0:T(8,128)(2,1)} %copy-done.133) | copy-start | bytes 24580
  330.2 89.6 %copy-start.102 = (bf16[32,128]{1,0:T(8,128)(2,1)S(1)}, bf16[32,128]{1,0:T(8,128)(2,1)}, u32[]{:S(2)}) copy-start(bf16[32,128]{1,0:T(8,128)(2,1)} %copy-done.101) | copy-start | bytes 24580
  330.2 89.7 %copy-start.118 = (bf16[32,128]{1,0:T(8,128)(2,1)S(1)}, bf16[32,128]{1,0:T(8,128)(2,1)}, u32[]{:S(2)}) copy-start(bf16[32,128]{1,0:T(8,128)(2,1)} %copy-done.117) | copy-start | bytes 24580
  330.3 89.8 %copy-start.130 = (bf16[32,128]{1,0:T(8,128)(2,1)S(1)}, bf16[32,128]{1,0:T(8,128)(2,1)}, u32[]{:S(2)}) copy-start(bf16[32,128]{1,0:T(8,128)(2,1)} %copy-done.129) | copy-start | bytes 24580
  330.3 89.9 %copy-start.100 = (bf16[32,128]{1,0:T(8,128)(2,1)S(1)}, bf16[32,128]{1,0:T(8,128)(2,1)}, u32[]{:S(2)}) copy-start(bf16[32,128]{1,0:T(8,128)(2,1)} %copy-done.99) | copy-start | bytes 24580
  330.5 89.9 %copy-start.114 = (bf16[32,128]{1,0:T(8,128)(2,1)S(1)}, bf16[32,128]{1,0:T(8,128)(2,1)}, u32[]{:S(2)}) copy-start(bf16[32,128]{1,0:T(8,128)(2,1)} %copy-done.113) | copy-start | bytes 24580
  330.5 90.0 %copy-start.128 = (bf16[32,128]{1,0:T(8,128)(2,1)S(1)}, bf16[32,128]{1,0:T(8,128)(2,1)}, u32[]{:S(2)}) copy-start(bf16[32,128]{1,0:T(8,128)(2,1)} %copy-done.127) | copy-start | bytes 24580
  330.5 90.1 %copy-start.98 = (bf16[32,128]{1,0:T(8,128)(2,1)S(1)}, bf16[32,128]{1,0:T(8,128)(2,1)}, u32[]{:S(2)}) copy-start(bf16[32,128]{1,0:T(8,128)(2,1)} %copy-done.97) | copy-start | bytes 24580
  330.8 90.0 %copy-start.110 = (bf16[32,128]{1,0:T(8,128)(2,1)S(1)}, bf16[32,128]{1,0:T(8,128)(2,1)}, u32[]{:S(2)}) copy-start(bf16[32,128]{1,0:T(8,128)(2,1)} %copy-done.109) | copy-start | bytes 24580
  330.8 90.1 %copy-start.126 = (bf16[32,128]{1,0:T(8,128)(2,1)S(1)}, bf16[32,128]{1,0:T(8,128)(2,1)}, u32[]{:S(2)}) copy-start(bf16[32,128]{1,0:T(8,128)(2,1)} %copy-done.125) | copy-start | bytes 24580
  330.8 90.2 %copy-start.96 = (bf16[32,128]{1,0:T(8,128)(2,1)S(1)}, bf16[32,128]{1,0:T(8,128)(2,1)}, u32[]{:S(2)}) copy-start(bf16[32,128]{1,0:T(8,128)(2,1)} %copy-done.95) | copy-start | bytes 24580
  331.0 90.1 %copy-start.106 = (bf16[32,128]{1,0:T(8,128)(2,1)S(1)}, bf16[32,128]{1,0:T(8,128)(2,1)}, u32[]{:S(2)}) copy-start(bf16[32,128]{1,0:T(8,128)(2,1)} %copy-done.105) | copy-start | bytes 24580
  331.0 90.3 %copy-start.122 = (bf16[32,128]{1,0:T(8,128)(2,1)S(1)}, bf16[32,128]{1,0:T(8,128)(2,1)}, u32[]{:S(2)}) copy-start(bf16[32,128]{1,0:T(8,128)(2,1)} %copy-done.121) | copy-start | bytes 24580
  331.0 90.4 %copy-start.94 = (bf16[32,128]{1,0:T(8,128)(2,1)S(1)}, bf16[32,128]{1,0:T(8,128)(2,1)}, u32[]{:S(2)}) copy-start(bf16[32,128]{1,0:T(8,128)(2,1)} %copy-done.93) | copy-start | bytes 24580
  331.0 90.5 %copy-start.162 = (bf16[32,128]{1,0:T(8,128)(2,1)S(1)}, bf16[32,128]{1,0:T(8,128)(2,1)}, u32[]{:S(2)}) copy-start(bf16[32,128]{1,0:T(8,128)(2,1)} %copy-done.161) | copy-start | bytes 24580
  333.2 355.3 %all-reduce.13.cloned.1.call-start = ((), (), s32[]{:S(2)}) async-start(), calls=%async_computation.4 | async-start | bytes 4259840 | tf_op jit(solution)/shard_map/psum | solution.py:214
  403.9 17.8 %collective-permute-start.24 = (bf16[64,1,64]{2,1,0:T(2,128)(2,1)S(1)}, bf16[64,1,64]{2,1,0:T(2,128)(2,1)S(1)}, u32[]{:S(2)}, u32[]{:S(2)}) collective-permute-start(bf16[64,1,64]{2,1,0:T(2,128)(2,1)S(1)} %get-tuple-element.272), channel_id=1, source_target_pairs={{0,16},{16,32},{32,48},{48,64},{64,80},{80,96},{96,112},{112,128},... | collective-permute-start | bytes 24584 | tf_op jit(solution)/shard_map/ppermute | solution.py:19
  416.2 5.5 collective-permute-start.25
  422.0 3.7 collective-permute-start.26
  423.3 5.0 collective-permute-start.27
  (144 other events, 1236.7 us)
Sparse Core Ops, SparseCore 0:
  333.4 68.6 reduce-scatter.1
  425.8 262.6 all-reduce.12
where the time goes:
time: 705 us; the launch traced here: 700 us
  waiting for transfers between devices  308 us (44%)
  starting transfers between devices  111 us (16%)
  blocking collectives  98 us (14%)
  matrix products  87.8 us (12%)
  local copies, waits for them, and re-layouts  58.3 us (8%)
  other arithmetic  19.2 us (3%)
  between operations  17.8 us (3%)
    psum x1, waiting for transfers between devices, per_device(): grad_encoder = lax.psum(local_encoder, ('gx', 'gy'))  247 us
    psum x1, blocking collectives, per_device(): lax.psum((part_bottom * scale_low).astype(jnp.bfloat16), 'gy')  62.8 us
    ppermute x14, starting transfers between devices, extended_2(): lax.ppermute(tail, axis, [(i, (i + 1) % count) for i in range(ends)])  55.9 us
    ppermute x14, waiting for transfers between devices, extended_2(): lax.ppermute(head, axis, [((i + 1) % count, i) for i in range(ends)])  38.4 us
    all_gather x1, blocking collectives, per_device(): whole_rows = lax.all_gather(col_ext, 'gx', axis=1, tiled=True)  35.2 us
    dot_general x108, matrix products, weight_grad(): lax.dot_general(error_flat, tap_piece(shifted_set, a, b, c, row_count, co...  33.3 us
    dot_general x108, matrix products, conv_backward(): lax.dot_general(weight[:, tap_number * in_chan:(tap_number + 1) * in_chan...  32.1 us
    reshape x108, local copies, waits for them, and re-layouts, tap_piece(): return tap_slice.reshape(source.shape[0], row_count * col_count * z_depth)  30.8 us
  transfers between devices with their start and end apart: 32, of which 17 were waited for; matrix products, arithmetic and copies ran while one was open for 4% of the time, Pallas kernels for 0%

commit v1 on v0

v1 whole, which is shorter than its diff:
```python
import math

import jax
import jax.numpy as jnp
import numpy as np
from jax import lax
from jax.experimental import pallas as pl
from jax.experimental.pallas import tpu as pltpu
from jax.sharding import PartitionSpec as P

BF = jnp.bfloat16
F32 = jnp.float32


def columns(lanes, depth, split):
    col = np.arange(lanes) // depth
    return np.where(col >= split, col - lanes // depth, col), np.arange(lanes) % depth


def upsampling(coarse, fine):
    (col_c, z_c), (col_f, z_f) = (columns(*coarse), columns(*fine))
    hit = (col_c[:, None] == col_f[None, :] // 2) & (z_c[:, None] == z_f[None, :] // 2)
    return hit.astype(np.float32)


TOP = (384, 16, 20)
WIDE = (256, 8, 16)
MID = (128, 8, 12)
LOW = (128, 4, 16)


def constants():
    low_mid = upsampling(LOW, MID)
    mid_top = upsampling(MID, TOP)
    wide_low = upsampling(LOW, WIDE).T / 8.0
    tile_pool = mid_top[:64, :256].T / 8.0
    tile_pool = np.concatenate([tile_pool, tile_pool], axis=1)
    return {
        "up_low": low_mid,
        "sum_low": low_mid.T,
        "up_mid": mid_top,
        "sum_mid": mid_top.T,
        "pool_low": wide_low,
        "pool_tile": tile_pool,
    }


def dot(a, b):
    return jnp.dot(a, b, preferred_element_type=F32)


def dot_nt(a, b):
    return lax.dot_general(a, b, (((1,), (1,)), ((), ())), preferred_element_type=F32)


def dot_split(a, b):
    head = a.astype(BF)
    rest = (a - head.astype(F32)).astype(BF)
    return dot(head, b) + dot(rest, b)


def loop(count, body):
    def step(i, carry):
        body(i)
        return carry

    lax.fori_loop(0, count, step, 0)


def lane(length):
    return lax.broadcasted_iota(jnp.int32, (1, length), 1)


def inside(region, tile_cols, total_cols, index):
    lanes, depth, split = region
    col = lane(lanes) // depth
    col = jnp.where(col >= split, col - lanes // depth, col) + index * tile_cols
    return jnp.where((col >= 0) & (col < total_cols), 1.0, 0.0)


def row_ok(row, total):
    return jnp.where((row >= 0) & (row < total), 1.0, 0.0)


def depth_masks(shape, depth):
    z = lax.broadcasted_iota(jnp.int32, shape, 1) % depth
    below = jnp.where(z == depth - 1, 0.0, 1.0).astype(BF)
    above = jnp.where(z == 0, 0.0, 1.0).astype(BF)
    return below, above


def put_taps(dst, row, first, width, value, depth):
    chans, lanes = value.shape
    below, above = depth_masks(value.shape, depth)
    kinds = (value * below, value, value * above)
    for b in range(3):
        for e in range(3):
            shift = (b - 1) * depth + (e - 1)
            piece = kinds[e]
            if shift:
                piece = pltpu.roll(piece, (-shift) % lanes, 1)
            start = (3 * b + e) * width + first
            dst[row, start : start + chans, :] = piece


def sigmoid(v):
    return 1.0 / (1.0 + jnp.exp(-v))


def silu(v):
    return v * sigmoid(v)


def slope(v):
    s = sigmoid(v)
    return s * (1.0 + v * (1.0 - s))


def row_sum(ref, row, chans):
    return (
        ref[row, 0:chans, :]
        + ref[row + 1, chans : 2 * chans, :]
        + ref[row + 2, 2 * chans : 3 * chans, :]
    )


def pool_kernel(skip, cot, pool_tile, to_left, to_right):
    for r in range(4):
        to_left[r] = skip[r, :, 0:128]
        to_left[4 + r] = cot[r, :, 0:128]
        to_right[r] = skip[r, :, 128:256]
        to_right[4 + r] = cot[r, :, 128:256]
    for q in range(2):
        pooled = dot(skip[2 * q], pool_tile[...]) + dot(skip[2 * q + 1], pool_tile[...])
        pooled = pooled.astype(BF)
        to_left[8 + q] = pooled
        to_right[8 + q] = pooled


def widen_kernel(skip, cot, own, right, left, out):
    first = jnp.where(lax.broadcasted_iota(jnp.int32, (32, 128), 1) < 64, 1.0, 0.0)
    head = first.astype(BF)
    tail = (1.0 - first).astype(BF)
    for r in range(4):
        for k, tile in enumerate((skip, cot)):
            base = 12 * k + 3 * r
            out[base] = tile[r, :, 0:128]
            out[base + 1] = tile[r, :, 128:256]
            out[base + 2] = right[4 * k + r] * head + left[4 * k + r] * tail
    for q in range(2):
        out[24 + 2 * q] = own[8 + q] * head + right[8 + q] * tail
        out[25 + 2 * q] = left[8 + q] * tail


def main_kernel(sizes, scales, *refs):
    (ids, own, up, down, far_up, far_down) = refs[:6]
    (w_enc, w_bot, w_mid, w_top, t_top, t_mid) = refs[6:12]
    (up_low, sum_low, up_mid, sum_mid, pool_low) = refs[12:17]
    (feat, dskip, packed, pre_one, taps_out, g_top, g_mid, g_bot) = refs[17:25]
    (pool_s, taps_a, sum_a, act_a, pool_l, taps_b, sum_b, act_b) = refs[25:33]
    (taps_c, sum_c, act_c, pre_c, taps_d, sum_d, err_d) = refs[33:40]
    (taps_e, sum_e, err_c, stack, taps_f, sum_f) = refs[40:46]
    (rows_all, cols_all) = sizes
    (scale_top, scale_mid, scale_low) = scales
    gx, gy = ids[0], ids[1]
    rows_mid, rows_low = rows_all // 2, rows_all // 4

    sources = (
        [(far_up, 2 * k) for k in range(1, 6)]
        + [(up, 24), (up, 26), (own, 24), (own, 26), (down, 24), (down, 26)]
        + [(far_down, 2 * k) for k in range(5)]
    )
    for k, (ref, slab) in enumerate(sources):
        keep = jnp.full((32, 128), row_ok(gx * 2 + k - 7, rows_mid)).astype(BF)
        pool_s[k, :, 0:128] = ref[slab] * keep
        pool_s[k, :, 128:256] = ref[slab + 1] * keep

    def enc_taps(k):
        put_taps(taps_a, k, 0, 32, pool_s[k], 8)
        sum_a[k] = dot(w_enc[...], taps_a[k])

    loop(16, enc_taps)
    wide_in = inside(WIDE, 8, cols_all // 2, gy)

    def enc_act(k):
        value = silu(row_sum(sum_a, k, 64)) * (wide_in * row_ok(gx * 2 + k - 6, rows_mid))
        act_a[k] = value.astype(BF)

    loop(14, enc_act)
    for m in range(4):
        pre = row_sum(sum_a, m + 5, 64)
        pre_one[m] = jnp.where(lane(128) < 96, pre[:, 0:128], pre[:, 128:256])
        taps_out[m] = taps_a[m + 6, :, 0:128]

    def low_taps(k):
        pooled = dot(act_a[2 * k], pool_low[...]) + dot(act_a[2 * k + 1], pool_low[...])
        put_taps(taps_b, k, 0, 64, pooled.astype(BF), 4)
        sum_b[k] = dot(w_bot[...], taps_b[k])

    loop(7, low_taps)
    low_in = inside(LOW, 4, cols_all // 4, gy)
    mid_in = inside(MID, 8, cols_all // 2, gy)
    pick = jnp.where(lax.broadcasted_iota(jnp.int32, (64, 128), 1) < 96, 1.0, 0.0)
    near = pick.astype(BF)
    away = (1.0 - pick).astype(BF)

    def low_act(k):
        value = silu(row_sum(sum_b, k, 128)) * (low_in * row_ok(gx + k - 2, rows_low))
        act_b[k] = dot(value.astype(BF), up_low[...]).astype(BF)

    loop(5, low_act)

    def mid_taps(k):
        put_taps(taps_c, k, 0, 192, act_b[(k + 1) // 2], 8)
        narrow = act_a[k + 3, :, 0:128] * near + act_a[k + 3, :, 128:256] * away
        put_taps(taps_c, k, 128, 192, narrow, 8)
        sum_c[k] = dot(w_mid[...], taps_c[k])

    loop(8, mid_taps)

    def mid_act(k):
        pre = row_sum(sum_c, k, 64)
        pre_c[k] = pre
        value = silu(pre) * (mid_in * row_ok(gx * 2 + k - 2, rows_mid))
        act_c[k] = dot(value.astype(BF), up_mid[...]).astype(BF)

    loop(6, mid_act)

    def skip_row(kind, k):
        part = (up, own, down)[k // 4]
        base = 12 * kind + 3 * (k % 4)
        row = jnp.concatenate([part[base], part[base + 1], part[base + 2]], axis=1)
        if 4 <= k < 8:
            return row
        return row * jnp.full((32, 384), row_ok(gx * 4 + k - 4, rows_all)).astype(BF)

    for k in range(12):
        put_taps(taps_d, k, 64, 96, skip_row(0, k), 16)

    def top_taps(j):
        for half in range(2):
            put_taps(taps_d, 2 * j + half, 0, 96, act_c[j], 16)
            sum_d[2 * j + half] = dot(w_top[...], taps_d[2 * j + half])

    loop(6, top_taps)
    for k in range(10):
        pre = row_sum(sum_d, k, 32)
        s = sigmoid(pre)
        if 3 <= k < 7:
            feat[k - 3] = (pre * s)[:, 0:256].astype(BF)
        cot = skip_row(1, k + 1).astype(F32)
        err_d[k] = (cot * (s * (1.0 + pre * (1.0 - s)))).astype(BF)

    def top_back(k):
        put_taps(taps_e, k, 0, 32, err_d[k], 16)
        sum_e[k] = dot(t_top[...], taps_e[k])

    loop(10, top_back)

    total = None
    for k in range(6):
        parts = []
        for a in range(3):
            r = k - a
            own_row = 0 <= r < 4
            parts.append(err_d[r + 3, :, 0:256] if own_row else jnp.zeros((32, 256), BF))
        term = dot_nt(jnp.concatenate(parts, axis=0), taps_d[k + 3, :, 0:256])
        total = term if total is None else total + term
    g_top[...] = (total * scale_top).astype(BF)

    def mid_err(m):
        one = row_sum(sum_e, 2 * m, 96)
        two = row_sum(sum_e, 2 * m + 1, 96)
        whole = dot_split(one[0:64] + two[0:64], sum_mid[...])
        keep = mid_in * row_ok(gx * 2 + m - 1, rows_mid)
        err_c[m] = (whole * slope(pre_c[m + 1]) * keep).astype(BF)

    loop(4, mid_err)
    for r in range(4):
        dskip[r] = row_sum(sum_e, r + 2, 96)[64:96, 0:256]

    def mid_back(m):
        put_taps(taps_f, m, 0, 64, err_c[m], 8)
        sum_f[m] = dot(t_mid[...], taps_f[m])

    loop(4, mid_back)
    own_mid = jnp.where(lax.broadcasted_iota(jnp.int32, (64, 128), 1) < 64, 1.0, 0.0).astype(BF)
    for k in range(4):
        for a in range(3):
            r = k - a
            piece = err_c[r + 1] * own_mid if 0 <= r < 2 else jnp.zeros((64, 128), BF)
            stack[k, 64 * a : 64 * a + 64, :] = piece
    total = None
    for k in range(4):
        term = dot_nt(stack[k], taps_c[k + 2])
        total = term if total is None else total + term
    g_mid[...] = (total * scale_mid).astype(BF)

    one = row_sum(sum_f, 0, 192)
    two = row_sum(sum_f, 1, 192)
    whole = dot_split(one[0:128] + two[0:128], sum_low[...])
    keep = jnp.where(lane(128) < 16, 1.0, 0.0)
    err_low = (whole * slope(row_sum(sum_b, 2, 128)) * keep).astype(BF)
    packed[0:128, :] = err_low
    both = jnp.where(lane(128) < 64, one[128:192], pltpu.roll(two[128:192], 64, 1))
    packed[128:192, :] = both.astype(BF)
    for a in range(3):
        g_bot[128 * a : 128 * a + 128, :] = (dot_nt(err_low, taps_b[a + 2]) * scale_low).astype(BF)


def tail_kernel(sizes, scale_mid, *refs):
    (ids, own, up, down, up_two, down_two, pre_one, taps_in, dskip) = refs[:9]
    (t_bot, t_enc, up_low, up_mid) = refs[9:13]
    (grad_skip, g_enc) = refs[13:15]
    (taps_a, sum_a, err_s, taps_b, sum_b) = refs[15:20]
    (rows_all, cols_all) = sizes
    gx, gy = ids[0], ids[1]
    rows_mid = rows_all // 2
    mid_in = inside(MID, 8, cols_all // 2, gy)

    for k, ref in enumerate((up_two, up, own, down, down_two)):
        value = (
            ref[0, 0:128, :].astype(F32)
            + pltpu.roll(ref[2, 0:128, :].astype(F32), 16, 1)
            + pltpu.roll(ref[1, 0:128, :].astype(F32), 112, 1)
        )
        put_taps(taps_a, k, 0, 128, value.astype(BF), 4)
        sum_a[k] = dot(t_bot[...], taps_a[k])
    ups = [dot_split(row_sum(sum_a, k, 64), up_low[...]) * 0.125 for k in range(3)]
    for m in range(4):
        ref = (up, own, own, down)[m]
        odd = m % 2 == 0
        tiles = [ref[k, 128:192, :].astype(F32) for k in range(3)]
        mine, left, right = tiles
        if odd:
            mine = pltpu.roll(mine, 64, 1)
        else:
            left, right = pltpu.roll(left, 64, 1), pltpu.roll(right, 64, 1)
        at = lane(128)
        part = jnp.where(at < 64, mine, jnp.where(at < 96, right, left))
        keep = mid_in * row_ok(gx * 2 + m - 1, rows_mid)
        err = (part + ups[(m + 1) // 2]) * slope(pre_one[m]) * keep
        err = err.astype(BF)
        err_s[m] = err
        put_taps(taps_b, m, 0, 64, err, 8)
        sum_b[m] = dot(t_enc[...], taps_b[m])
    own_mid = jnp.where(lax.broadcasted_iota(jnp.int32, (64, 128), 1) < 64, 1.0, 0.0).astype(BF)
    total = None
    for k in range(4):
        parts = []
        for a in range(3):
            r = k - a
            parts.append(err_s[r + 1] * own_mid if 0 <= r < 2 else jnp.zeros((64, 128), BF))
        term = dot_nt(jnp.concatenate(parts, axis=0), taps_in[k])
        total = term if total is None else total + term
    g_enc[...] = (total * scale_mid).astype(BF)
    for q in range(2):
        fine = dot_split(row_sum(sum_b, q, 32), up_mid[:, 0:256]) * 0.125
        for half in range(2):
            r = 2 * q + half
            grad_skip[r] = (dskip[r] + fine).astype(BF)


VMEM = pl.BlockSpec(memory_space=pltpu.VMEM)
SMEM = pl.BlockSpec(memory_space=pltpu.SMEM)


def call(kernel, name, outs, scratch, scalars, *args):
    return pl.pallas_call(
        kernel,
        name=name,
        out_shape=[jax.ShapeDtypeStruct(s, d) for s, d in outs],
        in_specs=[SMEM] * scalars + [VMEM] * (len(args) - scalars),
        out_specs=[VMEM] * len(outs),
        scratch_shapes=[pltpu.VMEM(s, d) for s, d in scratch],
        compiler_params=pltpu.CompilerParams(vmem_limit_bytes=56 * 1024 * 1024),
    )(*args)


def shift(value, axis, count, step):
    return lax.ppermute(value, axis, [(i, i + step) for i in range(count) if 0 <= i + step < count])


def turn(value, axis, count, step):
    return lax.ppermute(value, axis, [(i, (i + step) % count) for i in range(count)])


def forward_weight(w):
    out, width = w.shape
    return w.reshape(out, 3, width // 3).transpose(1, 0, 2).reshape(3 * out, width // 3)


def backward_weight(w):
    out, width = w.shape
    chans = width // 27
    taps = w.reshape(out, 27, chans)[:, ::-1, :].reshape(out, 3, 9, chans)
    return taps.transpose(1, 3, 2, 0).reshape(3 * chans, 9 * out)


def tiles_of(g):
    rows, width = g.shape
    pad = -width % 128
    g = jnp.pad(g, ((0, 0), (0, pad)))
    wide = (width + pad) // 128
    return g.reshape(rows // 8, 8, wide, 128).transpose(0, 2, 1, 3).reshape(-1, 8, 128)


def from_tiles(tiles, rows, width):
    wide = -(-width // 128)
    g = tiles.reshape(rows // 8, wide, 8, 128).transpose(0, 2, 1, 3).reshape(rows, wide * 128)
    return g[:, :width]


def full_gradient(g):
    rows, width = g.shape
    out = rows // 3
    return jnp.concatenate([g[out * a : out * a + out] for a in range(3)], axis=1).astype(F32)


def solution(mesh):
    ngx, ngy = mesh.shape["gx"], mesh.shape["gy"]
    devices = ngx * ngy
    const = {k: np.asarray(v) for k, v in constants().items()}

    def per_device(skip_input, w_encoder, w_bottom, w_middle, w_upper, cotangent):
        gx, gy = lax.axis_index("gx"), lax.axis_index("gy")
        ids = jnp.stack([gx, gy]).astype(jnp.int32)
        rows_all, cols_all = 4 * ngx, 16 * ngy
        sizes = (rows_all, cols_all)
        cells = rows_all * cols_all * 16
        scales = tuple(1.0 / math.sqrt(cells // k) for k in (1, 8, 64))
        c = {k: jnp.asarray(v, BF) for k, v in const.items()}

        blocks = jnp.broadcast_to(w_bottom[None], (ngx,) + w_bottom.shape)
        w_bot = lax.all_to_all(blocks, "gx", split_axis=0, concat_axis=0, tiled=True)
        w_bot = w_bot.reshape(ngx * w_bottom.shape[0], -1)

        skip = skip_input.transpose(1, 0, 2)
        cot = cotangent.transpose(1, 0, 2)
        to_left, to_right = call(
            pool_kernel, "pool", [((10, 32, 128), BF)] * 2, [], 0, skip, cot, c["pool_tile"]
        )
        right = shift(to_left, "gy", ngy, -1)
        left = shift(to_right, "gy", ngy, 1)
        (own,) = call(
            widen_kernel, "widen", [((28, 32, 128), BF)], [], 0, skip, cot, to_left, right, left
        )
        up = turn(own, "gx", ngx, 1)
        down = turn(own, "gx", ngx, -1)
        three = jnp.concatenate([up[24:28], own[24:28], down[24:28]], axis=0)
        far_up = turn(three, "gx", ngx, 3)
        far_down = turn(three, "gx", ngx, -3)

        outs = [
            ((4, 32, 256), BF),
            ((4, 32, 256), F32),
            ((192, 128), BF),
            ((4, 64, 128), F32),
            ((4, 288, 128), BF),
            ((96, 864), BF),
            ((192, 1728), BF),
            ((384, 576), BF),
        ]
        scratch = [
            ((16, 32, 256), BF),
            ((16, 288, 256), BF),
            ((16, 192, 256), F32),
            ((14, 64, 256), BF),
            ((8, 128), BF),
            ((7, 576, 128), BF),
            ((7, 384, 128), F32),
            ((5, 128, 128), BF),
            ((8, 1728, 128), BF),
            ((8, 192, 128), F32),
            ((6, 64, 384), BF),
            ((6, 64, 128), F32),
            ((12, 864, 384), BF),
            ((12, 96, 384), F32),
            ((10, 32, 384), BF),
            ((10, 288, 384), BF),
            ((10, 288, 384), F32),
            ((4, 64, 128), BF),
            ((4, 192, 128), BF),
            ((4, 576, 128), BF),
            ((4, 576, 128), F32),
        ]
        feat, dskip, packed, pre_one, taps_one, g_top, g_mid, g_bot = call(
            lambda *refs: main_kernel(sizes, scales, *refs),
            "main",
            outs,
            scratch,
            1,
            ids,
            own,
            up,
            down,
            far_up,
            far_down,
            forward_weight(w_encoder),
            forward_weight(w_bot),
            forward_weight(w_middle),
            forward_weight(w_upper),
            backward_weight(w_upper),
            backward_weight(w_middle),
            c["up_low"],
            c["sum_low"],
            c["up_mid"],
            c["sum_mid"],
            c["pool_low"],
        )

        from_left = shift(packed, "gy", ngy, 1)
        from_right = shift(packed, "gy", ngy, -1)
        line = jnp.stack([packed, from_left, from_right])
        line_up = shift(line, "gx", ngx, 1)
        line_down = shift(line, "gx", ngx, -1)
        low = line[:, 0:128]
        low_up = shift(low, "gx", ngx, 2)
        low_down = shift(low, "gx", ngx, -2)
        grad_skip, g_enc = call(
            lambda *refs: tail_kernel(sizes, scales[1], *refs),
            "tail",
            [((4, 32, 256), BF), ((192, 288), BF)],
            [
                ((5, 1152, 128), BF),
                ((5, 192, 128), F32),
                ((4, 64, 128), BF),
                ((4, 576, 128), BF),
                ((4, 96, 128), F32),
            ],
            1,
            ids,
            line,
            line_up,
            line_down,
            low_up,
            low_down,
            pre_one,
            taps_one,
            dskip,
            backward_weight(w_bot),
            backward_weight(w_encoder),
            c["up_low"],
            c["up_mid"],
        )

        grads = (g_top, g_mid, g_bot, g_enc)
        tiles = [tiles_of(g) for g in grads]
        count = sum(t.shape[0] for t in tiles)
        spare = -count % devices
        flat = jnp.concatenate(tiles + [jnp.zeros((spare, 8, 128), BF)], axis=0)
        parts = flat.reshape(devices, -1, 128)
        parts = lax.all_to_all(parts, ("gx", "gy"), split_axis=0, concat_axis=0, tiled=True)
        mine = parts.astype(F32).sum(axis=0).astype(BF)
        spread = jnp.broadcast_to(mine[None], (devices,) + mine.shape)
        spread = lax.all_to_all(spread, ("gx", "gy"), split_axis=0, concat_axis=0, tiled=True)
        spread = spread.reshape(-1, 8, 128)
        whole = []
        start = 0
        for g, t in zip(grads, tiles):
            whole.append(from_tiles(spread[start : start + t.shape[0]], *g.shape))
            start += t.shape[0]
        full_top, full_mid, full_bot, full_enc = whole
        block = w_bottom.shape[0]
        mine_bot = full_bot.reshape(3, ngx, block, -1)
        mine_bot = lax.dynamic_index_in_dim(mine_bot, gx, 1, keepdims=False)
        mine_bot = mine_bot.reshape(3 * block, -1)
        return (
            feat.transpose(1, 0, 2),
            grad_skip.transpose(1, 0, 2),
            full_gradient(full_enc),
            full_gradient(mine_bot),
            full_gradient(full_mid),
            full_gradient(full_top),
        )

    in_specs = (P(None, "gx", "gy"), P(), P("gx", None), P(), P(), P(None, "gx", "gy"))
    out_specs = (P(None, "gx", "gy"), P(None, "gx", "gy"), P(), P("gx", None), P(), P())
    return jax.shard_map(
        per_device, mesh=mesh, in_specs=in_specs, out_specs=out_specs, check_vma=False
    )
```

time: 705 us -> 262 us (0.37)
  waiting for transfers between devices: 308 us -> 57.9 us
  matrix products: 87.8 us -> 0 us
  starting transfers between devices: 111 us -> 54.4 us
  Pallas kernels: 0 us -> 37 us
  blocking collectives: 98 us -> 70.5 us
  local copies, waits for them, and re-layouts: 58.3 us -> 35.6 us
  between operations: 17.8 us -> 1.1 us
  other arithmetic: 19.2 us -> 4.28 us
    psum x1 -> x0, waiting for transfers between devices: 247 us -> none  [per_device(): grad_encoder = lax.psum(local_encoder, ('gx', 'gy'))]
    dot_general x324 -> x0, matrix products: 87.8 us -> none  [the longest x108 33.3 us: weight_grad(): lax.dot_general(error_flat, tap_piece(shifted_set, a, b, c, row_count, co...]
    all_to_all x0 -> x1, blocking collectives: none -> 70.5 us  [per_device(): lax.all_to_all(parts, ('gx', 'gy'), split_axis=0, concat_axis=0, tiled=True)]
    psum x1 -> x0, blocking collectives: 62.8 us -> none  [per_device(): lax.psum((part_bottom * scale_low).astype(jnp.bfloat16), 'gy')]
    ppermute x28 -> x12, starting transfers between devices: 78.4 us -> 35.5 us  [the longest x8 24.6 us: shift(): lax.ppermute(value, axis, [(i, i + step) for i in range(count) if 0 <= i...]
    pallas_call x0 -> x4, Pallas kernels: none -> 37 us  [call(): pl.pallas_call(kernel, name=name, out_shape=[jax.ShapeDtypeStruct(s, d) f...]
    all_gather x1 -> x0, blocking collectives: 35.2 us -> none  [per_device(): whole_rows = lax.all_gather(col_ext, 'gx', axis=1, tiled=True)]
    reshape x118 -> x11, local copies, waits for them, and re-layouts: 33.2 us -> 8.59 us  [the longest x5 4.03 us: backward_weight(): return taps.transpose(1, 3, 2, 0).reshape(3 * chans, 9 * out)]
  transfers between devices with their start and end apart: 32 -> 14, of which waited for: 17 -> 8; matrix products, arithmetic and copies ran while one was open for 4% -> 11% of each run, Pallas kernels for 0% -> 1%
where the time goes in v1:
time: 262 us; the launch traced here: 261 us
  blocking collectives  70.5 us (27%)
  waiting for transfers between devices  57.9 us (22%)
  starting transfers between devices  54.4 us (21%)
  Pallas kernels  37 us (14%)
  local copies, waits for them, and re-layouts  35.6 us (14%)
  other arithmetic  4.28 us (2%)
    all_to_all x1, blocking collectives, per_device(): lax.all_to_all(parts, ('gx', 'gy'), split_axis=0, concat_axis=0, tiled=True)  70.5 us
    all_to_all x1, waiting for transfers between devices, per_device(): lax.all_to_all(spread, ('gx', 'gy'), split_axis=0, concat_axis=0, tiled=T...  41.9 us
    pallas_call x4, Pallas kernels, call(): pl.pallas_call(kernel, name=name, out_shape=[jax.ShapeDtypeStruct(s, d) f...  37 us
    ppermute x8, starting transfers between devices, shift(): lax.ppermute(value, axis, [(i, i + step) for i in range(count) if 0 <= i...  24.6 us
    ppermute x8, waiting for transfers between devices, shift(): lax.ppermute(value, axis, [(i, i + step) for i in range(count) if 0 <= i...  14.5 us
    all_to_all x1, starting transfers between devices, per_device(): lax.all_to_all(blocks, 'gx', split_axis=0, concat_axis=0, tiled=True)  12.6 us
    ppermute x4, starting transfers between devices, turn(): lax.ppermute(value, axis, [(i, (i + step) % count) for i in range(count)])  10.9 us
    unnamed x52, local copies, waits for them, and re-layouts  6.51 us
  transfers between devices with their start and end apart: 14, of which 8 were waited for; matrix products, arithmetic and copies ran while one was open for 11% of the time, Pallas kernels for 1%

profile of v1, /device:TPU:1, one launch (start us, length us, event | category | flops | bytes accessed | tf_op | source)
XLA Modules:
  0.0 260.8 jit_solution(10542306478830085133)
XLA Ops:
  0.6 1.6 broadcast_in_dim.6
  2.3 12.6 %all-to-all-start = ((bf16[16,8,1728]{2,1,0:T(8,128)(2,1)}), bf16[16,8,1728]{2,1,0:T(8,128)(2,1)S(1)}, u32[]{:S(2)}, u32[]{:S(2)}) async-start(bf16[16,8,1728]{2,1,0:T(8,128)(2,1)} %broadcast_in_dim.6), calls=%async_computation | async-start | bytes 917504 | tf_op jit(solution)/shard_map/all_to_all | solution.py:435
  14.9 1.5 copy_bitcast_fusion.1
  16.4 1.7 pool.1
  18.1 1.3 collective-permute-start
  19.4 4.0 %collective-permute-start.1 = (bf16[10,32,128]{2,1,0:T(8,128)(2,1)}, bf16[10,32,128]{2,1,0:T(8,128)(2,1)S(1)}, u32[]{:S(2)}, u32[]{:S(2)}) collective-permute-start(bf16[10,32,128]{2,1,0:T(8,128)(2,1)} %get-tuple-element.19), channel_id=1, source_target_pairs={{0,1},{1,2},{2,3},{3,4},{4,5},{5,6},{6,7},{7,8},{8,9},{9,10},{10,1... | collective-permute-start | bytes 245768 | tf_op jit(solution)/shard_map/ppermute | solution.py:381
  23.4 0.7 collective-permute-done.right
  24.1 1.1 collective-permute-done.1.left
  25.2 0.6 copy-done.18
  25.8 1.8 widen.1.refs_1_
  27.6 2.8 %collective-permute-start.2 = (bf16[28,32,128]{2,1,0:T(8,128)(2,1)}, bf16[28,32,128]{2,1,0:T(8,128)(2,1)}, u32[]{:S(2)}, u32[]{:S(2)}) collective-permute-start(bf16[28,32,128]{2,1,0:T(8,128)(2,1)} %widen.1.refs_1_), channel_id=1, source_target_pairs={{0,16},{16,32},{32,48},{48,64},{64,80},{80,96},{96,112},{112,128},... | collective-permute-start | bytes 688136 | tf_op jit(solution)/shard_map/ppermute | solution.py:385
  30.4 1.1 reshape.146
  31.5 0.7 reshape.139
  32.2 1.0 reshape.143
  33.2 0.9 reshape.141
  34.1 0.9 reshape.136
  35.0 0.8 copy.39
  35.8 1.1 rev.13
  37.4 0.8 copy.34
  38.2 0.9 reshape.148
  39.2 1.2 copy.36.refs_11_
  40.3 0.9 copy.29
  41.9 0.8 copy.35.refs_10_
  42.8 0.7 copy.30
  43.5 0.7 copy.27
  44.3 0.9 reshape.153.refs_10_
  45.2 0.8 slice.113
  45.9 0.8 slice.112
  46.7 0.8 slice.114
  47.5 3.3 %collective-permute-start.4 = (bf16[12,32,128]{2,1,0:T(8,128)(2,1)S(1)}, bf16[12,32,128]{2,1,0:T(8,128)(2,1)S(1)}, u32[]{:S(2)}, u32[]{:S(2)}) collective-permute-start(bf16[12,32,128]{2,1,0:T(8,128)(2,1)S(1)} %pad_maximum_fusion.1), channel_id=1, source_target_pairs={{0,48},{16,64},{32,80},{48,96},{64,112},{80,128},{96,144},{112,160... | collective-permute-start | bytes 294920 | tf_op jit(solution)/shard_map/ppermute | solution.py:385
  50.8 4.8 %collective-permute-start.5 = (bf16[12,32,128]{2,1,0:T(8,128)(2,1)S(1)}, bf16[12,32,128]{2,1,0:T(8,128)(2,1)S(1)}, u32[]{:S(2)}, u32[]{:S(2)}) collective-permute-start(bf16[12,32,128]{2,1,0:T(8,128)(2,1)S(1)} %pad_maximum_fusion.1), channel_id=1, source_target_pairs={{0,208},{16,224},{32,240},{48,0},{64,16},{80,32},{96,48},{112,64},... | collective-permute-start | bytes 294920 | tf_op jit(solution)/shard_map/ppermute | solution.py:385
  55.6 0.6 pad_add_fusion.refs_0_
  56.5 0.8 copy.28
  57.9 0.9 collective-permute-done.5.refs_5_
  58.8 0.6 copy-done.16
  59.4 29.5 %main.1 = (bf16[4,32,256]{2,1,0:T(8,128)(2,1)}, f32[4,32,256]{2,1,0:T(8,128)}, bf16[192,128]{1,0:T(8,128)(2,1)}, f32[4,64,128]{2,1,0:T(8,128)}, bf16[4,288,128]{...) custom-call(s32[2]{0:T(128)} %pad_add_fusion.refs_0_, ...), custom_call_target="tpu_custom_call" | custom-call | tf_op jit(solution)/shard_map/main/pallas_call | solution.py:369
  89.0 4.1 %collective-permute-start.6 = (bf16[192,128]{1,0:T(8,128)(2,1)}, bf16[192,128]{1,0:T(8,128)(2,1)S(1)}, u32[]{:S(2)}, u32[]{:S(2)}) collective-permute-start(bf16[192,128]{1,0:T(8,128)(2,1)} %get-tuple-element.21), channel_id=1, source_target_pairs={{0,1},{1,2},{2,3},{3,4},{4,5},{5,6},{6,7},{7,8},{8,9},{9,10},{10,1... | collective-permute-start | bytes 147464 | tf_op jit(solution)/shard_map/ppermute | solution.py:381
  93.0 1.3 collective-permute-start.7
  94.3 0.9 pad.16
  95.3 1.2 pad.17
  96.5 1.5 collective-permute-done.7
  98.1 8.7 %collective-permute-start.8 = (bf16[3,192,128]{2,1,0:T(8,128)(2,1)S(1)}, bf16[3,192,128]{2,1,0:T(8,128)(2,1)S(1)}, u32[]{:S(2)}, u32[]{:S(2)}) collective-permute-start(bf16[3,192,128]{2,1,0:T(8,128)(2,1)S(1)} %pad_maximum_fusion.refs_1_), channel_id=1, source_target_pairs={{0,16},{16,32},{32,48},{48,64},{64,80},{80,96},{96,112},{112,128},... | collective-permute-start | bytes 442376 | tf_op jit(solution)/shard_map/ppermute | solution.py:381
  106.8 1.9 collective-permute-start.9
  108.9 1.2 copy-done.1
  110.1 1.0 reshape_reshape.7
  111.1 1.0 rev.14
  112.1 1.0 copy.37
  113.5 0.9 copy.47
  114.4 2.0 collective-permute-start.10
  116.4 1.3 collective-permute-start.11
  118.0 10.9 %collective-permute-done.11.refs_5_ = bf16[3,128,128]{2,1,0:T(8,128)(2,1)S(1)} collective-permute-done((bf16[3,128,128]{2,1,0:T(8,128)(2,1)S(1)}, bf16[3,128,128]{2,1,0:T(8,128)(2,1)S(1)}, u32[]{:S(2)}, u32[]{:S(2)}) %collective-permute-start.11) | collective-permute-done | bytes 98336 | tf_op jit(solution)/shard_map/ppermute | solution.py:381
  129.0 0.6 copy-done.14
  129.7 4.0 %tail.1 = (bf16[4,32,256]{2,1,0:T(8,128)(2,1)}, bf16[192,288]{1,0:T(8,128)(2,1)}) custom-call(s32[2]{0:T(128)} %pad_add_fusion.refs_0_, bf16[3,192,128]{2,1,0:T(8,128)(2,1)} %copy-done.4, bf16[3,192,128]{2,1,0:T(8,128)(2,1)} %copy-done.11, bf16[3,192,128]{2,1,0:T(8,128)(2,1)} %copy-done.12, bf16[3,128,128]{2,1,0:T(8,128)(2,1)} %copy-done.13, ...), custom_call_target="tpu_custom_call" | custom-call | tf_op jit(solution)/shard_map/tail/pallas_call | solution.py:369
  133.7 0.9 pad.19
  134.7 70.5 %all_to_all.15 = bf16[256,24,128]{2,1,0:T(8,128)(2,1)S(1)} all-to-all(bf16[256,24,128]{2,1,0:T(8,128)(2,1)S(1)} %bitcast.100), channel_id=1, replica_groups=mesh['gx'=16,'gy'=16] {'gx','gy'}, dimensions={0} | all-to-all | bytes 3145728 | tf_op jit(solution)/shard_map/all_to_all | solution.py:553
  205.5 1.4 broadcast_in_dim.8
  206.9 6.3 %all-to-all-start.2 = ((bf16[256,24,128]{2,1,0:T(8,128)(2,1)}), bf16[256,24,128]{2,1,0:T(8,128)(2,1)S(1)}, u32[]{:S(2)}, u32[]{:S(2)}) async-start(bf16[256,24,128]{2,1,0:T(8,128)(2,1)} %broadcast_in_dim.8), calls=%async_computation.2 | async-start | bytes 3145728 | tf_op jit(solution)/shard_map/all_to_all | solution.py:556
  213.2 0.7 copy.41
  213.9 0.7 copy.42
  214.6 41.9 %all-to-all-done.2 = bf16[256,24,128]{2,1,0:T(8,128)(2,1)S(1)} async-done(((bf16[256,24,128]{2,1,0:T(8,128)(2,1)}), bf16[256,24,128]{2,1,0:T(8,128)(2,1)S(1)}, u32[]{:S(2)}, u32[]{:S(2)}) %all-to-all-start.2) | async-done | bytes 1572896 | tf_op jit(solution)/shard_map/all_to_all | solution.py:556
  256.7 0.8 convert_element_type.25
  258.0 1.2 convert_element_type.24
  259.3 0.6 convert_element_type.23
  260.0 0.8 maximum_convert_fusion
  (79 shorter events, 4.4 us)
Async XLA Ops:
  0.6 29.7 %copy-start = (bf16[64,5184]{1,0:T(8,128)(2,1)S(1)}, bf16[64,5184]{1,0:T(8,128)(2,1)}, u32[]{:S(2)}) copy-start(bf16[64,5184]{1,0:T(8,128)(2,1)} %param.15) | copy-start | bytes 1990660
  2.3 53.9 %all-to-all-start = ((bf16[16,8,1728]{2,1,0:T(8,128)(2,1)}), bf16[16,8,1728]{2,1,0:T(8,128)(2,1)S(1)}, u32[]{:S(2)}, u32[]{:S(2)}) async-start(bf16[16,8,1728]{2,1,0:T(8,128)(2,1)} %broadcast_in_dim.6), calls=%async_computation | async-start | bytes 917504 | tf_op jit(solution)/shard_map/all_to_all | solution.py:435
  18.1 6.0 %collective-permute-start = (bf16[10,32,128]{2,1,0:T(8,128)(2,1)}, bf16[10,32,128]{2,1,0:T(8,128)(2,1)S(1)}, u32[]{:S(2)}, u32[]{:S(2)}) collective-permute-start(bf16[10,32,128]{2,1,0:T(8,128)(2,1)} %get-tuple-element.18.own), channel_id=1, source_target_pairs={{1,0},{2,1},{3,2},{4,3},{5,4},{6,5},{7,6},{8,7},{9,8},{10,9},{11,1... | collective-permute-start | bytes 245768 | tf_op jit(solution)/shard_map/ppermute | solution.py:381
  19.4 5.8 %collective-permute-start.1 = (bf16[10,32,128]{2,1,0:T(8,128)(2,1)}, bf16[10,32,128]{2,1,0:T(8,128)(2,1)S(1)}, u32[]{:S(2)}, u32[]{:S(2)}) collective-permute-start(bf16[10,32,128]{2,1,0:T(8,128)(2,1)} %get-tuple-element.19), channel_id=1, source_target_pairs={{0,1},{1,2},{2,3},{3,4},{4,5},{5,6},{6,7},{7,8},{8,9},{9,10},{10,1... | collective-permute-start | bytes 245768 | tf_op jit(solution)/shard_map/ppermute | solution.py:381
  24.1 1.1 copy-start.17
  25.2 0.6 copy-start.18
  27.6 18.3 %collective-permute-start.2 = (bf16[28,32,128]{2,1,0:T(8,128)(2,1)}, bf16[28,32,128]{2,1,0:T(8,128)(2,1)}, u32[]{:S(2)}, u32[]{:S(2)}) collective-permute-start(bf16[28,32,128]{2,1,0:T(8,128)(2,1)} %widen.1.refs_1_), channel_id=1, source_target_pairs={{0,16},{16,32},{32,48},{48,64},{64,80},{80,96},{96,112},{112,128},... | collective-permute-start | bytes 688136 | tf_op jit(solution)/shard_map/ppermute | solution.py:385
  30.4 16.3 %collective-permute-start.3 = (bf16[28,32,128]{2,1,0:T(8,128)(2,1)}, bf16[28,32,128]{2,1,0:T(8,128)(2,1)}, u32[]{:S(2)}, u32[]{:S(2)}) collective-permute-start(bf16[28,32,128]{2,1,0:T(8,128)(2,1)} %widen.1.refs_1_), channel_id=1, source_target_pairs={{0,240},{16,0},{32,16},{48,32},{64,48},{80,64},{96,80},{112,96},{1... | collective-permute-start | bytes 688136 | tf_op jit(solution)/shard_map/ppermute | solution.py:385
  30.4 1.8 copy-start.8
  31.5 2.6 copy-start.10
  39.2 2.1 copy-start.3
  41.3 1.5 copy-start.5
  41.3 2.2 copy-start.7
  41.3 2.9 %copy-start.6 = (bf16[64,864]{0,1:T(8,128)(2,1)S(1)}, bf16[64,864]{0,1:T(8,128)(2,1)}, u32[]{:S(2)}) copy-start(bf16[64,864]{0,1:T(8,128)(2,1)} %copy.39) | copy-start | bytes 331780
  47.5 10.4 %collective-permute-start.4 = (bf16[12,32,128]{2,1,0:T(8,128)(2,1)S(1)}, bf16[12,32,128]{2,1,0:T(8,128)(2,1)S(1)}, u32[]{:S(2)}, u32[]{:S(2)}) collective-permute-start(bf16[12,32,128]{2,1,0:T(8,128)(2,1)S(1)} %pad_maximum_fusion.1), channel_id=1, source_target_pairs={{0,48},{16,64},{32,80},{48,96},{64,112},{80,128},{96,144},{112,160... | collective-permute-start | bytes 294920 | tf_op jit(solution)/shard_map/ppermute | solution.py:385
  50.8 8.0 %collective-permute-start.5 = (bf16[12,32,128]{2,1,0:T(8,128)(2,1)S(1)}, bf16[12,32,128]{2,1,0:T(8,128)(2,1)S(1)}, u32[]{:S(2)}, u32[]{:S(2)}) collective-permute-start(bf16[12,32,128]{2,1,0:T(8,128)(2,1)S(1)} %pad_maximum_fusion.1), channel_id=1, source_target_pairs={{0,208},{16,224},{32,240},{48,0},{64,16},{80,32},{96,48},{112,64},... | collective-permute-start | bytes 294920 | tf_op jit(solution)/shard_map/ppermute | solution.py:385
  57.9 0.9 copy-start.15
  58.8 0.6 copy-start.16
  89.0 9.1 %copy-start.21 = (bf16[192,128]{1,0:T(8,128)(2,1)S(1)}, bf16[192,128]{1,0:T(8,128)(2,1)}, u32[]{:S(2)}) copy-start(bf16[192,128]{1,0:T(8,128)(2,1)} %get-tuple-element.21) | copy-start | bytes 147460
  89.0 7.6 %collective-permute-start.6 = (bf16[192,128]{1,0:T(8,128)(2,1)}, bf16[192,128]{1,0:T(8,128)(2,1)S(1)}, u32[]{:S(2)}, u32[]{:S(2)}) collective-permute-start(bf16[192,128]{1,0:T(8,128)(2,1)} %get-tuple-element.21), channel_id=1, source_target_pairs={{0,1},{1,2},{2,3},{3,4},{4,5},{5,6},{6,7},{7,8},{8,9},{9,10},{10,1... | collective-permute-start | bytes 147464 | tf_op jit(solution)/shard_map/ppermute | solution.py:381
  93.0 5.0 %collective-permute-start.7 = (bf16[192,128]{1,0:T(8,128)(2,1)}, bf16[192,128]{1,0:T(8,128)(2,1)S(1)}, u32[]{:S(2)}, u32[]{:S(2)}) collective-permute-start(bf16[192,128]{1,0:T(8,128)(2,1)} %get-tuple-element.21), channel_id=1, source_target_pairs={{1,0},{2,1},{3,2},{4,3},{5,4},{6,5},{7,6},{8,7},{9,8},{10,9},{11,1... | collective-permute-start | bytes 147464 | tf_op jit(solution)/shard_map/ppermute | solution.py:381
  95.3 14.7 %copy-start.9 = (bf16[384,576]{1,0:T(8,128)(2,1)S(1)}, bf16[384,576]{1,0:T(8,128)(2,1)}, u32[]{:S(2)}) copy-start(bf16[384,576]{1,0:T(8,128)(2,1)} %get-tuple-element.28) | copy-start | bytes 1327108
  98.1 16.2 %copy-start.4 = (bf16[3,192,128]{2,1,0:T(8,128)(2,1)}, bf16[3,192,128]{2,1,0:T(8,128)(2,1)S(1)}, u32[]{:S(2)}) copy-start(bf16[3,192,128]{2,1,0:T(8,128)(2,1)S(1)} %pad_maximum_fusion.refs_1_) | copy-start | bytes 442372
  98.1 30.8 %collective-permute-start.8 = (bf16[3,192,128]{2,1,0:T(8,128)(2,1)S(1)}, bf16[3,192,128]{2,1,0:T(8,128)(2,1)S(1)}, u32[]{:S(2)}, u32[]{:S(2)}) collective-permute-start(bf16[3,192,128]{2,1,0:T(8,128)(2,1)S(1)} %pad_maximum_fusion.refs_1_), channel_id=1, source_target_pairs={{0,16},{16,32},{32,48},{48,64},{64,80},{80,96},{96,112},{112,128},... | collective-permute-start | bytes 442376 | tf_op jit(solution)/shard_map/ppermute | solution.py:381
  106.8 22.1 %collective-permute-start.9 = (bf16[3,192,128]{2,1,0:T(8,128)(2,1)S(1)}, bf16[3,192,128]{2,1,0:T(8,128)(2,1)S(1)}, u32[]{:S(2)}, u32[]{:S(2)}) collective-permute-start(bf16[3,192,128]{2,1,0:T(8,128)(2,1)S(1)} %pad_maximum_fusion.refs_1_), channel_id=1, source_target_pairs={{16,0},{32,16},{48,32},{64,48},{80,64},{96,80},{112,96},{128,112},... | collective-permute-start | bytes 442376 | tf_op jit(solution)/shard_map/ppermute | solution.py:381
  108.9 1.2 copy-start.1
  113.1 4.6 %copy-start.2 = (bf16[768,8,128]{2,1,0:T(8,128)(2,1)S(1)}, bf16[768,8,128]{2,1,0:T(8,128)(2,1)}, u32[]{:S(2)}) copy-start(bf16[768,8,128]{2,1,0:T(8,128)(2,1)} %copy-done.1) | copy-start | bytes 4718596
  114.4 3.6 %collective-permute-start.10 = (bf16[3,128,128]{2,1,0:T(8,128)(2,1)S(1)}, bf16[3,128,128]{2,1,0:T(8,128)(2,1)S(1)}, u32[]{:S(2)}, u32[]{:S(2)}) collective-permute-start(bf16[3,128,128]{2,1,0:T(8,128)(2,1)S(1)} %slice.115), channel_id=1, source_target_pairs={{0,32},{16,48},{32,64},{48,80},{64,96},{80,112},{96,128},{112,144}... | collective-permute-start | bytes 294920 | tf_op jit(solution)/shard_map/ppermute | solution.py:381
  116.4 12.6 %collective-permute-start.11 = (bf16[3,128,128]{2,1,0:T(8,128)(2,1)S(1)}, bf16[3,128,128]{2,1,0:T(8,128)(2,1)S(1)}, u32[]{:S(2)}, u32[]{:S(2)}) collective-permute-start(bf16[3,128,128]{2,1,0:T(8,128)(2,1)S(1)} %slice.115), channel_id=1, source_target_pairs={{32,0},{48,16},{64,32},{80,48},{96,64},{112,80},{128,96},{144,112}... | collective-permute-start | bytes 294920 | tf_op jit(solution)/shard_map/ppermute | solution.py:381
  118.0 11.0 %copy-start.13 = (bf16[3,128,128]{2,1,0:T(8,128)(2,1)}, bf16[3,128,128]{2,1,0:T(8,128)(2,1)S(1)}, u32[]{:S(2)}) copy-start(bf16[3,128,128]{2,1,0:T(8,128)(2,1)S(1)} %collective-permute-done.10.refs_4_) | copy-start | bytes 294916
  129.0 0.6 copy-start.14
  129.0 0.7 copy-start.11
  129.0 0.8 copy-start.12
  206.9 6.3 %copy-start.19 = (bf16[4,32,256]{2,1,0:T(8,128)(2,1)S(1)}, bf16[4,32,256]{2,1,0:T(8,128)(2,1)}, u32[]{:S(2)}) copy-start(bf16[4,32,256]{2,1,0:T(8,128)(2,1)} %get-tuple-element.20) | copy-start | bytes 196612
  206.9 7.0 %copy-start.20 = (bf16[4,32,256]{2,1,0:T(8,128)(2,1)S(1)}, bf16[4,32,256]{2,1,0:T(8,128)(2,1)}, u32[]{:S(2)}) copy-start(bf16[4,32,256]{2,1,0:T(8,128)(2,1)} %get-tuple-element.25) | copy-start | bytes 196612
  206.9 49.6 %all-to-all-start.2 = ((bf16[256,24,128]{2,1,0:T(8,128)(2,1)}), bf16[256,24,128]{2,1,0:T(8,128)(2,1)S(1)}, u32[]{:S(2)}, u32[]{:S(2)}) async-start(bf16[256,24,128]{2,1,0:T(8,128)(2,1)} %broadcast_in_dim.8), calls=%async_computation.2 | async-start | bytes 3145728 | tf_op jit(solution)/shard_map/all_to_all | solution.py:556

commit v2 on v1

--- a/solution.py
+++ b/solution.py
@@ -8,6 +8,8 @@
 from jax.experimental.pallas import tpu as pltpu
 from jax.sharding import PartitionSpec as P
 
+
+AXES = ("gx", "gy")
 BF = jnp.bfloat16
 F32 = jnp.float32
 
@@ -124,6 +126,12 @@
     )
 
 
+def put_padded(out, row, value):
+    rows, width = value.shape
+    out[row : row + rows, 0:width] = value.astype(BF)
+    out[row : row + rows, width:] = jnp.zeros((rows, out.shape[1] - width), BF)
+
+
 def pool_kernel(skip, cot, pool_tile, to_left, to_right):
     for r in range(4):
         to_left[r] = skip[r, :, 0:128]
@@ -137,7 +145,7 @@
         to_right[8 + q] = pooled
 
 
-def widen_kernel(skip, cot, own, right, left, out):
+def widen_kernel(skip, cot, own, right, left, weight, out, spread):
     first = jnp.where(lax.broadcasted_iota(jnp.int32, (32, 128), 1) < 64, 1.0, 0.0)
     head = first.astype(BF)
     tail = (1.0 - first).astype(BF)
@@ -147,33 +155,68 @@
             out[base] = tile[r, :, 0:128]
             out[base + 1] = tile[r, :, 128:256]
             out[base + 2] = right[4 * k + r] * head + left[4 * k + r] * tail
+    pieces = []
     for q in range(2):
-        out[24 + 2 * q] = own[8 + q] * head + right[8 + q] * tail
-        out[25 + 2 * q] = left[8 + q] * tail
+        pieces.append(own[8 + q] * head + right[8 + q] * tail)
+        pieces.append(left[8 + q] * tail)
+    for p in range(spread.shape[0]):
+        for q in range(4):
+            spread[p, q] = pieces[q]
+        for q in range(weight.shape[0]):
+            spread[p, 4 + q] = weight[q]
+
+
+def put_forward(w, out):
+    rows = w.shape[0]
+    width = out.shape[1]
+    for a in range(3):
+        out[rows * a : rows * a + rows, :] = w[:, a * width : (a + 1) * width]
+
+
+def put_backward(w, out):
+    chans = out.shape[0] // 3
+    i = lax.broadcasted_iota(jnp.int32, (chans, chans), 0)
+    j = lax.broadcasted_iota(jnp.int32, (chans, chans), 1)
+    unit = jnp.where(i == j, 1.0, 0.0).astype(BF)
+    for a in range(3):
+        taps = [26 - 9 * a - k for k in range(9)]
+        stacked = jnp.concatenate([w[:, t * chans : t * chans + chans] for t in taps], axis=0)
+        out[chans * a : chans * a + chans, :] = dot_nt(unit, stacked).astype(BF)
+
+
+def weight_kernel(forward, backward, *refs):
+    sources, outs = refs[: len(forward)], refs[len(forward) :]
+    k = 0
+    for w, fwd, bwd in zip(sources, forward, backward):
+        if fwd:
+            put_forward(w, outs[k])
+            k += 1
+        if bwd:
+            put_backward(w, outs[k])
+            k += 1
 
 
 def main_kernel(sizes, scales, *refs):
-    (ids, own, up, down, far_up, far_down) = refs[:6]
-    (w_enc, w_bot, w_mid, w_top, t_top, t_mid) = refs[6:12]
-    (up_low, sum_low, up_mid, sum_mid, pool_low) = refs[12:17]
-    (feat, dskip, packed, pre_one, taps_out, g_top, g_mid, g_bot) = refs[17:25]
-    (pool_s, taps_a, sum_a, act_a, pool_l, taps_b, sum_b, act_b) = refs[25:33]
-    (taps_c, sum_c, act_c, pre_c, taps_d, sum_d, err_d) = refs[33:40]
-    (taps_e, sum_e, err_c, stack, taps_f, sum_f) = refs[40:46]
+    (ids, own, up, down, pools) = refs[:5]
+    (w_enc, w_bot, w_mid, w_top, t_top, t_mid) = refs[5:11]
+    (up_low, sum_low, up_mid, sum_mid, pool_low) = refs[11:16]
+    (feat, dskip, packed, pre_one, taps_out, g_top, g_mid, g_bot) = refs[16:24]
+    (pool_s, taps_a, sum_a, act_a, taps_b, sum_b, act_b) = refs[24:31]
+    (taps_c, sum_c, act_c, pre_c, taps_d, sum_d, err_d) = refs[31:38]
+    (taps_e, sum_e, err_c, stack, taps_f, sum_f) = refs[38:44]
     (rows_all, cols_all) = sizes
     (scale_top, scale_mid, scale_low) = scales
     gx, gy = ids[0], ids[1]
     rows_mid, rows_low = rows_all // 2, rows_all // 4
 
-    sources = (
-        [(far_up, 2 * k) for k in range(1, 6)]
-        + [(up, 24), (up, 26), (own, 24), (own, 26), (down, 24), (down, 26)]
-        + [(far_down, 2 * k) for k in range(5)]
-    )
-    for k, (ref, slab) in enumerate(sources):
-        keep = jnp.full((32, 128), row_ok(gx * 2 + k - 7, rows_mid)).astype(BF)
-        pool_s[k, :, 0:128] = ref[slab] * keep
-        pool_s[k, :, 128:256] = ref[slab + 1] * keep
+    tiles = rows_all // 4
+    for k in range(16):
+        tile = gx + (k - 7) // 2
+        keep = jnp.full((32, 128), row_ok(tile, tiles)).astype(BF)
+        tile = jnp.clip(tile, 0, tiles - 1)
+        slab = 2 * ((k - 7) % 2)
+        pool_s[k, :, 0:128] = pools[tile, slab] * keep
+        pool_s[k, :, 128:256] = pools[tile, slab + 1] * keep
 
     def enc_taps(k):
         put_taps(taps_a, k, 0, 32, pool_s[k], 8)
@@ -229,10 +272,7 @@
     def skip_row(kind, k):
         part = (up, own, down)[k // 4]
         base = 12 * kind + 3 * (k % 4)
-        row = jnp.concatenate([part[base], part[base + 1], part[base + 2]], axis=1)
-        if 4 <= k < 8:
-            return row
-        return row * jnp.full((32, 384), row_ok(gx * 4 + k - 4, rows_all)).astype(BF)
+        return jnp.concatenate([part[base], part[base + 1], part[base + 2]], axis=1)
 
     for k in range(12):
         put_taps(taps_d, k, 64, 96, skip_row(0, k), 16)
@@ -266,7 +306,7 @@
             parts.append(err_d[r + 3, :, 0:256] if own_row else jnp.zeros((32, 256), BF))
         term = dot_nt(jnp.concatenate(parts, axis=0), taps_d[k + 3, :, 0:256])
         total = term if total is None else total + term
-    g_top[...] = (total * scale_top).astype(BF)
+    put_padded(g_top, 0, total * scale_top)
 
     def mid_err(m):
         one = row_sum(sum_e, 2 * m, 96)
@@ -294,7 +334,7 @@
     for k in range(4):
         term = dot_nt(stack[k], taps_c[k + 2])
         total = term if total is None else total + term
-    g_mid[...] = (total * scale_mid).astype(BF)
+    put_padded(g_mid, 0, total * scale_mid)
 
     one = row_sum(sum_f, 0, 192)
     two = row_sum(sum_f, 1, 192)
@@ -305,7 +345,7 @@
     both = jnp.where(lane(128) < 64, one[128:192], pltpu.roll(two[128:192], 64, 1))
     packed[128:192, :] = both.astype(BF)
     for a in range(3):
-        g_bot[128 * a : 128 * a + 128, :] = (dot_nt(err_low, taps_b[a + 2]) * scale_low).astype(BF)
+        put_padded(g_bot, 128 * a, dot_nt(err_low, taps_b[a + 2]) * scale_low)
 
 
 def tail_kernel(sizes, scale_mid, *refs):
@@ -353,7 +393,13 @@
             parts.append(err_s[r + 1] * own_mid if 0 <= r < 2 else jnp.zeros((64, 128), BF))
         term = dot_nt(jnp.concatenate(parts, axis=0), taps_in[k])
         total = term if total is None else total + term
-    g_enc[...] = (total * scale_mid).astype(BF)
+    total = (total * scale_mid).astype(BF)
+    g_enc[0:192, :] = total[:, 0:128]
+    g_enc[192:384, :] = total[:, 128:256]
+    rest = [total[48 * q : 48 * q + 48, 256:288] for q in range(4)]
+    g_enc[384:432, :] = jnp.concatenate(rest, axis=1)
+    if g_enc.shape[0] > 432:
+        g_enc[432:, :] = jnp.zeros((g_enc.shape[0] - 432, 128), BF)
     for q in range(2):
         fine = dot_split(row_sum(sum_b, q, 32), up_mid[:, 0:256]) * 0.125
         for half in range(2):
@@ -361,19 +407,30 @@
             grad_skip[r] = (dskip[r] + fine).astype(BF)
 
 
+def finish_kernel(g, out):
+    rest = jnp.concatenate([g[384:432, 32 * q : 32 * q + 32] for q in range(4)], axis=0)
+    pieces = []
+    for a in range(3):
+        at = 64 * a
+        pieces += [g[at : at + 64, :], g[192 + at : 256 + at, :], rest[at : at + 64, :]]
+    out[...] = jnp.concatenate(pieces, axis=1).astype(F32)
+
+
 VMEM = pl.BlockSpec(memory_space=pltpu.VMEM)
 SMEM = pl.BlockSpec(memory_space=pltpu.SMEM)
 
 
-def call(kernel, name, outs, scratch, scalars, *args):
+def call(kernel, outs, scratch, scalars, *args, cost=1):
     return pl.pallas_call(
         kernel,
-        name=name,
         out_shape=[jax.ShapeDtypeStruct(s, d) for s, d in outs],
         in_specs=[SMEM] * scalars + [VMEM] * (len(args) - scalars),
         out_specs=[VMEM] * len(outs),
         scratch_shapes=[pltpu.VMEM(s, d) for s, d in scratch],
         compiler_params=pltpu.CompilerParams(vmem_limit_bytes=56 * 1024 * 1024),
+        cost_estimate=pl.CostEstimate(
+            flops=cost * 500_000_000, bytes_accessed=cost * 1_000_000, transcendentals=0
+        ),
     )(*args)
 
 
@@ -381,28 +438,9 @@
     return lax.ppermute(value, axis, [(i, i + step) for i in range(count) if 0 <= i + step < count])
 
 
-def turn(value, axis, count, step):
-    return lax.ppermute(value, axis, [(i, (i + step) % count) for i in range(count)])
-
-
-def forward_weight(w):
-    out, width = w.shape
-    return w.reshape(out, 3, width // 3).transpose(1, 0, 2).reshape(3 * out, width // 3)
-
-
-def backward_weight(w):
-    out, width = w.shape
-    chans = width // 27
-    taps = w.reshape(out, 27, chans)[:, ::-1, :].reshape(out, 3, 9, chans)
-    return taps.transpose(1, 3, 2, 0).reshape(3 * chans, 9 * out)
-
-
 def tiles_of(g):
     rows, width = g.shape
-    pad = -width % 128
-    g = jnp.pad(g, ((0, 0), (0, pad)))
-    wide = (width + pad) // 128
-    return g.reshape(rows // 8, 8, wide, 128).transpose(0, 2, 1, 3).reshape(-1, 8, 128)
+    return g.reshape(rows // 8, 8, width // 128, 128).transpose(0, 2, 1, 3).reshape(-1, 8, 128)
 
 
 def from_tiles(tiles, rows, width):
@@ -412,7 +450,7 @@
 
 
 def full_gradient(g):
-    rows, width = g.shape
+    rows, _ = g.shape
     out = rows // 3
     return jnp.concatenate([g[out * a : out * a + out] for a in range(3)], axis=1).astype(F32)
 
@@ -422,7 +460,7 @@
     devices = ngx * ngy
     const = {k: np.asarray(v) for k, v in constants().items()}
 
-    def per_device(skip_input, w_encoder, w_bottom, w_middle, w_upper, cotangent):
+    def step(skip_input, w_encoder, w_bottom, w_middle, w_upper, cotangent):
         gx, gy = lax.axis_index("gx"), lax.axis_index("gy")
         ids = jnp.stack([gx, gy]).astype(jnp.int32)
         rows_all, cols_all = 4 * ngx, 16 * ngy
@@ -431,25 +469,61 @@
         scales = tuple(1.0 / math.sqrt(cells // k) for k in (1, 8, 64))
         c = {k: jnp.asarray(v, BF) for k, v in const.items()}
 
-        blocks = jnp.broadcast_to(w_bottom[None], (ngx,) + w_bottom.shape)
-        w_bot = lax.all_to_all(blocks, "gx", split_axis=0, concat_axis=0, tiled=True)
-        w_bot = w_bot.reshape(ngx * w_bottom.shape[0], -1)
+        block, width = w_bottom.shape
+        slabs = block * 2048 // 4096
+        weight = jnp.pad(w_bottom, ((0, 0), (0, 2048 - width)))
+        lanes = weight.shape[1] // 128
+        weight = weight.reshape(block, lanes, 128).transpose(1, 0, 2).reshape(slabs, 32, 128)
 
         skip = skip_input.transpose(1, 0, 2)
         cot = cotangent.transpose(1, 0, 2)
         to_left, to_right = call(
-            pool_kernel, "pool", [((10, 32, 128), BF)] * 2, [], 0, skip, cot, c["pool_tile"]
+            pool_kernel, [((10, 32, 128), BF)] * 2, [], 0, skip, cot, c["pool_tile"]
         )
         right = shift(to_left, "gy", ngy, -1)
         left = shift(to_right, "gy", ngy, 1)
-        (own,) = call(
-            widen_kernel, "widen", [((28, 32, 128), BF)], [], 0, skip, cot, to_left, right, left
-        )
-        up = turn(own, "gx", ngx, 1)
-        down = turn(own, "gx", ngx, -1)
-        three = jnp.concatenate([up[24:28], own[24:28], down[24:28]], axis=0)
-        far_up = turn(three, "gx", ngx, 3)
-        far_down = turn(three, "gx", ngx, -3)
+        own, spread = call(
+            widen_kernel,
+            [((24, 32, 128), BF), ((ngx, 4 + slabs, 32, 128), BF)],
+            [],
+            0,
+            skip,
+            cot,
+            to_left,
+            right,
+            left,
+            weight,
+        )
+        up = shift(own, "gx", ngx, 1)
+        down = shift(own, "gx", ngx, -1)
+        pools = lax.all_to_all(spread, "gx", split_axis=0, concat_axis=0, tiled=True)
+        w_all = pools[:, 4:].reshape(ngx, lanes, block, 128).transpose(0, 2, 1, 3)
+        w_all = w_all.reshape(ngx * block, lanes * 128)[:, :width]
+        w_enc, t_enc, w_mid, t_mid, w_top, t_top = call(
+            lambda *refs: weight_kernel((1, 1, 1), (1, 1, 1), *refs),
+            [
+                ((192, 288), BF),
+                ((96, 576), BF),
+                ((192, 1728), BF),
+                ((576, 576), BF),
+                ((96, 864), BF),
+                ((288, 288), BF),
+            ],
+            [],
+            0,
+            w_encoder,
+            w_middle,
+            w_upper,
+            cost=4,
+        )
+        w_bot, t_bot = call(
+            lambda *refs: weight_kernel((1,), (1,), *refs),
+            [((384, 576), BF), ((192, 1152), BF)],
+            [],
+            0,
+            w_all,
+            cost=2,
+        )
 
         outs = [
             ((4, 32, 256), BF),
@@ -457,16 +531,15 @@
             ((192, 128), BF),
             ((4, 64, 128), F32),
             ((4, 288, 128), BF),
-            ((96, 864), BF),
-            ((192, 1728), BF),
-            ((384, 576), BF),
+            ((96, 896), BF),
+            ((192, 1792), BF),
+            ((384, 640), BF),
         ]
         scratch = [
             ((16, 32, 256), BF),
             ((16, 288, 256), BF),
             ((16, 192, 256), F32),
             ((14, 64, 256), BF),
-            ((8, 128), BF),
             ((7, 576, 128), BF),
             ((7, 384, 128), F32),
             ((5, 128, 128), BF),
@@ -486,7 +559,6 @@
         ]
         feat, dskip, packed, pre_one, taps_one, g_top, g_mid, g_bot = call(
             lambda *refs: main_kernel(sizes, scales, *refs),
-            "main",
             outs,
             scratch,
             1,
@@ -494,20 +566,32 @@
             own,
             up,
             down,
-            far_up,
-            far_down,
-            forward_weight(w_encoder),
-            forward_weight(w_bot),
-            forward_weight(w_middle),
-            forward_weight(w_upper),
-            backward_weight(w_upper),
-            backward_weight(w_middle),
+            pools,
+            w_enc,
+            w_bot,
+            w_mid,
+            w_top,
+            t_top,
+            t_mid,
             c["up_low"],
             c["sum_low"],
             c["up_mid"],
             c["sum_mid"],
             c["pool_low"],
-        )
+            cost=20,
+        )
+
+        def scatter(pairs):
+            pairs = lax.all_to_all(pairs, AXES, split_axis=0, concat_axis=0, tiled=True)
+            pairs = pairs.reshape(devices, -1, 2, 128)
+            return pairs.astype(F32).sum(axis=0).astype(BF)
+
+        grads = ((g_top, 864), (g_mid, 1728), (g_bot, 576))
+        tiles = [tiles_of(g) for g, _ in grads]
+        used = 4 * sum(t.shape[0] for t in tiles)
+        flat = [t.reshape(-1, 2, 128) for t in tiles]
+        flat = jnp.concatenate(flat + [jnp.zeros((-used % devices, 2, 128), BF)], axis=0)
+        mine_main = scatter(flat)
 
         from_left = shift(packed, "gy", ngy, 1)
         from_right = shift(packed, "gy", ngy, -1)
@@ -519,8 +603,7 @@
         low_down = shift(low, "gx", ngx, -2)
         grad_skip, g_enc = call(
             lambda *refs: tail_kernel(sizes, scales[1], *refs),
-            "tail",
-            [((4, 32, 256), BF), ((192, 288), BF)],
+            [((4, 32, 256), BF), ((432 + 2 * (-216 % devices), 128), BF)],
             [
                 ((5, 1152, 128), BF),
                 ((5, 192, 128), F32),
@@ -538,37 +621,36 @@
             pre_one,
             taps_one,
             dskip,
-            backward_weight(w_bot),
-            backward_weight(w_encoder),
+            t_bot,
+            t_enc,
             c["up_low"],
             c["up_mid"],
-        )
-
-        grads = (g_top, g_mid, g_bot, g_enc)
-        tiles = [tiles_of(g) for g in grads]
-        count = sum(t.shape[0] for t in tiles)
-        spare = -count % devices
-        flat = jnp.concatenate(tiles + [jnp.zeros((spare, 8, 128), BF)], axis=0)
-        parts = flat.reshape(devices, -1, 128)
-        parts = lax.all_to_all(parts, ("gx", "gy"), split_axis=0, concat_axis=0, tiled=True)
-        mine = parts.astype(F32).sum(axis=0).astype(BF)
-        spread = jnp.broadcast_to(mine[None], (devices,) + mine.shape)
-        spread = lax.all_to_all(spread, ("gx", "gy"), split_axis=0, concat_axis=0, tiled=True)
-        spread = spread.reshape(-1, 8, 128)
-        whole = []
+            cost=4,
+        )
+
+        mine_enc = scatter(g_enc.reshape(-1, 2, 128))
+        share = mine_main.shape[0]
+        mine = jnp.concatenate([mine_main, mine_enc], axis=0)
+        spread = jnp.broadcast_to(mine[None], (devices,) + mine.shape).reshape(-1, 2, 128)
+        spread = lax.all_to_all(spread, AXES, split_axis=0, concat_axis=0, tiled=True)
+        spread = spread.reshape(devices, -1, 2, 128)
+        full_enc = spread[:, share:].reshape(-1, 128)
+        whole = spread[:, :share].reshape(-1, 2, 128)[:used].reshape(-1, 8, 128)
+        (full_enc,) = call(finish_kernel, [((64, 864), F32)], [], 0, full_enc)
+
+        full = []
         start = 0
-        for g, t in zip(grads, tiles):
-            whole.append(from_tiles(spread[start : start + t.shape[0]], *g.shape))
+        for (g, width), t in zip(grads, tiles):
+            full.append(from_tiles(whole[start : start + t.shape[0]], g.shape[0], width))
             start += t.shape[0]
-        full_top, full_mid, full_bot, full_enc = whole
-        block = w_bottom.shape[0]
+        full_top, full_mid, full_bot = full
         mine_bot = full_bot.reshape(3, ngx, block, -1)
         mine_bot = lax.dynamic_index_in_dim(mine_bot, gx, 1, keepdims=False)
         mine_bot = mine_bot.reshape(3 * block, -1)
         return (
             feat.transpose(1, 0, 2),
             grad_skip.transpose(1, 0, 2),
-            full_gradient(full_enc),
+            full_enc,
             full_gradient(mine_bot),
             full_gradient(full_mid),
             full_gradient(full_top),
@@ -576,6 +658,4 @@
 
     in_specs = (P(None, "gx", "gy"), P(), P("gx", None), P(), P(), P(None, "gx", "gy"))
     out_specs = (P(None, "gx", "gy"), P(None, "gx", "gy"), P(), P("gx", None), P(), P())
-    return jax.shard_map(
-        per_device, mesh=mesh, in_specs=in_specs, out_specs=out_specs, check_vma=False
-    )
+    return jax.shard_map(step, mesh=mesh, in_specs=in_specs, out_specs=out_specs, check_vma=False)

time: 262 us -> 310 us (1.18)
  blocking collectives: 70.5 us -> 0 us
  waiting for transfers between devices: 57.9 us -> 106 us
  other arithmetic: 4.28 us -> 48.8 us
  starting transfers between devices: 54.4 us -> 97 us
  local copies, waits for them, and re-layouts: 35.6 us -> 11.1 us
  Pallas kernels: 37 us -> 45.2 us
    all_to_all x1 -> x0, blocking collectives: 70.5 us -> none  [per_device(): lax.all_to_all(parts, ('gx', 'gy'), split_axis=0, concat_axis=0, tiled=True)]
    all_to_all x2 -> x4, starting transfers between devices: 18.9 us -> 72.3 us  [the longest x2 52.7 us: scatter(): pairs = lax.all_to_all(pairs, AXES, split_axis=0, concat_axis=0, tiled=True)]
    all_to_all x2 -> x4, waiting for transfers between devices: 41.9 us -> 92.1 us  [the longest x1 41.9 us: step(): lax.all_to_all(spread, AXES, split_axis=0, concat_axis=0, tiled=True)]
    concatenate x1 -> x2, other arithmetic: 0.01 us -> 43.2 us  [the longest x1 43.2 us: step(): jnp.concatenate(flat + [jnp.zeros((-used % devices, 2, 128), BF)], axis=0)]
    ppermute x4 -> x0, starting transfers between devices: 10.9 us -> none  [turn(): lax.ppermute(value, axis, [(i, (i + step) % count) for i in range(count)])]
    reshape x11 -> x0, local copies, waits for them, and re-layouts: 8.59 us -> none  [the longest x5 4.03 us: backward_weight(): return taps.transpose(1, 3, 2, 0).reshape(3 * chans, 9 * out)]
    pallas_call x4 -> x7, Pallas kernels: 37 us -> 45.2 us  [call(): pl.pallas_call(kernel, out_shape=[jax.ShapeDtypeStruct(s, d) for s, d in...]
    transpose x9 -> x1, local copies, waits for them, and re-layouts: 6.02 us -> 1.54 us  [step(): cot = cotangent.transpose(1, 0, 2)]
  transfers between devices with their start and end apart: 14 -> 14, of which waited for: 8 -> 8; matrix products, arithmetic and copies ran while one was open for 11% -> 15% of each run, Pallas kernels for 1% -> 2%
where the time goes in v2:
time: 310 us; the launch traced here: 309 us
  waiting for transfers between devices  106 us (34%)
  starting transfers between devices  97 us (31%)
  other arithmetic  48.8 us (16%)
  Pallas kernels  45.2 us (15%)
  local copies, waits for them, and re-layouts  11.1 us (4%)
    all_to_all x2, starting transfers between devices, scatter(): pairs = lax.all_to_all(pairs, AXES, split_axis=0, concat_axis=0, tiled=True)  52.7 us
    pallas_call x7, Pallas kernels, call(): pl.pallas_call(kernel, out_shape=[jax.ShapeDtypeStruct(s, d) for s, d in...  45.2 us
    concatenate x1, other arithmetic, step(): jnp.concatenate(flat + [jnp.zeros((-used % devices, 2, 128), BF)], axis=0)  43.2 us
    all_to_all x1, waiting for transfers between devices, step(): lax.all_to_all(spread, AXES, split_axis=0, concat_axis=0, tiled=True)  41.9 us
    all_to_all x2, waiting for transfers between devices, scatter(): pairs = lax.all_to_all(pairs, AXES, split_axis=0, concat_axis=0, tiled=True)  39.9 us
    ppermute x10, starting transfers between devices, shift(): lax.ppermute(value, axis, [(i, i + step) for i in range(count) if 0 <= i...  24.7 us
    ppermute x10, waiting for transfers between devices, shift(): lax.ppermute(value, axis, [(i, i + step) for i in range(count) if 0 <= i...  13.5 us
    all_to_all x1, starting transfers between devices, step(): lax.all_to_all(spread, 'gx', split_axis=0, concat_axis=0, tiled=True)  13.2 us
  transfers between devices with their start and end apart: 14, of which 8 were waited for; matrix products, arithmetic and copies ran while one was open for 15% of the time, Pallas kernels for 2%

profile of v2, /device:TPU:1, one launch (start us, length us, event | category | flops | bytes accessed | tf_op | source)
XLA Modules:
  0.0 308.7 jit_solution(3778724263063354985)
XLA Ops:
  0.6 0.0 copy-start.7
  0.6 1.5 copy_bitcast_fusion
  2.2 1.7 shard_map.163
  3.9 1.3 collective-permute-start
  5.2 4.6 %collective-permute-start.1 = (bf16[10,32,128]{2,1,0:T(8,128)(2,1)}, bf16[10,32,128]{2,1,0:T(8,128)(2,1)S(1)}, u32[]{:S(2)}, u32[]{:S(2)}) collective-permute-start(bf16[10,32,128]{2,1,0:T(8,128)(2,1)} %get-tuple-element.29), channel_id=1, source_target_pairs={{0,1},{1,2},{2,3},{3,4},{4,5},{5,6},{6,7},{7,8},{8,9},{9,10},{10,1... | collective-permute-start | bytes 245768 | tf_op jit(solution)/shard_map/ppermute | solution.py:438
  9.8 0.6 pad.4
  10.4 0.0 collective-permute-done.right
  10.4 1.1 collective-permute-done.1.left
  11.6 0.6 copy-done.16
  12.2 2.2 shard_map.164
  14.4 13.2 %all-to-all-start = ((bf16[16,8,32,128]{3,2,1,0:T(8,128)(2,1)}), bf16[16,8,32,128]{3,2,1,0:T(8,128)(2,1)S(1)}, u32[]{:S(2)}, u32[]{:S(2)}) async-start(bf16[16,8,32,128]{3,2,1,0:T(8,128)(2,1)} %get-tuple-element.31), calls=%async_computation | async-start | bytes 2097152 | tf_op jit(solution)/shard_map/all_to_all | solution.py:499
  27.5 3.2 %shard_map.165 = (bf16[192,288]{1,0:T(8,128)(2,1)}, bf16[96,576]{1,0:T(8,128)(2,1)}, bf16[192,1728]{1,0:T(8,128)(2,1)}, bf16[576,576]{1,0:T(8,128)(2,1)}, bf16[9...) custom-call(bf16[64,864]{1,0:T(8,128)(2,1)} %refs_0_.1, bf16[64,5184]{1,0:T(8,128)(2,1)} %refs_1_.1, bf16[32,2592]{1,0:T(8,128)(2,1)} %refs_2_.1), custom_call_target="tpu_custom_call" | custom-call | flops 2000000000 | bytes 4000000 | tf_op jit(solution)/shard_map/pallas_call | solution.py:424
  30.8 0.0 copy-done.8
  30.8 3.5 %collective-permute-start.2 = (bf16[24,32,128]{2,1,0:T(8,128)(2,1)S(1)}, bf16[24,32,128]{2,1,0:T(8,128)(2,1)S(1)}, u32[]{:S(2)}, u32[]{:S(2)}) collective-permute-start(bf16[24,32,128]{2,1,0:T(8,128)(2,1)S(1)} %copy-done.8), channel_id=1, source_target_pairs={{0,16},{16,32},{32,48},{48,64},{64,80},{80,96},{96,112},{112,128},... | collective-permute-start | bytes 589832 | tf_op jit(solution)/shard_map/ppermute | solution.py:438
  34.3 1.9 collective-permute-start.3
  36.2 0.6 pad_add_fusion.refs_0_
  36.8 10.3 %all-to-all-done.refs_4_ = bf16[16,8,32,128]{3,2,1,0:T(8,128)(2,1)S(1)} async-done(((bf16[16,8,32,128]{3,2,1,0:T(8,128)(2,1)}), bf16[16,8,32,128]{3,2,1,0:T(8,128)(2,1)S(1)}, u32[]{:S(2)}, u32[]{:S(2)}) %all-to-all-start) | async-done | bytes 1048608 | tf_op jit(solution)/shard_map/all_to_all | solution.py:499
  47.2 0.9 slice.96.refs_0_
  48.1 2.5 shard_map.166
  50.6 0.0 collective-permute-done.2.refs_2_
  50.6 0.0 collective-permute-done.3.refs_3_
  50.6 0.6 copy-done.9
  51.3 0.1 copy-done.10
  51.4 29.7 %shard_map.167 = (bf16[4,32,256]{2,1,0:T(8,128)(2,1)}, f32[4,32,256]{2,1,0:T(8,128)}, bf16[192,128]{1,0:T(8,128)(2,1)}, f32[4,64,128]{2,1,0:T(8,128)}, bf16[4,28...) custom-call(s32[2]{0:T(128)} %pad_add_fusion.refs_0_, ...), custom_call_target="tpu_custom_call" | custom-call | flops 10000000000 | bytes 20000000 | tf_op jit(solution)/shard_map/pallas_call | solution.py:424
  81.1 3.9 %collective-permute-start.4 = (bf16[192,128]{1,0:T(8,128)(2,1)}, bf16[192,128]{1,0:T(8,128)(2,1)S(1)}, u32[]{:S(2)}, u32[]{:S(2)}) collective-permute-start(bf16[192,128]{1,0:T(8,128)(2,1)} %get-tuple-element.39), channel_id=1, source_target_pairs={{0,1},{1,2},{2,3},{3,4},{4,5},{5,6},{6,7},{7,8},{8,9},{9,10},{10,1... | collective-permute-start | bytes 147464 | tf_op jit(solution)/shard_map/ppermute | solution.py:438
  85.0 1.3 collective-permute-start.5
  86.3 0.2 collective-permute-done.4
  86.5 5.5 %collective-permute-done.5 = bf16[192,128]{1,0:T(8,128)(2,1)S(1)} collective-permute-done((bf16[192,128]{1,0:T(8,128)(2,1)}, bf16[192,128]{1,0:T(8,128)(2,1)S(1)}, u32[]{:S(2)}, u32[]{:S(2)}) %collective-permute-start.5) | collective-permute-done | bytes 49184 | tf_op jit(solution)/shard_map/ppermute | solution.py:438
  92.0 0.8 pad_maximum_fusion.refs_1_
  92.8 0.0 copy-start.3
  92.8 1.9 collective-permute-start.6
  94.7 3.4 %collective-permute-start.7 = (bf16[3,192,128]{2,1,0:T(8,128)(2,1)S(1)}, bf16[3,192,128]{2,1,0:T(8,128)(2,1)S(1)}, u32[]{:S(2)}, u32[]{:S(2)}) collective-permute-start(bf16[3,192,128]{2,1,0:T(8,128)(2,1)S(1)} %pad_maximum_fusion.refs_1_), channel_id=1, source_target_pairs={{16,0},{32,16},{48,32},{64,48},{80,64},{96,80},{112,96},{128,112},... | collective-permute-start | bytes 442376 | tf_op jit(solution)/shard_map/ppermute | solution.py:438
  98.2 1.5 collective-permute-start.8
  99.7 1.3 collective-permute-start.9
  101.0 0.1 pad.10.clone
  101.1 0.2 collective-permute-done.8.refs_4_
  101.3 6.5 %collective-permute-done.9.refs_5_ = bf16[3,128,128]{2,1,0:T(8,128)(2,1)S(1)} collective-permute-done((bf16[3,128,128]{2,1,0:T(8,128)(2,1)S(1)}, bf16[3,128,128]{2,1,0:T(8,128)(2,1)S(1)}, u32[]{:S(2)}, u32[]{:S(2)}) %collective-permute-start.9) | collective-permute-done | bytes 98336 | tf_op jit(solution)/shard_map/ppermute | solution.py:438
  107.8 0.0 collective-permute-done.6.refs_2_
  107.8 0.0 collective-permute-done.7.refs_3_
  107.9 0.6 copy-done.14
  108.4 0.1 copy-done.11
  108.5 0.1 copy-done.12
  108.6 4.1 %shard_map.168 = (bf16[4,32,256]{2,1,0:T(8,128)(2,1)}, bf16[512,128]{1,0:T(8,128)(2,1)}) custom-call(s32[2]{0:T(128)} %pad_add_fusion.refs_0_, bf16[3,192,128]{2,1,0:T(8,128)(2,1)} %copy-done.3, bf16[3,192,128]{2,1,0:T(8,128)(2,1)} %copy-done.11, bf16[3,192,128]{2,1,0:T(8,128)(2,1)} %copy-done.12, bf16[3,128,128]{2,1,0:T(8,128)(2,1)} %copy-done.13, ...), custom_call_target="tpu_custom_call" | custom-call | flops 2000000000 | bytes 4000000 | tf_op jit(solution)/shard_map/pallas_call | solution.py:424
  112.7 39.0 %all-to-all-start.2 = ((bf16[256,2,128]{2,1,0:T(2,128)(2,1)}), bf16[256,2,128]{2,1,0:T(2,128)(2,1)S(1)}, u32[]{:S(2)}, u32[]{:S(2)}) async-start(bf16[256,2,128]{2,1,0:T(2,128)(2,1)} %bitcast.80), calls=%async_computation.2 | async-start | bytes 262144 | tf_op jit(solution)/shard_map/all_to_all | solution.py:585
  151.7 43.2 %maximum_maximum_fusion = bf16[2816,2,128]{2,1,0:T(2,128)(2,1)} fusion(bf16[960,2,128]{2,1,0:T(2,128)(2,1)S(1)} %bitcast.77, bf16[1344,2,128]{2,1,0:T(2,128)(2,1)S(1)} %bitcast.74, bf16[336,2,128]{2,1,0:T(2,128)(2,1)S(1)} %bitcast.78, bf16[2816]{0:T(1024)(128)(2,1)S(1)} %pad.10.clone), kind=kLoop, calls=%fused_computation | loop fusion | flops 2162688 | bytes 2799104 | tf_op jit(solution)/shard_map/concatenate | solution.py:593
  194.9 0.0 all-to-all-done.2
  194.9 13.7 %all-to-all-start.1 = ((bf16[2816,2,128]{2,1,0:T(2,128)(2,1)}), bf16[2816,2,128]{2,1,0:T(2,128)(2,1)S(1)}, u32[]{:S(2)}, u32[]{:S(2)}) async-start(bf16[2816,2,128]{2,1,0:T(2,128)(2,1)} %maximum_maximum_fusion), calls=%async_computation.1 | async-start | bytes 2883584 | tf_op jit(solution)/shard_map/all_to_all | solution.py:585
  208.6 0.3 reduce_sum.27
  208.9 39.9 %all-to-all-done.1 = bf16[2816,2,128]{2,1,0:T(2,128)(2,1)S(1)} async-done(((bf16[2816,2,128]{2,1,0:T(2,128)(2,1)}), bf16[2816,2,128]{2,1,0:T(2,128)(2,1)S(1)}, u32[]{:S(2)}, u32[]{:S(2)}) %all-to-all-start.1) | async-done | bytes 1441824 | tf_op jit(solution)/shard_map/all_to_all | solution.py:585
  248.7 1.3 reduce_sum.26
  250.1 2.0 broadcast_in_dim.10
  252.1 6.5 %all-to-all-start.3 = ((bf16[3072,2,128]{2,1,0:T(2,128)(2,1)}), bf16[3072,2,128]{2,1,0:T(2,128)(2,1)S(1)}, u32[]{:S(2)}, u32[]{:S(2)}) async-start(bf16[3072,2,128]{2,1,0:T(2,128)(2,1)} %bitcast.27), calls=%async_computation.3 | async-start | bytes 3145728 | tf_op jit(solution)/shard_map/all_to_all | solution.py:635
  258.6 0.7 copy.24
  259.3 0.7 copy.25
  260.0 41.9 %all-to-all-done.3 = bf16[3072,2,128]{2,1,0:T(2,128)(2,1)S(1)} async-done(((bf16[3072,2,128]{2,1,0:T(2,128)(2,1)}), bf16[3072,2,128]{2,1,0:T(2,128)(2,1)S(1)}, u32[]{:S(2)}, u32[]{:S(2)}) %all-to-all-start.3) | async-done | bytes 1572896 | tf_op jit(solution)/shard_map/all_to_all | solution.py:635
  301.9 0.9 slice.99
  302.9 0.7 slice.98
  303.7 0.1 concatenate.19
  303.8 0.8 convert_element_type.17
  304.6 0.4 concatenate.18
  305.0 1.2 convert_element_type.16
  306.2 0.1 concatenate.17
  306.3 0.6 convert_element_type.8
  306.9 1.7 shard_map.169
  (35 shorter events, 0.3 us)
Async XLA Ops:
  0.6 9.1 %copy-start.7 = (bf16[8,1728]{1,0:T(8,128)(2,1)S(1)}, bf16[8,1728]{1,0:T(8,128)(2,1)}, u32[]{:S(2)}) copy-start(bf16[8,1728]{1,0:T(8,128)(2,1)} %param.14) | copy-start | bytes 82948
  3.9 6.5 %collective-permute-start = (bf16[10,32,128]{2,1,0:T(8,128)(2,1)}, bf16[10,32,128]{2,1,0:T(8,128)(2,1)S(1)}, u32[]{:S(2)}, u32[]{:S(2)}) collective-permute-start(bf16[10,32,128]{2,1,0:T(8,128)(2,1)} %get-tuple-element.28.own), channel_id=1, source_target_pairs={{1,0},{2,1},{3,2},{4,3},{5,4},{6,5},{7,6},{8,7},{9,8},{10,9},{11,1... | collective-permute-start | bytes 245768 | tf_op jit(solution)/shard_map/ppermute | solution.py:438
  5.2 6.4 %collective-permute-start.1 = (bf16[10,32,128]{2,1,0:T(8,128)(2,1)}, bf16[10,32,128]{2,1,0:T(8,128)(2,1)S(1)}, u32[]{:S(2)}, u32[]{:S(2)}) collective-permute-start(bf16[10,32,128]{2,1,0:T(8,128)(2,1)} %get-tuple-element.29), channel_id=1, source_target_pairs={{0,1},{1,2},{2,3},{3,4},{4,5},{5,6},{6,7},{7,8},{8,9},{9,10},{10,1... | collective-permute-start | bytes 245768 | tf_op jit(solution)/shard_map/ppermute | solution.py:438
  10.4 1.1 copy-start.15
  11.6 0.6 copy-start.16
  14.4 32.8 %all-to-all-start = ((bf16[16,8,32,128]{3,2,1,0:T(8,128)(2,1)}), bf16[16,8,32,128]{3,2,1,0:T(8,128)(2,1)S(1)}, u32[]{:S(2)}, u32[]{:S(2)}) async-start(bf16[16,8,32,128]{3,2,1,0:T(8,128)(2,1)} %get-tuple-element.31), calls=%async_computation | async-start | bytes 2097152 | tf_op jit(solution)/shard_map/all_to_all | solution.py:499
  27.5 3.2 %copy-start.8 = (bf16[24,32,128]{2,1,0:T(8,128)(2,1)S(1)}, bf16[24,32,128]{2,1,0:T(8,128)(2,1)}, u32[]{:S(2)}) copy-start(bf16[24,32,128]{2,1,0:T(8,128)(2,1)} %get-tuple-element.30.refs_1_) | copy-start | bytes 589828
  30.8 19.9 %collective-permute-start.2 = (bf16[24,32,128]{2,1,0:T(8,128)(2,1)S(1)}, bf16[24,32,128]{2,1,0:T(8,128)(2,1)S(1)}, u32[]{:S(2)}, u32[]{:S(2)}) collective-permute-start(bf16[24,32,128]{2,1,0:T(8,128)(2,1)S(1)} %copy-done.8), channel_id=1, source_target_pairs={{0,16},{16,32},{32,48},{48,64},{64,80},{80,96},{96,112},{112,128},... | collective-permute-start | bytes 589832 | tf_op jit(solution)/shard_map/ppermute | solution.py:438
  34.3 16.3 %collective-permute-start.3 = (bf16[24,32,128]{2,1,0:T(8,128)(2,1)S(1)}, bf16[24,32,128]{2,1,0:T(8,128)(2,1)S(1)}, u32[]{:S(2)}, u32[]{:S(2)}) collective-permute-start(bf16[24,32,128]{2,1,0:T(8,128)(2,1)S(1)} %copy-done.8), channel_id=1, source_target_pairs={{16,0},{32,16},{48,32},{64,48},{80,64},{96,80},{112,96},{128,112},... | collective-permute-start | bytes 589832 | tf_op jit(solution)/shard_map/ppermute | solution.py:438
  47.1 3.5 %copy-start = (bf16[16,8,32,128]{3,2,1,0:T(8,128)(2,1)}, bf16[16,8,32,128]{3,2,1,0:T(8,128)(2,1)S(1)}, u32[]{:S(2)}) copy-start(bf16[16,8,32,128]{3,2,1,0:T(8,128)(2,1)S(1)} %all-to-all-done.refs_4_) | copy-start | bytes 3145732
  50.6 0.7 copy-start.9
  50.6 0.7 copy-start.10
  81.1 5.4 %collective-permute-start.4 = (bf16[192,128]{1,0:T(8,128)(2,1)}, bf16[192,128]{1,0:T(8,128)(2,1)S(1)}, u32[]{:S(2)}, u32[]{:S(2)}) collective-permute-start(bf16[192,128]{1,0:T(8,128)(2,1)} %get-tuple-element.39), channel_id=1, source_target_pairs={{0,1},{1,2},{2,3},{3,4},{4,5},{5,6},{6,7},{7,8},{8,9},{9,10},{10,1... | collective-permute-start | bytes 147464 | tf_op jit(solution)/shard_map/ppermute | solution.py:438
  85.0 6.9 %collective-permute-start.5 = (bf16[192,128]{1,0:T(8,128)(2,1)}, bf16[192,128]{1,0:T(8,128)(2,1)S(1)}, u32[]{:S(2)}, u32[]{:S(2)}) collective-permute-start(bf16[192,128]{1,0:T(8,128)(2,1)} %get-tuple-element.39), channel_id=1, source_target_pairs={{1,0},{2,1},{3,2},{4,3},{5,4},{6,5},{7,6},{8,7},{9,8},{10,9},{11,1... | collective-permute-start | bytes 147464 | tf_op jit(solution)/shard_map/ppermute | solution.py:438
  92.8 15.0 %copy-start.3 = (bf16[3,192,128]{2,1,0:T(8,128)(2,1)}, bf16[3,192,128]{2,1,0:T(8,128)(2,1)S(1)}, u32[]{:S(2)}) copy-start(bf16[3,192,128]{2,1,0:T(8,128)(2,1)S(1)} %pad_maximum_fusion.refs_1_) | copy-start | bytes 442372
  92.8 15.0 %collective-permute-start.6 = (bf16[3,192,128]{2,1,0:T(8,128)(2,1)S(1)}, bf16[3,192,128]{2,1,0:T(8,128)(2,1)S(1)}, u32[]{:S(2)}, u32[]{:S(2)}) collective-permute-start(bf16[3,192,128]{2,1,0:T(8,128)(2,1)S(1)} %pad_maximum_fusion.refs_1_), channel_id=1, source_target_pairs={{0,16},{16,32},{32,48},{48,64},{64,80},{80,96},{96,112},{112,128},... | collective-permute-start | bytes 442376 | tf_op jit(solution)/shard_map/ppermute | solution.py:438
  94.7 13.1 %collective-permute-start.7 = (bf16[3,192,128]{2,1,0:T(8,128)(2,1)S(1)}, bf16[3,192,128]{2,1,0:T(8,128)(2,1)S(1)}, u32[]{:S(2)}, u32[]{:S(2)}) collective-permute-start(bf16[3,192,128]{2,1,0:T(8,128)(2,1)S(1)} %pad_maximum_fusion.refs_1_), channel_id=1, source_target_pairs={{16,0},{32,16},{48,32},{64,48},{80,64},{96,80},{112,96},{128,112},... | collective-permute-start | bytes 442376 | tf_op jit(solution)/shard_map/ppermute | solution.py:438
  98.2 3.1 %collective-permute-start.8 = (bf16[3,128,128]{2,1,0:T(8,128)(2,1)S(1)}, bf16[3,128,128]{2,1,0:T(8,128)(2,1)S(1)}, u32[]{:S(2)}, u32[]{:S(2)}) collective-permute-start(bf16[3,128,128]{2,1,0:T(8,128)(2,1)S(1)} %slice.97), channel_id=1, source_target_pairs={{0,32},{16,48},{32,64},{48,80},{64,96},{80,112},{96,128},{112,144}... | collective-permute-start | bytes 294920 | tf_op jit(solution)/shard_map/ppermute | solution.py:438
  99.7 8.1 %collective-permute-start.9 = (bf16[3,128,128]{2,1,0:T(8,128)(2,1)S(1)}, bf16[3,128,128]{2,1,0:T(8,128)(2,1)S(1)}, u32[]{:S(2)}, u32[]{:S(2)}) collective-permute-start(bf16[3,128,128]{2,1,0:T(8,128)(2,1)S(1)} %slice.97), channel_id=1, source_target_pairs={{32,0},{48,16},{64,32},{80,48},{96,64},{112,80},{128,96},{144,112}... | collective-permute-start | bytes 294920 | tf_op jit(solution)/shard_map/ppermute | solution.py:438
  101.3 6.5 %copy-start.13 = (bf16[3,128,128]{2,1,0:T(8,128)(2,1)}, bf16[3,128,128]{2,1,0:T(8,128)(2,1)S(1)}, u32[]{:S(2)}) copy-start(bf16[3,128,128]{2,1,0:T(8,128)(2,1)S(1)} %collective-permute-done.8.refs_4_) | copy-start | bytes 294916
  107.8 0.6 copy-start.14
  107.8 0.7 copy-start.11
  107.8 0.7 copy-start.12
  108.6 43.1 %copy-start.1 = (bf16[192,1792]{1,0:T(8,128)(2,1)S(1)}, bf16[192,1792]{1,0:T(8,128)(2,1)}, u32[]{:S(2)}) copy-start(bf16[192,1792]{1,0:T(8,128)(2,1)} %get-tuple-element.47) | copy-start | bytes 2064388
  108.6 43.1 %copy-start.2 = (bf16[384,640]{1,0:T(8,128)(2,1)S(1)}, bf16[384,640]{1,0:T(8,128)(2,1)}, u32[]{:S(2)}) copy-start(bf16[384,640]{1,0:T(8,128)(2,1)} %get-tuple-element.48) | copy-start | bytes 1474564
  108.6 43.1 %copy-start.4 = (bf16[96,896]{1,0:T(8,128)(2,1)S(1)}, bf16[96,896]{1,0:T(8,128)(2,1)}, u32[]{:S(2)}) copy-start(bf16[96,896]{1,0:T(8,128)(2,1)} %get-tuple-element.46) | copy-start | bytes 516100
  112.7 82.2 %all-to-all-start.2 = ((bf16[256,2,128]{2,1,0:T(2,128)(2,1)}), bf16[256,2,128]{2,1,0:T(2,128)(2,1)S(1)}, u32[]{:S(2)}, u32[]{:S(2)}) async-start(bf16[256,2,128]{2,1,0:T(2,128)(2,1)} %bitcast.80), calls=%async_computation.2 | async-start | bytes 262144 | tf_op jit(solution)/shard_map/all_to_all | solution.py:585
  194.9 53.9 %all-to-all-start.1 = ((bf16[2816,2,128]{2,1,0:T(2,128)(2,1)}), bf16[2816,2,128]{2,1,0:T(2,128)(2,1)S(1)}, u32[]{:S(2)}, u32[]{:S(2)}) async-start(bf16[2816,2,128]{2,1,0:T(2,128)(2,1)} %maximum_maximum_fusion), calls=%async_computation.1 | async-start | bytes 2883584 | tf_op jit(solution)/shard_map/all_to_all | solution.py:585
  252.1 6.5 %copy-start.5 = (bf16[4,32,256]{2,1,0:T(8,128)(2,1)S(1)}, bf16[4,32,256]{2,1,0:T(8,128)(2,1)}, u32[]{:S(2)}) copy-start(bf16[4,32,256]{2,1,0:T(8,128)(2,1)} %get-tuple-element.38) | copy-start | bytes 196612
  252.1 7.2 %copy-start.6 = (bf16[4,32,256]{2,1,0:T(8,128)(2,1)S(1)}, bf16[4,32,256]{2,1,0:T(8,128)(2,1)}, u32[]{:S(2)}) copy-start(bf16[4,32,256]{2,1,0:T(8,128)(2,1)} %get-tuple-element.45) | copy-start | bytes 196612
  252.1 49.8 %all-to-all-start.3 = ((bf16[3072,2,128]{2,1,0:T(2,128)(2,1)}), bf16[3072,2,128]{2,1,0:T(2,128)(2,1)S(1)}, u32[]{:S(2)}, u32[]{:S(2)}) async-start(bf16[3072,2,128]{2,1,0:T(2,128)(2,1)} %bitcast.27), calls=%async_computation.3 | async-start | bytes 3145728 | tf_op jit(solution)/shard_map/all_to_all | solution.py:635

commit v3 on v2

--- a/solution.py
+++ b/solution.py
@@ -7,7 +7,6 @@
 from jax.experimental import pallas as pl
 from jax.experimental.pallas import tpu as pltpu
 from jax.sharding import PartitionSpec as P
-
 
 AXES = ("gx", "gy")
 BF = jnp.bfloat16
@@ -398,8 +397,6 @@
     g_enc[192:384, :] = total[:, 128:256]
     rest = [total[48 * q : 48 * q + 48, 256:288] for q in range(4)]
     g_enc[384:432, :] = jnp.concatenate(rest, axis=1)
-    if g_enc.shape[0] > 432:
-        g_enc[432:, :] = jnp.zeros((g_enc.shape[0] - 432, 128), BF)
     for q in range(2):
         fine = dot_split(row_sum(sum_b, q, 32), up_mid[:, 0:256]) * 0.125
         for half in range(2):
@@ -581,18 +578,6 @@
             cost=20,
         )
 
-        def scatter(pairs):
-            pairs = lax.all_to_all(pairs, AXES, split_axis=0, concat_axis=0, tiled=True)
-            pairs = pairs.reshape(devices, -1, 2, 128)
-            return pairs.astype(F32).sum(axis=0).astype(BF)
-
-        grads = ((g_top, 864), (g_mid, 1728), (g_bot, 576))
-        tiles = [tiles_of(g) for g, _ in grads]
-        used = 4 * sum(t.shape[0] for t in tiles)
-        flat = [t.reshape(-1, 2, 128) for t in tiles]
-        flat = jnp.concatenate(flat + [jnp.zeros((-used % devices, 2, 128), BF)], axis=0)
-        mine_main = scatter(flat)
-
         from_left = shift(packed, "gy", ngy, 1)
         from_right = shift(packed, "gy", ngy, -1)
         line = jnp.stack([packed, from_left, from_right])
@@ -603,7 +588,7 @@
         low_down = shift(low, "gx", ngx, -2)
         grad_skip, g_enc = call(
             lambda *refs: tail_kernel(sizes, scales[1], *refs),
-            [((4, 32, 256), BF), ((432 + 2 * (-216 % devices), 128), BF)],
+            [((4, 32, 256), BF), ((432, 128), BF)],
             [
                 ((5, 1152, 128), BF),
                 ((5, 192, 128), F32),
@@ -628,22 +613,40 @@
             cost=4,
         )
 
-        mine_enc = scatter(g_enc.reshape(-1, 2, 128))
-        share = mine_main.shape[0]
-        mine = jnp.concatenate([mine_main, mine_enc], axis=0)
-        spread = jnp.broadcast_to(mine[None], (devices,) + mine.shape).reshape(-1, 2, 128)
-        spread = lax.all_to_all(spread, AXES, split_axis=0, concat_axis=0, tiled=True)
-        spread = spread.reshape(devices, -1, 2, 128)
-        full_enc = spread[:, share:].reshape(-1, 128)
-        whole = spread[:, :share].reshape(-1, 2, 128)[:used].reshape(-1, 8, 128)
-        (full_enc,) = call(finish_kernel, [((64, 864), F32)], [], 0, full_enc)
+        grads = ((g_top, 864), (g_mid, 1728), (g_bot, 576), (g_enc, 128))
+        tiles = [tiles_of(g) for g, _ in grads]
+        spare = -sum(t.shape[0] for t in tiles) % devices
+        flat = jnp.concatenate(tiles + [jnp.zeros((spare, 8, 128), BF)], axis=0)
+        half = flat.shape[0] // 2
+        core = gx % 2
+        swap = [(i, i ^ 1) for i in range(ngx)]
+        keep = lax.dynamic_slice_in_dim(flat, core * half, half, 0)
+        other = lax.dynamic_slice_in_dim(flat, (1 - core) * half, half, 0)
+        other = lax.ppermute(other, "gx", swap)
+        mine = (keep.astype(F32) + other.astype(F32)).astype(BF)
+        parts = mine.reshape(devices // 2, -1, 128)
+        groups = [[i for i in range(devices) if i // ngy % 2 == k] for k in range(2)]
+        parts = lax.all_to_all(
+            parts, AXES, split_axis=0, concat_axis=0, axis_index_groups=groups, tiled=True
+        )
+        total = parts.astype(F32).sum(axis=0).astype(BF)
+        spread = jnp.broadcast_to(total[None], parts.shape)
+        spread = lax.all_to_all(
+            spread, AXES, split_axis=0, concat_axis=0, axis_index_groups=groups, tiled=True
+        )
+        mine = spread.reshape(half, 8, 128)
+        other = lax.ppermute(mine, "gx", swap)
+        first = jnp.where(core == 0, mine, other)
+        second = jnp.where(core == 0, other, mine)
+        whole = jnp.concatenate([first, second], axis=0)
 
         full = []
         start = 0
         for (g, width), t in zip(grads, tiles):
             full.append(from_tiles(whole[start : start + t.shape[0]], g.shape[0], width))
             start += t.shape[0]
-        full_top, full_mid, full_bot = full
+        full_top, full_mid, full_bot, full_enc = full
+        (full_enc,) = call(finish_kernel, [((64, 864), F32)], [], 0, full_enc)
         mine_bot = full_bot.reshape(3, ngx, block, -1)
         mine_bot = lax.dynamic_index_in_dim(mine_bot, gx, 1, keepdims=False)
         mine_bot = mine_bot.reshape(3 * block, -1)

time: 310 us -> 224 us (0.72)
  blocking collectives: 0 us -> 94.2 us
  waiting for transfers between devices: 106 us -> 25.3 us
  starting transfers between devices: 97 us -> 42.3 us
  other arithmetic: 48.8 us -> 4.48 us
    all_to_all x0 -> x2, blocking collectives: none -> 94.2 us  [the longest x1 63.9 us: step(): lax.all_to_all(parts, AXES, split_axis=0, concat_axis=0, axis_index_group...]
    all_to_all x3 -> x0, waiting for transfers between devices: 81.8 us -> none  [the longest x1 41.9 us: step(): lax.all_to_all(spread, AXES, split_axis=0, concat_axis=0, tiled=True)]
    all_to_all x3 -> x0, starting transfers between devices: 59.2 us -> none  [the longest x2 52.7 us: scatter(): pairs = lax.all_to_all(pairs, AXES, split_axis=0, concat_axis=0, tiled=True)]
    concatenate x2 -> x1, other arithmetic: 43.2 us -> 0.06 us  [step(): whole = jnp.concatenate([first, second], axis=0)]
    ppermute x0 -> x2, starting transfers between devices: none -> 4.27 us  [the longest x1 3.74 us: step(): other = lax.ppermute(mine, 'gx', swap)]
  transfers between devices with their start and end apart: 14 -> 13, of which waited for: 8 -> 7; matrix products, arithmetic and copies ran while one was open for 15% -> 3% of each run, Pallas kernels for 2% -> 3%
where the time goes in v3:
time: 224 us; the launch traced here: 223 us
  blocking collectives  94.2 us (42%)
  Pallas kernels  45 us (20%)
  starting transfers between devices  42.3 us (19%)
  waiting for transfers between devices  25.3 us (11%)
  local copies, waits for them, and re-layouts  11.2 us (5%)
  other arithmetic  4.48 us (2%)
    all_to_all x1, blocking collectives, step(): lax.all_to_all(parts, AXES, split_axis=0, concat_axis=0, axis_index_group...  63.9 us
    pallas_call x7, Pallas kernels, call(): pl.pallas_call(kernel, out_shape=[jax.ShapeDtypeStruct(s, d) for s, d in...  45 us
    all_to_all x1, blocking collectives, step(): lax.all_to_all(spread, AXES, split_axis=0, concat_axis=0, axis_index_grou...  30.3 us
    ppermute x10, starting transfers between devices, shift(): lax.ppermute(value, axis, [(i, i + step) for i in range(count) if 0 <= i...  24.8 us
    all_to_all x1, starting transfers between devices, step(): lax.all_to_all(spread, 'gx', split_axis=0, concat_axis=0, tiled=True)  13.2 us
    ppermute x10, waiting for transfers between devices, shift(): lax.ppermute(value, axis, [(i, i + step) for i in range(count) if 0 <= i...  12.6 us
    all_to_all x1, waiting for transfers between devices, step(): lax.all_to_all(spread, 'gx', split_axis=0, concat_axis=0, tiled=True)  10.3 us
    unnamed x36, local copies, waits for them, and re-layouts  6.55 us
  transfers between devices with their start and end apart: 13, of which 7 were waited for; matrix products, arithmetic and copies ran while one was open for 3% of the time, Pallas kernels for 3%

profile of v3, /device:TPU:1, one launch (start us, length us, event | category | flops | bytes accessed | tf_op | source)
XLA Modules:
  0.0 223.4 jit_solution(12498973651704986259)
XLA Ops:
  0.6 1.5 copy_bitcast_fusion
  2.2 1.7 shard_map.163
  3.9 1.3 collective-permute-start
  5.2 4.6 %collective-permute-start.1 = (bf16[10,32,128]{2,1,0:T(8,128)(2,1)}, bf16[10,32,128]{2,1,0:T(8,128)(2,1)S(1)}, u32[]{:S(2)}, u32[]{:S(2)}) collective-permute-start(bf16[10,32,128]{2,1,0:T(8,128)(2,1)} %get-tuple-element.29), channel_id=1, source_target_pairs={{0,1},{1,2},{2,3},{3,4},{4,5},{5,6},{6,7},{7,8},{8,9},{9,10},{10,1... | collective-permute-start | bytes 245768 | tf_op jit(solution)/shard_map/ppermute | solution.py:435
  9.8 0.6 pad.4
  10.4 0.0 collective-permute-done.right
  10.4 1.1 collective-permute-done.1.left
  11.6 0.6 copy-done.14
  12.2 2.2 shard_map.164
  14.4 13.2 %all-to-all-start = ((bf16[16,8,32,128]{3,2,1,0:T(8,128)(2,1)}), bf16[16,8,32,128]{3,2,1,0:T(8,128)(2,1)S(1)}, u32[]{:S(2)}, u32[]{:S(2)}) async-start(bf16[16,8,32,128]{3,2,1,0:T(8,128)(2,1)} %get-tuple-element.31), calls=%async_computation | async-start | bytes 2097152 | tf_op jit(solution)/shard_map/all_to_all | solution.py:496
  27.5 3.2 %shard_map.165 = (bf16[192,288]{1,0:T(8,128)(2,1)}, bf16[96,576]{1,0:T(8,128)(2,1)}, bf16[192,1728]{1,0:T(8,128)(2,1)}, bf16[576,576]{1,0:T(8,128)(2,1)}, bf16[9...) custom-call(bf16[64,864]{1,0:T(8,128)(2,1)} %refs_0_.1, bf16[64,5184]{1,0:T(8,128)(2,1)} %refs_1_.1, bf16[32,2592]{1,0:T(8,128)(2,1)} %refs_2_.1), custom_call_target="tpu_custom_call" | custom-call | flops 2000000000 | bytes 4000000 | tf_op jit(solution)/shard_map/pallas_call | solution.py:421
  30.8 3.5 %collective-permute-start.2 = (bf16[24,32,128]{2,1,0:T(8,128)(2,1)S(1)}, bf16[24,32,128]{2,1,0:T(8,128)(2,1)S(1)}, u32[]{:S(2)}, u32[]{:S(2)}) collective-permute-start(bf16[24,32,128]{2,1,0:T(8,128)(2,1)S(1)} %copy-done.6), channel_id=1, source_target_pairs={{0,16},{16,32},{32,48},{48,64},{64,80},{80,96},{96,112},{112,128},... | collective-permute-start | bytes 589832 | tf_op jit(solution)/shard_map/ppermute | solution.py:435
  34.3 1.9 collective-permute-start.3
  36.2 0.6 pad_add_fusion.refs_0_
  36.8 10.3 %all-to-all-done.refs_4_ = bf16[16,8,32,128]{3,2,1,0:T(8,128)(2,1)S(1)} async-done(((bf16[16,8,32,128]{3,2,1,0:T(8,128)(2,1)}), bf16[16,8,32,128]{3,2,1,0:T(8,128)(2,1)S(1)}, u32[]{:S(2)}, u32[]{:S(2)}) %all-to-all-start) | async-done | bytes 1048608 | tf_op jit(solution)/shard_map/all_to_all | solution.py:496
  47.2 0.9 slice.89.refs_0_
  48.1 2.5 %shard_map.166 = (bf16[384,576]{1,0:T(8,128)(2,1)}, bf16[192,1152]{1,0:T(8,128)(2,1)}) custom-call(bf16[128,1728]{1,0:T(8,128)(2,1)} %slice.89.refs_0_), custom_call_target="tpu_custom_call" | custom-call | flops 1000000000 | bytes 2000000 | tf_op jit(solution)/shard_map/pallas_call | solution.py:421
  50.6 0.0 collective-permute-done.2.refs_2_
  50.6 0.7 copy-done.7
  51.2 0.1 copy-done.8
  51.3 29.7 %shard_map.167 = (bf16[4,32,256]{2,1,0:T(8,128)(2,1)}, f32[4,32,256]{2,1,0:T(8,128)}, bf16[192,128]{1,0:T(8,128)(2,1)}, f32[4,64,128]{2,1,0:T(8,128)}, bf16[4,28...) custom-call(s32[2]{0:T(128)} %pad_add_fusion.refs_0_, ...), custom_call_target="tpu_custom_call" | custom-call | flops 10000000000 | bytes 20000000 | tf_op jit(solution)/shard_map/pallas_call | solution.py:421
  81.0 4.1 %collective-permute-start.4 = (bf16[192,128]{1,0:T(8,128)(2,1)}, bf16[192,128]{1,0:T(8,128)(2,1)S(1)}, u32[]{:S(2)}, u32[]{:S(2)}) collective-permute-start(bf16[192,128]{1,0:T(8,128)(2,1)} %get-tuple-element.39), channel_id=1, source_target_pairs={{0,1},{1,2},{2,3},{3,4},{4,5},{5,6},{6,7},{7,8},{8,9},{9,10},{10,1... | collective-permute-start | bytes 147464 | tf_op jit(solution)/shard_map/ppermute | solution.py:435
  85.1 1.3 collective-permute-start.5
  86.4 0.9 constant_dynamic-update-slice_fusion.2
  87.4 4.7 %collective-permute-done.5 = bf16[192,128]{1,0:T(8,128)(2,1)S(1)} collective-permute-done((bf16[192,128]{1,0:T(8,128)(2,1)}, bf16[192,128]{1,0:T(8,128)(2,1)S(1)}, u32[]{:S(2)}, u32[]{:S(2)}) %collective-permute-start.5) | collective-permute-done | bytes 49184 | tf_op jit(solution)/shard_map/ppermute | solution.py:435
  92.1 0.8 pad_maximum_fusion.1.refs_1_
  92.9 0.0 copy-start.2
  92.9 1.9 collective-permute-start.6
  94.8 3.4 %collective-permute-start.7 = (bf16[3,192,128]{2,1,0:T(8,128)(2,1)S(1)}, bf16[3,192,128]{2,1,0:T(8,128)(2,1)S(1)}, u32[]{:S(2)}, u32[]{:S(2)}) collective-permute-start(bf16[3,192,128]{2,1,0:T(8,128)(2,1)S(1)} %pad_maximum_fusion.1.refs_1_), channel_id=1, source_target_pairs={{16,0},{32,16},{48,32},{64,48},{80,64},{96,80},{112,96},{128,112},... | collective-permute-start | bytes 442376 | tf_op jit(solution)/shard_map/ppermute | solution.py:435
  98.2 1.2 constant_dynamic-update-slice_fusion.1
  99.5 1.5 collective-permute-start.8
  101.0 1.3 collective-permute-start.9
  102.3 0.1 constant_dynamic-update-slice_fusion
  102.4 0.2 collective-permute-done.8.refs_4_
  102.6 6.5 %collective-permute-done.9.refs_5_ = bf16[3,128,128]{2,1,0:T(8,128)(2,1)S(1)} collective-permute-done((bf16[3,128,128]{2,1,0:T(8,128)(2,1)S(1)}, bf16[3,128,128]{2,1,0:T(8,128)(2,1)S(1)}, u32[]{:S(2)}, u32[]{:S(2)}) %collective-permute-start.9) | collective-permute-done | bytes 98336 | tf_op jit(solution)/shard_map/ppermute | solution.py:435
  109.1 0.0 collective-permute-done.6.refs_2_
  109.1 0.0 collective-permute-done.7.refs_3_
  109.1 0.6 copy-done.12
  109.7 0.1 copy-done.9
  109.8 0.0 copy-done.10
  109.8 4.0 %shard_map.168 = (bf16[4,32,256]{2,1,0:T(8,128)(2,1)}, bf16[432,128]{1,0:T(8,128)(2,1)}) custom-call(s32[2]{0:T(128)} %pad_add_fusion.refs_0_, bf16[3,192,128]{2,1,0:T(8,128)(2,1)} %copy-done.2, bf16[3,192,128]{2,1,0:T(8,128)(2,1)} %copy-done.9, bf16[3,192,128]{2,1,0:T(8,128)(2,1)} %copy-done.10, bf16[3,128,128]{2,1,0:T(8,128)(2,1)} %copy-done.11, ...), custom_call_target="tpu_custom_call" | custom-call | flops 2000000000 | bytes 4000000 | tf_op jit(solution)/shard_map/pallas_call | solution.py:421
  113.8 0.9 bitcast_dynamic-update-slice_fusion
  114.7 0.1 constant_dynamic-slice_fusion
  114.8 0.5 collective-permute-start.10
  115.3 1.9 collective-permute-done.10
  117.2 0.2 add_convert_fusion
  117.4 63.9 %all_to_all.15 = bf16[128,24,128]{2,1,0:T(8,128)(2,1)S(1)} all-to-all(bf16[128,24,128]{2,1,0:T(8,128)(2,1)S(1)} %bitcast.65), channel_id=1, replica_groups={{0,1,2,3,4,5,6,7,8,9,10,11,12,13,14,15,32,33,34,35,36,37,38,39,40,41,42..., dimensions={0} | all-to-all | bytes 1572864 | tf_op jit(solution)/shard_map/all_to_all | solution.py:629
  181.3 0.2 reduce_sum.12
  181.4 0.1 broadcast_in_dim.10
  181.6 30.3 %all_to_all.16 = bf16[128,24,128]{2,1,0:T(8,128)(2,1)S(1)} all-to-all(bf16[128,24,128]{2,1,0:T(8,128)(2,1)S(1)} %broadcast_in_dim.10), channel_id=1, replica_groups={{0,1,2,3,4,5,6,7,8,9,10,11,12,13,14,15,32,33,34,35,36,37,38,39,40,41,42..., dimensions={0} | all-to-all | bytes 1572864 | tf_op jit(solution)/shard_map/all_to_all | solution.py:634
  211.9 3.7 %collective-permute-start.11 = (bf16[384,8,128]{2,1,0:T(8,128)(2,1)S(1)}, bf16[384,8,128]{2,1,0:T(8,128)(2,1)S(1)}, u32[]{:S(2)}, u32[]{:S(2)}) collective-permute-start(bf16[384,8,128]{2,1,0:T(8,128)(2,1)S(1)} %bitcast.66), channel_id=1, source_target_pairs={{0,16},{16,0},{32,48},{48,32},{64,80},{80,64},{96,112},{112,96},{1... | collective-permute-start | bytes 2359304 | tf_op jit(solution)/shard_map/ppermute | solution.py:638
  215.6 0.7 copy.20
  216.3 0.7 copy.21
  217.0 0.5 collective-permute-done.11
  217.5 0.1 broadcast_select_fusion
  217.7 0.1 pad_maximum_fusion
  217.8 0.6 slice_bitcast_fusion.g
  218.4 0.1 concatenate.19
  218.6 0.8 convert_element_type.27
  219.4 0.4 concatenate.18
  219.8 1.2 convert_element_type.26
  221.0 0.1 concatenate.16
  221.0 0.6 convert_element_type.25
  221.7 1.7 shard_map.169
  (33 shorter events, 0.2 us)
Async XLA Ops:
  0.6 9.1 %copy-start.5 = (bf16[8,1728]{1,0:T(8,128)(2,1)S(1)}, bf16[8,1728]{1,0:T(8,128)(2,1)}, u32[]{:S(2)}) copy-start(bf16[8,1728]{1,0:T(8,128)(2,1)} %param.14) | copy-start | bytes 82948
  3.9 6.5 %collective-permute-start = (bf16[10,32,128]{2,1,0:T(8,128)(2,1)}, bf16[10,32,128]{2,1,0:T(8,128)(2,1)S(1)}, u32[]{:S(2)}, u32[]{:S(2)}) collective-permute-start(bf16[10,32,128]{2,1,0:T(8,128)(2,1)} %get-tuple-element.28.own), channel_id=1, source_target_pairs={{1,0},{2,1},{3,2},{4,3},{5,4},{6,5},{7,6},{8,7},{9,8},{10,9},{11,1... | collective-permute-start | bytes 245768 | tf_op jit(solution)/shard_map/ppermute | solution.py:435
  5.2 6.4 %collective-permute-start.1 = (bf16[10,32,128]{2,1,0:T(8,128)(2,1)}, bf16[10,32,128]{2,1,0:T(8,128)(2,1)S(1)}, u32[]{:S(2)}, u32[]{:S(2)}) collective-permute-start(bf16[10,32,128]{2,1,0:T(8,128)(2,1)} %get-tuple-element.29), channel_id=1, source_target_pairs={{0,1},{1,2},{2,3},{3,4},{4,5},{5,6},{6,7},{7,8},{8,9},{9,10},{10,1... | collective-permute-start | bytes 245768 | tf_op jit(solution)/shard_map/ppermute | solution.py:435
  10.4 1.1 copy-start.13
  11.6 0.6 copy-start.14
  14.4 32.8 %all-to-all-start = ((bf16[16,8,32,128]{3,2,1,0:T(8,128)(2,1)}), bf16[16,8,32,128]{3,2,1,0:T(8,128)(2,1)S(1)}, u32[]{:S(2)}, u32[]{:S(2)}) async-start(bf16[16,8,32,128]{3,2,1,0:T(8,128)(2,1)} %get-tuple-element.31), calls=%async_computation | async-start | bytes 2097152 | tf_op jit(solution)/shard_map/all_to_all | solution.py:496
  27.5 3.2 %copy-start.6 = (bf16[24,32,128]{2,1,0:T(8,128)(2,1)S(1)}, bf16[24,32,128]{2,1,0:T(8,128)(2,1)}, u32[]{:S(2)}) copy-start(bf16[24,32,128]{2,1,0:T(8,128)(2,1)} %get-tuple-element.30.refs_1_) | copy-start | bytes 589828
  30.8 19.8 %collective-permute-start.2 = (bf16[24,32,128]{2,1,0:T(8,128)(2,1)S(1)}, bf16[24,32,128]{2,1,0:T(8,128)(2,1)S(1)}, u32[]{:S(2)}, u32[]{:S(2)}) collective-permute-start(bf16[24,32,128]{2,1,0:T(8,128)(2,1)S(1)} %copy-done.6), channel_id=1, source_target_pairs={{0,16},{16,32},{32,48},{48,64},{64,80},{80,96},{96,112},{112,128},... | collective-permute-start | bytes 589832 | tf_op jit(solution)/shard_map/ppermute | solution.py:435
  34.3 16.3 %collective-permute-start.3 = (bf16[24,32,128]{2,1,0:T(8,128)(2,1)S(1)}, bf16[24,32,128]{2,1,0:T(8,128)(2,1)S(1)}, u32[]{:S(2)}, u32[]{:S(2)}) collective-permute-start(bf16[24,32,128]{2,1,0:T(8,128)(2,1)S(1)} %copy-done.6), channel_id=1, source_target_pairs={{16,0},{32,16},{48,32},{64,48},{80,64},{96,80},{112,96},{128,112},... | collective-permute-start | bytes 589832 | tf_op jit(solution)/shard_map/ppermute | solution.py:435
  47.1 3.4 %copy-start = (bf16[16,8,32,128]{3,2,1,0:T(8,128)(2,1)}, bf16[16,8,32,128]{3,2,1,0:T(8,128)(2,1)S(1)}, u32[]{:S(2)}) copy-start(bf16[16,8,32,128]{3,2,1,0:T(8,128)(2,1)S(1)} %all-to-all-done.refs_4_) | copy-start | bytes 3145732
  50.6 0.7 copy-start.7
  50.6 0.7 copy-start.8
  81.0 21.3 %copy-start.1 = (bf16[384,640]{1,0:T(8,128)(2,1)S(1)}, bf16[384,640]{1,0:T(8,128)(2,1)}, u32[]{:S(2)}) copy-start(bf16[384,640]{1,0:T(8,128)(2,1)} %get-tuple-element.48) | copy-start | bytes 1474564
  81.0 6.3 %collective-permute-start.4 = (bf16[192,128]{1,0:T(8,128)(2,1)}, bf16[192,128]{1,0:T(8,128)(2,1)S(1)}, u32[]{:S(2)}, u32[]{:S(2)}) collective-permute-start(bf16[192,128]{1,0:T(8,128)(2,1)} %get-tuple-element.39), channel_id=1, source_target_pairs={{0,1},{1,2},{2,3},{3,4},{4,5},{5,6},{6,7},{7,8},{8,9},{9,10},{10,1... | collective-permute-start | bytes 147464 | tf_op jit(solution)/shard_map/ppermute | solution.py:435
  85.1 6.9 %collective-permute-start.5 = (bf16[192,128]{1,0:T(8,128)(2,1)}, bf16[192,128]{1,0:T(8,128)(2,1)S(1)}, u32[]{:S(2)}, u32[]{:S(2)}) collective-permute-start(bf16[192,128]{1,0:T(8,128)(2,1)} %get-tuple-element.39), channel_id=1, source_target_pairs={{1,0},{2,1},{3,2},{4,3},{5,4},{6,5},{7,6},{8,7},{9,8},{10,9},{11,1... | collective-permute-start | bytes 147464 | tf_op jit(solution)/shard_map/ppermute | solution.py:435
  92.9 16.2 %copy-start.2 = (bf16[3,192,128]{2,1,0:T(8,128)(2,1)}, bf16[3,192,128]{2,1,0:T(8,128)(2,1)S(1)}, u32[]{:S(2)}) copy-start(bf16[3,192,128]{2,1,0:T(8,128)(2,1)S(1)} %pad_maximum_fusion.1.refs_1_) | copy-start | bytes 442372
  92.9 16.2 %collective-permute-start.6 = (bf16[3,192,128]{2,1,0:T(8,128)(2,1)S(1)}, bf16[3,192,128]{2,1,0:T(8,128)(2,1)S(1)}, u32[]{:S(2)}, u32[]{:S(2)}) collective-permute-start(bf16[3,192,128]{2,1,0:T(8,128)(2,1)S(1)} %pad_maximum_fusion.1.refs_1_), channel_id=1, source_target_pairs={{0,16},{16,32},{32,48},{48,64},{64,80},{80,96},{96,112},{112,128},... | collective-permute-start | bytes 442376 | tf_op jit(solution)/shard_map/ppermute | solution.py:435
  94.8 14.3 %collective-permute-start.7 = (bf16[3,192,128]{2,1,0:T(8,128)(2,1)S(1)}, bf16[3,192,128]{2,1,0:T(8,128)(2,1)S(1)}, u32[]{:S(2)}, u32[]{:S(2)}) collective-permute-start(bf16[3,192,128]{2,1,0:T(8,128)(2,1)S(1)} %pad_maximum_fusion.1.refs_1_), channel_id=1, source_target_pairs={{16,0},{32,16},{48,32},{64,48},{80,64},{96,80},{112,96},{128,112},... | collective-permute-start | bytes 442376 | tf_op jit(solution)/shard_map/ppermute | solution.py:435
  99.5 3.1 %collective-permute-start.8 = (bf16[3,128,128]{2,1,0:T(8,128)(2,1)S(1)}, bf16[3,128,128]{2,1,0:T(8,128)(2,1)S(1)}, u32[]{:S(2)}, u32[]{:S(2)}) collective-permute-start(bf16[3,128,128]{2,1,0:T(8,128)(2,1)S(1)} %slice.90), channel_id=1, source_target_pairs={{0,32},{16,48},{32,64},{48,80},{64,96},{80,112},{96,128},{112,144}... | collective-permute-start | bytes 294920 | tf_op jit(solution)/shard_map/ppermute | solution.py:435
  101.0 8.1 %collective-permute-start.9 = (bf16[3,128,128]{2,1,0:T(8,128)(2,1)S(1)}, bf16[3,128,128]{2,1,0:T(8,128)(2,1)S(1)}, u32[]{:S(2)}, u32[]{:S(2)}) collective-permute-start(bf16[3,128,128]{2,1,0:T(8,128)(2,1)S(1)} %slice.90), channel_id=1, source_target_pairs={{32,0},{48,16},{64,32},{80,48},{96,64},{112,80},{128,96},{144,112}... | collective-permute-start | bytes 294920 | tf_op jit(solution)/shard_map/ppermute | solution.py:435
  102.6 6.5 %copy-start.11 = (bf16[3,128,128]{2,1,0:T(8,128)(2,1)}, bf16[3,128,128]{2,1,0:T(8,128)(2,1)S(1)}, u32[]{:S(2)}) copy-start(bf16[3,128,128]{2,1,0:T(8,128)(2,1)S(1)} %collective-permute-done.8.refs_4_) | copy-start | bytes 294916
  109.1 0.6 copy-start.12
  109.1 0.7 copy-start.9
  109.1 0.7 copy-start.10
  114.8 2.4 %collective-permute-start.10 = (bf16[384,8,128]{2,1,0:T(8,128)(2,1)S(1)}, bf16[384,8,128]{2,1,0:T(8,128)(2,1)S(1)}, u32[]{:S(2)}, u32[]{:S(2)}) collective-permute-start(bf16[384,8,128]{2,1,0:T(8,128)(2,1)S(1)} %constant_dynamic-slice_fusion), channel_id=1, source_target_pairs={{0,16},{16,0},{32,48},{48,32},{64,80},{80,64},{96,112},{112,96},{1... | collective-permute-start | bytes 2359304 | tf_op jit(solution)/shard_map/ppermute | solution.py:625
  181.3 34.3 %copy-start.3 = (bf16[4,32,256]{2,1,0:T(8,128)(2,1)S(1)}, bf16[4,32,256]{2,1,0:T(8,128)(2,1)}, u32[]{:S(2)}) copy-start(bf16[4,32,256]{2,1,0:T(8,128)(2,1)} %get-tuple-element.38) | copy-start | bytes 196612
  181.3 35.0 %copy-start.4 = (bf16[4,32,256]{2,1,0:T(8,128)(2,1)S(1)}, bf16[4,32,256]{2,1,0:T(8,128)(2,1)}, u32[]{:S(2)}) copy-start(bf16[4,32,256]{2,1,0:T(8,128)(2,1)} %get-tuple-element.45) | copy-start | bytes 196612
  211.9 5.7 %collective-permute-start.11 = (bf16[384,8,128]{2,1,0:T(8,128)(2,1)S(1)}, bf16[384,8,128]{2,1,0:T(8,128)(2,1)S(1)}, u32[]{:S(2)}, u32[]{:S(2)}) collective-permute-start(bf16[384,8,128]{2,1,0:T(8,128)(2,1)S(1)} %bitcast.66), channel_id=1, source_target_pairs={{0,16},{16,0},{32,48},{48,32},{64,80},{80,64},{96,112},{112,96},{1... | collective-permute-start | bytes 2359304 | tf_op jit(solution)/shard_map/ppermute | solution.py:638

commit v4 on v3

--- a/solution.py
+++ b/solution.py
@@ -60,12 +60,16 @@
     return dot(head, b) + dot(rest, b)
 
 
-def loop(count, body):
+def loop(count, body, unroll=1):
     def step(i, carry):
-        body(i)
+        for u in range(unroll):
+            body(i * unroll + u)
         return carry
 
-    lax.fori_loop(0, count, step, 0)
+    if unroll == count:
+        step(0, 0)
+    else:
+        lax.fori_loop(0, count // unroll, step, 0)
 
 
 def lane(length):
@@ -221,14 +225,14 @@
         put_taps(taps_a, k, 0, 32, pool_s[k], 8)
         sum_a[k] = dot(w_enc[...], taps_a[k])
 
-    loop(16, enc_taps)
+    loop(16, enc_taps, 4)
     wide_in = inside(WIDE, 8, cols_all // 2, gy)
 
     def enc_act(k):
         value = silu(row_sum(sum_a, k, 64)) * (wide_in * row_ok(gx * 2 + k - 6, rows_mid))
         act_a[k] = value.astype(BF)
 
-    loop(14, enc_act)
+    loop(14, enc_act, 2)
     for m in range(4):
         pre = row_sum(sum_a, m + 5, 64)
         pre_one[m] = jnp.where(lane(128) < 96, pre[:, 0:128], pre[:, 128:256])
@@ -239,7 +243,7 @@
         put_taps(taps_b, k, 0, 64, pooled.astype(BF), 4)
         sum_b[k] = dot(w_bot[...], taps_b[k])
 
-    loop(7, low_taps)
+    loop(7, low_taps, 7)
     low_in = inside(LOW, 4, cols_all // 4, gy)
     mid_in = inside(MID, 8, cols_all // 2, gy)
     pick = jnp.where(lax.broadcasted_iota(jnp.int32, (64, 128), 1) < 96, 1.0, 0.0)
@@ -250,7 +254,7 @@
         value = silu(row_sum(sum_b, k, 128)) * (low_in * row_ok(gx + k - 2, rows_low))
         act_b[k] = dot(value.astype(BF), up_low[...]).astype(BF)
 
-    loop(5, low_act)
+    loop(5, low_act, 5)
 
     def mid_taps(k):
         put_taps(taps_c, k, 0, 192, act_b[(k + 1) // 2], 8)
@@ -258,7 +262,7 @@
         put_taps(taps_c, k, 128, 192, narrow, 8)
         sum_c[k] = dot(w_mid[...], taps_c[k])
 
-    loop(8, mid_taps)
+    loop(8, mid_taps, 2)
 
     def mid_act(k):
         pre = row_sum(sum_c, k, 64)
@@ -266,7 +270,7 @@
         value = silu(pre) * (mid_in * row_ok(gx * 2 + k - 2, rows_mid))
         act_c[k] = dot(value.astype(BF), up_mid[...]).astype(BF)
 
-    loop(6, mid_act)
+    loop(6, mid_act, 6)
 
     def skip_row(kind, k):
         part = (up, own, down)[k // 4]
@@ -281,7 +285,7 @@
             put_taps(taps_d, 2 * j + half, 0, 96, act_c[j], 16)
             sum_d[2 * j + half] = dot(w_top[...], taps_d[2 * j + half])
 
-    loop(6, top_taps)
+    loop(6, top_taps, 2)
     for k in range(10):
         pre = row_sum(sum_d, k, 32)
         s = sigmoid(pre)
@@ -294,7 +298,7 @@
         put_taps(taps_e, k, 0, 32, err_d[k], 16)
         sum_e[k] = dot(t_top[...], taps_e[k])
 
-    loop(10, top_back)
+    loop(10, top_back, 2)
 
     total = None
     for k in range(6):
@@ -314,7 +318,7 @@
         keep = mid_in * row_ok(gx * 2 + m - 1, rows_mid)
         err_c[m] = (whole * slope(pre_c[m + 1]) * keep).astype(BF)
 
-    loop(4, mid_err)
+    loop(4, mid_err, 4)
     for r in range(4):
         dskip[r] = row_sum(sum_e, r + 2, 96)[64:96, 0:256]
 
@@ -322,7 +326,7 @@
         put_taps(taps_f, m, 0, 64, err_c[m], 8)
         sum_f[m] = dot(t_mid[...], taps_f[m])
 
-    loop(4, mid_back)
+    loop(4, mid_back, 2)
     own_mid = jnp.where(lax.broadcasted_iota(jnp.int32, (64, 128), 1) < 64, 1.0, 0.0).astype(BF)
     for k in range(4):
         for a in range(3):
@@ -348,14 +352,20 @@
 
 
 def tail_kernel(sizes, scale_mid, *refs):
-    (ids, own, up, down, up_two, down_two, pre_one, taps_in, dskip) = refs[:9]
+    (ids, own, up_two, down_two, mate, beyond, pre_one, taps_in, dskip) = refs[:9]
     (t_bot, t_enc, up_low, up_mid) = refs[9:13]
     (grad_skip, g_enc) = refs[13:15]
-    (taps_a, sum_a, err_s, taps_b, sum_b) = refs[15:20]
+    (taps_a, sum_a, err_s, taps_b, sum_b, near) = refs[15:21]
     (rows_all, cols_all) = sizes
     gx, gy = ids[0], ids[1]
     rows_mid = rows_all // 2
     mid_in = inside(MID, 8, cols_all // 2, gy)
+
+    below = jnp.full((3, 192, 128), jnp.where(gx % 2 == 0, 1.0, 0.0)).astype(BF)
+    above = (1.0 - below.astype(F32)).astype(BF)
+    near[0] = beyond[...] * below + mate[...] * above
+    near[1] = mate[...] * below + beyond[...] * above
+    up, down = near.at[0], near.at[1]
 
     for k, ref in enumerate((up_two, up, own, down, down_two)):
         value = (
@@ -417,14 +427,14 @@
 SMEM = pl.BlockSpec(memory_space=pltpu.SMEM)
 
 
-def call(kernel, outs, scratch, scalars, *args, cost=1):
+def call(kernel, outs, scratch, scalars, *args, cost=1, grant=8):
     return pl.pallas_call(
         kernel,
         out_shape=[jax.ShapeDtypeStruct(s, d) for s, d in outs],
         in_specs=[SMEM] * scalars + [VMEM] * (len(args) - scalars),
         out_specs=[VMEM] * len(outs),
         scratch_shapes=[pltpu.VMEM(s, d) for s, d in scratch],
-        compiler_params=pltpu.CompilerParams(vmem_limit_bytes=56 * 1024 * 1024),
+        compiler_params=pltpu.CompilerParams(vmem_limit_bytes=grant * 1024 * 1024),
         cost_estimate=pl.CostEstimate(
             flops=cost * 500_000_000, bytes_accessed=cost * 1_000_000, transcendentals=0
         ),
@@ -513,9 +523,12 @@
             w_upper,
             cost=4,
         )
-        w_bot, t_bot = call(
-            lambda *refs: weight_kernel((1,), (1,), *refs),
-            [((384, 576), BF), ((192, 1152), BF)],
+        (w_bot,) = call(
+            lambda *refs: weight_kernel((1,), (0,), *refs), [((384, 576), BF)], [], 0, w_all
+        )
+        (t_bot,) = call(
+            lambda *refs: weight_kernel((0,), (1,), *refs),
+            [((192, 1152), BF)],
             [],
             0,
             w_all,
@@ -576,16 +589,18 @@
             c["sum_mid"],
             c["pool_low"],
             cost=20,
+            grant=40,
         )
 
         from_left = shift(packed, "gy", ngy, 1)
         from_right = shift(packed, "gy", ngy, -1)
         line = jnp.stack([packed, from_left, from_right])
-        line_up = shift(line, "gx", ngx, 1)
-        line_down = shift(line, "gx", ngx, -1)
-        low = line[:, 0:128]
-        low_up = shift(low, "gx", ngx, 2)
-        low_down = shift(low, "gx", ngx, -2)
+        core = gx % 2
+        swap = [(i, i ^ 1) for i in range(ngx)]
+        mate = lax.ppermute(line, "gx", swap)
+        line_up = shift(line, "gx", ngx, 2)
+        line_down = shift(line, "gx", ngx, -2)
+        beyond = lax.ppermute(jnp.where(core == 0, line_down, line_up), "gx", swap)
         grad_skip, g_enc = call(
             lambda *refs: tail_kernel(sizes, scales[1], *refs),
             [((4, 32, 256), BF), ((432, 128), BF)],
@@ -595,14 +610,15 @@
                 ((4, 64, 128), BF),
                 ((4, 576, 128), BF),
                 ((4, 96, 128), F32),
+                ((2, 3, 192, 128), BF),
             ],
             1,
             ids,
             line,
             line_up,
             line_down,
-            low_up,
-            low_down,
+            mate,
+            beyond,
             pre_one,
             taps_one,
             dskip,
@@ -618,8 +634,6 @@
         spare = -sum(t.shape[0] for t in tiles) % devices
         flat = jnp.concatenate(tiles + [jnp.zeros((spare, 8, 128), BF)], axis=0)
         half = flat.shape[0] // 2
-        core = gx % 2
-        swap = [(i, i ^ 1) for i in range(ngx)]
         keep = lax.dynamic_slice_in_dim(flat, core * half, half, 0)
         other = lax.dynamic_slice_in_dim(flat, (1 - core) * half, half, 0)
         other = lax.ppermute(other, "gx", swap)

time: 224 us -> 194 us (0.87)
  Pallas kernels: 45 us -> 23.3 us
  blocking collectives: 94.2 us -> 86.9 us
  waiting for transfers between devices: 25.3 us -> 20.2 us
    pallas_call x7 -> x8, Pallas kernels: 45 us -> 23.3 us  [call(): pl.pallas_call(kernel, out_shape=[jax.ShapeDtypeStruct(s, d) for s, d in...]
    ppermute x10 -> x8, waiting for transfers between devices: 12.6 us -> 5 us  [shift(): lax.ppermute(value, axis, [(i, i + step) for i in range(count) if 0 <= i...]
    all_to_all x1, blocking collectives: 63.9 us -> 56.8 us  [step(): lax.all_to_all(parts, AXES, split_axis=0, concat_axis=0, axis_index_group...]
    ppermute x0 -> x2, starting transfers between devices: none -> 5.2 us  [the longest x1 2.7 us: step(): beyond = lax.ppermute(jnp.where(core == 0, line_down, line_up), 'gx', swap)]
    unnamed x36 -> x68, local copies, waits for them, and re-layouts: 6.55 us -> 11.2 us
    ppermute x10 -> x8, starting transfers between devices: 24.8 us -> 21.6 us  [shift(): lax.ppermute(value, axis, [(i, i + step) for i in range(count) if 0 <= i...]
  transfers between devices with their start and end apart: 13 -> 13, of which waited for: 7 -> 7; matrix products, arithmetic and copies ran while one was open for 3% -> 1% of each run, Pallas kernels for 3% -> 1%
where the time goes in v4:
time: 194 us; the launch traced here: 193 us
  blocking collectives  86.9 us (45%)
  starting transfers between devices  44.2 us (23%)
  Pallas kernels  23.3 us (12%)
  waiting for transfers between devices  20.2 us (10%)
  local copies, waits for them, and re-layouts  13.1 us (7%)
  other arithmetic  4.37 us (2%)
    all_to_all x1, blocking collectives, step(): lax.all_to_all(parts, AXES, split_axis=0, concat_axis=0, axis_index_group...  56.8 us
    all_to_all x1, blocking collectives, step(): lax.all_to_all(spread, AXES, split_axis=0, concat_axis=0, axis_index_grou...  30.1 us
    pallas_call x8, Pallas kernels, call(): pl.pallas_call(kernel, out_shape=[jax.ShapeDtypeStruct(s, d) for s, d in...  23.3 us
    ppermute x8, starting transfers between devices, shift(): lax.ppermute(value, axis, [(i, i + step) for i in range(count) if 0 <= i...  21.6 us
    all_to_all x1, starting transfers between devices, step(): lax.all_to_all(spread, 'gx', split_axis=0, concat_axis=0, tiled=True)  13.2 us
    all_to_all x1, waiting for transfers between devices, step(): lax.all_to_all(spread, 'gx', split_axis=0, concat_axis=0, tiled=True)  12.4 us
    unnamed x68, local copies, waits for them, and re-layouts  11.2 us
    ppermute x8, waiting for transfers between devices, shift(): lax.ppermute(value, axis, [(i, i + step) for i in range(count) if 0 <= i...  5 us
  transfers between devices with their start and end apart: 13, of which 7 were waited for; matrix products, arithmetic and copies ran while one was open for 1% of the time, Pallas kernels for 1%

profile of v4, /device:TPU:1, one launch (start us, length us, event | category | flops | bytes accessed | tf_op | source)
XLA Modules:
  0.0 193.3 jit_solution(7645600608229681269)
XLA Ops:
  0.6 0.9 copy_bitcast_fusion
  1.5 0.0 copy-start.8
  1.6 0.8 copy-done.8
  2.4 0.2 shard_map.163
  2.5 3.9 %collective-permute-start.1 = (bf16[10,32,128]{2,1,0:T(8,128)(2,1)S(1)}, bf16[10,32,128]{2,1,0:T(8,128)(2,1)S(1)}, u32[]{:S(2)}, u32[]{:S(2)}) collective-permute-start(bf16[10,32,128]{2,1,0:T(8,128)(2,1)S(1)} %get-tuple-element.27), channel_id=1, source_target_pairs={{0,1},{1,2},{2,3},{3,4},{4,5},{5,6},{6,7},{7,8},{8,9},{9,10},{10,1... | collective-permute-start | bytes 245768 | tf_op jit(solution)/shard_map/ppermute | solution.py:445
  6.5 1.3 collective-permute-start
  7.8 0.1 collective-permute-done.1.left
  7.9 3.7 %collective-permute-done.right = bf16[10,32,128]{2,1,0:T(8,128)(2,1)S(1)} collective-permute-done((bf16[10,32,128]{2,1,0:T(8,128)(2,1)S(1)}, bf16[10,32,128]{2,1,0:T(8,128)(2,1)S(1)}, u32[]{:S(2)}, u32[]{:S(2)}) %collective-permute-start) | collective-permute-done | bytes 81952 | tf_op jit(solution)/shard_map/ppermute | solution.py:445
  11.7 1.1 shard_map.164
  12.8 13.2 %all-to-all-start = ((bf16[16,8,32,128]{3,2,1,0:T(8,128)(2,1)}), bf16[16,8,32,128]{3,2,1,0:T(8,128)(2,1)S(1)}, u32[]{:S(2)}, u32[]{:S(2)}) async-start(bf16[16,8,32,128]{3,2,1,0:T(8,128)(2,1)} %get-tuple-element.29), calls=%async_computation | async-start | bytes 2097152 | tf_op jit(solution)/shard_map/all_to_all | solution.py:506
  26.0 2.0 %collective-permute-start.3 = (bf16[24,32,128]{2,1,0:T(8,128)(2,1)S(1)}, bf16[24,32,128]{2,1,0:T(8,128)(2,1)S(1)}, u32[]{:S(2)}, u32[]{:S(2)}) collective-permute-start(bf16[24,32,128]{2,1,0:T(8,128)(2,1)S(1)} %get-tuple-element.28.refs_1_), channel_id=1, source_target_pairs={{16,0},{32,16},{48,32},{64,48},{80,64},{96,80},{112,96},{128,112},... | collective-permute-start | bytes 589832 | tf_op jit(solution)/shard_map/ppermute | solution.py:445
  28.0 3.5 %collective-permute-start.2 = (bf16[24,32,128]{2,1,0:T(8,128)(2,1)S(1)}, bf16[24,32,128]{2,1,0:T(8,128)(2,1)S(1)}, u32[]{:S(2)}, u32[]{:S(2)}) collective-permute-start(bf16[24,32,128]{2,1,0:T(8,128)(2,1)S(1)} %get-tuple-element.28.refs_1_), channel_id=1, source_target_pairs={{0,16},{16,32},{32,48},{48,64},{64,80},{80,96},{96,112},{112,128},... | collective-permute-start | bytes 589832 | tf_op jit(solution)/shard_map/ppermute | solution.py:445
  31.6 0.9 shard_map.165
  32.5 0.9 copy-done.11
  33.4 0.8 copy-done.13
  34.2 0.6 copy-done.23
  34.9 0.1 pad_add_fusion.refs_0_
  34.9 12.4 %all-to-all-done.refs_4_ = bf16[16,8,32,128]{3,2,1,0:T(8,128)(2,1)S(1)} async-done(((bf16[16,8,32,128]{3,2,1,0:T(8,128)(2,1)}), bf16[16,8,32,128]{3,2,1,0:T(8,128)(2,1)S(1)}, u32[]{:S(2)}, u32[]{:S(2)}) %all-to-all-start) | async-done | bytes 1048608 | tf_op jit(solution)/shard_map/all_to_all | solution.py:506
  47.5 0.1 shard_map.166.refs_6_
  47.7 0.7 copy-done.1
  48.4 0.4 copy-done.12
  48.8 0.2 copy-done.14
  49.0 0.0 copy-done.26
  49.0 0.0 copy-done.28
  49.0 0.9 copy-done.2
  50.0 0.9 copy-done.18
  50.9 17.3 %shard_map.167 = (bf16[4,32,256]{2,1,0:T(8,128)(2,1)S(1)}, f32[4,32,256]{2,1,0:T(8,128)S(1)}, bf16[192,128]{1,0:T(8,128)(2,1)S(1)}, f32[4,64,128]{2,1,0:T(8,128)...) custom-call(s32[2]{0:T(128)S(1)} %pad_add_fusion.refs_0_, ...), custom_call_target="tpu_custom_call" | custom-call | flops 10000000000 | bytes 20000000 | tf_op jit(solution)/shard_map/pallas_call | solution.py:431
  68.2 0.7 copy-done.15
  68.9 0.7 copy-done.19
  69.6 0.7 copy-done.21
  70.2 1.3 collective-permute-start.5
  71.5 4.3 %collective-permute-start.4 = (bf16[192,128]{1,0:T(8,128)(2,1)S(1)}, bf16[192,128]{1,0:T(8,128)(2,1)S(1)}, u32[]{:S(2)}, u32[]{:S(2)}) collective-permute-start(bf16[192,128]{1,0:T(8,128)(2,1)S(1)} %get-tuple-element.36), channel_id=1, source_target_pairs={{0,1},{1,2},{2,3},{3,4},{4,5},{5,6},{6,7},{7,8},{8,9},{9,10},{10,1... | collective-permute-start | bytes 147464 | tf_op jit(solution)/shard_map/ppermute | solution.py:445
  75.8 1.1 collective-permute-done.4
  77.0 1.3 collective-permute-start.7
  78.3 4.0 %collective-permute-start.6 = (bf16[3,192,128]{2,1,0:T(8,128)(2,1)S(1)}, bf16[3,192,128]{2,1,0:T(8,128)(2,1)S(1)}, u32[]{:S(2)}, u32[]{:S(2)}) collective-permute-start(bf16[3,192,128]{2,1,0:T(8,128)(2,1)S(1)} %pad_maximum_fusion.1.refs_1_), channel_id=1, source_target_pairs={{0,32},{16,48},{32,64},{48,80},{64,96},{80,112},{96,128},{112,144}... | collective-permute-start | bytes 442376 | tf_op jit(solution)/shard_map/ppermute | solution.py:445
  82.3 0.1 constant_dynamic-update-slice_fusion.1
  82.4 2.5 %collective-permute-start.8 = (bf16[3,192,128]{2,1,0:T(8,128)(2,1)S(1)}, bf16[3,192,128]{2,1,0:T(8,128)(2,1)S(1)}, u32[]{:S(2)}, u32[]{:S(2)}) collective-permute-start(bf16[3,192,128]{2,1,0:T(8,128)(2,1)S(1)} %pad_maximum_fusion.1.refs_1_), channel_id=1, source_target_pairs={{0,16},{16,0},{32,48},{48,32},{64,80},{80,64},{96,112},{112,96},{1... | collective-permute-start | bytes 442376 | tf_op jit(solution)/shard_map/ppermute | solution.py:600
  85.0 2.7 %collective-permute-start.9 = (bf16[3,192,128]{2,1,0:T(8,128)(2,1)S(1)}, bf16[3,192,128]{2,1,0:T(8,128)(2,1)S(1)}, u32[]{:S(2)}, u32[]{:S(2)}) collective-permute-start(bf16[3,192,128]{2,1,0:T(8,128)(2,1)S(1)} %broadcast_select_fusion.2), channel_id=1, source_target_pairs={{0,16},{16,0},{32,48},{48,32},{64,80},{80,64},{96,112},{112,96},{1... | collective-permute-start | bytes 442376 | tf_op jit(solution)/shard_map/ppermute | solution.py:603
  87.7 0.6 shard_map.168.refs_9_
  88.3 0.1 constant_dynamic-update-slice_fusion
  88.3 0.3 collective-permute-done.9.refs_5_
  88.7 2.3 %shard_map.169 = (bf16[4,32,256]{2,1,0:T(8,128)(2,1)S(1)}, bf16[432,128]{1,0:T(8,128)(2,1)S(1)}) custom-call(s32[2]{0:T(128)S(1)} %pad_add_fusion.refs_0_, bf16[3,192,128]{2,1,0:T(8,128)(2,1)S(1)} %pad_maximum_fusion.1.refs_1_, bf16[3,192,128]{2,1,0:T(8,128)(2,1)S(1)} %collective-permute-done.6.refs_2_, ...), custom_call_target="tpu_custom_call" | custom-call | flops 2000000000 | bytes 4000000 | tf_op jit(solution)/shard_map/pallas_call | solution.py:431
  91.1 1.2 copy-done.29
  92.2 0.1 constant_dynamic-slice_fusion
  92.3 0.5 collective-permute-start.10
  92.7 1.9 collective-permute-done.10
  94.7 1.4 add_convert_fusion
  96.0 56.8 %all_to_all.15 = bf16[128,24,128]{2,1,0:T(8,128)(2,1)S(1)} all-to-all(bf16[128,24,128]{2,1,0:T(8,128)(2,1)S(1)} %bitcast.72), channel_id=1, replica_groups={{0,1,2,3,4,5,6,7,8,9,10,11,12,13,14,15,32,33,34,35,36,37,38,39,40,41,42..., dimensions={0} | all-to-all | bytes 1572864 | tf_op jit(solution)/shard_map/all_to_all | solution.py:643
  152.8 0.2 reduce_sum.12
  153.0 0.1 broadcast_in_dim.10
  153.1 30.1 %all_to_all.16 = bf16[128,24,128]{2,1,0:T(8,128)(2,1)S(1)} all-to-all(bf16[128,24,128]{2,1,0:T(8,128)(2,1)S(1)} %broadcast_in_dim.10), channel_id=1, replica_groups={{0,1,2,3,4,5,6,7,8,9,10,11,12,13,14,15,32,33,34,35,36,37,38,39,40,41,42..., dimensions={0} | all-to-all | bytes 1572864 | tf_op jit(solution)/shard_map/all_to_all | solution.py:648
  183.2 3.7 %collective-permute-start.11 = (bf16[384,8,128]{2,1,0:T(8,128)(2,1)S(1)}, bf16[384,8,128]{2,1,0:T(8,128)(2,1)S(1)}, u32[]{:S(2)}, u32[]{:S(2)}) collective-permute-start(bf16[384,8,128]{2,1,0:T(8,128)(2,1)S(1)} %bitcast.73), channel_id=1, source_target_pairs={{0,16},{16,0},{32,48},{48,32},{64,80},{80,64},{96,112},{112,96},{1... | collective-permute-start | bytes 2359304 | tf_op jit(solution)/shard_map/ppermute | solution.py:652
  187.0 0.7 copy.20
  187.7 0.7 copy.21
  188.4 0.5 collective-permute-done.11
  188.9 0.1 broadcast_select_fusion
  189.1 0.1 pad_maximum_fusion
  189.2 0.8 shard_map.170
  190.1 0.1 concatenate.16
  190.2 0.6 convert_element_type.25
  190.8 0.1 concatenate.19
  191.0 0.8 convert_element_type.27
  191.7 0.4 concatenate.18
  192.1 1.2 convert_element_type.26
  (66 shorter events, 0.4 us)
Async XLA Ops:
  0.6 7.2 %copy-start.30 = (bf16[8,1728]{1,0:T(8,128)(2,1)S(1)}, bf16[8,1728]{1,0:T(8,128)(2,1)}, u32[]{:S(2)}) copy-start(bf16[8,1728]{1,0:T(8,128)(2,1)} %param.14) | copy-start | bytes 82948
  1.5 0.8 copy-start.8
  2.5 5.4 %collective-permute-start.1 = (bf16[10,32,128]{2,1,0:T(8,128)(2,1)S(1)}, bf16[10,32,128]{2,1,0:T(8,128)(2,1)S(1)}, u32[]{:S(2)}, u32[]{:S(2)}) collective-permute-start(bf16[10,32,128]{2,1,0:T(8,128)(2,1)S(1)} %get-tuple-element.27), channel_id=1, source_target_pairs={{0,1},{1,2},{2,3},{3,4},{4,5},{5,6},{6,7},{7,8},{8,9},{9,10},{10,1... | collective-permute-start | bytes 245768 | tf_op jit(solution)/shard_map/ppermute | solution.py:445
  6.5 5.2 %collective-permute-start = (bf16[10,32,128]{2,1,0:T(8,128)(2,1)S(1)}, bf16[10,32,128]{2,1,0:T(8,128)(2,1)S(1)}, u32[]{:S(2)}, u32[]{:S(2)}) collective-permute-start(bf16[10,32,128]{2,1,0:T(8,128)(2,1)S(1)} %get-tuple-element.26.own), channel_id=1, source_target_pairs={{1,0},{2,1},{3,2},{4,3},{5,4},{6,5},{7,6},{8,7},{9,8},{10,9},{11,1... | collective-permute-start | bytes 245768 | tf_op jit(solution)/shard_map/ppermute | solution.py:445
  11.7 19.9 %copy-start = (bf16[64,5184]{1,0:T(8,128)(2,1)S(1)}, bf16[64,5184]{1,0:T(8,128)(2,1)}, u32[]{:S(2)}) copy-start(bf16[64,5184]{1,0:T(8,128)(2,1)} %refs_1_.1) | copy-start | bytes 1990660
  11.7 19.9 %copy-start.3 = (bf16[32,2592]{1,0:T(8,128)(2,1)S(1)}, bf16[32,2592]{1,0:T(8,128)(2,1)}, u32[]{:S(2)}) copy-start(bf16[32,2592]{1,0:T(8,128)(2,1)} %refs_2_.1) | copy-start | bytes 497668
  11.7 19.9 %copy-start.4 = (bf16[64,864]{1,0:T(8,128)(2,1)S(1)}, bf16[64,864]{1,0:T(8,128)(2,1)}, u32[]{:S(2)}) copy-start(bf16[64,864]{1,0:T(8,128)(2,1)} %refs_0_.1) | copy-start | bytes 331780
  12.8 34.5 %all-to-all-start = ((bf16[16,8,32,128]{3,2,1,0:T(8,128)(2,1)}), bf16[16,8,32,128]{3,2,1,0:T(8,128)(2,1)S(1)}, u32[]{:S(2)}, u32[]{:S(2)}) async-start(bf16[16,8,32,128]{3,2,1,0:T(8,128)(2,1)} %get-tuple-element.29), calls=%async_computation | async-start | bytes 2097152 | tf_op jit(solution)/shard_map/all_to_all | solution.py:506
  26.0 21.6 %collective-permute-start.3 = (bf16[24,32,128]{2,1,0:T(8,128)(2,1)S(1)}, bf16[24,32,128]{2,1,0:T(8,128)(2,1)S(1)}, u32[]{:S(2)}, u32[]{:S(2)}) collective-permute-start(bf16[24,32,128]{2,1,0:T(8,128)(2,1)S(1)} %get-tuple-element.28.refs_1_), channel_id=1, source_target_pairs={{16,0},{32,16},{48,32},{64,48},{80,64},{96,80},{112,96},{128,112},... | collective-permute-start | bytes 589832 | tf_op jit(solution)/shard_map/ppermute | solution.py:445
  28.0 19.6 %collective-permute-start.2 = (bf16[24,32,128]{2,1,0:T(8,128)(2,1)S(1)}, bf16[24,32,128]{2,1,0:T(8,128)(2,1)S(1)}, u32[]{:S(2)}, u32[]{:S(2)}) collective-permute-start(bf16[24,32,128]{2,1,0:T(8,128)(2,1)S(1)} %get-tuple-element.28.refs_1_), channel_id=1, source_target_pairs={{0,16},{16,32},{32,48},{48,64},{64,80},{80,96},{96,112},{112,128},... | collective-permute-start | bytes 589832 | tf_op jit(solution)/shard_map/ppermute | solution.py:445
  32.5 0.9 copy-start.11
  33.4 0.9 copy-start.13
  34.2 0.6 copy-start.23
  34.9 12.5 %copy-start.25 = (bf16[96,864]{1,0:T(8,128)(2,1)}, bf16[96,864]{1,0:T(8,128)(2,1)S(1)}, u32[]{:S(2)}) copy-start(bf16[96,864]{1,0:T(8,128)(2,1)S(1)} %get-tuple-element.32.refs_8_) | copy-start | bytes 497668
  34.9 12.5 %copy-start.27 = (bf16[192,288]{1,0:T(8,128)(2,1)}, bf16[192,288]{1,0:T(8,128)(2,1)S(1)}, u32[]{:S(2)}) copy-start(bf16[192,288]{1,0:T(8,128)(2,1)S(1)} %get-tuple-element.30.refs_5_) | copy-start | bytes 331780
  34.9 12.8 %copy-start.17 = (bf16[288,288]{1,0:T(8,128)(2,1)}, bf16[288,288]{1,0:T(8,128)(2,1)S(1)}, u32[]{:S(2)}) copy-start(bf16[288,288]{1,0:T(8,128)(2,1)S(1)} %get-tuple-element.33.refs_9_) | copy-start | bytes 497668
  47.4 1.0 copy-start.5
  47.4 1.0 copy-start.6
  47.4 1.0 copy-start.7
  47.4 1.0 copy-start.9
  47.4 0.9 copy-start.10
  47.4 1.3 copy-start.12
  47.5 1.5 copy-start.14
  47.5 1.5 copy-start.26
  47.5 1.6 copy-start.28
  47.7 0.7 copy-start.1
  49.0 0.9 copy-start.2
  50.0 0.9 copy-start.18
  68.2 0.7 copy-start.15
  68.9 0.7 copy-start.19
  69.6 0.7 copy-start.21
  70.2 5.6 %collective-permute-start.5 = (bf16[192,128]{1,0:T(8,128)(2,1)S(1)}, bf16[192,128]{1,0:T(8,128)(2,1)S(1)}, u32[]{:S(2)}, u32[]{:S(2)}) collective-permute-start(bf16[192,128]{1,0:T(8,128)(2,1)S(1)} %get-tuple-element.36), channel_id=1, source_target_pairs={{1,0},{2,1},{3,2},{4,3},{5,4},{6,5},{7,6},{8,7},{9,8},{10,9},{11,1... | collective-permute-start | bytes 147464 | tf_op jit(solution)/shard_map/ppermute | solution.py:445
  71.5 5.4 %collective-permute-start.4 = (bf16[192,128]{1,0:T(8,128)(2,1)S(1)}, bf16[192,128]{1,0:T(8,128)(2,1)S(1)}, u32[]{:S(2)}, u32[]{:S(2)}) collective-permute-start(bf16[192,128]{1,0:T(8,128)(2,1)S(1)} %get-tuple-element.36), channel_id=1, source_target_pairs={{0,1},{1,2},{2,3},{3,4},{4,5},{5,6},{6,7},{7,8},{8,9},{9,10},{10,1... | collective-permute-start | bytes 147464 | tf_op jit(solution)/shard_map/ppermute | solution.py:445
  77.0 7.9 %collective-permute-start.7 = (bf16[3,192,128]{2,1,0:T(8,128)(2,1)S(1)}, bf16[3,192,128]{2,1,0:T(8,128)(2,1)S(1)}, u32[]{:S(2)}, u32[]{:S(2)}) collective-permute-start(bf16[3,192,128]{2,1,0:T(8,128)(2,1)S(1)} %pad_maximum_fusion.1.refs_1_), channel_id=1, source_target_pairs={{32,0},{48,16},{64,32},{80,48},{96,64},{112,80},{128,96},{144,112}... | collective-permute-start | bytes 442376 | tf_op jit(solution)/shard_map/ppermute | solution.py:445
  78.3 6.6 %collective-permute-start.6 = (bf16[3,192,128]{2,1,0:T(8,128)(2,1)S(1)}, bf16[3,192,128]{2,1,0:T(8,128)(2,1)S(1)}, u32[]{:S(2)}, u32[]{:S(2)}) collective-permute-start(bf16[3,192,128]{2,1,0:T(8,128)(2,1)S(1)} %pad_maximum_fusion.1.refs_1_), channel_id=1, source_target_pairs={{0,32},{16,48},{32,64},{48,80},{64,96},{80,112},{96,128},{112,144}... | collective-permute-start | bytes 442376 | tf_op jit(solution)/shard_map/ppermute | solution.py:445
  82.4 5.9 %collective-permute-start.8 = (bf16[3,192,128]{2,1,0:T(8,128)(2,1)S(1)}, bf16[3,192,128]{2,1,0:T(8,128)(2,1)S(1)}, u32[]{:S(2)}, u32[]{:S(2)}) collective-permute-start(bf16[3,192,128]{2,1,0:T(8,128)(2,1)S(1)} %pad_maximum_fusion.1.refs_1_), channel_id=1, source_target_pairs={{0,16},{16,0},{32,48},{48,32},{64,80},{80,64},{96,112},{112,96},{1... | collective-permute-start | bytes 442376 | tf_op jit(solution)/shard_map/ppermute | solution.py:600
  84.9 3.8 %copy-start.16 = (bf16[4,288,128]{2,1,0:T(8,128)(2,1)S(1)}, bf16[4,288,128]{2,1,0:T(8,128)(2,1)}, u32[]{:S(2)}) copy-start(bf16[4,288,128]{2,1,0:T(8,128)(2,1)} %copy-done.15) | copy-start | bytes 884740
  84.9 3.7 %copy-start.20 = (f32[4,32,256]{2,1,0:T(8,128)S(1)}, f32[4,32,256]{2,1,0:T(8,128)}, u32[]{:S(2)}) copy-start(f32[4,32,256]{2,1,0:T(8,128)} %copy-done.19) | copy-start | bytes 393220
  85.0 3.7 %copy-start.22 = (f32[4,64,128]{2,1,0:T(8,128)S(1)}, f32[4,64,128]{2,1,0:T(8,128)}, u32[]{:S(2)}) copy-start(f32[4,64,128]{2,1,0:T(8,128)} %copy-done.21) | copy-start | bytes 393220
  85.0 3.7 %copy-start.24 = (bf16[96,576]{1,0:T(8,128)(2,1)S(1)}, bf16[96,576]{1,0:T(8,128)(2,1)}, u32[]{:S(2)}) copy-start(bf16[96,576]{1,0:T(8,128)(2,1)} %copy-done.23) | copy-start | bytes 331780
  85.0 3.7 %collective-permute-start.9 = (bf16[3,192,128]{2,1,0:T(8,128)(2,1)S(1)}, bf16[3,192,128]{2,1,0:T(8,128)(2,1)S(1)}, u32[]{:S(2)}, u32[]{:S(2)}) collective-permute-start(bf16[3,192,128]{2,1,0:T(8,128)(2,1)S(1)} %broadcast_select_fusion.2), channel_id=1, source_target_pairs={{0,16},{16,0},{32,48},{48,32},{64,80},{80,64},{96,112},{112,96},{1... | collective-permute-start | bytes 442376 | tf_op jit(solution)/shard_map/ppermute | solution.py:603
  91.1 1.2 copy-start.29
  92.3 2.4 %collective-permute-start.10 = (bf16[384,8,128]{2,1,0:T(8,128)(2,1)S(1)}, bf16[384,8,128]{2,1,0:T(8,128)(2,1)S(1)}, u32[]{:S(2)}, u32[]{:S(2)}) collective-permute-start(bf16[384,8,128]{2,1,0:T(8,128)(2,1)S(1)} %constant_dynamic-slice_fusion), channel_id=1, source_target_pairs={{0,16},{16,0},{32,48},{48,32},{64,80},{80,64},{96,112},{112,96},{1... | collective-permute-start | bytes 2359304 | tf_op jit(solution)/shard_map/ppermute | solution.py:639
  183.2 5.7 %collective-permute-start.11 = (bf16[384,8,128]{2,1,0:T(8,128)(2,1)S(1)}, bf16[384,8,128]{2,1,0:T(8,128)(2,1)S(1)}, u32[]{:S(2)}, u32[]{:S(2)}) collective-permute-start(bf16[384,8,128]{2,1,0:T(8,128)(2,1)S(1)} %bitcast.73), channel_id=1, source_target_pairs={{0,16},{16,0},{32,48},{48,32},{64,80},{80,64},{96,112},{112,96},{1... | collective-permute-start | bytes 2359304 | tf_op jit(solution)/shard_map/ppermute | solution.py:652

commit v5 on v4

--- a/solution.py
+++ b/solution.py
@@ -148,7 +148,7 @@
         to_right[8 + q] = pooled
 
 
-def widen_kernel(skip, cot, own, right, left, weight, out, spread):
+def widen_kernel(skip, cot, own, right, left, weight, out):
     first = jnp.where(lax.broadcasted_iota(jnp.int32, (32, 128), 1) < 64, 1.0, 0.0)
     head = first.astype(BF)
     tail = (1.0 - first).astype(BF)
@@ -158,15 +158,61 @@
             out[base] = tile[r, :, 0:128]
             out[base + 1] = tile[r, :, 128:256]
             out[base + 2] = right[4 * k + r] * head + left[4 * k + r] * tail
-    pieces = []
     for q in range(2):
-        pieces.append(own[8 + q] * head + right[8 + q] * tail)
-        pieces.append(left[8 + q] * tail)
-    for p in range(spread.shape[0]):
-        for q in range(4):
-            spread[p, q] = pieces[q]
-        for q in range(weight.shape[0]):
-            spread[p, 4 + q] = weight[q]
+        out[24 + 2 * q] = own[8 + q] * head + right[8 + q] * tail
+        out[25 + 2 * q] = left[8 + q] * tail
+    for q in range(weight.shape[0]):
+        out[28 + q] = weight[q]
+
+
+def gather_kernel(tiles, block, *refs):
+    (ids, own, up, down, mate, beyond, far_up, far_down, three_m, far_up_m, far_down_m) = refs[:11]
+    (fine, pools, w_out, w_all, w_flat) = refs[11:16]
+    gx = ids[0]
+    core = gx % 2
+    wide = own.shape[0] - 24
+    low = jnp.where(core == 0, 1.0, 0.0)
+    below = jnp.full((24, 32, 128), low).astype(BF)
+    above = jnp.full((24, 32, 128), 1.0 - low).astype(BF)
+    first = beyond[...] * below + mate[0:24] * above
+    last = mate[0:24] * below + beyond[...] * above
+    top = jnp.full((12, 32, 128), row_ok(gx - 1, tiles)).astype(BF)
+    bottom = jnp.full((12, 32, 128), row_ok(gx + 1, tiles)).astype(BF)
+    for k in range(2):
+        fine[0, 12 * k : 12 * k + 12] = first[12 * k : 12 * k + 12] * top
+        fine[1, 12 * k : 12 * k + 12] = last[12 * k : 12 * k + 12] * bottom
+
+    def chips(own_at, down_at, up_at, far_down_ref, far_up_ref):
+        return [
+            own_at,
+            down_at,
+            (far_down_ref, 0),
+            (far_down_ref, wide),
+            (far_down_ref, 2 * wide),
+            (far_up_ref, wide),
+            (far_up_ref, 2 * wide),
+            up_at,
+        ]
+
+    mine = chips((own, 24), (down, 24), (up, 24), far_down, far_up)
+    other = chips((three_m, wide), (three_m, 2 * wide), (three_m, 0), far_down_m, far_up_m)
+    for parity, entries in ((gx, mine), (gx + 1 - 2 * core, other)):
+        for j, (ref, at) in enumerate(entries):
+            w_all[(parity + 2 * j) % tiles] = ref[at + 4 : at + wide]
+        for j, step in ((0, 0), (1, 2), (2, 4), (6, -4), (7, -2)):
+            tile = parity + step
+            ref, at = entries[j]
+            place = tile - gx + 5
+            keep = jnp.full((4, 32, 128), row_ok(tile, tiles)).astype(BF)
+            pools[place] = ref[at : at + 4] * keep
+    lanes = w_flat.shape[1] // 128
+    for b in range(tiles):
+        rows = w_all[b].reshape(lanes * block, 128)
+        for l in range(lanes):
+            w_flat[b * block : b * block + block, 128 * l : 128 * l + 128] = rows[
+                l * block : l * block + block
+            ]
+    put_forward(w_flat, w_out)
 
 
 def put_forward(w, out):
@@ -200,26 +246,23 @@
 
 
 def main_kernel(sizes, scales, *refs):
-    (ids, own, up, down, pools) = refs[:5]
-    (w_enc, w_bot, w_mid, w_top, t_top, t_mid) = refs[5:11]
-    (up_low, sum_low, up_mid, sum_mid, pool_low) = refs[11:16]
-    (feat, dskip, packed, pre_one, taps_out, g_top, g_mid, g_bot) = refs[16:24]
-    (pool_s, taps_a, sum_a, act_a, taps_b, sum_b, act_b) = refs[24:31]
-    (taps_c, sum_c, act_c, pre_c, taps_d, sum_d, err_d) = refs[31:38]
-    (taps_e, sum_e, err_c, stack, taps_f, sum_f) = refs[38:44]
+    (ids, own, fine, pools) = refs[:4]
+    up, down = fine.at[0], fine.at[1]
+    (w_enc, w_bot, w_mid, w_top, t_top, t_mid) = refs[4:10]
+    (up_low, sum_low, up_mid, sum_mid, pool_low) = refs[10:15]
+    (feat, dskip, packed, pre_one, taps_out, g_top, g_mid, g_bot) = refs[15:23]
+    (pool_s, taps_a, sum_a, act_a, taps_b, sum_b, act_b) = refs[23:30]
+    (taps_c, sum_c, act_c, pre_c, taps_d, sum_d, err_d) = refs[30:37]
+    (taps_e, sum_e, err_c, stack, taps_f, sum_f) = refs[37:43]
     (rows_all, cols_all) = sizes
     (scale_top, scale_mid, scale_low) = scales
     gx, gy = ids[0], ids[1]
     rows_mid, rows_low = rows_all // 2, rows_all // 4
 
-    tiles = rows_all // 4
     for k in range(16):
-        tile = gx + (k - 7) // 2
-        keep = jnp.full((32, 128), row_ok(tile, tiles)).astype(BF)
-        tile = jnp.clip(tile, 0, tiles - 1)
-        slab = 2 * ((k - 7) % 2)
-        pool_s[k, :, 0:128] = pools[tile, slab] * keep
-        pool_s[k, :, 128:256] = pools[tile, slab + 1] * keep
+        tile, slab = 5 + (k - 7) // 2, 2 * ((k - 7) % 2)
+        pool_s[k, :, 0:128] = pools[tile, slab]
+        pool_s[k, :, 128:256] = pools[tile, slab + 1]
 
     def enc_taps(k):
         put_taps(taps_a, k, 0, 32, pool_s[k], 8)
@@ -445,6 +488,10 @@
     return lax.ppermute(value, axis, [(i, i + step) for i in range(count) if 0 <= i + step < count])
 
 
+def turn(value, axis, count, step):
+    return lax.ppermute(value, axis, [(i, (i + step) % count) for i in range(count)])
+
+
 def tiles_of(g):
     rows, width = g.shape
     return g.reshape(rows // 8, 8, width // 128, 128).transpose(0, 2, 1, 3).reshape(-1, 8, 128)
@@ -489,9 +536,9 @@
         )
         right = shift(to_left, "gy", ngy, -1)
         left = shift(to_right, "gy", ngy, 1)
-        own, spread = call(
+        (own,) = call(
             widen_kernel,
-            [((24, 32, 128), BF), ((ngx, 4 + slabs, 32, 128), BF)],
+            [((28 + slabs, 32, 128), BF)],
             [],
             0,
             skip,
@@ -501,11 +548,41 @@
             left,
             weight,
         )
-        up = shift(own, "gx", ngx, 1)
-        down = shift(own, "gx", ngx, -1)
-        pools = lax.all_to_all(spread, "gx", split_axis=0, concat_axis=0, tiled=True)
-        w_all = pools[:, 4:].reshape(ngx, lanes, block, 128).transpose(0, 2, 1, 3)
-        w_all = w_all.reshape(ngx * block, lanes * 128)[:, :width]
+        core = gx % 2
+        swap = [(i, i ^ 1) for i in range(ngx)]
+        up = turn(own, "gx", ngx, 2)
+        down = turn(own, "gx", ngx, -2)
+        mate = lax.ppermute(own[0:24], "gx", swap)
+        three = jnp.concatenate([up[24:], own[24:], down[24:]], axis=0)
+        far_up = turn(three, "gx", ngx, 6)
+        far_down = turn(three, "gx", ngx, -6)
+        three_m = lax.ppermute(three, "gx", swap)
+        beyond = lax.ppermute(jnp.where(core == 0, down[0:24], up[0:24]), "gx", swap)
+        far_up_m = lax.ppermute(far_up, "gx", swap)
+        far_down_m = lax.ppermute(far_down, "gx", swap)
+        fine, pools, w_bot, _, w_flat = call(
+            lambda *refs: gather_kernel(ngx, block, *refs),
+            [
+                ((2, 24, 32, 128), BF),
+                ((11, 4, 32, 128), BF),
+                ((384, 576), BF),
+                ((ngx, slabs, 32, 128), BF),
+                ((ngx * block, lanes * 128), BF),
+            ],
+            [],
+            1,
+            ids,
+            own,
+            up,
+            down,
+            mate,
+            beyond,
+            far_up,
+            far_down,
+            three_m,
+            far_up_m,
+            far_down_m,
+        )
         w_enc, t_enc, w_mid, t_mid, w_top, t_top = call(
             lambda *refs: weight_kernel((1, 1, 1), (1, 1, 1), *refs),
             [
@@ -523,15 +600,12 @@
             w_upper,
             cost=4,
         )
-        (w_bot,) = call(
-            lambda *refs: weight_kernel((1,), (0,), *refs), [((384, 576), BF)], [], 0, w_all
-        )
         (t_bot,) = call(
             lambda *refs: weight_kernel((0,), (1,), *refs),
             [((192, 1152), BF)],
             [],
             0,
-            w_all,
+            w_flat,
             cost=2,
         )
 
@@ -574,8 +648,7 @@
             1,
             ids,
             own,
-            up,
-            down,
+            fine,
             pools,
             w_enc,
             w_bot,
@@ -589,14 +662,12 @@
             c["sum_mid"],
             c["pool_low"],
             cost=20,
-            grant=40,
+            grant=33,
         )
 
         from_left = shift(packed, "gy", ngy, 1)
         from_right = shift(packed, "gy", ngy, -1)
         line = jnp.stack([packed, from_left, from_right])
-        core = gx % 2
-        swap = [(i, i ^ 1) for i in range(ngx)]
         mate = lax.ppermute(line, "gx", swap)
         line_up = shift(line, "gx", ngx, 2)
         line_down = shift(line, "gx", ngx, -2)

time: 194 us -> 188 us (0.969)
  blocking collectives: 86.9 us -> 75.1 us
  waiting for transfers between devices: 20.2 us -> 28 us
  local copies, waits for them, and re-layouts: 13.1 us -> 5.47 us
  starting transfers between devices: 44.2 us -> 50.4 us
    ppermute x0 -> x9, starting transfers between devices: none -> 25.5 us  [the longest x4 12.1 us: turn(): lax.ppermute(value, axis, [(i, (i + step) % count) for i in range(count)])]
    ppermute x0 -> x9, waiting for transfers between devices: none -> 20.2 us  [the longest x4 20.2 us: turn(): lax.ppermute(value, axis, [(i, (i + step) % count) for i in range(count)])]
    all_to_all x1 -> x0, starting transfers between devices: 13.2 us -> none  [step(): lax.all_to_all(spread, 'gx', split_axis=0, concat_axis=0, tiled=True)]
    all_to_all x1 -> x0, waiting for transfers between devices: 12.4 us -> none  [step(): lax.all_to_all(spread, 'gx', split_axis=0, concat_axis=0, tiled=True)]
    all_to_all x1, blocking collectives: 56.8 us -> 45 us  [step(): lax.all_to_all(parts, AXES, split_axis=0, concat_axis=0, axis_index_group...]
    unnamed x68 -> x28, local copies, waits for them, and re-layouts: 11.2 us -> 3.61 us
    ppermute x8 -> x6, starting transfers between devices: 21.6 us -> 15.8 us  [shift(): lax.ppermute(value, axis, [(i, i + step) for i in range(count) if 0 <= i...]
    ppermute x8 -> x6, waiting for transfers between devices: 5 us -> 5.01 us  [shift(): lax.ppermute(value, axis, [(i, i + step) for i in range(count) if 0 <= i...]
  transfers between devices with their start and end apart: 13 -> 19, of which waited for: 7 -> 10; matrix products, arithmetic and copies ran while one was open for 1% -> 1% of each run, Pallas kernels for 1% -> 1%
where the time goes in v5:
time: 188 us
  blocking collectives  75.1 us (40%)
  starting transfers between devices  50.4 us (27%)
  waiting for transfers between devices  28 us (15%)
  Pallas kernels  23.6 us (13%)
  local copies, waits for them, and re-layouts  5.47 us (3%)
  other arithmetic  4.38 us (2%)
    all_to_all x1, blocking collectives, step(): lax.all_to_all(parts, AXES, split_axis=0, concat_axis=0, axis_index_group...  45 us
    all_to_all x1, blocking collectives, step(): lax.all_to_all(spread, AXES, split_axis=0, concat_axis=0, axis_index_grou...  30.1 us
    pallas_call x8, Pallas kernels, call(): pl.pallas_call(kernel, out_shape=[jax.ShapeDtypeStruct(s, d) for s, d in...  23.6 us
    ppermute x4, waiting for transfers between devices, turn(): lax.ppermute(value, axis, [(i, (i + step) % count) for i in range(count)])  20.2 us
    ppermute x6, starting transfers between devices, shift(): lax.ppermute(value, axis, [(i, i + step) for i in range(count) if 0 <= i...  15.8 us
    ppermute x4, starting transfers between devices, turn(): lax.ppermute(value, axis, [(i, (i + step) % count) for i in range(count)])  12.1 us
    ppermute x1, starting transfers between devices, step(): three_m = lax.ppermute(three, 'gx', swap)  8.78 us
    ppermute x6, waiting for transfers between devices, shift(): lax.ppermute(value, axis, [(i, i + step) for i in range(count) if 0 <= i...  5.01 us
  transfers between devices with their start and end apart: 19, of which 10 were waited for; matrix products, arithmetic and copies ran while one was open for 1% of the time, Pallas kernels for 1%

profile of v5, /device:TPU:1, one launch (start us, length us, event | category | flops | bytes accessed | tf_op | source)
XLA Modules:
  0.0 188.0 jit_solution(13462201696266650158)
XLA Ops:
  0.6 0.9 copy_bitcast_fusion
  1.5 0.0 copy-start.6
  1.6 0.8 copy-done.6
  2.4 0.2 shard_map.163
  2.5 3.9 %collective-permute-start.1 = (bf16[10,32,128]{2,1,0:T(8,128)(2,1)S(1)}, bf16[10,32,128]{2,1,0:T(8,128)(2,1)S(1)}, u32[]{:S(2)}, u32[]{:S(2)}) collective-permute-start(bf16[10,32,128]{2,1,0:T(8,128)(2,1)S(1)} %get-tuple-element.29), channel_id=1, source_target_pairs={{0,1},{1,2},{2,3},{3,4},{4,5},{5,6},{6,7},{7,8},{8,9},{9,10},{10,1... | collective-permute-start | bytes 245768 | tf_op jit(solution)/shard_map/ppermute | solution.py:488
  6.5 1.3 collective-permute-start
  7.8 0.1 collective-permute-done.1.left
  7.9 3.7 %collective-permute-done.right = bf16[10,32,128]{2,1,0:T(8,128)(2,1)S(1)} collective-permute-done((bf16[10,32,128]{2,1,0:T(8,128)(2,1)S(1)}, bf16[10,32,128]{2,1,0:T(8,128)(2,1)S(1)}, u32[]{:S(2)}, u32[]{:S(2)}) %collective-permute-start) | collective-permute-done | bytes 81952 | tf_op jit(solution)/shard_map/ppermute | solution.py:488
  11.7 9.4 %collective-permute-start.3 = (bf16[32,32,128]{2,1,0:T(8,128)(2,1)S(1)}, bf16[32,32,128]{2,1,0:T(8,128)(2,1)S(1)}, u32[]{:S(2)}, u32[]{:S(2)}) collective-permute-start(bf16[32,32,128]{2,1,0:T(8,128)(2,1)S(1)} %shard_map.164.refs_1_), channel_id=1, source_target_pairs={{0,224},{16,240},{32,0},{48,16},{64,32},{80,48},{96,64},{112,80},{... | collective-permute-start | bytes 786440 | tf_op jit(solution)/shard_map/ppermute | solution.py:492
  21.2 0.0 collective-permute-start.2
  21.2 2.5 %collective-permute-start.4 = (bf16[24,32,128]{2,1,0:T(8,128)(2,1)S(1)}, bf16[24,32,128]{2,1,0:T(8,128)(2,1)S(1)}, u32[]{:S(2)}, u32[]{:S(2)}) collective-permute-start(bf16[24,32,128]{2,1,0:T(8,128)(2,1)S(1)} %slice.100), channel_id=1, source_target_pairs={{0,16},{16,0},{32,48},{48,32},{64,80},{80,64},{96,112},{112,96},{1... | collective-permute-start | bytes 589832 | tf_op jit(solution)/shard_map/ppermute | solution.py:555
  23.7 1.2 collective-permute-done.3.refs_3_
  24.9 7.9 %collective-permute-done.2.refs_2_ = bf16[32,32,128]{2,1,0:T(8,128)(2,1)S(1)} collective-permute-done((bf16[32,32,128]{2,1,0:T(8,128)(2,1)S(1)}, bf16[32,32,128]{2,1,0:T(8,128)(2,1)S(1)}, u32[]{:S(2)}, u32[]{:S(2)}) %collective-permute-start.2) | collective-permute-done | bytes 262176 | tf_op jit(solution)/shard_map/ppermute | solution.py:492
  32.8 8.8 %collective-permute-start.8 = (bf16[24,32,128]{2,1,0:T(8,128)(2,1)S(1)}, bf16[24,32,128]{2,1,0:T(8,128)(2,1)S(1)}, u32[]{:S(2)}, u32[]{:S(2)}) collective-permute-start(bf16[24,32,128]{2,1,0:T(8,128)(2,1)S(1)} %pad_maximum_fusion.1), channel_id=1, source_target_pairs={{0,16},{16,0},{32,48},{48,32},{64,80},{80,64},{96,112},{112,96},{1... | collective-permute-start | bytes 589832 | tf_op jit(solution)/shard_map/ppermute | solution.py:559
  41.6 2.7 %collective-permute-start.6 = (bf16[24,32,128]{2,1,0:T(8,128)(2,1)S(1)}, bf16[24,32,128]{2,1,0:T(8,128)(2,1)S(1)}, u32[]{:S(2)}, u32[]{:S(2)}) collective-permute-start(bf16[24,32,128]{2,1,0:T(8,128)(2,1)S(1)} %pad_maximum_fusion.1), channel_id=1, source_target_pairs={{0,96},{16,112},{32,128},{48,144},{64,160},{80,176},{96,192},{112,... | collective-permute-start | bytes 589832 | tf_op jit(solution)/shard_map/ppermute | solution.py:492
  44.3 0.7 collective-permute-start.5
  45.1 4.1 %collective-permute-done.7.refs_7_ = bf16[24,32,128]{2,1,0:T(8,128)(2,1)S(1)} collective-permute-done((bf16[24,32,128]{2,1,0:T(8,128)(2,1)S(1)}, bf16[24,32,128]{2,1,0:T(8,128)(2,1)S(1)}, u32[]{:S(2)}, u32[]{:S(2)}) %collective-permute-start.7) | collective-permute-done | bytes 196640 | tf_op jit(solution)/shard_map/ppermute | solution.py:492
  49.2 0.9 collective-permute-start.10
  50.1 7.0 %collective-permute-done.6.refs_6_ = bf16[24,32,128]{2,1,0:T(8,128)(2,1)S(1)} collective-permute-done((bf16[24,32,128]{2,1,0:T(8,128)(2,1)S(1)}, bf16[24,32,128]{2,1,0:T(8,128)(2,1)S(1)}, u32[]{:S(2)}, u32[]{:S(2)}) %collective-permute-start.6) | collective-permute-done | bytes 196640 | tf_op jit(solution)/shard_map/ppermute | solution.py:492
  57.1 0.5 collective-permute-start.9
  57.6 0.1 pad_add_fusion.refs_0_
  57.6 0.9 shard_map.166
  58.5 0.0 copy-start.3
  58.5 0.0 copy-start.4
  58.5 0.0 copy-start.5
  58.6 0.0 copy-start.7
  58.6 0.0 copy-start.8
  58.6 0.0 collective-permute-done.5.refs_5_
  58.6 1.5 shard_map.165
  60.2 17.2 %shard_map.167 = (bf16[4,32,256]{2,1,0:T(8,128)(2,1)S(1)}, f32[4,32,256]{2,1,0:T(8,128)S(1)}, bf16[192,128]{1,0:T(8,128)(2,1)S(1)}, f32[4,64,128]{2,1,0:T(8,128)...) custom-call(s32[2]{0:T(128)S(1)} %pad_add_fusion.refs_0_, ...), custom_call_target="tpu_custom_call" | custom-call | flops 10000000000 | bytes 20000000 | tf_op jit(solution)/shard_map/pallas_call | solution.py:474
  77.4 1.3 collective-permute-start.12
  78.7 4.0 %collective-permute-start.11 = (bf16[192,128]{1,0:T(8,128)(2,1)S(1)}, bf16[192,128]{1,0:T(8,128)(2,1)S(1)}, u32[]{:S(2)}, u32[]{:S(2)}) collective-permute-start(bf16[192,128]{1,0:T(8,128)(2,1)S(1)} %get-tuple-element.39), channel_id=1, source_target_pairs={{0,1},{1,2},{2,3},{3,4},{4,5},{5,6},{6,7},{7,8},{8,9},{9,10},{10,1... | collective-permute-start | bytes 147464 | tf_op jit(solution)/shard_map/ppermute | solution.py:488
  82.7 1.1 collective-permute-done.11
  83.9 1.3 collective-permute-start.14
  85.2 4.0 %collective-permute-start.13 = (bf16[3,192,128]{2,1,0:T(8,128)(2,1)S(1)}, bf16[3,192,128]{2,1,0:T(8,128)(2,1)S(1)}, u32[]{:S(2)}, u32[]{:S(2)}) collective-permute-start(bf16[3,192,128]{2,1,0:T(8,128)(2,1)S(1)} %pad_maximum_fusion.2.refs_1_), channel_id=1, source_target_pairs={{0,32},{16,48},{32,64},{48,80},{64,96},{80,112},{96,128},{112,144}... | collective-permute-start | bytes 442376 | tf_op jit(solution)/shard_map/ppermute | solution.py:488
  89.2 0.1 constant_dynamic-update-slice_fusion.1
  89.3 2.2 %collective-permute-start.15 = (bf16[3,192,128]{2,1,0:T(8,128)(2,1)S(1)}, bf16[3,192,128]{2,1,0:T(8,128)(2,1)S(1)}, u32[]{:S(2)}, u32[]{:S(2)}) collective-permute-start(bf16[3,192,128]{2,1,0:T(8,128)(2,1)S(1)} %pad_maximum_fusion.2.refs_1_), channel_id=1, source_target_pairs={{0,16},{16,0},{32,48},{48,32},{64,80},{80,64},{96,112},{112,96},{1... | collective-permute-start | bytes 442376 | tf_op jit(solution)/shard_map/ppermute | solution.py:671
  91.5 2.5 %collective-permute-start.16 = (bf16[3,192,128]{2,1,0:T(8,128)(2,1)S(1)}, bf16[3,192,128]{2,1,0:T(8,128)(2,1)S(1)}, u32[]{:S(2)}, u32[]{:S(2)}) collective-permute-start(bf16[3,192,128]{2,1,0:T(8,128)(2,1)S(1)} %broadcast_select_fusion.2), channel_id=1, source_target_pairs={{0,16},{16,0},{32,48},{48,32},{64,80},{80,64},{96,112},{112,96},{1... | collective-permute-start | bytes 442376 | tf_op jit(solution)/shard_map/ppermute | solution.py:674
  94.0 0.6 shard_map.168.refs_9_
  94.6 0.1 constant_dynamic-update-slice_fusion
  94.7 0.3 collective-permute-done.16.refs_5_
  95.0 2.3 %shard_map.169 = (bf16[4,32,256]{2,1,0:T(8,128)(2,1)S(1)}, bf16[432,128]{1,0:T(8,128)(2,1)S(1)}) custom-call(s32[2]{0:T(128)S(1)} %pad_add_fusion.refs_0_, bf16[3,192,128]{2,1,0:T(8,128)(2,1)S(1)} %pad_maximum_fusion.2.refs_1_, bf16[3,192,128]{2,1,0:T(8,128)(2,1)S(1)} %collective-permute-done.13.refs_2_, ...), custom_call_target="tpu_custom_call" | custom-call | flops 2000000000 | bytes 4000000 | tf_op jit(solution)/shard_map/pallas_call | solution.py:474
  97.4 1.2 copy-done.9
  98.6 0.1 constant_dynamic-slice_fusion
  98.6 0.7 collective-permute-start.17
  99.3 1.9 %collective-permute-done.17 = bf16[384,8,128]{2,1,0:T(8,128)(2,1)S(1)} collective-permute-done((bf16[384,8,128]{2,1,0:T(8,128)(2,1)S(1)}, bf16[384,8,128]{2,1,0:T(8,128)(2,1)S(1)}, u32[]{:S(2)}, u32[]{:S(2)}) %collective-permute-start.17) | collective-permute-done | bytes 786464 | tf_op jit(solution)/shard_map/ppermute | solution.py:710
  101.2 1.3 add_convert_fusion
  102.6 45.0 %all_to_all.10 = bf16[128,24,128]{2,1,0:T(8,128)(2,1)S(1)} all-to-all(bf16[128,24,128]{2,1,0:T(8,128)(2,1)S(1)} %bitcast.67), channel_id=1, replica_groups={{0,1,2,3,4,5,6,7,8,9,10,11,12,13,14,15,32,33,34,35,36,37,38,39,40,41,42..., dimensions={0} | all-to-all | bytes 1572864 | tf_op jit(solution)/shard_map/all_to_all | solution.py:714
  147.5 0.2 reduce_sum.12
  147.7 0.1 broadcast_in_dim.10
  147.8 30.1 %all_to_all.11 = bf16[128,24,128]{2,1,0:T(8,128)(2,1)S(1)} all-to-all(bf16[128,24,128]{2,1,0:T(8,128)(2,1)S(1)} %broadcast_in_dim.10), channel_id=1, replica_groups={{0,1,2,3,4,5,6,7,8,9,10,11,12,13,14,15,32,33,34,35,36,37,38,39,40,41,42..., dimensions={0} | all-to-all | bytes 1572864 | tf_op jit(solution)/shard_map/all_to_all | solution.py:719
  177.9 3.7 %collective-permute-start.18 = (bf16[384,8,128]{2,1,0:T(8,128)(2,1)S(1)}, bf16[384,8,128]{2,1,0:T(8,128)(2,1)S(1)}, u32[]{:S(2)}, u32[]{:S(2)}) collective-permute-start(bf16[384,8,128]{2,1,0:T(8,128)(2,1)S(1)} %bitcast.68), channel_id=1, source_target_pairs={{0,16},{16,0},{32,48},{48,32},{64,80},{80,64},{96,112},{112,96},{1... | collective-permute-start | bytes 2359304 | tf_op jit(solution)/shard_map/ppermute | solution.py:723
  181.7 0.7 copy.20
  182.4 0.7 copy.21
  183.0 0.5 collective-permute-done.18
  183.6 0.1 broadcast_select_fusion
  183.7 0.1 pad_maximum_fusion
  183.8 0.8 shard_map.170
  184.8 0.1 concatenate.20
  184.9 0.6 convert_element_type.25
  185.5 0.1 concatenate.23
  185.7 0.8 convert_element_type.27
  186.4 0.4 concatenate.22
  186.8 1.2 convert_element_type.26
  (42 shorter events, 0.4 us)
Async XLA Ops:
  0.6 7.2 %copy-start.10 = (bf16[8,1728]{1,0:T(8,128)(2,1)S(1)}, bf16[8,1728]{1,0:T(8,128)(2,1)}, u32[]{:S(2)}) copy-start(bf16[8,1728]{1,0:T(8,128)(2,1)} %param.14) | copy-start | bytes 82948
  1.5 0.8 copy-start.6
  2.5 5.4 %collective-permute-start.1 = (bf16[10,32,128]{2,1,0:T(8,128)(2,1)S(1)}, bf16[10,32,128]{2,1,0:T(8,128)(2,1)S(1)}, u32[]{:S(2)}, u32[]{:S(2)}) collective-permute-start(bf16[10,32,128]{2,1,0:T(8,128)(2,1)S(1)} %get-tuple-element.29), channel_id=1, source_target_pairs={{0,1},{1,2},{2,3},{3,4},{4,5},{5,6},{6,7},{7,8},{8,9},{9,10},{10,1... | collective-permute-start | bytes 245768 | tf_op jit(solution)/shard_map/ppermute | solution.py:488
  6.5 5.2 %collective-permute-start = (bf16[10,32,128]{2,1,0:T(8,128)(2,1)S(1)}, bf16[10,32,128]{2,1,0:T(8,128)(2,1)S(1)}, u32[]{:S(2)}, u32[]{:S(2)}) collective-permute-start(bf16[10,32,128]{2,1,0:T(8,128)(2,1)S(1)} %get-tuple-element.28.own), channel_id=1, source_target_pairs={{1,0},{2,1},{3,2},{4,3},{5,4},{6,5},{7,6},{8,7},{9,8},{10,9},{11,1... | collective-permute-start | bytes 245768 | tf_op jit(solution)/shard_map/ppermute | solution.py:488
  11.7 46.0 %copy-start = (bf16[64,5184]{1,0:T(8,128)(2,1)S(1)}, bf16[64,5184]{1,0:T(8,128)(2,1)}, u32[]{:S(2)}) copy-start(bf16[64,5184]{1,0:T(8,128)(2,1)} %refs_1_.1) | copy-start | bytes 1990660
  11.7 46.0 %copy-start.1 = (bf16[32,2592]{1,0:T(8,128)(2,1)S(1)}, bf16[32,2592]{1,0:T(8,128)(2,1)}, u32[]{:S(2)}) copy-start(bf16[32,2592]{1,0:T(8,128)(2,1)} %refs_2_.1) | copy-start | bytes 497668
  11.7 46.0 %copy-start.2 = (bf16[64,864]{1,0:T(8,128)(2,1)S(1)}, bf16[64,864]{1,0:T(8,128)(2,1)}, u32[]{:S(2)}) copy-start(bf16[64,864]{1,0:T(8,128)(2,1)} %refs_0_.1) | copy-start | bytes 331780
  11.7 13.1 %collective-permute-start.3 = (bf16[32,32,128]{2,1,0:T(8,128)(2,1)S(1)}, bf16[32,32,128]{2,1,0:T(8,128)(2,1)S(1)}, u32[]{:S(2)}, u32[]{:S(2)}) collective-permute-start(bf16[32,32,128]{2,1,0:T(8,128)(2,1)S(1)} %shard_map.164.refs_1_), channel_id=1, source_target_pairs={{0,224},{16,240},{32,0},{48,16},{64,32},{80,48},{96,64},{112,80},{... | collective-permute-start | bytes 786440 | tf_op jit(solution)/shard_map/ppermute | solution.py:492
  21.2 11.6 %collective-permute-start.2 = (bf16[32,32,128]{2,1,0:T(8,128)(2,1)S(1)}, bf16[32,32,128]{2,1,0:T(8,128)(2,1)S(1)}, u32[]{:S(2)}, u32[]{:S(2)}) collective-permute-start(bf16[32,32,128]{2,1,0:T(8,128)(2,1)S(1)} %shard_map.164.refs_1_), channel_id=1, source_target_pairs={{0,32},{16,48},{32,64},{48,80},{64,96},{80,112},{96,128},{112,144}... | collective-permute-start | bytes 786440 | tf_op jit(solution)/shard_map/ppermute | solution.py:492
  21.2 37.4 %collective-permute-start.4 = (bf16[24,32,128]{2,1,0:T(8,128)(2,1)S(1)}, bf16[24,32,128]{2,1,0:T(8,128)(2,1)S(1)}, u32[]{:S(2)}, u32[]{:S(2)}) collective-permute-start(bf16[24,32,128]{2,1,0:T(8,128)(2,1)S(1)} %slice.100), channel_id=1, source_target_pairs={{0,16},{16,0},{32,48},{48,32},{64,80},{80,64},{96,112},{112,96},{1... | collective-permute-start | bytes 589832 | tf_op jit(solution)/shard_map/ppermute | solution.py:555
  32.8 25.8 %collective-permute-start.8 = (bf16[24,32,128]{2,1,0:T(8,128)(2,1)S(1)}, bf16[24,32,128]{2,1,0:T(8,128)(2,1)S(1)}, u32[]{:S(2)}, u32[]{:S(2)}) collective-permute-start(bf16[24,32,128]{2,1,0:T(8,128)(2,1)S(1)} %pad_maximum_fusion.1), channel_id=1, source_target_pairs={{0,16},{16,0},{32,48},{48,32},{64,80},{80,64},{96,112},{112,96},{1... | collective-permute-start | bytes 589832 | tf_op jit(solution)/shard_map/ppermute | solution.py:559
  41.6 7.6 %collective-permute-start.7 = (bf16[24,32,128]{2,1,0:T(8,128)(2,1)S(1)}, bf16[24,32,128]{2,1,0:T(8,128)(2,1)S(1)}, u32[]{:S(2)}, u32[]{:S(2)}) collective-permute-start(bf16[24,32,128]{2,1,0:T(8,128)(2,1)S(1)} %pad_maximum_fusion.1), channel_id=1, source_target_pairs={{0,160},{16,176},{32,192},{48,208},{64,224},{80,240},{96,0},{112,1... | collective-permute-start | bytes 589832 | tf_op jit(solution)/shard_map/ppermute | solution.py:492
  41.6 15.5 %collective-permute-start.6 = (bf16[24,32,128]{2,1,0:T(8,128)(2,1)S(1)}, bf16[24,32,128]{2,1,0:T(8,128)(2,1)S(1)}, u32[]{:S(2)}, u32[]{:S(2)}) collective-permute-start(bf16[24,32,128]{2,1,0:T(8,128)(2,1)S(1)} %pad_maximum_fusion.1), channel_id=1, source_target_pairs={{0,96},{16,112},{32,128},{48,144},{64,160},{80,176},{96,192},{112,... | collective-permute-start | bytes 589832 | tf_op jit(solution)/shard_map/ppermute | solution.py:492
  44.3 14.3 %collective-permute-start.5 = (bf16[24,32,128]{2,1,0:T(8,128)(2,1)S(1)}, bf16[24,32,128]{2,1,0:T(8,128)(2,1)S(1)}, u32[]{:S(2)}, u32[]{:S(2)}) collective-permute-start(bf16[24,32,128]{2,1,0:T(8,128)(2,1)S(1)} %slice_select_fusion), channel_id=1, source_target_pairs={{0,16},{16,0},{32,48},{48,32},{64,80},{80,64},{96,112},{112,96},{1... | collective-permute-start | bytes 589832 | tf_op jit(solution)/shard_map/ppermute | solution.py:560
  49.2 9.4 %collective-permute-start.10 = (bf16[24,32,128]{2,1,0:T(8,128)(2,1)S(1)}, bf16[24,32,128]{2,1,0:T(8,128)(2,1)S(1)}, u32[]{:S(2)}, u32[]{:S(2)}) collective-permute-start(bf16[24,32,128]{2,1,0:T(8,128)(2,1)S(1)} %collective-permute-done.7.refs_7_), channel_id=1, source_target_pairs={{0,16},{16,0},{32,48},{48,32},{64,80},{80,64},{96,112},{112,96},{1... | collective-permute-start | bytes 589832 | tf_op jit(solution)/shard_map/ppermute | solution.py:562
  57.1 1.5 collective-permute-start.9
  58.5 1.6 copy-start.3
  58.5 1.6 copy-start.4
  58.5 1.6 copy-start.5
  58.6 1.6 copy-start.7
  58.6 1.6 copy-start.8
  77.4 5.3 %collective-permute-start.12 = (bf16[192,128]{1,0:T(8,128)(2,1)S(1)}, bf16[192,128]{1,0:T(8,128)(2,1)S(1)}, u32[]{:S(2)}, u32[]{:S(2)}) collective-permute-start(bf16[192,128]{1,0:T(8,128)(2,1)S(1)} %get-tuple-element.39), channel_id=1, source_target_pairs={{1,0},{2,1},{3,2},{4,3},{5,4},{6,5},{7,6},{8,7},{9,8},{10,9},{11,1... | collective-permute-start | bytes 147464 | tf_op jit(solution)/shard_map/ppermute | solution.py:488
  78.7 5.2 %collective-permute-start.11 = (bf16[192,128]{1,0:T(8,128)(2,1)S(1)}, bf16[192,128]{1,0:T(8,128)(2,1)S(1)}, u32[]{:S(2)}, u32[]{:S(2)}) collective-permute-start(bf16[192,128]{1,0:T(8,128)(2,1)S(1)} %get-tuple-element.39), channel_id=1, source_target_pairs={{0,1},{1,2},{2,3},{3,4},{4,5},{5,6},{6,7},{7,8},{8,9},{9,10},{10,1... | collective-permute-start | bytes 147464 | tf_op jit(solution)/shard_map/ppermute | solution.py:488
  83.9 7.6 %collective-permute-start.14 = (bf16[3,192,128]{2,1,0:T(8,128)(2,1)S(1)}, bf16[3,192,128]{2,1,0:T(8,128)(2,1)S(1)}, u32[]{:S(2)}, u32[]{:S(2)}) collective-permute-start(bf16[3,192,128]{2,1,0:T(8,128)(2,1)S(1)} %pad_maximum_fusion.2.refs_1_), channel_id=1, source_target_pairs={{32,0},{48,16},{64,32},{80,48},{96,64},{112,80},{128,96},{144,112}... | collective-permute-start | bytes 442376 | tf_op jit(solution)/shard_map/ppermute | solution.py:488
  85.2 6.3 %collective-permute-start.13 = (bf16[3,192,128]{2,1,0:T(8,128)(2,1)S(1)}, bf16[3,192,128]{2,1,0:T(8,128)(2,1)S(1)}, u32[]{:S(2)}, u32[]{:S(2)}) collective-permute-start(bf16[3,192,128]{2,1,0:T(8,128)(2,1)S(1)} %pad_maximum_fusion.2.refs_1_), channel_id=1, source_target_pairs={{0,32},{16,48},{32,64},{48,80},{64,96},{80,112},{96,128},{112,144}... | collective-permute-start | bytes 442376 | tf_op jit(solution)/shard_map/ppermute | solution.py:488
  89.3 5.4 %collective-permute-start.15 = (bf16[3,192,128]{2,1,0:T(8,128)(2,1)S(1)}, bf16[3,192,128]{2,1,0:T(8,128)(2,1)S(1)}, u32[]{:S(2)}, u32[]{:S(2)}) collective-permute-start(bf16[3,192,128]{2,1,0:T(8,128)(2,1)S(1)} %pad_maximum_fusion.2.refs_1_), channel_id=1, source_target_pairs={{0,16},{16,0},{32,48},{48,32},{64,80},{80,64},{96,112},{112,96},{1... | collective-permute-start | bytes 442376 | tf_op jit(solution)/shard_map/ppermute | solution.py:671
  91.5 3.5 %collective-permute-start.16 = (bf16[3,192,128]{2,1,0:T(8,128)(2,1)S(1)}, bf16[3,192,128]{2,1,0:T(8,128)(2,1)S(1)}, u32[]{:S(2)}, u32[]{:S(2)}) collective-permute-start(bf16[3,192,128]{2,1,0:T(8,128)(2,1)S(1)} %broadcast_select_fusion.2), channel_id=1, source_target_pairs={{0,16},{16,0},{32,48},{48,32},{64,80},{80,64},{96,112},{112,96},{1... | collective-permute-start | bytes 442376 | tf_op jit(solution)/shard_map/ppermute | solution.py:674
  97.4 1.2 copy-start.9
  98.6 2.6 %collective-permute-start.17 = (bf16[384,8,128]{2,1,0:T(8,128)(2,1)S(1)}, bf16[384,8,128]{2,1,0:T(8,128)(2,1)S(1)}, u32[]{:S(2)}, u32[]{:S(2)}) collective-permute-start(bf16[384,8,128]{2,1,0:T(8,128)(2,1)S(1)} %constant_dynamic-slice_fusion), channel_id=1, source_target_pairs={{0,16},{16,0},{32,48},{48,32},{64,80},{80,64},{96,112},{112,96},{1... | collective-permute-start | bytes 2359304 | tf_op jit(solution)/shard_map/ppermute | solution.py:710
  177.9 5.7 %collective-permute-start.18 = (bf16[384,8,128]{2,1,0:T(8,128)(2,1)S(1)}, bf16[384,8,128]{2,1,0:T(8,128)(2,1)S(1)}, u32[]{:S(2)}, u32[]{:S(2)}) collective-permute-start(bf16[384,8,128]{2,1,0:T(8,128)(2,1)S(1)} %bitcast.68), channel_id=1, source_target_pairs={{0,16},{16,0},{32,48},{48,32},{64,80},{80,64},{96,112},{112,96},{1... | collective-permute-start | bytes 2359304 | tf_op jit(solution)/shard_map/ppermute | solution.py:723

commit v6 on v5

--- a/solution.py
+++ b/solution.py
@@ -148,7 +148,7 @@
         to_right[8 + q] = pooled
 
 
-def widen_kernel(skip, cot, own, right, left, weight, out):
+def widen_kernel(skip, cot, own, right, left, out):
     first = jnp.where(lax.broadcasted_iota(jnp.int32, (32, 128), 1) < 64, 1.0, 0.0)
     head = first.astype(BF)
     tail = (1.0 - first).astype(BF)
@@ -161,50 +161,46 @@
     for q in range(2):
         out[24 + 2 * q] = own[8 + q] * head + right[8 + q] * tail
         out[25 + 2 * q] = left[8 + q] * tail
-    for q in range(weight.shape[0]):
-        out[28 + q] = weight[q]
 
 
 def gather_kernel(tiles, block, *refs):
-    (ids, own, up, down, mate, beyond, far_up, far_down, three_m, far_up_m, far_down_m) = refs[:11]
-    (fine, pools, w_out, w_all, w_flat) = refs[11:16]
+    (ids, own, up, down, far_up, far_down, mate, beyond, w_mine, w_mate) = refs[:10]
+    (fine, pools, w_out, w_all, w_flat) = refs[10:15]
     gx = ids[0]
     core = gx % 2
-    wide = own.shape[0] - 24
     low = jnp.where(core == 0, 1.0, 0.0)
     below = jnp.full((24, 32, 128), low).astype(BF)
     above = jnp.full((24, 32, 128), 1.0 - low).astype(BF)
-    first = beyond[...] * below + mate[0:24] * above
-    last = mate[0:24] * below + beyond[...] * above
-    top = jnp.full((12, 32, 128), row_ok(gx - 1, tiles)).astype(BF)
-    bottom = jnp.full((12, 32, 128), row_ok(gx + 1, tiles)).astype(BF)
-    for k in range(2):
-        fine[0, 12 * k : 12 * k + 12] = first[12 * k : 12 * k + 12] * top
-        fine[1, 12 * k : 12 * k + 12] = last[12 * k : 12 * k + 12] * bottom
-
-    def chips(own_at, down_at, up_at, far_down_ref, far_up_ref):
-        return [
-            own_at,
-            down_at,
-            (far_down_ref, 0),
-            (far_down_ref, wide),
-            (far_down_ref, 2 * wide),
-            (far_up_ref, wide),
-            (far_up_ref, 2 * wide),
-            up_at,
-        ]
-
-    mine = chips((own, 24), (down, 24), (up, 24), far_down, far_up)
-    other = chips((three_m, wide), (three_m, 2 * wide), (three_m, 0), far_down_m, far_up_m)
-    for parity, entries in ((gx, mine), (gx + 1 - 2 * core, other)):
-        for j, (ref, at) in enumerate(entries):
-            w_all[(parity + 2 * j) % tiles] = ref[at + 4 : at + wide]
-        for j, step in ((0, 0), (1, 2), (2, 4), (6, -4), (7, -2)):
-            tile = parity + step
-            ref, at = entries[j]
-            place = tile - gx + 5
-            keep = jnp.full((4, 32, 128), row_ok(tile, tiles)).astype(BF)
-            pools[place] = ref[at : at + 4] * keep
+    first = beyond[0:24] * below + mate[0:24] * above
+    last = mate[0:24] * below + beyond[0:24] * above
+    fine[0] = first
+    fine[1] = last
+
+    for place, (ref, at) in (
+        (1, (far_up, 0)),
+        (3, (up, 24)),
+        (5, (own, 24)),
+        (7, (down, 24)),
+        (9, (far_down, 0)),
+    ):
+        pools[place] = ref[at : at + 4]
+    centre = 6 - 2 * core
+    pools[centre - 2] = beyond[24:28]
+    pools[centre] = mate[24:28]
+    pools[centre + 2] = beyond[28:32]
+    pools[centre - 4 + 8 * core] = beyond[32:36]
+
+    slabs = w_all.shape[1]
+    around = tiles // 4
+    y = (gx // 2) % around
+    side = gx // (2 * around)
+    for lane_core, ref in ((core, w_mine), (1 - core, w_mate)):
+        for far in range(2):
+            for k in range(around):
+                z_part = (side + far) % 2
+                y_part = (y + around - k) % around
+                at = (far * around + k) * slabs
+                w_all[(z_part * around + y_part) * 2 + lane_core] = ref[at : at + slabs]
     lanes = w_flat.shape[1] // 128
     for b in range(tiles):
         rows = w_all[b].reshape(lanes * block, 128)
@@ -488,10 +484,6 @@
     return lax.ppermute(value, axis, [(i, i + step) for i in range(count) if 0 <= i + step < count])
 
 
-def turn(value, axis, count, step):
-    return lax.ppermute(value, axis, [(i, (i + step) % count) for i in range(count)])
-
-
 def tiles_of(g):
     rows, width = g.shape
     return g.reshape(rows // 8, 8, width // 128, 128).transpose(0, 2, 1, 3).reshape(-1, 8, 128)
@@ -529,6 +521,28 @@
         lanes = weight.shape[1] // 128
         weight = weight.reshape(block, lanes, 128).transpose(1, 0, 2).reshape(slabs, 32, 128)
 
+        swap = [(i, i ^ 1) for i in range(ngx)]
+        around = ngx // 4
+
+        def along_y(i, k):
+            side, y, core = i // (2 * around), i // 2 % around, i % 2
+            return (side * around + (y + k) % around) * 2 + core
+
+        part = ngy // 4 if ngy % 4 == 0 else ngy
+
+        def mirrored(i):
+            x, y = i // ngy, i % ngy
+            y = (ngy // part - 1 - y // part) * part + y % part
+            return (x + ngx // 2) % ngx * ngy + y
+
+        w_line = [weight]
+        for k in range(1, around):
+            w_line.append(lax.ppermute(weight, "gx", [(i, along_y(i, k)) for i in range(ngx)]))
+        w_line = jnp.concatenate(w_line, axis=0)
+        w_far = lax.ppermute(w_line, AXES, [(i, mirrored(i)) for i in range(devices)])
+        w_mine = jnp.concatenate([w_line, w_far], axis=0)
+        w_mate = lax.ppermute(w_mine, "gx", swap)
+
         skip = skip_input.transpose(1, 0, 2)
         cot = cotangent.transpose(1, 0, 2)
         to_left, to_right = call(
@@ -536,30 +550,20 @@
         )
         right = shift(to_left, "gy", ngy, -1)
         left = shift(to_right, "gy", ngy, 1)
-        (own,) = call(
-            widen_kernel,
-            [((28 + slabs, 32, 128), BF)],
-            [],
-            0,
-            skip,
-            cot,
-            to_left,
-            right,
-            left,
-            weight,
-        )
+        (own,) = call(widen_kernel, [((28, 32, 128), BF)], [], 0, skip, cot, to_left, right, left)
         core = gx % 2
-        swap = [(i, i ^ 1) for i in range(ngx)]
-        up = turn(own, "gx", ngx, 2)
-        down = turn(own, "gx", ngx, -2)
-        mate = lax.ppermute(own[0:24], "gx", swap)
-        three = jnp.concatenate([up[24:], own[24:], down[24:]], axis=0)
-        far_up = turn(three, "gx", ngx, 6)
-        far_down = turn(three, "gx", ngx, -6)
-        three_m = lax.ppermute(three, "gx", swap)
-        beyond = lax.ppermute(jnp.where(core == 0, down[0:24], up[0:24]), "gx", swap)
-        far_up_m = lax.ppermute(far_up, "gx", swap)
-        far_down_m = lax.ppermute(far_down, "gx", swap)
+        up = shift(own, "gx", ngx, 2)
+        down = shift(own, "gx", ngx, -2)
+        far_up = shift(own[24:28], "gx", ngx, 4)
+        far_down = shift(own[24:28], "gx", ngx, -4)
+        mate = lax.ppermute(own, "gx", swap)
+        beyond = [
+            jnp.where(core == 0, down[0:24], up[0:24]),
+            up[24:28],
+            down[24:28],
+            jnp.where(core == 0, far_down, far_up),
+        ]
+        beyond = lax.ppermute(jnp.concatenate(beyond, axis=0), "gx", swap)
         fine, pools, w_bot, _, w_flat = call(
             lambda *refs: gather_kernel(ngx, block, *refs),
             [
@@ -575,13 +579,12 @@
             own,
             up,
             down,
+            far_up,
+            far_down,
             mate,
             beyond,
-            far_up,
-            far_down,
-            three_m,
-            far_up_m,
-            far_down_m,
+            w_mine,
+            w_mate,
         )
         w_enc, t_enc, w_mid, t_mid, w_top, t_top = call(
             lambda *refs: weight_kernel((1, 1, 1), (1, 1, 1), *refs),

time: 188 us -> 193 us (1.027)
  waiting for transfers between devices: 28 us -> 8.4 us
  blocking collectives: 75.1 us -> 91.3 us
  starting transfers between devices: 50.4 us -> 57.2 us
    ppermute x9 -> x7, waiting for transfers between devices: 20.2 us -> 0.17 us  [the longest x1 0.16 us: step(): beyond = lax.ppermute(jnp.concatenate(beyond, axis=0), 'gx', swap)]
    all_to_all x1, blocking collectives: 45 us -> 61.2 us  [step(): lax.all_to_all(parts, AXES, split_axis=0, concat_axis=0, axis_index_group...]
    ppermute x6 -> x10, starting transfers between devices: 15.8 us -> 30.4 us  [shift(): lax.ppermute(value, axis, [(i, i + step) for i in range(count) if 0 <= i...]
    ppermute x9 -> x7, starting transfers between devices: 25.5 us -> 18 us  [the longest x1 8.64 us: step(): lax.ppermute(w_line, AXES, [(i, mirrored(i)) for i in range(devices)])]
    ppermute x6 -> x10, waiting for transfers between devices: 5.01 us -> 5.42 us  [shift(): lax.ppermute(value, axis, [(i, i + step) for i in range(count) if 0 <= i...]
  transfers between devices with their start and end apart: 19 -> 21, of which waited for: 10 -> 8; matrix products, arithmetic and copies ran while one was open for 1% -> 1% of each run, Pallas kernels for 1% -> 1%
where the time goes in v6:
time: 193 us; the launch traced here: 192 us
  blocking collectives  91.3 us (47%)
  starting transfers between devices  57.2 us (30%)
  Pallas kernels  23.6 us (12%)
  waiting for transfers between devices  8.4 us (4%)
  local copies, waits for them, and re-layouts  6.25 us (3%)
  other arithmetic  4.43 us (2%)
    all_to_all x1, blocking collectives, step(): lax.all_to_all(parts, AXES, split_axis=0, concat_axis=0, axis_index_group...  61.2 us
    ppermute x10, starting transfers between devices, shift(): lax.ppermute(value, axis, [(i, i + step) for i in range(count) if 0 <= i...  30.4 us
    all_to_all x1, blocking collectives, step(): lax.all_to_all(spread, AXES, split_axis=0, concat_axis=0, axis_index_grou...  30.1 us
    pallas_call x8, Pallas kernels, call(): pl.pallas_call(kernel, out_shape=[jax.ShapeDtypeStruct(s, d) for s, d in...  23.6 us
    ppermute x1, starting transfers between devices, step(): lax.ppermute(w_line, AXES, [(i, mirrored(i)) for i in range(devices)])  8.64 us
    ppermute x10, waiting for transfers between devices, shift(): lax.ppermute(value, axis, [(i, i + step) for i in range(count) if 0 <= i...  5.42 us
    ppermute x3, starting transfers between devices, step(): lax.ppermute(weight, 'gx', [(i, along_y(i, k)) for i in range(ngx)])  4.59 us
  transfers between devices with their start and end apart: 21, of which 8 were waited for; matrix products, arithmetic and copies ran while one was open for 1% of the time, Pallas kernels for 1%

profile of v6, /device:TPU:1, one launch (start us, length us, event | category | flops | bytes accessed | tf_op | source)
XLA Modules:
  0.0 192.4 jit_solution(6028606826444949541)
XLA Ops:
  0.6 0.8 pad.4
  1.4 3.6 %collective-permute-start.10 = (bf16[4,32,128]{2,1,0:T(8,128)(2,1)S(1)}, bf16[4,32,128]{2,1,0:T(8,128)(2,1)S(1)}, u32[]{:S(2)}, u32[]{:S(2)}) collective-permute-start(bf16[4,32,128]{2,1,0:T(8,128)(2,1)S(1)} %bitcast.72), channel_id=1, source_target_pairs={{0,96},{16,112},{32,0},{48,16},{64,32},{80,48},{96,64},{112,80},{1... | collective-permute-start | bytes 98312 | tf_op jit(solution)/shard_map/ppermute | solution.py:540
  4.9 0.3 collective-permute-start.9
  5.3 0.7 collective-permute-start.8
  6.0 0.9 copy_bitcast_fusion
  6.9 0.0 copy-start.6
  6.9 0.8 copy-done.6
  7.7 0.2 shard_map.163
  7.9 3.1 %collective-permute-start.1 = (bf16[10,32,128]{2,1,0:T(8,128)(2,1)S(1)}, bf16[10,32,128]{2,1,0:T(8,128)(2,1)S(1)}, u32[]{:S(2)}, u32[]{:S(2)}) collective-permute-start(bf16[10,32,128]{2,1,0:T(8,128)(2,1)S(1)} %get-tuple-element.29), channel_id=1, source_target_pairs={{0,1},{1,2},{2,3},{3,4},{4,5},{5,6},{6,7},{7,8},{8,9},{9,10},{10,1... | collective-permute-start | bytes 245768 | tf_op jit(solution)/shard_map/ppermute | solution.py:484
  11.0 1.3 collective-permute-start
  12.4 8.6 %collective-permute-start.11 = (bf16[16,32,128]{2,1,0:T(8,128)(2,1)S(1)}, bf16[16,32,128]{2,1,0:T(8,128)(2,1)S(1)}, u32[]{:S(2)}, u32[]{:S(2)}) collective-permute-start(bf16[16,32,128]{2,1,0:T(8,128)(2,1)S(1)} %pad_maximum_fusion.3), channel_id=1, source_target_pairs={{0,140},{1,141},{2,142},{3,143},{4,136},{5,137},{6,138},{7,139},{8... | collective-permute-start | bytes 393224 | tf_op jit(solution)/shard_map/ppermute | solution.py:542
  21.2 1.4 collective-permute-start.5
  22.6 5.5 %collective-permute-start.4 = (bf16[4,32,128]{2,1,0:T(8,128)(2,1)S(1)}, bf16[4,32,128]{2,1,0:T(8,128)(2,1)S(1)}, u32[]{:S(2)}, u32[]{:S(2)}) collective-permute-start(bf16[4,32,128]{2,1,0:T(8,128)(2,1)S(1)} %slice.97), channel_id=1, source_target_pairs={{0,64},{16,80},{32,96},{48,112},{64,128},{80,144},{96,160},{112,17... | collective-permute-start | bytes 98312 | tf_op jit(solution)/shard_map/ppermute | solution.py:484
  28.1 3.0 %collective-permute-start.6 = (bf16[28,32,128]{2,1,0:T(8,128)(2,1)S(1)}, bf16[28,32,128]{2,1,0:T(8,128)(2,1)S(1)}, u32[]{:S(2)}, u32[]{:S(2)}) collective-permute-start(bf16[28,32,128]{2,1,0:T(8,128)(2,1)S(1)} %shard_map.164.refs_1_), channel_id=1, source_target_pairs={{0,16},{16,0},{32,48},{48,32},{64,80},{80,64},{96,112},{112,96},{1... | collective-permute-start | bytes 688136 | tf_op jit(solution)/shard_map/ppermute | solution.py:559
  31.1 1.3 collective-permute-start.3
  32.4 4.2 %collective-permute-start.2 = (bf16[28,32,128]{2,1,0:T(8,128)(2,1)S(1)}, bf16[28,32,128]{2,1,0:T(8,128)(2,1)S(1)}, u32[]{:S(2)}, u32[]{:S(2)}) collective-permute-start(bf16[28,32,128]{2,1,0:T(8,128)(2,1)S(1)} %shard_map.164.refs_1_), channel_id=1, source_target_pairs={{0,32},{16,48},{32,64},{48,80},{64,96},{80,112},{96,128},{112,144}... | collective-permute-start | bytes 688136 | tf_op jit(solution)/shard_map/ppermute | solution.py:484
  36.6 0.5 collective-permute-start.12
  37.2 3.3 %collective-permute-done.3.refs_3_ = bf16[28,32,128]{2,1,0:T(8,128)(2,1)S(1)} collective-permute-done((bf16[28,32,128]{2,1,0:T(8,128)(2,1)S(1)}, bf16[28,32,128]{2,1,0:T(8,128)(2,1)S(1)}, u32[]{:S(2)}, u32[]{:S(2)}) %collective-permute-start.3) | collective-permute-done | bytes 229408 | tf_op jit(solution)/shard_map/ppermute | solution.py:484
  40.5 0.9 collective-permute-done.2.refs_2_
  41.4 1.3 collective-permute-start.7
  42.7 0.1 pad_add_fusion.refs_0_
  42.8 0.9 shard_map.166
  43.7 0.0 copy-start.3
  43.7 0.0 copy-start.5
  43.7 0.0 copy-start.7
  43.7 0.0 copy-start.8
  43.8 0.2 collective-permute-done.7.refs_7_
  43.9 1.5 shard_map.165
  45.5 17.3 %shard_map.167 = (bf16[4,32,256]{2,1,0:T(8,128)(2,1)S(1)}, f32[4,32,256]{2,1,0:T(8,128)S(1)}, bf16[192,128]{1,0:T(8,128)(2,1)S(1)}, f32[4,64,128]{2,1,0:T(8,128)...) custom-call(s32[2]{0:T(128)S(1)} %pad_add_fusion.refs_0_, ...), custom_call_target="tpu_custom_call" | custom-call | flops 10000000000 | bytes 20000000 | tf_op jit(solution)/shard_map/pallas_call | solution.py:470
  62.8 1.3 collective-permute-start.14
  64.1 4.0 %collective-permute-start.13 = (bf16[192,128]{1,0:T(8,128)(2,1)S(1)}, bf16[192,128]{1,0:T(8,128)(2,1)S(1)}, u32[]{:S(2)}, u32[]{:S(2)}) collective-permute-start(bf16[192,128]{1,0:T(8,128)(2,1)S(1)} %get-tuple-element.39), channel_id=1, source_target_pairs={{0,1},{1,2},{2,3},{3,4},{4,5},{5,6},{6,7},{7,8},{8,9},{9,10},{10,1... | collective-permute-start | bytes 147464 | tf_op jit(solution)/shard_map/ppermute | solution.py:484
  68.1 1.1 collective-permute-done.13
  69.3 1.3 collective-permute-start.16
  70.6 7.1 %collective-permute-start.15 = (bf16[3,192,128]{2,1,0:T(8,128)(2,1)S(1)}, bf16[3,192,128]{2,1,0:T(8,128)(2,1)S(1)}, u32[]{:S(2)}, u32[]{:S(2)}) collective-permute-start(bf16[3,192,128]{2,1,0:T(8,128)(2,1)S(1)} %pad_maximum_fusion.2.refs_1_), channel_id=1, source_target_pairs={{0,32},{16,48},{32,64},{48,80},{64,96},{80,112},{96,128},{112,144}... | collective-permute-start | bytes 442376 | tf_op jit(solution)/shard_map/ppermute | solution.py:484
  77.6 0.1 constant_dynamic-update-slice_fusion.6
  77.7 1.9 collective-permute-start.17
  79.6 0.1 collective-permute-done.15.refs_2_
  79.7 2.5 %collective-permute-start.18 = (bf16[3,192,128]{2,1,0:T(8,128)(2,1)S(1)}, bf16[3,192,128]{2,1,0:T(8,128)(2,1)S(1)}, u32[]{:S(2)}, u32[]{:S(2)}) collective-permute-start(bf16[3,192,128]{2,1,0:T(8,128)(2,1)S(1)} %broadcast_select_fusion.2), channel_id=1, source_target_pairs={{0,16},{16,0},{32,48},{48,32},{64,80},{80,64},{96,112},{112,96},{1... | collective-permute-start | bytes 442376 | tf_op jit(solution)/shard_map/ppermute | solution.py:677
  82.2 0.6 shard_map.168.refs_9_
  82.8 0.1 constant_dynamic-update-slice_fusion.5
  82.8 0.3 collective-permute-done.18.refs_5_
  83.2 2.3 %shard_map.169 = (bf16[4,32,256]{2,1,0:T(8,128)(2,1)S(1)}, bf16[432,128]{1,0:T(8,128)(2,1)S(1)}) custom-call(s32[2]{0:T(128)S(1)} %pad_add_fusion.refs_0_, bf16[3,192,128]{2,1,0:T(8,128)(2,1)S(1)} %pad_maximum_fusion.2.refs_1_, bf16[3,192,128]{2,1,0:T(8,128)(2,1)S(1)} %collective-permute-done.15.refs_2_, ...), custom_call_target="tpu_custom_call" | custom-call | flops 2000000000 | bytes 4000000 | tf_op jit(solution)/shard_map/pallas_call | solution.py:470
  85.6 1.2 copy-done.9
  86.7 0.1 constant_dynamic-slice_fusion
  86.8 0.7 collective-permute-start.19
  87.5 1.9 collective-permute-done.19
  89.4 1.3 add_convert_fusion
  90.7 61.2 %all_to_all.10 = bf16[128,24,128]{2,1,0:T(8,128)(2,1)S(1)} all-to-all(bf16[128,24,128]{2,1,0:T(8,128)(2,1)S(1)} %bitcast.66), channel_id=1, replica_groups={{0,1,2,3,4,5,6,7,8,9,10,11,12,13,14,15,32,33,34,35,36,37,38,39,40,41,42..., dimensions={0} | all-to-all | bytes 1572864 | tf_op jit(solution)/shard_map/all_to_all | solution.py:717
  152.0 0.2 reduce_sum.12
  152.1 0.1 broadcast_in_dim.10
  152.2 30.1 %all_to_all.11 = bf16[128,24,128]{2,1,0:T(8,128)(2,1)S(1)} all-to-all(bf16[128,24,128]{2,1,0:T(8,128)(2,1)S(1)} %broadcast_in_dim.10), channel_id=1, replica_groups={{0,1,2,3,4,5,6,7,8,9,10,11,12,13,14,15,32,33,34,35,36,37,38,39,40,41,42..., dimensions={0} | all-to-all | bytes 1572864 | tf_op jit(solution)/shard_map/all_to_all | solution.py:722
  182.4 3.7 %collective-permute-start.20 = (bf16[384,8,128]{2,1,0:T(8,128)(2,1)S(1)}, bf16[384,8,128]{2,1,0:T(8,128)(2,1)S(1)}, u32[]{:S(2)}, u32[]{:S(2)}) collective-permute-start(bf16[384,8,128]{2,1,0:T(8,128)(2,1)S(1)} %bitcast.67), channel_id=1, source_target_pairs={{0,16},{16,0},{32,48},{48,32},{64,80},{80,64},{96,112},{112,96},{1... | collective-permute-start | bytes 2359304 | tf_op jit(solution)/shard_map/ppermute | solution.py:726
  186.1 0.7 copy.20
  186.8 0.7 copy.21
  187.5 0.5 collective-permute-done.20
  188.0 0.1 broadcast_select_fusion
  188.2 0.1 pad_maximum_fusion
  188.3 0.8 shard_map.170
  189.2 0.1 concatenate.29
  189.3 0.6 convert_element_type.25
  189.9 0.1 concatenate.32
  190.1 0.8 convert_element_type.27
  190.8 0.4 concatenate.31
  191.2 1.2 convert_element_type.26
  (50 shorter events, 0.5 us)
Async XLA Ops:
  1.4 10.9 %collective-permute-start.10 = (bf16[4,32,128]{2,1,0:T(8,128)(2,1)S(1)}, bf16[4,32,128]{2,1,0:T(8,128)(2,1)S(1)}, u32[]{:S(2)}, u32[]{:S(2)}) collective-permute-start(bf16[4,32,128]{2,1,0:T(8,128)(2,1)S(1)} %bitcast.72), channel_id=1, source_target_pairs={{0,96},{16,112},{32,0},{48,16},{64,32},{80,48},{96,64},{112,80},{1... | collective-permute-start | bytes 98312 | tf_op jit(solution)/shard_map/ppermute | solution.py:540
  4.9 7.4 %collective-permute-start.9 = (bf16[4,32,128]{2,1,0:T(8,128)(2,1)S(1)}, bf16[4,32,128]{2,1,0:T(8,128)(2,1)S(1)}, u32[]{:S(2)}, u32[]{:S(2)}) collective-permute-start(bf16[4,32,128]{2,1,0:T(8,128)(2,1)S(1)} %bitcast.73), channel_id=1, source_target_pairs={{0,64},{16,80},{32,96},{48,112},{64,0},{80,16},{96,32},{112,48},{1... | collective-permute-start | bytes 98312 | tf_op jit(solution)/shard_map/ppermute | solution.py:540
  5.3 7.1 %collective-permute-start.8 = (bf16[4,32,128]{2,1,0:T(8,128)(2,1)S(1)}, bf16[4,32,128]{2,1,0:T(8,128)(2,1)S(1)}, u32[]{:S(2)}, u32[]{:S(2)}) collective-permute-start(bf16[4,32,128]{2,1,0:T(8,128)(2,1)S(1)} %bitcast.74), channel_id=1, source_target_pairs={{0,32},{16,48},{32,64},{48,80},{64,96},{80,112},{96,0},{112,16},{1... | collective-permute-start | bytes 98312 | tf_op jit(solution)/shard_map/ppermute | solution.py:540
  6.9 0.8 copy-start.6
  7.9 13.2 %collective-permute-start.1 = (bf16[10,32,128]{2,1,0:T(8,128)(2,1)S(1)}, bf16[10,32,128]{2,1,0:T(8,128)(2,1)S(1)}, u32[]{:S(2)}, u32[]{:S(2)}) collective-permute-start(bf16[10,32,128]{2,1,0:T(8,128)(2,1)S(1)} %get-tuple-element.29), channel_id=1, source_target_pairs={{0,1},{1,2},{2,3},{3,4},{4,5},{5,6},{6,7},{7,8},{8,9},{9,10},{10,1... | collective-permute-start | bytes 245768 | tf_op jit(solution)/shard_map/ppermute | solution.py:484
  11.0 10.1 %collective-permute-start = (bf16[10,32,128]{2,1,0:T(8,128)(2,1)S(1)}, bf16[10,32,128]{2,1,0:T(8,128)(2,1)S(1)}, u32[]{:S(2)}, u32[]{:S(2)}) collective-permute-start(bf16[10,32,128]{2,1,0:T(8,128)(2,1)S(1)} %get-tuple-element.28.own), channel_id=1, source_target_pairs={{1,0},{2,1},{3,2},{4,3},{5,4},{6,5},{7,6},{8,7},{9,8},{10,9},{11,1... | collective-permute-start | bytes 245768 | tf_op jit(solution)/shard_map/ppermute | solution.py:484
  12.4 24.2 %collective-permute-start.11 = (bf16[16,32,128]{2,1,0:T(8,128)(2,1)S(1)}, bf16[16,32,128]{2,1,0:T(8,128)(2,1)S(1)}, u32[]{:S(2)}, u32[]{:S(2)}) collective-permute-start(bf16[16,32,128]{2,1,0:T(8,128)(2,1)S(1)} %pad_maximum_fusion.3), channel_id=1, source_target_pairs={{0,140},{1,141},{2,142},{3,143},{4,136},{5,137},{6,138},{7,139},{8... | collective-permute-start | bytes 393224 | tf_op jit(solution)/shard_map/ppermute | solution.py:542
  21.1 21.7 %copy-start = (bf16[64,5184]{1,0:T(8,128)(2,1)S(1)}, bf16[64,5184]{1,0:T(8,128)(2,1)}, u32[]{:S(2)}) copy-start(bf16[64,5184]{1,0:T(8,128)(2,1)} %refs_1_.1) | copy-start | bytes 1990660
  21.1 21.7 %copy-start.1 = (bf16[32,2592]{1,0:T(8,128)(2,1)S(1)}, bf16[32,2592]{1,0:T(8,128)(2,1)}, u32[]{:S(2)}) copy-start(bf16[32,2592]{1,0:T(8,128)(2,1)} %refs_2_.1) | copy-start | bytes 497668
  21.1 21.7 %copy-start.2 = (bf16[64,864]{1,0:T(8,128)(2,1)S(1)}, bf16[64,864]{1,0:T(8,128)(2,1)}, u32[]{:S(2)}) copy-start(bf16[64,864]{1,0:T(8,128)(2,1)} %refs_0_.1) | copy-start | bytes 331780
  21.2 11.2 %collective-permute-start.5 = (bf16[4,32,128]{2,1,0:T(8,128)(2,1)S(1)}, bf16[4,32,128]{2,1,0:T(8,128)(2,1)S(1)}, u32[]{:S(2)}, u32[]{:S(2)}) collective-permute-start(bf16[4,32,128]{2,1,0:T(8,128)(2,1)S(1)} %slice.97), channel_id=1, source_target_pairs={{64,0},{80,16},{96,32},{112,48},{128,64},{144,80},{160,96},{176,11... | collective-permute-start | bytes 98312 | tf_op jit(solution)/shard_map/ppermute | solution.py:484
  22.6 14.0 %collective-permute-start.4 = (bf16[4,32,128]{2,1,0:T(8,128)(2,1)S(1)}, bf16[4,32,128]{2,1,0:T(8,128)(2,1)S(1)}, u32[]{:S(2)}, u32[]{:S(2)}) collective-permute-start(bf16[4,32,128]{2,1,0:T(8,128)(2,1)S(1)} %slice.97), channel_id=1, source_target_pairs={{0,64},{16,80},{32,96},{48,112},{64,128},{80,144},{96,160},{112,17... | collective-permute-start | bytes 98312 | tf_op jit(solution)/shard_map/ppermute | solution.py:484
  28.1 15.6 %collective-permute-start.6 = (bf16[28,32,128]{2,1,0:T(8,128)(2,1)S(1)}, bf16[28,32,128]{2,1,0:T(8,128)(2,1)S(1)}, u32[]{:S(2)}, u32[]{:S(2)}) collective-permute-start(bf16[28,32,128]{2,1,0:T(8,128)(2,1)S(1)} %shard_map.164.refs_1_), channel_id=1, source_target_pairs={{0,16},{16,0},{32,48},{48,32},{64,80},{80,64},{96,112},{112,96},{1... | collective-permute-start | bytes 688136 | tf_op jit(solution)/shard_map/ppermute | solution.py:559
  31.1 9.3 %collective-permute-start.3 = (bf16[28,32,128]{2,1,0:T(8,128)(2,1)S(1)}, bf16[28,32,128]{2,1,0:T(8,128)(2,1)S(1)}, u32[]{:S(2)}, u32[]{:S(2)}) collective-permute-start(bf16[28,32,128]{2,1,0:T(8,128)(2,1)S(1)} %shard_map.164.refs_1_), channel_id=1, source_target_pairs={{32,0},{48,16},{64,32},{80,48},{96,64},{112,80},{128,96},{144,112}... | collective-permute-start | bytes 688136 | tf_op jit(solution)/shard_map/ppermute | solution.py:484
  32.4 8.9 %collective-permute-start.2 = (bf16[28,32,128]{2,1,0:T(8,128)(2,1)S(1)}, bf16[28,32,128]{2,1,0:T(8,128)(2,1)S(1)}, u32[]{:S(2)}, u32[]{:S(2)}) collective-permute-start(bf16[28,32,128]{2,1,0:T(8,128)(2,1)S(1)} %shard_map.164.refs_1_), channel_id=1, source_target_pairs={{0,32},{16,48},{32,64},{48,80},{64,96},{80,112},{96,128},{112,144}... | collective-permute-start | bytes 688136 | tf_op jit(solution)/shard_map/ppermute | solution.py:484
  36.6 7.1 %collective-permute-start.12 = (bf16[32,32,128]{2,1,0:T(8,128)(2,1)S(1)}, bf16[32,32,128]{2,1,0:T(8,128)(2,1)S(1)}, u32[]{:S(2)}, u32[]{:S(2)}) collective-permute-start(bf16[32,32,128]{2,1,0:T(8,128)(2,1)S(1)} %constant_dynamic-update-slice_fusion.refs_8_), channel_id=1, source_target_pairs={{0,16},{16,0},{32,48},{48,32},{64,80},{80,64},{96,112},{112,96},{1... | collective-permute-start | bytes 786440 | tf_op jit(solution)/shard_map/ppermute | solution.py:544
  41.4 2.5 %collective-permute-start.7 = (bf16[36,32,128]{2,1,0:T(8,128)(2,1)S(1)}, bf16[36,32,128]{2,1,0:T(8,128)(2,1)S(1)}, u32[]{:S(2)}, u32[]{:S(2)}) collective-permute-start(bf16[36,32,128]{2,1,0:T(8,128)(2,1)S(1)} %pad_maximum_fusion.1), channel_id=1, source_target_pairs={{0,16},{16,0},{32,48},{48,32},{64,80},{80,64},{96,112},{112,96},{1... | collective-permute-start | bytes 884744 | tf_op jit(solution)/shard_map/ppermute | solution.py:566
  43.7 1.8 copy-start.3
  43.7 1.8 copy-start.4
  43.7 1.8 copy-start.5
  43.7 1.8 copy-start.7
  43.7 1.8 copy-start.8
  62.8 5.3 %collective-permute-start.14 = (bf16[192,128]{1,0:T(8,128)(2,1)S(1)}, bf16[192,128]{1,0:T(8,128)(2,1)S(1)}, u32[]{:S(2)}, u32[]{:S(2)}) collective-permute-start(bf16[192,128]{1,0:T(8,128)(2,1)S(1)} %get-tuple-element.39), channel_id=1, source_target_pairs={{1,0},{2,1},{3,2},{4,3},{5,4},{6,5},{7,6},{8,7},{9,8},{10,9},{11,1... | collective-permute-start | bytes 147464 | tf_op jit(solution)/shard_map/ppermute | solution.py:484
  64.1 5.2 %collective-permute-start.13 = (bf16[192,128]{1,0:T(8,128)(2,1)S(1)}, bf16[192,128]{1,0:T(8,128)(2,1)S(1)}, u32[]{:S(2)}, u32[]{:S(2)}) collective-permute-start(bf16[192,128]{1,0:T(8,128)(2,1)S(1)} %get-tuple-element.39), channel_id=1, source_target_pairs={{0,1},{1,2},{2,3},{3,4},{4,5},{5,6},{6,7},{7,8},{8,9},{9,10},{10,1... | collective-permute-start | bytes 147464 | tf_op jit(solution)/shard_map/ppermute | solution.py:484
  69.3 10.4 %collective-permute-start.16 = (bf16[3,192,128]{2,1,0:T(8,128)(2,1)S(1)}, bf16[3,192,128]{2,1,0:T(8,128)(2,1)S(1)}, u32[]{:S(2)}, u32[]{:S(2)}) collective-permute-start(bf16[3,192,128]{2,1,0:T(8,128)(2,1)S(1)} %pad_maximum_fusion.2.refs_1_), channel_id=1, source_target_pairs={{32,0},{48,16},{64,32},{80,48},{96,64},{112,80},{128,96},{144,112}... | collective-permute-start | bytes 442376 | tf_op jit(solution)/shard_map/ppermute | solution.py:484
  70.6 9.1 %collective-permute-start.15 = (bf16[3,192,128]{2,1,0:T(8,128)(2,1)S(1)}, bf16[3,192,128]{2,1,0:T(8,128)(2,1)S(1)}, u32[]{:S(2)}, u32[]{:S(2)}) collective-permute-start(bf16[3,192,128]{2,1,0:T(8,128)(2,1)S(1)} %pad_maximum_fusion.2.refs_1_), channel_id=1, source_target_pairs={{0,32},{16,48},{32,64},{48,80},{64,96},{80,112},{96,128},{112,144}... | collective-permute-start | bytes 442376 | tf_op jit(solution)/shard_map/ppermute | solution.py:484
  77.7 5.1 %collective-permute-start.17 = (bf16[3,192,128]{2,1,0:T(8,128)(2,1)S(1)}, bf16[3,192,128]{2,1,0:T(8,128)(2,1)S(1)}, u32[]{:S(2)}, u32[]{:S(2)}) collective-permute-start(bf16[3,192,128]{2,1,0:T(8,128)(2,1)S(1)} %pad_maximum_fusion.2.refs_1_), channel_id=1, source_target_pairs={{0,16},{16,0},{32,48},{48,32},{64,80},{80,64},{96,112},{112,96},{1... | collective-permute-start | bytes 442376 | tf_op jit(solution)/shard_map/ppermute | solution.py:674
  79.7 3.5 %collective-permute-start.18 = (bf16[3,192,128]{2,1,0:T(8,128)(2,1)S(1)}, bf16[3,192,128]{2,1,0:T(8,128)(2,1)S(1)}, u32[]{:S(2)}, u32[]{:S(2)}) collective-permute-start(bf16[3,192,128]{2,1,0:T(8,128)(2,1)S(1)} %broadcast_select_fusion.2), channel_id=1, source_target_pairs={{0,16},{16,0},{32,48},{48,32},{64,80},{80,64},{96,112},{112,96},{1... | collective-permute-start | bytes 442376 | tf_op jit(solution)/shard_map/ppermute | solution.py:677
  85.6 1.2 copy-start.9
  86.8 2.6 %collective-permute-start.19 = (bf16[384,8,128]{2,1,0:T(8,128)(2,1)S(1)}, bf16[384,8,128]{2,1,0:T(8,128)(2,1)S(1)}, u32[]{:S(2)}, u32[]{:S(2)}) collective-permute-start(bf16[384,8,128]{2,1,0:T(8,128)(2,1)S(1)} %constant_dynamic-slice_fusion), channel_id=1, source_target_pairs={{0,16},{16,0},{32,48},{48,32},{64,80},{80,64},{96,112},{112,96},{1... | collective-permute-start | bytes 2359304 | tf_op jit(solution)/shard_map/ppermute | solution.py:713
  182.4 5.6 %collective-permute-start.20 = (bf16[384,8,128]{2,1,0:T(8,128)(2,1)S(1)}, bf16[384,8,128]{2,1,0:T(8,128)(2,1)S(1)}, u32[]{:S(2)}, u32[]{:S(2)}) collective-permute-start(bf16[384,8,128]{2,1,0:T(8,128)(2,1)S(1)} %bitcast.67), channel_id=1, source_target_pairs={{0,16},{16,0},{32,48},{48,32},{64,80},{80,64},{96,112},{112,96},{1... | collective-permute-start | bytes 2359304 | tf_op jit(solution)/shard_map/ppermute | solution.py:726

commit v7 on v6

--- a/solution.py
+++ b/solution.py
@@ -169,26 +169,26 @@
     gx = ids[0]
     core = gx % 2
     low = jnp.where(core == 0, 1.0, 0.0)
-    below = jnp.full((24, 32, 128), low).astype(BF)
-    above = jnp.full((24, 32, 128), 1.0 - low).astype(BF)
-    first = beyond[0:24] * below + mate[0:24] * above
-    last = mate[0:24] * below + beyond[0:24] * above
-    fine[0] = first
-    fine[1] = last
+    below = jnp.full((12, 32, 128), low).astype(BF)
+    above = jnp.full((12, 32, 128), 1.0 - low).astype(BF)
+    fine[0, 0:12] = up[0:12] * below + mate[0:12] * above
+    fine[0, 12:24] = beyond[0:12] * below + mate[12:24] * above
+    fine[1, 0:12] = mate[0:12] * below + beyond[0:12] * above
+    fine[1, 12:24] = mate[12:24] * below + down[0:12] * above
 
     for place, (ref, at) in (
         (1, (far_up, 0)),
-        (3, (up, 24)),
+        (3, (up, 12)),
         (5, (own, 24)),
-        (7, (down, 24)),
+        (7, (down, 12)),
         (9, (far_down, 0)),
     ):
         pools[place] = ref[at : at + 4]
     centre = 6 - 2 * core
-    pools[centre - 2] = beyond[24:28]
+    pools[centre - 2] = beyond[12:16]
     pools[centre] = mate[24:28]
-    pools[centre + 2] = beyond[28:32]
-    pools[centre - 4 + 8 * core] = beyond[32:36]
+    pools[centre + 2] = beyond[16:20]
+    pools[centre - 4 + 8 * core] = beyond[20:24]
 
     slabs = w_all.shape[1]
     around = tiles // 4
@@ -390,42 +390,52 @@
         put_padded(g_bot, 128 * a, dot_nt(err_low, taps_b[a + 2]) * scale_low)
 
 
+def join_kernel(own, left, right, out):
+    wide = [ref[0:128, :].astype(F32) for ref in (own, right, left)]
+    err = wide[0] + pltpu.roll(wide[1], 16, 1) + pltpu.roll(wide[2], 112, 1)
+    out[0:128, :] = err.astype(BF)
+    at = lane(128)
+    mine, right, left = [ref[128:192, :].astype(F32) for ref in (own, right, left)]
+    turned = [pltpu.roll(v, 64, 1) for v in (mine, right, left)]
+    for row, (a, b, c) in enumerate(((mine, turned[1], turned[2]), (turned[0], right, left))):
+        value = jnp.where(at < 64, a, jnp.where(at < 96, b, c))
+        out[128 + 64 * row : 192 + 64 * row, :] = value.astype(BF)
+
+
 def tail_kernel(sizes, scale_mid, *refs):
     (ids, own, up_two, down_two, mate, beyond, pre_one, taps_in, dskip) = refs[:9]
     (t_bot, t_enc, up_low, up_mid) = refs[9:13]
     (grad_skip, g_enc) = refs[13:15]
-    (taps_a, sum_a, err_s, taps_b, sum_b, near) = refs[15:21]
+    (taps_a, sum_a, err_s, taps_b, sum_b) = refs[15:20]
     (rows_all, cols_all) = sizes
     gx, gy = ids[0], ids[1]
     rows_mid = rows_all // 2
     mid_in = inside(MID, 8, cols_all // 2, gy)
 
-    below = jnp.full((3, 192, 128), jnp.where(gx % 2 == 0, 1.0, 0.0)).astype(BF)
-    above = (1.0 - below.astype(F32)).astype(BF)
-    near[0] = beyond[...] * below + mate[...] * above
-    near[1] = mate[...] * below + beyond[...] * above
-    up, down = near.at[0], near.at[1]
-
-    for k, ref in enumerate((up_two, up, own, down, down_two)):
-        value = (
-            ref[0, 0:128, :].astype(F32)
-            + pltpu.roll(ref[2, 0:128, :].astype(F32), 16, 1)
-            + pltpu.roll(ref[1, 0:128, :].astype(F32), 112, 1)
-        )
-        put_taps(taps_a, k, 0, 128, value.astype(BF), 4)
+    low = jnp.where(gx % 2 == 0, 1.0, 0.0)
+    high = 1.0 - low
+    below = jnp.full((128, 128), low).astype(BF)
+    above = jnp.full((128, 128), high).astype(BF)
+    rows = (
+        up_two[0:128, :],
+        beyond[0:128, :] * below + mate[0:128, :] * above,
+        own[0:128, :],
+        mate[0:128, :] * below + beyond[0:128, :] * above,
+        down_two[0:128, :],
+    )
+    for k, value in enumerate(rows):
+        put_taps(taps_a, k, 0, 128, value, 4)
         sum_a[k] = dot(t_bot[...], taps_a[k])
     ups = [dot_split(row_sum(sum_a, k, 64), up_low[...]) * 0.125 for k in range(3)]
+    next_row = beyond[128:192, :].astype(F32)
+    parts = (
+        next_row * low + mate[192:256, :].astype(F32) * high,
+        own[128:192, :].astype(F32),
+        own[192:256, :].astype(F32),
+        mate[128:192, :].astype(F32) * low + next_row * high,
+    )
     for m in range(4):
-        ref = (up, own, own, down)[m]
-        odd = m % 2 == 0
-        tiles = [ref[k, 128:192, :].astype(F32) for k in range(3)]
-        mine, left, right = tiles
-        if odd:
-            mine = pltpu.roll(mine, 64, 1)
-        else:
-            left, right = pltpu.roll(left, 64, 1), pltpu.roll(right, 64, 1)
-        at = lane(128)
-        part = jnp.where(at < 64, mine, jnp.where(at < 96, right, left))
+        part = parts[m]
         keep = mid_in * row_ok(gx * 2 + m - 1, rows_mid)
         err = (part + ups[(m + 1) // 2]) * slope(pre_one[m]) * keep
         err = err.astype(BF)
@@ -552,15 +562,17 @@
         left = shift(to_right, "gy", ngy, 1)
         (own,) = call(widen_kernel, [((28, 32, 128), BF)], [], 0, skip, cot, to_left, right, left)
         core = gx % 2
-        up = shift(own, "gx", ngx, 2)
-        down = shift(own, "gx", ngx, -2)
+        mate = lax.ppermute(own, "gx", swap)
+        rise = jnp.where(core == 0, own[0:12], mate[12:24])
+        fall = jnp.where(core == 0, mate[0:12], own[12:24])
+        up = shift(jnp.concatenate([fall, own[24:28]], axis=0), "gx", ngx, 2)
+        down = shift(jnp.concatenate([rise, own[24:28]], axis=0), "gx", ngx, -2)
         far_up = shift(own[24:28], "gx", ngx, 4)
         far_down = shift(own[24:28], "gx", ngx, -4)
-        mate = lax.ppermute(own, "gx", swap)
         beyond = [
-            jnp.where(core == 0, down[0:24], up[0:24]),
-            up[24:28],
-            down[24:28],
+            jnp.where(core == 0, down[0:12], up[0:12]),
+            up[12:16],
+            down[12:16],
             jnp.where(core == 0, far_down, far_up),
         ]
         beyond = lax.ppermute(jnp.concatenate(beyond, axis=0), "gx", swap)
@@ -670,10 +682,11 @@
 
         from_left = shift(packed, "gy", ngy, 1)
         from_right = shift(packed, "gy", ngy, -1)
-        line = jnp.stack([packed, from_left, from_right])
+        (line,) = call(join_kernel, [((256, 128), BF)], [], 0, packed, from_left, from_right)
         mate = lax.ppermute(line, "gx", swap)
-        line_up = shift(line, "gx", ngx, 2)
-        line_down = shift(line, "gx", ngx, -2)
+        fall = jnp.concatenate([line[0:128], line[192:256]], axis=0)
+        line_up = shift(fall, "gx", ngx, 2)
+        line_down = shift(line[0:192], "gx", ngx, -2)
         beyond = lax.ppermute(jnp.where(core == 0, line_down, line_up), "gx", swap)
         grad_skip, g_enc = call(
             lambda *refs: tail_kernel(sizes, scales[1], *refs),
@@ -684,7 +697,6 @@
                 ((4, 64, 128), BF),
                 ((4, 576, 128), BF),
                 ((4, 96, 128), F32),
-                ((2, 3, 192, 128), BF),
             ],
             1,
             ids,

time: 193 us -> 182 us (0.943)
  starting transfers between devices: 57.2 us -> 53.1 us
  waiting for transfers between devices: 8.4 us -> 4.74 us
    ppermute x10, starting transfers between devices: 30.4 us -> 26.6 us  [shift(): lax.ppermute(value, axis, [(i, i + step) for i in range(count) if 0 <= i...]
    ppermute x10, waiting for transfers between devices: 5.42 us -> 1.7 us  [shift(): lax.ppermute(value, axis, [(i, i + step) for i in range(count) if 0 <= i...]
    pallas_call x8 -> x9, Pallas kernels: 23.6 us -> 23.4 us  [call(): pl.pallas_call(kernel, out_shape=[jax.ShapeDtypeStruct(s, d) for s, d in...]
  transfers between devices with their start and end apart: 21 -> 21, of which waited for: 8 -> 6; matrix products, arithmetic and copies ran while one was open for 1% -> 1% of each run, Pallas kernels for 1% -> 1%
where the time goes in v7:
time: 182 us; the launch traced here: 181 us
  blocking collectives  89.4 us (49%)
  starting transfers between devices  53.1 us (29%)
  Pallas kernels  23.4 us (13%)
  local copies, waits for them, and re-layouts  5.96 us (3%)
  waiting for transfers between devices  4.74 us (3%)
  other arithmetic  3.3 us (2%)
    all_to_all x1, blocking collectives, step(): lax.all_to_all(parts, AXES, split_axis=0, concat_axis=0, axis_index_group...  59.3 us
    all_to_all x1, blocking collectives, step(): lax.all_to_all(spread, AXES, split_axis=0, concat_axis=0, axis_index_grou...  30.1 us
    ppermute x10, starting transfers between devices, shift(): lax.ppermute(value, axis, [(i, i + step) for i in range(count) if 0 <= i...  26.6 us
    pallas_call x9, Pallas kernels, call(): pl.pallas_call(kernel, out_shape=[jax.ShapeDtypeStruct(s, d) for s, d in...  23.4 us
    ppermute x1, starting transfers between devices, step(): lax.ppermute(w_line, AXES, [(i, mirrored(i)) for i in range(devices)])  8.64 us
    ppermute x3, starting transfers between devices, step(): lax.ppermute(weight, 'gx', [(i, along_y(i, k)) for i in range(ngx)])  4.59 us
    ppermute x1, starting transfers between devices, step(): other = lax.ppermute(mine, 'gx', swap)  3.74 us
  transfers between devices with their start and end apart: 21, of which 6 were waited for; matrix products, arithmetic and copies ran while one was open for 1% of the time, Pallas kernels for 1%

profile of v7, /device:TPU:1, one launch (start us, length us, event | category | flops | bytes accessed | tf_op | source)
XLA Modules:
  0.0 181.1 jit_solution(14470929750964219788)
XLA Ops:
  0.6 0.8 pad.4
  1.4 3.6 %collective-permute-start.10 = (bf16[4,32,128]{2,1,0:T(8,128)(2,1)S(1)}, bf16[4,32,128]{2,1,0:T(8,128)(2,1)S(1)}, u32[]{:S(2)}, u32[]{:S(2)}) collective-permute-start(bf16[4,32,128]{2,1,0:T(8,128)(2,1)S(1)} %bitcast.68), channel_id=1, source_target_pairs={{0,96},{16,112},{32,0},{48,16},{64,32},{80,48},{96,64},{112,80},{1... | collective-permute-start | bytes 98312 | tf_op jit(solution)/shard_map/ppermute | solution.py:550
  4.9 0.3 collective-permute-start.9
  5.3 0.7 collective-permute-start.8
  6.0 0.9 copy_bitcast_fusion
  6.9 0.0 copy-start.6
  6.9 0.8 copy-done.6
  7.7 0.2 shard_map.163
  7.9 3.1 %collective-permute-start.1 = (bf16[10,32,128]{2,1,0:T(8,128)(2,1)S(1)}, bf16[10,32,128]{2,1,0:T(8,128)(2,1)S(1)}, u32[]{:S(2)}, u32[]{:S(2)}) collective-permute-start(bf16[10,32,128]{2,1,0:T(8,128)(2,1)S(1)} %get-tuple-element.29), channel_id=1, source_target_pairs={{0,1},{1,2},{2,3},{3,4},{4,5},{5,6},{6,7},{7,8},{8,9},{9,10},{10,1... | collective-permute-start | bytes 245768 | tf_op jit(solution)/shard_map/ppermute | solution.py:494
  11.0 1.3 collective-permute-start
  12.4 8.6 %collective-permute-start.11 = (bf16[16,32,128]{2,1,0:T(8,128)(2,1)S(1)}, bf16[16,32,128]{2,1,0:T(8,128)(2,1)S(1)}, u32[]{:S(2)}, u32[]{:S(2)}) collective-permute-start(bf16[16,32,128]{2,1,0:T(8,128)(2,1)S(1)} %pad_maximum_fusion.4), channel_id=1, source_target_pairs={{0,140},{1,141},{2,142},{3,143},{4,136},{5,137},{6,138},{7,139},{8... | collective-permute-start | bytes 393224 | tf_op jit(solution)/shard_map/ppermute | solution.py:552
  21.1 2.4 %collective-permute-start.2 = (bf16[28,32,128]{2,1,0:T(8,128)(2,1)S(1)}, bf16[28,32,128]{2,1,0:T(8,128)(2,1)S(1)}, u32[]{:S(2)}, u32[]{:S(2)}) collective-permute-start(bf16[28,32,128]{2,1,0:T(8,128)(2,1)S(1)} %shard_map.164.refs_1_), channel_id=1, source_target_pairs={{0,16},{16,0},{32,48},{48,32},{64,80},{80,64},{96,112},{112,96},{1... | collective-permute-start | bytes 688136 | tf_op jit(solution)/shard_map/ppermute | solution.py:565
  23.6 3.6 %collective-permute-start.5 = (bf16[4,32,128]{2,1,0:T(8,128)(2,1)S(1)}, bf16[4,32,128]{2,1,0:T(8,128)(2,1)S(1)}, u32[]{:S(2)}, u32[]{:S(2)}) collective-permute-start(bf16[4,32,128]{2,1,0:T(8,128)(2,1)S(1)} %slice.129), channel_id=1, source_target_pairs={{0,64},{16,80},{32,96},{48,112},{64,128},{80,144},{96,160},{112,17... | collective-permute-start | bytes 98312 | tf_op jit(solution)/shard_map/ppermute | solution.py:494
  27.2 1.3 collective-permute-start.6
  28.6 1.3 collective-permute-start.4
  29.9 4.0 %collective-permute-start.3 = (bf16[16,32,128]{2,1,0:T(8,128)(2,1)S(1)}, bf16[16,32,128]{2,1,0:T(8,128)(2,1)S(1)}, u32[]{:S(2)}, u32[]{:S(2)}) collective-permute-start(bf16[16,32,128]{2,1,0:T(8,128)(2,1)S(1)} %get-tuple-element.70), channel_id=1, source_target_pairs={{0,32},{16,48},{32,64},{48,80},{64,96},{80,112},{96,128},{112,144}... | collective-permute-start | bytes 393224 | tf_op jit(solution)/shard_map/ppermute | solution.py:494
  33.9 0.2 collective-permute-done.6.refs_5_
  34.1 1.4 collective-permute-start.12
  35.5 0.5 collective-permute-done.3.refs_2_
  36.0 1.8 %collective-permute-start.7 = (bf16[24,32,128]{2,1,0:T(8,128)(2,1)S(1)}, bf16[24,32,128]{2,1,0:T(8,128)(2,1)S(1)}, u32[]{:S(2)}, u32[]{:S(2)}) collective-permute-start(bf16[24,32,128]{2,1,0:T(8,128)(2,1)S(1)} %pad_maximum_fusion.1), channel_id=1, source_target_pairs={{0,16},{16,0},{32,48},{48,32},{64,80},{80,64},{96,112},{112,96},{1... | collective-permute-start | bytes 589832 | tf_op jit(solution)/shard_map/ppermute | solution.py:578
  37.9 0.1 pad_add_fusion.refs_0_
  38.0 0.9 shard_map.166
  38.8 0.0 copy-start.3
  38.8 0.0 copy-start.4
  38.9 0.0 copy-start.5
  38.9 0.0 copy-start.7
  38.9 0.0 copy-start.8
  38.9 0.0 collective-permute-done.7.refs_7_
  38.9 1.5 shard_map.165
  40.5 17.2 %shard_map.167 = (bf16[4,32,256]{2,1,0:T(8,128)(2,1)S(1)}, f32[4,32,256]{2,1,0:T(8,128)S(1)}, bf16[192,128]{1,0:T(8,128)(2,1)S(1)}, f32[4,64,128]{2,1,0:T(8,128)...) custom-call(s32[2]{0:T(128)S(1)} %pad_add_fusion.refs_0_, ...), custom_call_target="tpu_custom_call" | custom-call | flops 10000000000 | bytes 20000000 | tf_op jit(solution)/shard_map/pallas_call | solution.py:480
  57.7 1.3 collective-permute-start.14
  59.0 4.0 %collective-permute-start.13 = (bf16[192,128]{1,0:T(8,128)(2,1)S(1)}, bf16[192,128]{1,0:T(8,128)(2,1)S(1)}, u32[]{:S(2)}, u32[]{:S(2)}) collective-permute-start(bf16[192,128]{1,0:T(8,128)(2,1)S(1)} %get-tuple-element.39.own), channel_id=1, source_target_pairs={{0,1},{1,2},{2,3},{3,4},{4,5},{5,6},{6,7},{7,8},{8,9},{9,10},{10,1... | collective-permute-start | bytes 147464 | tf_op jit(solution)/shard_map/ppermute | solution.py:494
  63.0 0.1 constant_dynamic-update-slice_fusion.6
  63.1 1.0 collective-permute-done.13.left
  64.2 0.1 shard_map.168.refs_1_
  64.3 1.3 collective-permute-start.16
  65.6 5.4 %collective-permute-start.15 = (bf16[192,128]{1,0:T(8,128)(2,1)S(1)}, bf16[192,128]{1,0:T(8,128)(2,1)S(1)}, u32[]{:S(2)}, u32[]{:S(2)}) collective-permute-start(bf16[192,128]{1,0:T(8,128)(2,1)S(1)} %pad_maximum_fusion.5), channel_id=1, source_target_pairs={{0,32},{16,48},{32,64},{48,80},{64,96},{80,112},{96,128},{112,144}... | collective-permute-start | bytes 147464 | tf_op jit(solution)/shard_map/ppermute | solution.py:494
  71.1 0.1 constant_dynamic-update-slice_fusion.5
  71.2 1.9 %collective-permute-start.17 = (bf16[256,128]{1,0:T(8,128)(2,1)S(1)}, bf16[256,128]{1,0:T(8,128)(2,1)S(1)}, u32[]{:S(2)}, u32[]{:S(2)}) collective-permute-start(bf16[256,128]{1,0:T(8,128)(2,1)S(1)} %shard_map.168.refs_1_), channel_id=1, source_target_pairs={{0,16},{16,0},{32,48},{48,32},{64,80},{80,64},{96,112},{112,96},{1... | collective-permute-start | bytes 196616 | tf_op jit(solution)/shard_map/ppermute | solution.py:686
  73.1 1.6 collective-permute-start.18
  74.7 0.6 shard_map.169.refs_9_
  75.3 0.3 collective-permute-done.18.refs_5_
  75.6 2.1 %shard_map.170 = (bf16[4,32,256]{2,1,0:T(8,128)(2,1)S(1)}, bf16[432,128]{1,0:T(8,128)(2,1)S(1)}) custom-call(s32[2]{0:T(128)S(1)} %pad_add_fusion.refs_0_, bf16[256,128]{1,0:T(8,128)(2,1)S(1)} %shard_map.168.refs_1_, bf16[192,128]{1,0:T(8,128)(2,1)S(1)} %collective-permute-done.15.refs_2_, bf16[192,128]{1,0:T(8,128)(2,1)S(1)} %collective-permute-done.16.refs_3_, ...), custom_call_target="tpu_custom_call" | custom-call | flops 2000000000 | bytes 4000000 | tf_op jit(solution)/shard_map/pallas_call | solution.py:480
  77.8 0.9 constant_dynamic-slice_fusion
  78.7 0.3 collective-permute-start.19
  79.0 2.1 %collective-permute-done.19 = bf16[384,8,128]{2,1,0:T(8,128)(2,1)S(1)} collective-permute-done((bf16[384,8,128]{2,1,0:T(8,128)(2,1)}, bf16[384,8,128]{2,1,0:T(8,128)(2,1)S(1)}, u32[]{:S(2)}, u32[]{:S(2)}) %collective-permute-start.19) | collective-permute-done | bytes 786464 | tf_op jit(solution)/shard_map/ppermute | solution.py:725
  81.2 0.2 add_convert_fusion
  81.4 59.3 %all_to_all.10 = bf16[128,24,128]{2,1,0:T(8,128)(2,1)S(1)} all-to-all(bf16[128,24,128]{2,1,0:T(8,128)(2,1)S(1)} %bitcast.62), channel_id=1, replica_groups={{0,1,2,3,4,5,6,7,8,9,10,11,12,13,14,15,32,33,34,35,36,37,38,39,40,41,42..., dimensions={0} | all-to-all | bytes 1572864 | tf_op jit(solution)/shard_map/all_to_all | solution.py:729
  140.7 0.2 reduce_sum.12
  140.9 0.1 broadcast_in_dim.10
  141.0 30.1 %all_to_all.11 = bf16[128,24,128]{2,1,0:T(8,128)(2,1)S(1)} all-to-all(bf16[128,24,128]{2,1,0:T(8,128)(2,1)S(1)} %broadcast_in_dim.10), channel_id=1, replica_groups={{0,1,2,3,4,5,6,7,8,9,10,11,12,13,14,15,32,33,34,35,36,37,38,39,40,41,42..., dimensions={0} | all-to-all | bytes 1572864 | tf_op jit(solution)/shard_map/all_to_all | solution.py:734
  171.0 3.7 %collective-permute-start.20 = (bf16[384,8,128]{2,1,0:T(8,128)(2,1)S(1)}, bf16[384,8,128]{2,1,0:T(8,128)(2,1)S(1)}, u32[]{:S(2)}, u32[]{:S(2)}) collective-permute-start(bf16[384,8,128]{2,1,0:T(8,128)(2,1)S(1)} %bitcast.63), channel_id=1, source_target_pairs={{0,16},{16,0},{32,48},{48,32},{64,80},{80,64},{96,112},{112,96},{1... | collective-permute-start | bytes 2359304 | tf_op jit(solution)/shard_map/ppermute | solution.py:738
  174.8 0.7 copy.20
  175.5 0.7 copy.21
  176.1 0.5 collective-permute-done.20
  176.7 0.1 broadcast_select_fusion
  176.8 0.1 pad_maximum_fusion
  176.9 0.8 shard_map.171
  177.9 0.1 concatenate.41
  178.0 0.6 convert_element_type.25
  178.6 0.1 concatenate.44
  178.7 0.8 convert_element_type.27
  179.5 0.4 concatenate.43
  179.9 1.2 convert_element_type.26
  (54 shorter events, 0.5 us)
Async XLA Ops:
  1.4 10.9 %collective-permute-start.10 = (bf16[4,32,128]{2,1,0:T(8,128)(2,1)S(1)}, bf16[4,32,128]{2,1,0:T(8,128)(2,1)S(1)}, u32[]{:S(2)}, u32[]{:S(2)}) collective-permute-start(bf16[4,32,128]{2,1,0:T(8,128)(2,1)S(1)} %bitcast.68), channel_id=1, source_target_pairs={{0,96},{16,112},{32,0},{48,16},{64,32},{80,48},{96,64},{112,80},{1... | collective-permute-start | bytes 98312 | tf_op jit(solution)/shard_map/ppermute | solution.py:550
  4.9 7.4 %collective-permute-start.9 = (bf16[4,32,128]{2,1,0:T(8,128)(2,1)S(1)}, bf16[4,32,128]{2,1,0:T(8,128)(2,1)S(1)}, u32[]{:S(2)}, u32[]{:S(2)}) collective-permute-start(bf16[4,32,128]{2,1,0:T(8,128)(2,1)S(1)} %bitcast.69), channel_id=1, source_target_pairs={{0,64},{16,80},{32,96},{48,112},{64,0},{80,16},{96,32},{112,48},{1... | collective-permute-start | bytes 98312 | tf_op jit(solution)/shard_map/ppermute | solution.py:550
  5.3 7.1 %collective-permute-start.8 = (bf16[4,32,128]{2,1,0:T(8,128)(2,1)S(1)}, bf16[4,32,128]{2,1,0:T(8,128)(2,1)S(1)}, u32[]{:S(2)}, u32[]{:S(2)}) collective-permute-start(bf16[4,32,128]{2,1,0:T(8,128)(2,1)S(1)} %bitcast.70), channel_id=1, source_target_pairs={{0,32},{16,48},{32,64},{48,80},{64,96},{80,112},{96,0},{112,16},{1... | collective-permute-start | bytes 98312 | tf_op jit(solution)/shard_map/ppermute | solution.py:550
  6.9 0.8 copy-start.6
  7.9 13.2 %collective-permute-start.1 = (bf16[10,32,128]{2,1,0:T(8,128)(2,1)S(1)}, bf16[10,32,128]{2,1,0:T(8,128)(2,1)S(1)}, u32[]{:S(2)}, u32[]{:S(2)}) collective-permute-start(bf16[10,32,128]{2,1,0:T(8,128)(2,1)S(1)} %get-tuple-element.29), channel_id=1, source_target_pairs={{0,1},{1,2},{2,3},{3,4},{4,5},{5,6},{6,7},{7,8},{8,9},{9,10},{10,1... | collective-permute-start | bytes 245768 | tf_op jit(solution)/shard_map/ppermute | solution.py:494
  11.0 10.0 %collective-permute-start = (bf16[10,32,128]{2,1,0:T(8,128)(2,1)S(1)}, bf16[10,32,128]{2,1,0:T(8,128)(2,1)S(1)}, u32[]{:S(2)}, u32[]{:S(2)}) collective-permute-start(bf16[10,32,128]{2,1,0:T(8,128)(2,1)S(1)} %get-tuple-element.28.own), channel_id=1, source_target_pairs={{1,0},{2,1},{3,2},{4,3},{5,4},{6,5},{7,6},{8,7},{9,8},{10,9},{11,1... | collective-permute-start | bytes 245768 | tf_op jit(solution)/shard_map/ppermute | solution.py:494
  12.4 21.7 %collective-permute-start.11 = (bf16[16,32,128]{2,1,0:T(8,128)(2,1)S(1)}, bf16[16,32,128]{2,1,0:T(8,128)(2,1)S(1)}, u32[]{:S(2)}, u32[]{:S(2)}) collective-permute-start(bf16[16,32,128]{2,1,0:T(8,128)(2,1)S(1)} %pad_maximum_fusion.4), channel_id=1, source_target_pairs={{0,140},{1,141},{2,142},{3,143},{4,136},{5,137},{6,138},{7,139},{8... | collective-permute-start | bytes 393224 | tf_op jit(solution)/shard_map/ppermute | solution.py:552
  21.1 16.9 %copy-start = (bf16[64,5184]{1,0:T(8,128)(2,1)S(1)}, bf16[64,5184]{1,0:T(8,128)(2,1)}, u32[]{:S(2)}) copy-start(bf16[64,5184]{1,0:T(8,128)(2,1)} %refs_1_.1) | copy-start | bytes 1990660
  21.1 16.8 %copy-start.1 = (bf16[32,2592]{1,0:T(8,128)(2,1)S(1)}, bf16[32,2592]{1,0:T(8,128)(2,1)}, u32[]{:S(2)}) copy-start(bf16[32,2592]{1,0:T(8,128)(2,1)} %refs_2_.1) | copy-start | bytes 497668
  21.1 16.8 %copy-start.2 = (bf16[64,864]{1,0:T(8,128)(2,1)S(1)}, bf16[64,864]{1,0:T(8,128)(2,1)}, u32[]{:S(2)}) copy-start(bf16[64,864]{1,0:T(8,128)(2,1)} %refs_0_.1) | copy-start | bytes 331780
  21.1 7.4 %collective-permute-start.2 = (bf16[28,32,128]{2,1,0:T(8,128)(2,1)S(1)}, bf16[28,32,128]{2,1,0:T(8,128)(2,1)S(1)}, u32[]{:S(2)}, u32[]{:S(2)}) collective-permute-start(bf16[28,32,128]{2,1,0:T(8,128)(2,1)S(1)} %shard_map.164.refs_1_), channel_id=1, source_target_pairs={{0,16},{16,0},{32,48},{48,32},{64,80},{80,64},{96,112},{112,96},{1... | collective-permute-start | bytes 688136 | tf_op jit(solution)/shard_map/ppermute | solution.py:565
  23.6 10.2 %collective-permute-start.5 = (bf16[4,32,128]{2,1,0:T(8,128)(2,1)S(1)}, bf16[4,32,128]{2,1,0:T(8,128)(2,1)S(1)}, u32[]{:S(2)}, u32[]{:S(2)}) collective-permute-start(bf16[4,32,128]{2,1,0:T(8,128)(2,1)S(1)} %slice.129), channel_id=1, source_target_pairs={{0,64},{16,80},{32,96},{48,112},{64,128},{80,144},{96,160},{112,17... | collective-permute-start | bytes 98312 | tf_op jit(solution)/shard_map/ppermute | solution.py:494
  27.2 6.9 %collective-permute-start.6 = (bf16[4,32,128]{2,1,0:T(8,128)(2,1)S(1)}, bf16[4,32,128]{2,1,0:T(8,128)(2,1)S(1)}, u32[]{:S(2)}, u32[]{:S(2)}) collective-permute-start(bf16[4,32,128]{2,1,0:T(8,128)(2,1)S(1)} %slice.129), channel_id=1, source_target_pairs={{64,0},{80,16},{96,32},{112,48},{128,64},{144,80},{160,96},{176,11... | collective-permute-start | bytes 98312 | tf_op jit(solution)/shard_map/ppermute | solution.py:494
  28.6 7.0 %collective-permute-start.4 = (bf16[16,32,128]{2,1,0:T(8,128)(2,1)S(1)}, bf16[16,32,128]{2,1,0:T(8,128)(2,1)S(1)}, u32[]{:S(2)}, u32[]{:S(2)}) collective-permute-start(bf16[16,32,128]{2,1,0:T(8,128)(2,1)S(1)} %get-tuple-element.69), channel_id=1, source_target_pairs={{32,0},{48,16},{64,32},{80,48},{96,64},{112,80},{128,96},{144,112}... | collective-permute-start | bytes 393224 | tf_op jit(solution)/shard_map/ppermute | solution.py:494
  29.9 6.1 %collective-permute-start.3 = (bf16[16,32,128]{2,1,0:T(8,128)(2,1)S(1)}, bf16[16,32,128]{2,1,0:T(8,128)(2,1)S(1)}, u32[]{:S(2)}, u32[]{:S(2)}) collective-permute-start(bf16[16,32,128]{2,1,0:T(8,128)(2,1)S(1)} %get-tuple-element.70), channel_id=1, source_target_pairs={{0,32},{16,48},{32,64},{48,80},{64,96},{80,112},{96,128},{112,144}... | collective-permute-start | bytes 393224 | tf_op jit(solution)/shard_map/ppermute | solution.py:494
  34.1 4.8 %collective-permute-start.12 = (bf16[32,32,128]{2,1,0:T(8,128)(2,1)S(1)}, bf16[32,32,128]{2,1,0:T(8,128)(2,1)S(1)}, u32[]{:S(2)}, u32[]{:S(2)}) collective-permute-start(bf16[32,32,128]{2,1,0:T(8,128)(2,1)S(1)} %constant_dynamic-update-slice_fusion.refs_8_), channel_id=1, source_target_pairs={{0,16},{16,0},{32,48},{48,32},{64,80},{80,64},{96,112},{112,96},{1... | collective-permute-start | bytes 786440 | tf_op jit(solution)/shard_map/ppermute | solution.py:554
  36.0 2.9 %collective-permute-start.7 = (bf16[24,32,128]{2,1,0:T(8,128)(2,1)S(1)}, bf16[24,32,128]{2,1,0:T(8,128)(2,1)S(1)}, u32[]{:S(2)}, u32[]{:S(2)}) collective-permute-start(bf16[24,32,128]{2,1,0:T(8,128)(2,1)S(1)} %pad_maximum_fusion.1), channel_id=1, source_target_pairs={{0,16},{16,0},{32,48},{48,32},{64,80},{80,64},{96,112},{112,96},{1... | collective-permute-start | bytes 589832 | tf_op jit(solution)/shard_map/ppermute | solution.py:578
  38.8 1.7 copy-start.3
  38.8 1.6 copy-start.4
  38.9 1.6 copy-start.5
  38.9 1.6 copy-start.7
  38.9 1.6 copy-start.8
  57.7 5.4 %collective-permute-start.14 = (bf16[192,128]{1,0:T(8,128)(2,1)S(1)}, bf16[192,128]{1,0:T(8,128)(2,1)S(1)}, u32[]{:S(2)}, u32[]{:S(2)}) collective-permute-start(bf16[192,128]{1,0:T(8,128)(2,1)S(1)} %get-tuple-element.39.own), channel_id=1, source_target_pairs={{1,0},{2,1},{3,2},{4,3},{5,4},{6,5},{7,6},{8,7},{9,8},{10,9},{11,1... | collective-permute-start | bytes 147464 | tf_op jit(solution)/shard_map/ppermute | solution.py:494
  59.0 5.2 %collective-permute-start.13 = (bf16[192,128]{1,0:T(8,128)(2,1)S(1)}, bf16[192,128]{1,0:T(8,128)(2,1)S(1)}, u32[]{:S(2)}, u32[]{:S(2)}) collective-permute-start(bf16[192,128]{1,0:T(8,128)(2,1)S(1)} %get-tuple-element.39.own), channel_id=1, source_target_pairs={{0,1},{1,2},{2,3},{3,4},{4,5},{5,6},{6,7},{7,8},{8,9},{9,10},{10,1... | collective-permute-start | bytes 147464 | tf_op jit(solution)/shard_map/ppermute | solution.py:494
  64.3 8.7 %collective-permute-start.16 = (bf16[192,128]{1,0:T(8,128)(2,1)S(1)}, bf16[192,128]{1,0:T(8,128)(2,1)S(1)}, u32[]{:S(2)}, u32[]{:S(2)}) collective-permute-start(bf16[192,128]{1,0:T(8,128)(2,1)S(1)} %slice.138), channel_id=1, source_target_pairs={{32,0},{48,16},{64,32},{80,48},{96,64},{112,80},{128,96},{144,112}... | collective-permute-start | bytes 147464 | tf_op jit(solution)/shard_map/ppermute | solution.py:494
  65.6 7.4 %collective-permute-start.15 = (bf16[192,128]{1,0:T(8,128)(2,1)S(1)}, bf16[192,128]{1,0:T(8,128)(2,1)S(1)}, u32[]{:S(2)}, u32[]{:S(2)}) collective-permute-start(bf16[192,128]{1,0:T(8,128)(2,1)S(1)} %pad_maximum_fusion.5), channel_id=1, source_target_pairs={{0,32},{16,48},{32,64},{48,80},{64,96},{80,112},{96,128},{112,144}... | collective-permute-start | bytes 147464 | tf_op jit(solution)/shard_map/ppermute | solution.py:494
  71.2 4.1 %collective-permute-start.17 = (bf16[256,128]{1,0:T(8,128)(2,1)S(1)}, bf16[256,128]{1,0:T(8,128)(2,1)S(1)}, u32[]{:S(2)}, u32[]{:S(2)}) collective-permute-start(bf16[256,128]{1,0:T(8,128)(2,1)S(1)} %shard_map.168.refs_1_), channel_id=1, source_target_pairs={{0,16},{16,0},{32,48},{48,32},{64,80},{80,64},{96,112},{112,96},{1... | collective-permute-start | bytes 196616 | tf_op jit(solution)/shard_map/ppermute | solution.py:686
  73.1 2.5 %collective-permute-start.18 = (bf16[192,128]{1,0:T(8,128)(2,1)S(1)}, bf16[192,128]{1,0:T(8,128)(2,1)S(1)}, u32[]{:S(2)}, u32[]{:S(2)}) collective-permute-start(bf16[192,128]{1,0:T(8,128)(2,1)S(1)} %broadcast_select_fusion.2), channel_id=1, source_target_pairs={{0,16},{16,0},{32,48},{48,32},{64,80},{80,64},{96,112},{112,96},{1... | collective-permute-start | bytes 147464 | tf_op jit(solution)/shard_map/ppermute | solution.py:690
  78.7 2.5 %collective-permute-start.19 = (bf16[384,8,128]{2,1,0:T(8,128)(2,1)}, bf16[384,8,128]{2,1,0:T(8,128)(2,1)S(1)}, u32[]{:S(2)}, u32[]{:S(2)}) collective-permute-start(bf16[384,8,128]{2,1,0:T(8,128)(2,1)} %constant_dynamic-slice_fusion), channel_id=1, source_target_pairs={{0,16},{16,0},{32,48},{48,32},{64,80},{80,64},{96,112},{112,96},{1... | collective-permute-start | bytes 2359304 | tf_op jit(solution)/shard_map/ppermute | solution.py:725
  171.0 5.6 %collective-permute-start.20 = (bf16[384,8,128]{2,1,0:T(8,128)(2,1)S(1)}, bf16[384,8,128]{2,1,0:T(8,128)(2,1)S(1)}, u32[]{:S(2)}, u32[]{:S(2)}) collective-permute-start(bf16[384,8,128]{2,1,0:T(8,128)(2,1)S(1)} %bitcast.63), channel_id=1, source_target_pairs={{0,16},{16,0},{32,48},{48,32},{64,80},{80,64},{96,112},{112,96},{1... | collective-permute-start | bytes 2359304 | tf_op jit(solution)/shard_map/ppermute | solution.py:738

commit v8 on v7

--- a/solution.py
+++ b/solution.py
@@ -164,31 +164,34 @@
 
 
 def gather_kernel(tiles, block, *refs):
-    (ids, own, up, down, far_up, far_down, mate, beyond, w_mine, w_mate) = refs[:10]
-    (fine, pools, w_out, w_all, w_flat) = refs[10:15]
+    (ids, own, mate, got, got_m, far, far_m, w_mine, w_mate) = refs[:9]
+    (fine, pools, w_out, w_all, w_flat) = refs[9:14]
     gx = ids[0]
     core = gx % 2
     low = jnp.where(core == 0, 1.0, 0.0)
-    below = jnp.full((12, 32, 128), low).astype(BF)
-    above = jnp.full((12, 32, 128), 1.0 - low).astype(BF)
-    fine[0, 0:12] = up[0:12] * below + mate[0:12] * above
-    fine[0, 12:24] = beyond[0:12] * below + mate[12:24] * above
-    fine[1, 0:12] = mate[0:12] * below + beyond[0:12] * above
-    fine[1, 12:24] = mate[12:24] * below + down[0:12] * above
-
-    for place, (ref, at) in (
-        (1, (far_up, 0)),
-        (3, (up, 12)),
-        (5, (own, 24)),
-        (7, (down, 12)),
-        (9, (far_down, 0)),
+    below = jnp.full((32, 32, 128), low).astype(BF)
+    above = jnp.full((32, 32, 128), 1.0 - low).astype(BF)
+    lower = got[...] * below + got_m[...] * above
+    upper = got_m[...] * below + got[...] * above
+    fine[0] = upper[0:24] * below[0:24] + mate[0:24] * above[0:24]
+    fine[1] = mate[0:24] * below[0:24] + lower[0:24] * above[0:24]
+    far_lower = far[...] * below[0:8] + far_m[...] * above[0:8]
+    far_upper = far_m[...] * below[0:8] + far[...] * above[0:8]
+    first = own[24:28] * below[0:4] + mate[24:28] * above[0:4]
+    second = mate[24:28] * below[0:4] + own[24:28] * above[0:4]
+    for step, tile in (
+        (-4, far_upper[4:8]),
+        (-3, far_upper[0:4]),
+        (-2, upper[28:32]),
+        (-1, upper[24:28]),
+        (0, first),
+        (1, second),
+        (2, lower[24:28]),
+        (3, lower[28:32]),
+        (4, far_lower[0:4]),
+        (5, far_lower[4:8]),
     ):
-        pools[place] = ref[at : at + 4]
-    centre = 6 - 2 * core
-    pools[centre - 2] = beyond[12:16]
-    pools[centre] = mate[24:28]
-    pools[centre + 2] = beyond[16:20]
-    pools[centre - 4 + 8 * core] = beyond[20:24]
+        pools[step + 5 - core] = tile
 
     slabs = w_all.shape[1]
     around = tiles // 4
@@ -403,10 +406,10 @@
 
 
 def tail_kernel(sizes, scale_mid, *refs):
-    (ids, own, up_two, down_two, mate, beyond, pre_one, taps_in, dskip) = refs[:9]
-    (t_bot, t_enc, up_low, up_mid) = refs[9:13]
-    (grad_skip, g_enc) = refs[13:15]
-    (taps_a, sum_a, err_s, taps_b, sum_b) = refs[15:20]
+    (ids, own, mate, got, got_m, pre_one, taps_in, dskip) = refs[:8]
+    (t_bot, t_enc, up_low, up_mid) = refs[8:12]
+    (grad_skip, g_enc) = refs[12:14]
+    (taps_a, sum_a, err_s, taps_b, sum_b) = refs[14:19]
     (rows_all, cols_all) = sizes
     gx, gy = ids[0], ids[1]
     rows_mid = rows_all // 2
@@ -414,25 +417,27 @@
 
     low = jnp.where(gx % 2 == 0, 1.0, 0.0)
     high = 1.0 - low
-    below = jnp.full((128, 128), low).astype(BF)
-    above = jnp.full((128, 128), high).astype(BF)
+    below = jnp.full((320, 128), low).astype(BF)
+    above = jnp.full((320, 128), high).astype(BF)
+    lower = got[...] * below + got_m[...] * above
+    upper = got_m[...] * below + got[...] * above
+    below, above = below[0:128], above[0:128]
     rows = (
-        up_two[0:128, :],
-        beyond[0:128, :] * below + mate[0:128, :] * above,
+        upper[128:256] * below + upper[0:128] * above,
+        upper[0:128] * below + mate[0:128, :] * above,
         own[0:128, :],
-        mate[0:128, :] * below + beyond[0:128, :] * above,
-        down_two[0:128, :],
+        mate[0:128, :] * below + lower[0:128] * above,
+        lower[0:128] * below + lower[128:256] * above,
     )
     for k, value in enumerate(rows):
         put_taps(taps_a, k, 0, 128, value, 4)
         sum_a[k] = dot(t_bot[...], taps_a[k])
     ups = [dot_split(row_sum(sum_a, k, 64), up_low[...]) * 0.125 for k in range(3)]
-    next_row = beyond[128:192, :].astype(F32)
     parts = (
-        next_row * low + mate[192:256, :].astype(F32) * high,
+        upper[256:320].astype(F32) * low + mate[192:256, :].astype(F32) * high,
         own[128:192, :].astype(F32),
         own[192:256, :].astype(F32),
-        mate[128:192, :].astype(F32) * low + next_row * high,
+        mate[128:192, :].astype(F32) * low + lower[256:320].astype(F32) * high,
     )
     for m in range(4):
         part = parts[m]
@@ -494,6 +499,11 @@
     return lax.ppermute(value, axis, [(i, i + step) for i in range(count) if 0 <= i + step < count])
 
 
+def outward(value, count, step):
+    pairs = [(i, i + step if i % 2 else i - step) for i in range(count)]
+    return lax.ppermute(value, "gx", [(i, j) for i, j in pairs if 0 <= j < count])
+
+
 def tiles_of(g):
     rows, width = g.shape
     return g.reshape(rows // 8, 8, width // 128, 128).transpose(0, 2, 1, 3).reshape(-1, 8, 128)
@@ -563,19 +573,10 @@
         (own,) = call(widen_kernel, [((28, 32, 128), BF)], [], 0, skip, cot, to_left, right, left)
         core = gx % 2
         mate = lax.ppermute(own, "gx", swap)
-        rise = jnp.where(core == 0, own[0:12], mate[12:24])
-        fall = jnp.where(core == 0, mate[0:12], own[12:24])
-        up = shift(jnp.concatenate([fall, own[24:28]], axis=0), "gx", ngx, 2)
-        down = shift(jnp.concatenate([rise, own[24:28]], axis=0), "gx", ngx, -2)
-        far_up = shift(own[24:28], "gx", ngx, 4)
-        far_down = shift(own[24:28], "gx", ngx, -4)
-        beyond = [
-            jnp.where(core == 0, down[0:12], up[0:12]),
-            up[12:16],
-            down[12:16],
-            jnp.where(core == 0, far_down, far_up),
-        ]
-        beyond = lax.ppermute(jnp.concatenate(beyond, axis=0), "gx", swap)
+        got = outward(jnp.concatenate([own, mate[24:28]], axis=0), ngx, 2)
+        far = outward(jnp.concatenate([own[24:28], mate[24:28]], axis=0), ngx, 4)
+        got_m = lax.ppermute(got, "gx", swap)
+        far_m = lax.ppermute(far, "gx", swap)
         fine, pools, w_bot, _, w_flat = call(
             lambda *refs: gather_kernel(ngx, block, *refs),
             [
@@ -589,12 +590,11 @@
             1,
             ids,
             own,
-            up,
-            down,
-            far_up,
-            far_down,
             mate,
-            beyond,
+            got,
+            got_m,
+            far,
+            far_m,
             w_mine,
             w_mate,
         )
@@ -684,10 +684,9 @@
         from_right = shift(packed, "gy", ngy, -1)
         (line,) = call(join_kernel, [((256, 128), BF)], [], 0, packed, from_left, from_right)
         mate = lax.ppermute(line, "gx", swap)
-        fall = jnp.concatenate([line[0:128], line[192:256]], axis=0)
-        line_up = shift(fall, "gx", ngx, 2)
-        line_down = shift(line[0:192], "gx", ngx, -2)
-        beyond = lax.ppermute(jnp.where(core == 0, line_down, line_up), "gx", swap)
+        edge = jnp.where(core == 0, line[128:192], line[192:256])
+        got = outward(jnp.concatenate([line[0:128], mate[0:128], edge], axis=0), ngx, 2)
+        got_m = lax.ppermute(got, "gx", swap)
         grad_skip, g_enc = call(
             lambda *refs: tail_kernel(sizes, scales[1], *refs),
             [((4, 32, 256), BF), ((432, 128), BF)],
@@ -701,10 +700,9 @@
             1,
             ids,
             line,
-            line_up,
-            line_down,
             mate,
-            beyond,
+            got,
+            got_m,
             pre_one,
             taps_one,
             dskip,

time: 182 us -> 173 us (0.951)
  blocking collectives: 89.4 us -> 76.5 us
  waiting for transfers between devices: 4.74 us -> 13.8 us
  starting transfers between devices: 53.1 us -> 46.9 us
    ppermute x10 -> x4, starting transfers between devices: 26.6 us -> 9.69 us  [shift(): lax.ppermute(value, axis, [(i, i + step) for i in range(count) if 0 <= i...]
    ppermute x2 -> x6, starting transfers between devices: 3.5 us -> 17.2 us  [the longest x3 14.3 us: outward(): lax.ppermute(value, 'gx', [(i, j) for i, j in pairs if 0 <= j < count])]
    all_to_all x1, blocking collectives: 59.3 us -> 46.4 us  [step(): lax.all_to_all(parts, AXES, split_axis=0, concat_axis=0, axis_index_group...]
    ppermute x10 -> x4, waiting for transfers between devices: 1.7 us -> 4.87 us  [shift(): lax.ppermute(value, axis, [(i, i + step) for i in range(count) if 0 <= i...]
    ppermute x1, waiting for transfers between devices: 0.01 us -> 3.02 us  [step(): lax.ppermute(w_line, AXES, [(i, mirrored(i)) for i in range(devices)])]
    ppermute x1, starting transfers between devices: 8.64 us -> 5.92 us  [step(): lax.ppermute(w_line, AXES, [(i, mirrored(i)) for i in range(devices)])]
    ppermute x2 -> x6, waiting for transfers between devices: 0.33 us -> 2.56 us  [the longest x3 1.4 us: outward(): lax.ppermute(value, 'gx', [(i, j) for i, j in pairs if 0 <= j < count])]
    unnamed x28 -> x40, local copies, waits for them, and re-layouts: 2.47 us -> 4.44 us
  transfers between devices with their start and end apart: 21 -> 19, of which waited for: 6 -> 10; matrix products, arithmetic and copies ran while one was open for 1% -> 2% of each run, Pallas kernels for 1% -> 1%
where the time goes in v8:
time: 173 us
  blocking collectives  76.5 us (44%)
  starting transfers between devices  46.9 us (27%)
  Pallas kernels  23.6 us (14%)
  waiting for transfers between devices  13.8 us (8%)
  local copies, waits for them, and re-layouts  7.04 us (4%)
  other arithmetic  3.86 us (2%)
    all_to_all x1, blocking collectives, step(): lax.all_to_all(parts, AXES, split_axis=0, concat_axis=0, axis_index_group...  46.4 us
    all_to_all x1, blocking collectives, step(): lax.all_to_all(spread, AXES, split_axis=0, concat_axis=0, axis_index_grou...  30.1 us
    pallas_call x9, Pallas kernels, call(): pl.pallas_call(kernel, out_shape=[jax.ShapeDtypeStruct(s, d) for s, d in...  23.6 us
    ppermute x3, starting transfers between devices, outward(): lax.ppermute(value, 'gx', [(i, j) for i, j in pairs if 0 <= j < count])  14.3 us
    ppermute x4, starting transfers between devices, shift(): lax.ppermute(value, axis, [(i, i + step) for i in range(count) if 0 <= i...  9.69 us
    ppermute x1, starting transfers between devices, step(): lax.ppermute(w_line, AXES, [(i, mirrored(i)) for i in range(devices)])  5.92 us
    ppermute x4, waiting for transfers between devices, shift(): lax.ppermute(value, axis, [(i, i + step) for i in range(count) if 0 <= i...  4.87 us
    ppermute x3, starting transfers between devices, step(): lax.ppermute(weight, 'gx', [(i, along_y(i, k)) for i in range(ngx)])  4.59 us
  transfers between devices with their start and end apart: 19, of which 10 were waited for; matrix products, arithmetic and copies ran while one was open for 2% of the time, Pallas kernels for 1%

profile of v8, /device:TPU:1, one launch (start us, length us, event | category | flops | bytes accessed | tf_op | source)
XLA Modules:
  0.0 172.8 jit_solution(15390820891859064350)
XLA Ops:
  0.6 0.8 pad.4
  1.4 3.6 %collective-permute-start.9 = (bf16[4,32,128]{2,1,0:T(8,128)(2,1)S(1)}, bf16[4,32,128]{2,1,0:T(8,128)(2,1)S(1)}, u32[]{:S(2)}, u32[]{:S(2)}) collective-permute-start(bf16[4,32,128]{2,1,0:T(8,128)(2,1)S(1)} %bitcast.68), channel_id=1, source_target_pairs={{0,96},{16,112},{32,0},{48,16},{64,32},{80,48},{96,64},{112,80},{1... | collective-permute-start | bytes 98312 | tf_op jit(solution)/shard_map/ppermute | solution.py:560
  4.9 0.3 collective-permute-start.8
  5.3 0.7 collective-permute-start.7
  6.0 0.9 copy_bitcast_fusion
  6.9 0.0 copy-start.6
  6.9 0.8 copy-done.6
  7.7 0.2 shard_map.163
  7.9 3.1 %collective-permute-start.1 = (bf16[10,32,128]{2,1,0:T(8,128)(2,1)S(1)}, bf16[10,32,128]{2,1,0:T(8,128)(2,1)S(1)}, u32[]{:S(2)}, u32[]{:S(2)}) collective-permute-start(bf16[10,32,128]{2,1,0:T(8,128)(2,1)S(1)} %get-tuple-element.29), channel_id=1, source_target_pairs={{0,1},{1,2},{2,3},{3,4},{4,5},{5,6},{6,7},{7,8},{8,9},{9,10},{10,1... | collective-permute-start | bytes 245768 | tf_op jit(solution)/shard_map/ppermute | solution.py:499
  11.0 1.3 collective-permute-start
  12.3 0.1 collective-permute-done.1.left
  12.5 3.7 %collective-permute-done.right = bf16[10,32,128]{2,1,0:T(8,128)(2,1)S(1)} collective-permute-done((bf16[10,32,128]{2,1,0:T(8,128)(2,1)S(1)}, bf16[10,32,128]{2,1,0:T(8,128)(2,1)S(1)}, u32[]{:S(2)}, u32[]{:S(2)}) %collective-permute-start) | collective-permute-done | bytes 81952 | tf_op jit(solution)/shard_map/ppermute | solution.py:499
  16.2 3.0 %collective-permute-start.2 = (bf16[28,32,128]{2,1,0:T(8,128)(2,1)S(1)}, bf16[28,32,128]{2,1,0:T(8,128)(2,1)S(1)}, u32[]{:S(2)}, u32[]{:S(2)}) collective-permute-start(bf16[28,32,128]{2,1,0:T(8,128)(2,1)S(1)} %shard_map.164.refs_1_), channel_id=1, source_target_pairs={{0,16},{16,0},{32,48},{48,32},{64,80},{80,64},{96,112},{112,96},{1... | collective-permute-start | bytes 688136 | tf_op jit(solution)/shard_map/ppermute | solution.py:575
  19.3 5.9 %collective-permute-start.10 = (bf16[16,32,128]{2,1,0:T(8,128)(2,1)S(1)}, bf16[16,32,128]{2,1,0:T(8,128)(2,1)S(1)}, u32[]{:S(2)}, u32[]{:S(2)}) collective-permute-start(bf16[16,32,128]{2,1,0:T(8,128)(2,1)S(1)} %pad_maximum_fusion.2), channel_id=1, source_target_pairs={{0,140},{1,141},{2,142},{3,143},{4,136},{5,137},{6,138},{7,139},{8... | collective-permute-start | bytes 393224 | tf_op jit(solution)/shard_map/ppermute | solution.py:562
  25.3 3.5 %collective-permute-start.3 = (bf16[32,32,128]{2,1,0:T(8,128)(2,1)S(1)}, bf16[32,32,128]{2,1,0:T(8,128)(2,1)S(1)}, u32[]{:S(2)}, u32[]{:S(2)}) collective-permute-start(bf16[32,32,128]{2,1,0:T(8,128)(2,1)S(1)} %pad_maximum_fusion.1), channel_id=1, source_target_pairs={{16,48},{32,0},{48,80},{64,32},{80,112},{96,64},{112,144},{128,96}... | collective-permute-start | bytes 786440 | tf_op jit(solution)/shard_map/ppermute | solution.py:504
  28.9 3.0 %collective-permute-done.10 = bf16[16,32,128]{2,1,0:T(8,128)(2,1)S(1)} collective-permute-done((bf16[16,32,128]{2,1,0:T(8,128)(2,1)S(1)}, bf16[16,32,128]{2,1,0:T(8,128)(2,1)S(1)}, u32[]{:S(2)}, u32[]{:S(2)}) %collective-permute-start.10) | collective-permute-done | bytes 131104 | tf_op jit(solution)/shard_map/ppermute | solution.py:562
  31.9 0.7 collective-permute-start.11
  32.6 0.6 pad_maximum_fusion.4
  33.2 3.5 %collective-permute-start.5 = (bf16[8,32,128]{2,1,0:T(8,128)(2,1)}, bf16[8,32,128]{2,1,0:T(8,128)(2,1)S(1)}, u32[]{:S(2)}, u32[]{:S(2)}) collective-permute-start(bf16[8,32,128]{2,1,0:T(8,128)(2,1)} %pad_maximum_fusion.4), channel_id=1, source_target_pairs={{16,80},{48,112},{64,0},{80,144},{96,32},{112,176},{128,64},{144,2... | collective-permute-start | bytes 196616 | tf_op jit(solution)/shard_map/ppermute | solution.py:504
  36.8 0.1 collective-permute-start.4
  36.9 0.9 shard_map.166
  37.8 0.7 copy-done.9
  38.5 0.6 copy-done.11
  39.1 0.7 copy-done.13
  39.9 1.3 collective-permute-start.6
  41.1 0.1 pad_add_fusion.refs_0_
  41.2 0.8 collective-permute-done.6.refs_6_
  42.0 1.6 shard_map.165
  43.7 17.3 %shard_map.167 = (bf16[4,32,256]{2,1,0:T(8,128)(2,1)S(1)}, f32[4,32,256]{2,1,0:T(8,128)S(1)}, bf16[192,128]{1,0:T(8,128)(2,1)S(1)}, f32[4,64,128]{2,1,0:T(8,128)...) custom-call(s32[2]{0:T(128)S(1)} %pad_add_fusion.refs_0_, ...), custom_call_target="tpu_custom_call" | custom-call | flops 10000000000 | bytes 20000000 | tf_op jit(solution)/shard_map/pallas_call | solution.py:485
  60.9 1.3 collective-permute-start.13
  62.2 4.0 %collective-permute-start.12 = (bf16[192,128]{1,0:T(8,128)(2,1)S(1)}, bf16[192,128]{1,0:T(8,128)(2,1)S(1)}, u32[]{:S(2)}, u32[]{:S(2)}) collective-permute-start(bf16[192,128]{1,0:T(8,128)(2,1)S(1)} %get-tuple-element.39.own), channel_id=1, source_target_pairs={{0,1},{1,2},{2,3},{3,4},{4,5},{5,6},{6,7},{7,8},{8,9},{9,10},{10,1... | collective-permute-start | bytes 147464 | tf_op jit(solution)/shard_map/ppermute | solution.py:499
  66.2 0.1 constant_dynamic-update-slice_fusion.6
  66.3 1.0 collective-permute-done.12.left
  67.4 0.1 shard_map.168.refs_1_
  67.5 1.6 collective-permute-start.14
  69.1 0.9 collective-permute-done.14.refs_2_
  70.0 7.2 %collective-permute-start.15 = (bf16[320,128]{1,0:T(8,128)(2,1)S(1)}, bf16[320,128]{1,0:T(8,128)(2,1)S(1)}, u32[]{:S(2)}, u32[]{:S(2)}) collective-permute-start(bf16[320,128]{1,0:T(8,128)(2,1)S(1)} %pad_maximum_fusion.3), channel_id=1, source_target_pairs={{16,48},{32,0},{48,80},{64,32},{80,112},{96,64},{112,144},{128,96}... | collective-permute-start | bytes 245768 | tf_op jit(solution)/shard_map/ppermute | solution.py:504
  77.2 0.1 constant_dynamic-update-slice_fusion.5
  77.3 1.4 collective-permute-done.15.refs_3_
  78.7 1.6 collective-permute-start.16
  80.2 0.6 shard_map.169.refs_8_
  80.8 0.3 collective-permute-done.16.refs_4_
  81.2 2.1 %shard_map.170 = (bf16[4,32,256]{2,1,0:T(8,128)(2,1)S(1)}, bf16[432,128]{1,0:T(8,128)(2,1)S(1)}) custom-call(s32[2]{0:T(128)S(1)} %pad_add_fusion.refs_0_, bf16[256,128]{1,0:T(8,128)(2,1)S(1)} %shard_map.168.refs_1_, bf16[256,128]{1,0:T(8,128)(2,1)S(1)} %collective-permute-done.14.refs_2_, bf16[320,128]{1,0:T(8,128)(2,1)S(1)} %collective-permute-done.15.refs_3_, ...), custom_call_target="tpu_custom_call" | custom-call | flops 2000000000 | bytes 4000000 | tf_op jit(solution)/shard_map/pallas_call | solution.py:485
  83.4 0.1 constant_dynamic-slice_fusion
  83.4 0.4 collective-permute-start.17
  83.9 1.9 %collective-permute-done.17 = bf16[384,8,128]{2,1,0:T(8,128)(2,1)S(1)} collective-permute-done((bf16[384,8,128]{2,1,0:T(8,128)(2,1)S(1)}, bf16[384,8,128]{2,1,0:T(8,128)(2,1)S(1)}, u32[]{:S(2)}, u32[]{:S(2)}) %collective-permute-start.17) | collective-permute-done | bytes 786464 | tf_op jit(solution)/shard_map/ppermute | solution.py:723
  85.8 0.2 add_convert_fusion
  86.0 46.4 %all_to_all.10 = bf16[128,24,128]{2,1,0:T(8,128)(2,1)S(1)} all-to-all(bf16[128,24,128]{2,1,0:T(8,128)(2,1)S(1)} %bitcast.62), channel_id=1, replica_groups={{0,1,2,3,4,5,6,7,8,9,10,11,12,13,14,15,32,33,34,35,36,37,38,39,40,41,42..., dimensions={0} | all-to-all | bytes 1572864 | tf_op jit(solution)/shard_map/all_to_all | solution.py:727
  132.4 0.2 reduce_sum.12
  132.6 0.1 broadcast_in_dim.10
  132.7 30.1 %all_to_all.11 = bf16[128,24,128]{2,1,0:T(8,128)(2,1)S(1)} all-to-all(bf16[128,24,128]{2,1,0:T(8,128)(2,1)S(1)} %broadcast_in_dim.10), channel_id=1, replica_groups={{0,1,2,3,4,5,6,7,8,9,10,11,12,13,14,15,32,33,34,35,36,37,38,39,40,41,42..., dimensions={0} | all-to-all | bytes 1572864 | tf_op jit(solution)/shard_map/all_to_all | solution.py:732
  162.8 3.7 %collective-permute-start.18 = (bf16[384,8,128]{2,1,0:T(8,128)(2,1)S(1)}, bf16[384,8,128]{2,1,0:T(8,128)(2,1)S(1)}, u32[]{:S(2)}, u32[]{:S(2)}) collective-permute-start(bf16[384,8,128]{2,1,0:T(8,128)(2,1)S(1)} %bitcast.63), channel_id=1, source_target_pairs={{0,16},{16,0},{32,48},{48,32},{64,80},{80,64},{96,112},{112,96},{1... | collective-permute-start | bytes 2359304 | tf_op jit(solution)/shard_map/ppermute | solution.py:736
  166.5 0.7 copy.20
  167.2 0.7 copy.21
  167.9 0.5 collective-permute-done.18
  168.4 0.1 broadcast_select_fusion
  168.6 0.1 pad_maximum_fusion
  168.7 0.8 shard_map.171
  169.6 0.1 concatenate.37
  169.7 0.6 convert_element_type.25
  170.4 0.1 concatenate.40
  170.5 0.8 convert_element_type.27
  171.3 0.4 concatenate.39
  171.7 1.2 convert_element_type.26
  (57 shorter events, 0.4 us)
Async XLA Ops:
  1.4 17.9 %collective-permute-start.9 = (bf16[4,32,128]{2,1,0:T(8,128)(2,1)S(1)}, bf16[4,32,128]{2,1,0:T(8,128)(2,1)S(1)}, u32[]{:S(2)}, u32[]{:S(2)}) collective-permute-start(bf16[4,32,128]{2,1,0:T(8,128)(2,1)S(1)} %bitcast.68), channel_id=1, source_target_pairs={{0,96},{16,112},{32,0},{48,16},{64,32},{80,48},{96,64},{112,80},{1... | collective-permute-start | bytes 98312 | tf_op jit(solution)/shard_map/ppermute | solution.py:560
  4.9 14.3 %collective-permute-start.8 = (bf16[4,32,128]{2,1,0:T(8,128)(2,1)S(1)}, bf16[4,32,128]{2,1,0:T(8,128)(2,1)S(1)}, u32[]{:S(2)}, u32[]{:S(2)}) collective-permute-start(bf16[4,32,128]{2,1,0:T(8,128)(2,1)S(1)} %bitcast.69), channel_id=1, source_target_pairs={{0,64},{16,80},{32,96},{48,112},{64,0},{80,16},{96,32},{112,48},{1... | collective-permute-start | bytes 98312 | tf_op jit(solution)/shard_map/ppermute | solution.py:560
  5.3 14.0 %collective-permute-start.7 = (bf16[4,32,128]{2,1,0:T(8,128)(2,1)S(1)}, bf16[4,32,128]{2,1,0:T(8,128)(2,1)S(1)}, u32[]{:S(2)}, u32[]{:S(2)}) collective-permute-start(bf16[4,32,128]{2,1,0:T(8,128)(2,1)S(1)} %bitcast.70), channel_id=1, source_target_pairs={{0,32},{16,48},{32,64},{48,80},{64,96},{80,112},{96,0},{112,16},{1... | collective-permute-start | bytes 98312 | tf_op jit(solution)/shard_map/ppermute | solution.py:560
  6.9 0.8 copy-start.6
  7.9 4.6 %collective-permute-start.1 = (bf16[10,32,128]{2,1,0:T(8,128)(2,1)S(1)}, bf16[10,32,128]{2,1,0:T(8,128)(2,1)S(1)}, u32[]{:S(2)}, u32[]{:S(2)}) collective-permute-start(bf16[10,32,128]{2,1,0:T(8,128)(2,1)S(1)} %get-tuple-element.29), channel_id=1, source_target_pairs={{0,1},{1,2},{2,3},{3,4},{4,5},{5,6},{6,7},{7,8},{8,9},{9,10},{10,1... | collective-permute-start | bytes 245768 | tf_op jit(solution)/shard_map/ppermute | solution.py:499
  11.0 5.2 %collective-permute-start = (bf16[10,32,128]{2,1,0:T(8,128)(2,1)S(1)}, bf16[10,32,128]{2,1,0:T(8,128)(2,1)S(1)}, u32[]{:S(2)}, u32[]{:S(2)}) collective-permute-start(bf16[10,32,128]{2,1,0:T(8,128)(2,1)S(1)} %get-tuple-element.28.own), channel_id=1, source_target_pairs={{1,0},{2,1},{3,2},{4,3},{5,4},{6,5},{7,6},{8,7},{9,8},{10,9},{11,1... | collective-permute-start | bytes 245768 | tf_op jit(solution)/shard_map/ppermute | solution.py:499
  12.3 24.6 %copy-start = (bf16[64,5184]{1,0:T(8,128)(2,1)S(1)}, bf16[64,5184]{1,0:T(8,128)(2,1)}, u32[]{:S(2)}) copy-start(bf16[64,5184]{1,0:T(8,128)(2,1)} %refs_1_.1) | copy-start | bytes 1990660
  12.3 24.6 %copy-start.1 = (bf16[32,2592]{1,0:T(8,128)(2,1)S(1)}, bf16[32,2592]{1,0:T(8,128)(2,1)}, u32[]{:S(2)}) copy-start(bf16[32,2592]{1,0:T(8,128)(2,1)} %refs_2_.1) | copy-start | bytes 497668
  12.3 24.6 %copy-start.2 = (bf16[64,864]{1,0:T(8,128)(2,1)S(1)}, bf16[64,864]{1,0:T(8,128)(2,1)}, u32[]{:S(2)}) copy-start(bf16[64,864]{1,0:T(8,128)(2,1)} %refs_0_.1) | copy-start | bytes 331780
  16.2 9.0 %collective-permute-start.2 = (bf16[28,32,128]{2,1,0:T(8,128)(2,1)S(1)}, bf16[28,32,128]{2,1,0:T(8,128)(2,1)S(1)}, u32[]{:S(2)}, u32[]{:S(2)}) collective-permute-start(bf16[28,32,128]{2,1,0:T(8,128)(2,1)S(1)} %shard_map.164.refs_1_), channel_id=1, source_target_pairs={{0,16},{16,0},{32,48},{48,32},{64,80},{80,64},{96,112},{112,96},{1... | collective-permute-start | bytes 688136 | tf_op jit(solution)/shard_map/ppermute | solution.py:575
  19.3 12.6 %collective-permute-start.10 = (bf16[16,32,128]{2,1,0:T(8,128)(2,1)S(1)}, bf16[16,32,128]{2,1,0:T(8,128)(2,1)S(1)}, u32[]{:S(2)}, u32[]{:S(2)}) collective-permute-start(bf16[16,32,128]{2,1,0:T(8,128)(2,1)S(1)} %pad_maximum_fusion.2), channel_id=1, source_target_pairs={{0,140},{1,141},{2,142},{3,143},{4,136},{5,137},{6,138},{7,139},{8... | collective-permute-start | bytes 393224 | tf_op jit(solution)/shard_map/ppermute | solution.py:562
  25.3 11.5 %collective-permute-start.3 = (bf16[32,32,128]{2,1,0:T(8,128)(2,1)S(1)}, bf16[32,32,128]{2,1,0:T(8,128)(2,1)S(1)}, u32[]{:S(2)}, u32[]{:S(2)}) collective-permute-start(bf16[32,32,128]{2,1,0:T(8,128)(2,1)S(1)} %pad_maximum_fusion.1), channel_id=1, source_target_pairs={{16,48},{32,0},{48,80},{64,32},{80,112},{96,64},{112,144},{128,96}... | collective-permute-start | bytes 786440 | tf_op jit(solution)/shard_map/ppermute | solution.py:504
  31.9 9.3 %collective-permute-start.11 = (bf16[32,32,128]{2,1,0:T(8,128)(2,1)S(1)}, bf16[32,32,128]{2,1,0:T(8,128)(2,1)S(1)}, u32[]{:S(2)}, u32[]{:S(2)}) collective-permute-start(bf16[32,32,128]{2,1,0:T(8,128)(2,1)S(1)} %constant_dynamic-update-slice_fusion.refs_7_), channel_id=1, source_target_pairs={{0,16},{16,0},{32,48},{48,32},{64,80},{80,64},{96,112},{112,96},{1... | collective-permute-start | bytes 786440 | tf_op jit(solution)/shard_map/ppermute | solution.py:564
  33.2 6.6 %collective-permute-start.5 = (bf16[8,32,128]{2,1,0:T(8,128)(2,1)}, bf16[8,32,128]{2,1,0:T(8,128)(2,1)S(1)}, u32[]{:S(2)}, u32[]{:S(2)}) collective-permute-start(bf16[8,32,128]{2,1,0:T(8,128)(2,1)} %pad_maximum_fusion.4), channel_id=1, source_target_pairs={{16,80},{48,112},{64,0},{80,144},{96,32},{112,176},{128,64},{144,2... | collective-permute-start | bytes 196616 | tf_op jit(solution)/shard_map/ppermute | solution.py:504
  36.8 5.2 %collective-permute-start.4 = (bf16[32,32,128]{2,1,0:T(8,128)(2,1)S(1)}, bf16[32,32,128]{2,1,0:T(8,128)(2,1)S(1)}, u32[]{:S(2)}, u32[]{:S(2)}) collective-permute-start(bf16[32,32,128]{2,1,0:T(8,128)(2,1)S(1)} %collective-permute-done.3.refs_3_), channel_id=1, source_target_pairs={{0,16},{16,0},{32,48},{48,32},{64,80},{80,64},{96,112},{112,96},{1... | collective-permute-start | bytes 786440 | tf_op jit(solution)/shard_map/ppermute | solution.py:578
  37.8 0.7 copy-start.9
  38.5 0.6 copy-start.11
  39.1 0.7 copy-start.13
  39.8 3.8 %copy-start.3 = (bf16[128,384]{1,0:T(8,128)(2,1)S(1)}, bf16[128,384]{1,0:T(8,128)(2,1)}, u32[]{:S(2)}) copy-start(bf16[128,384]{1,0:T(8,128)(2,1)} %constant.50.clone.refs_12_.refs_11_) | copy-start | bytes 294916
  39.8 3.8 %copy-start.4 = (bf16[384,128]{1,0:T(8,128)(2,1)S(1)}, bf16[384,128]{1,0:T(8,128)(2,1)}, u32[]{:S(2)}) copy-start(bf16[384,128]{1,0:T(8,128)(2,1)} %constant.51.clone.refs_13_) | copy-start | bytes 294916
  39.8 3.8 %copy-start.5 = (bf16[256,128]{1,0:T(8,128)(2,1)S(1)}, bf16[256,128]{1,0:T(8,128)(2,1)}, u32[]{:S(2)}) copy-start(bf16[256,128]{1,0:T(8,128)(2,1)} %constant.52.clone.refs_14_) | copy-start | bytes 196612
  39.8 3.8 %copy-start.7 = (bf16[128,128]{1,0:T(8,128)(2,1)S(1)}, bf16[128,128]{1,0:T(8,128)(2,1)}, u32[]{:S(2)}) copy-start(bf16[128,128]{1,0:T(8,128)(2,1)} %constant.48.clone.refs_10_) | copy-start | bytes 98308
  39.8 3.8 %copy-start.8 = (bf16[128,128]{1,0:T(8,128)(2,1)S(1)}, bf16[128,128]{1,0:T(8,128)(2,1)}, u32[]{:S(2)}) copy-start(bf16[128,128]{1,0:T(8,128)(2,1)} %constant.49.clone.refs_11_) | copy-start | bytes 98308
  39.8 3.8 %copy-start.10 = (bf16[96,864]{1,0:T(8,128)(2,1)S(1)}, bf16[96,864]{1,0:T(8,128)(2,1)}, u32[]{:S(2)}) copy-start(bf16[96,864]{1,0:T(8,128)(2,1)} %copy-done.9) | copy-start | bytes 497668
  39.8 3.8 %copy-start.14 = (bf16[192,288]{1,0:T(8,128)(2,1)S(1)}, bf16[192,288]{1,0:T(8,128)(2,1)}, u32[]{:S(2)}) copy-start(bf16[192,288]{1,0:T(8,128)(2,1)} %copy-done.13) | copy-start | bytes 331780
  39.9 2.2 %collective-permute-start.6 = (bf16[8,32,128]{2,1,0:T(8,128)(2,1)S(1)}, bf16[8,32,128]{2,1,0:T(8,128)(2,1)S(1)}, u32[]{:S(2)}, u32[]{:S(2)}) collective-permute-start(bf16[8,32,128]{2,1,0:T(8,128)(2,1)S(1)} %collective-permute-done.5.refs_5_), channel_id=1, source_target_pairs={{0,16},{16,0},{32,48},{48,32},{64,80},{80,64},{96,112},{112,96},{1... | collective-permute-start | bytes 196616 | tf_op jit(solution)/shard_map/ppermute | solution.py:579
  60.9 5.4 %collective-permute-start.13 = (bf16[192,128]{1,0:T(8,128)(2,1)S(1)}, bf16[192,128]{1,0:T(8,128)(2,1)S(1)}, u32[]{:S(2)}, u32[]{:S(2)}) collective-permute-start(bf16[192,128]{1,0:T(8,128)(2,1)S(1)} %get-tuple-element.39.own), channel_id=1, source_target_pairs={{1,0},{2,1},{3,2},{4,3},{5,4},{6,5},{7,6},{8,7},{9,8},{10,9},{11,1... | collective-permute-start | bytes 147464 | tf_op jit(solution)/shard_map/ppermute | solution.py:499
  62.2 5.2 %collective-permute-start.12 = (bf16[192,128]{1,0:T(8,128)(2,1)S(1)}, bf16[192,128]{1,0:T(8,128)(2,1)S(1)}, u32[]{:S(2)}, u32[]{:S(2)}) collective-permute-start(bf16[192,128]{1,0:T(8,128)(2,1)S(1)} %get-tuple-element.39.own), channel_id=1, source_target_pairs={{0,1},{1,2},{2,3},{3,4},{4,5},{5,6},{6,7},{7,8},{8,9},{9,10},{10,1... | collective-permute-start | bytes 147464 | tf_op jit(solution)/shard_map/ppermute | solution.py:499
  67.5 2.5 %collective-permute-start.14 = (bf16[256,128]{1,0:T(8,128)(2,1)S(1)}, bf16[256,128]{1,0:T(8,128)(2,1)S(1)}, u32[]{:S(2)}, u32[]{:S(2)}) collective-permute-start(bf16[256,128]{1,0:T(8,128)(2,1)S(1)} %shard_map.168.refs_1_), channel_id=1, source_target_pairs={{0,16},{16,0},{32,48},{48,32},{64,80},{80,64},{96,112},{112,96},{1... | collective-permute-start | bytes 196616 | tf_op jit(solution)/shard_map/ppermute | solution.py:686
  70.0 8.7 %collective-permute-start.15 = (bf16[320,128]{1,0:T(8,128)(2,1)S(1)}, bf16[320,128]{1,0:T(8,128)(2,1)S(1)}, u32[]{:S(2)}, u32[]{:S(2)}) collective-permute-start(bf16[320,128]{1,0:T(8,128)(2,1)S(1)} %pad_maximum_fusion.3), channel_id=1, source_target_pairs={{16,48},{32,0},{48,80},{64,32},{80,112},{96,64},{112,144},{128,96}... | collective-permute-start | bytes 245768 | tf_op jit(solution)/shard_map/ppermute | solution.py:504
  78.7 2.5 %collective-permute-start.16 = (bf16[320,128]{1,0:T(8,128)(2,1)S(1)}, bf16[320,128]{1,0:T(8,128)(2,1)S(1)}, u32[]{:S(2)}, u32[]{:S(2)}) collective-permute-start(bf16[320,128]{1,0:T(8,128)(2,1)S(1)} %collective-permute-done.15.refs_3_), channel_id=1, source_target_pairs={{0,16},{16,0},{32,48},{48,32},{64,80},{80,64},{96,112},{112,96},{1... | collective-permute-start | bytes 245768 | tf_op jit(solution)/shard_map/ppermute | solution.py:689
  80.2 0.9 copy-start.12
  83.4 2.4 %collective-permute-start.17 = (bf16[384,8,128]{2,1,0:T(8,128)(2,1)S(1)}, bf16[384,8,128]{2,1,0:T(8,128)(2,1)S(1)}, u32[]{:S(2)}, u32[]{:S(2)}) collective-permute-start(bf16[384,8,128]{2,1,0:T(8,128)(2,1)S(1)} %constant_dynamic-slice_fusion), channel_id=1, source_target_pairs={{0,16},{16,0},{32,48},{48,32},{64,80},{80,64},{96,112},{112,96},{1... | collective-permute-start | bytes 2359304 | tf_op jit(solution)/shard_map/ppermute | solution.py:723
  162.8 5.6 %collective-permute-start.18 = (bf16[384,8,128]{2,1,0:T(8,128)(2,1)S(1)}, bf16[384,8,128]{2,1,0:T(8,128)(2,1)S(1)}, u32[]{:S(2)}, u32[]{:S(2)}) collective-permute-start(bf16[384,8,128]{2,1,0:T(8,128)(2,1)S(1)} %bitcast.63), channel_id=1, source_target_pairs={{0,16},{16,0},{32,48},{48,32},{64,80},{80,64},{96,112},{112,96},{1... | collective-permute-start | bytes 2359304 | tf_op jit(solution)/shard_map/ppermute | solution.py:736

commit v9 on v8

--- a/solution.py
+++ b/solution.py
@@ -7,6 +7,7 @@
 from jax.experimental import pallas as pl
 from jax.experimental.pallas import tpu as pltpu
 from jax.sharding import PartitionSpec as P
+
 
 AXES = ("gx", "gy")
 BF = jnp.bfloat16
@@ -560,8 +561,6 @@
             w_line.append(lax.ppermute(weight, "gx", [(i, along_y(i, k)) for i in range(ngx)]))
         w_line = jnp.concatenate(w_line, axis=0)
         w_far = lax.ppermute(w_line, AXES, [(i, mirrored(i)) for i in range(devices)])
-        w_mine = jnp.concatenate([w_line, w_far], axis=0)
-        w_mate = lax.ppermute(w_mine, "gx", swap)
 
         skip = skip_input.transpose(1, 0, 2)
         cot = cotangent.transpose(1, 0, 2)
@@ -575,6 +574,9 @@
         mate = lax.ppermute(own, "gx", swap)
         got = outward(jnp.concatenate([own, mate[24:28]], axis=0), ngx, 2)
         far = outward(jnp.concatenate([own[24:28], mate[24:28]], axis=0), ngx, 4)
+        got, w_far = lax.optimization_barrier((got, w_far))
+        w_mine = jnp.concatenate([w_line, w_far], axis=0)
+        w_mate = lax.ppermute(w_mine, "gx", swap)
         got_m = lax.ppermute(got, "gx", swap)
         far_m = lax.ppermute(far, "gx", swap)
         fine, pools, w_bot, _, w_flat = call(
@@ -680,6 +682,21 @@
             grant=33,
         )
 
+        def between_cores(tiles):
+            half = tiles.shape[0] // 2
+            keep = lax.dynamic_slice_in_dim(tiles, core * half, half, 0)
+            other = lax.dynamic_slice_in_dim(tiles, (1 - core) * half, half, 0)
+            other = lax.ppermute(other, "gx", swap)
+            return (keep.astype(F32) + other.astype(F32)).astype(BF)
+
+        grads = ((g_top, 864), (g_mid, 1728), (g_bot, 576))
+        tiles = [tiles_of(g) for g, _ in grads]
+        mine_main = between_cores(jnp.concatenate(tiles, axis=0))
+        cut = mine_main.shape[0]
+        last = cut + 27
+        spare = -last % (devices // 2) + 27
+        mine_main = jnp.pad(mine_main, ((0, spare), (0, 0), (0, 0)))
+
         from_left = shift(packed, "gy", ngy, 1)
         from_right = shift(packed, "gy", ngy, -1)
         (line,) = call(join_kernel, [((256, 128), BF)], [], 0, packed, from_left, from_right)
@@ -687,6 +704,7 @@
         edge = jnp.where(core == 0, line[128:192], line[192:256])
         got = outward(jnp.concatenate([line[0:128], mate[0:128], edge], axis=0), ngx, 2)
         got_m = lax.ppermute(got, "gx", swap)
+        got_m, mine_main = lax.optimization_barrier((got_m, mine_main))
         grad_skip, g_enc = call(
             lambda *refs: tail_kernel(sizes, scales[1], *refs),
             [((4, 32, 256), BF), ((432, 128), BF)],
@@ -713,15 +731,8 @@
             cost=4,
         )
 
-        grads = ((g_top, 864), (g_mid, 1728), (g_bot, 576), (g_enc, 128))
-        tiles = [tiles_of(g) for g, _ in grads]
-        spare = -sum(t.shape[0] for t in tiles) % devices
-        flat = jnp.concatenate(tiles + [jnp.zeros((spare, 8, 128), BF)], axis=0)
-        half = flat.shape[0] // 2
-        keep = lax.dynamic_slice_in_dim(flat, core * half, half, 0)
-        other = lax.dynamic_slice_in_dim(flat, (1 - core) * half, half, 0)
-        other = lax.ppermute(other, "gx", swap)
-        mine = (keep.astype(F32) + other.astype(F32)).astype(BF)
+        mine_enc = between_cores(tiles_of(g_enc))
+        mine = lax.dynamic_update_slice(mine_main, mine_enc, (cut, 0, 0))
         parts = mine.reshape(devices // 2, -1, 128)
         groups = [[i for i in range(devices) if i // ngy % 2 == k] for k in range(2)]
         parts = lax.all_to_all(
@@ -732,18 +743,20 @@
         spread = lax.all_to_all(
             spread, AXES, split_axis=0, concat_axis=0, axis_index_groups=groups, tiled=True
         )
-        mine = spread.reshape(half, 8, 128)
+        mine = spread.reshape(-1, 8, 128)
         other = lax.ppermute(mine, "gx", swap)
         first = jnp.where(core == 0, mine, other)
         second = jnp.where(core == 0, other, mine)
-        whole = jnp.concatenate([first, second], axis=0)
+        whole = jnp.concatenate([first[:cut], second[:cut]], axis=0)
+        full_enc = jnp.concatenate([first[cut:last], second[cut:last]], axis=0)
+        full_enc = from_tiles(full_enc, 432, 128)
 
         full = []
         start = 0
         for (g, width), t in zip(grads, tiles):
             full.append(from_tiles(whole[start : start + t.shape[0]], g.shape[0], width))
             start += t.shape[0]
-        full_top, full_mid, full_bot, full_enc = full
+        full_top, full_mid, full_bot = full
         (full_enc,) = call(finish_kernel, [((64, 864), F32)], [], 0, full_enc)
         mine_bot = full_bot.reshape(3, ngx, block, -1)
         mine_bot = lax.dynamic_index_in_dim(mine_bot, gx, 1, keepdims=False)

time: 173 us -> 172 us (level)
  waiting for transfers between devices: 13.8 us -> 6.87 us
  blocking collectives: 76.5 us -> 79.6 us
    ppermute x3, starting transfers between devices: 14.3 us -> 6.94 us  [outward(): lax.ppermute(value, 'gx', [(i, j) for i, j in pairs if 0 <= j < count])]
    ppermute x1, starting transfers between devices: 0.7 us -> 5.64 us  [step(): w_mate = lax.ppermute(w_mine, 'gx', swap)]
    ppermute x4, waiting for transfers between devices: 4.87 us -> 1.14 us  [shift(): lax.ppermute(value, axis, [(i, i + step) for i in range(count) if 0 <= i...]
    all_to_all x1, blocking collectives: 46.4 us -> 49.6 us  [step(): lax.all_to_all(parts, AXES, split_axis=0, concat_axis=0, axis_index_group...]
    ppermute x1, waiting for transfers between devices: 3.02 us -> 0.01 us  [step(): lax.ppermute(w_line, AXES, [(i, mirrored(i)) for i in range(devices)])]
    ppermute x1, starting transfers between devices: 5.92 us -> 8.64 us  [step(): lax.ppermute(w_line, AXES, [(i, mirrored(i)) for i in range(devices)])]
    ppermute x2, starting transfers between devices: 1.67 us -> 4.02 us  [step(): got_m = lax.ppermute(got, 'gx', swap)]
    unnamed x40 -> x42, local copies, waits for them, and re-layouts: 4.44 us -> 5.08 us
  transfers between devices with their start and end apart: 19 -> 20, of which waited for: 10 -> 8; matrix products, arithmetic and copies ran while one was open for 2% -> 2% of each run, Pallas kernels for 1% -> 1%
where the time goes in v9:
time: 172 us
  blocking collectives  79.6 us (46%)
  starting transfers between devices  48.1 us (28%)
  Pallas kernels  23.6 us (14%)
  local copies, waits for them, and re-layouts  7.09 us (4%)
  waiting for transfers between devices  6.87 us (4%)
  other arithmetic  5.11 us (3%)
    all_to_all x1, blocking collectives, step(): lax.all_to_all(parts, AXES, split_axis=0, concat_axis=0, axis_index_group...  49.6 us
    all_to_all x1, blocking collectives, step(): lax.all_to_all(spread, AXES, split_axis=0, concat_axis=0, axis_index_grou...  30 us
    pallas_call x9, Pallas kernels, call(): pl.pallas_call(kernel, out_shape=[jax.ShapeDtypeStruct(s, d) for s, d in...  23.6 us
    ppermute x4, starting transfers between devices, shift(): lax.ppermute(value, axis, [(i, i + step) for i in range(count) if 0 <= i...  10.5 us
    ppermute x1, starting transfers between devices, step(): lax.ppermute(w_line, AXES, [(i, mirrored(i)) for i in range(devices)])  8.64 us
    ppermute x3, starting transfers between devices, outward(): lax.ppermute(value, 'gx', [(i, j) for i, j in pairs if 0 <= j < count])  6.94 us
    ppermute x1, starting transfers between devices, step(): w_mate = lax.ppermute(w_mine, 'gx', swap)  5.64 us
    unnamed x42, local copies, waits for them, and re-layouts  5.08 us
  transfers between devices with their start and end apart: 20, of which 8 were waited for; matrix products, arithmetic and copies ran while one was open for 2% of the time, Pallas kernels for 1%

profile of v9, /device:TPU:1, one launch (start us, length us, event | category | flops | bytes accessed | tf_op | source)
XLA Modules:
  0.0 171.6 jit_solution(6553433578600562226)
XLA Ops:
  0.6 0.9 copy_bitcast_fusion
  1.5 0.0 copy-start.6
  1.6 0.8 copy-done.6
  2.4 0.2 shard_map.163
  2.5 3.9 %collective-permute-start.1 = (bf16[10,32,128]{2,1,0:T(8,128)(2,1)S(1)}, bf16[10,32,128]{2,1,0:T(8,128)(2,1)S(1)}, u32[]{:S(2)}, u32[]{:S(2)}) collective-permute-start(bf16[10,32,128]{2,1,0:T(8,128)(2,1)S(1)} %get-tuple-element.33), channel_id=1, source_target_pairs={{0,1},{1,2},{2,3},{3,4},{4,5},{5,6},{6,7},{7,8},{8,9},{9,10},{10,1... | collective-permute-start | bytes 245768 | tf_op jit(solution)/shard_map/ppermute | solution.py:500
  6.5 1.3 collective-permute-start
  7.8 2.8 %collective-permute-start.6 = (bf16[4,32,128]{2,1,0:T(8,128)(2,1)S(1)}, bf16[4,32,128]{2,1,0:T(8,128)(2,1)S(1)}, u32[]{:S(2)}, u32[]{:S(2)}) collective-permute-start(bf16[4,32,128]{2,1,0:T(8,128)(2,1)S(1)} %bitcast.69), channel_id=1, source_target_pairs={{0,96},{16,112},{32,0},{48,16},{64,32},{80,48},{96,64},{112,80},{1... | collective-permute-start | bytes 98312 | tf_op jit(solution)/shard_map/ppermute | solution.py:561
  10.7 0.3 collective-permute-start.5
  11.0 0.7 collective-permute-start.4
  11.8 2.2 %collective-permute-start.2 = (bf16[28,32,128]{2,1,0:T(8,128)(2,1)S(1)}, bf16[28,32,128]{2,1,0:T(8,128)(2,1)S(1)}, u32[]{:S(2)}, u32[]{:S(2)}) collective-permute-start(bf16[28,32,128]{2,1,0:T(8,128)(2,1)S(1)} %shard_map.164.refs_1_), channel_id=1, source_target_pairs={{0,16},{16,0},{32,48},{48,32},{64,80},{80,64},{96,112},{112,96},{1... | collective-permute-start | bytes 688136 | tf_op jit(solution)/shard_map/ppermute | solution.py:574
  13.9 1.0 collective-permute-done.5
  15.0 0.3 collective-permute-done.4
  15.3 8.6 %collective-permute-start.7 = (bf16[16,32,128]{2,1,0:T(8,128)(2,1)S(1)}, bf16[16,32,128]{2,1,0:T(8,128)(2,1)S(1)}, u32[]{:S(2)}, u32[]{:S(2)}) collective-permute-start(bf16[16,32,128]{2,1,0:T(8,128)(2,1)S(1)} %pad_maximum_fusion.3), channel_id=1, source_target_pairs={{0,140},{1,141},{2,142},{3,143},{4,136},{5,137},{6,138},{7,139},{8... | collective-permute-start | bytes 393224 | tf_op jit(solution)/shard_map/ppermute | solution.py:563
  24.0 2.2 %collective-permute-start.3 = (bf16[32,32,128]{2,1,0:T(8,128)(2,1)S(1)}, bf16[32,32,128]{2,1,0:T(8,128)(2,1)S(1)}, u32[]{:S(2)}, u32[]{:S(2)}) collective-permute-start(bf16[32,32,128]{2,1,0:T(8,128)(2,1)S(1)} %pad_maximum_fusion.2), channel_id=1, source_target_pairs={{16,48},{32,0},{48,80},{64,32},{80,112},{96,64},{112,144},{128,96}... | collective-permute-start | bytes 786440 | tf_op jit(solution)/shard_map/ppermute | solution.py:505
  26.2 0.6 pad_maximum_fusion.5
  26.9 3.4 %collective-permute-start.9 = (bf16[8,32,128]{2,1,0:T(8,128)(2,1)}, bf16[8,32,128]{2,1,0:T(8,128)(2,1)S(1)}, u32[]{:S(2)}, u32[]{:S(2)}) collective-permute-start(bf16[8,32,128]{2,1,0:T(8,128)(2,1)} %pad_maximum_fusion.5), channel_id=1, source_target_pairs={{16,80},{48,112},{64,0},{80,144},{96,32},{112,176},{128,64},{144,2... | collective-permute-start | bytes 196616 | tf_op jit(solution)/shard_map/ppermute | solution.py:505
  30.4 5.6 %collective-permute-start.11 = (bf16[32,32,128]{2,1,0:T(8,128)(2,1)S(1)}, bf16[32,32,128]{2,1,0:T(8,128)(2,1)S(1)}, u32[]{:S(2)}, u32[]{:S(2)}) collective-permute-start(bf16[32,32,128]{2,1,0:T(8,128)(2,1)S(1)} %constant_dynamic-update-slice_fusion.refs_7_), channel_id=1, source_target_pairs={{0,16},{16,0},{32,48},{48,32},{64,80},{80,64},{96,112},{112,96},{1... | collective-permute-start | bytes 786440 | tf_op jit(solution)/shard_map/ppermute | solution.py:579
  36.0 0.1 collective-permute-start.8
  36.1 0.9 shard_map.166
  37.0 0.8 copy-done.9
  37.9 0.7 copy-done.11
  38.5 0.7 copy-done.13
  39.2 0.0 copy-start.8
  39.3 0.7 collective-permute-start.10
  39.9 0.1 pad_add_fusion.refs_0_
  40.0 0.8 collective-permute-done.10.refs_6_
  40.9 1.6 shard_map.165
  42.5 17.3 %shard_map.167 = (bf16[4,32,256]{2,1,0:T(8,128)(2,1)S(1)}, f32[4,32,256]{2,1,0:T(8,128)S(1)}, bf16[192,128]{1,0:T(8,128)(2,1)S(1)}, f32[4,64,128]{2,1,0:T(8,128)...) custom-call(s32[2]{0:T(128)S(1)} %pad_add_fusion.refs_0_, ...), custom_call_target="tpu_custom_call" | custom-call | flops 10000000000 | bytes 20000000 | tf_op jit(solution)/shard_map/pallas_call | solution.py:486
  59.8 0.1 pad_maximum_fusion
  60.0 0.1 constant_dynamic-slice_fusion.1
  60.1 0.4 collective-permute-start.17
  60.5 0.6 copy-done.15
  61.1 1.3 collective-permute-start.13
  62.4 4.0 %collective-permute-start.12 = (bf16[192,128]{1,0:T(8,128)(2,1)S(1)}, bf16[192,128]{1,0:T(8,128)(2,1)S(1)}, u32[]{:S(2)}, u32[]{:S(2)}) collective-permute-start(bf16[192,128]{1,0:T(8,128)(2,1)S(1)} %get-tuple-element.45.own), channel_id=1, source_target_pairs={{0,1},{1,2},{2,3},{3,4},{4,5},{5,6},{6,7},{7,8},{8,9},{9,10},{10,1... | collective-permute-start | bytes 147464 | tf_op jit(solution)/shard_map/ppermute | solution.py:500
  66.4 1.1 collective-permute-done.12.left
  67.6 0.1 shard_map.168.refs_1_
  67.7 1.6 collective-permute-start.14
  69.2 0.9 collective-permute-done.14.refs_2_
  70.1 1.3 collective-permute-start.15
  71.5 0.6 shard_map.169.refs_8_
  72.0 0.9 collective-permute-done.15.refs_3_
  72.9 3.9 %collective-permute-start.16 = (bf16[320,128]{1,0:T(8,128)(2,1)S(1)}, bf16[320,128]{1,0:T(8,128)(2,1)S(1)}, u32[]{:S(2)}, u32[]{:S(2)}) collective-permute-start(bf16[320,128]{1,0:T(8,128)(2,1)S(1)} %collective-permute-done.15.refs_3_), channel_id=1, source_target_pairs={{0,16},{16,0},{32,48},{48,32},{64,80},{80,64},{96,112},{112,96},{1... | collective-permute-start | bytes 245768 | tf_op jit(solution)/shard_map/ppermute | solution.py:706
  76.8 1.3 add_convert_fusion
  78.1 0.1 pad.9
  78.2 2.1 %shard_map.170 = (bf16[4,32,256]{2,1,0:T(8,128)(2,1)S(1)}, bf16[432,128]{1,0:T(8,128)(2,1)S(1)}) custom-call(s32[2]{0:T(128)S(1)} %pad_add_fusion.refs_0_, bf16[256,128]{1,0:T(8,128)(2,1)S(1)} %shard_map.168.refs_1_, bf16[256,128]{1,0:T(8,128)(2,1)S(1)} %collective-permute-done.14.refs_2_, bf16[320,128]{1,0:T(8,128)(2,1)S(1)} %collective-permute-done.15.refs_3_, ...), custom_call_target="tpu_custom_call" | custom-call | flops 2000000000 | bytes 4000000 | tf_op jit(solution)/shard_map/pallas_call | solution.py:486
  80.3 0.1 collective-permute-start.18
  80.5 1.2 collective-permute-done.18
  81.7 49.6 %all_to_all.10 = bf16[128,24,128]{2,1,0:T(8,128)(2,1)S(1)} all-to-all(bf16[128,24,128]{2,1,0:T(8,128)(2,1)S(1)} %bitcast.63), channel_id=1, replica_groups={{0,1,2,3,4,5,6,7,8,9,10,11,12,13,14,15,32,33,34,35,36,37,38,39,40,41,42..., dimensions={0} | all-to-all | bytes 1572864 | tf_op jit(solution)/shard_map/all_to_all | solution.py:738
  131.3 0.2 reduce_sum.12
  131.5 0.1 broadcast_in_dim.2
  131.6 30.0 %all_to_all.11 = bf16[128,24,128]{2,1,0:T(8,128)(2,1)S(1)} all-to-all(bf16[128,24,128]{2,1,0:T(8,128)(2,1)S(1)} %broadcast_in_dim.2), channel_id=1, replica_groups={{0,1,2,3,4,5,6,7,8,9,10,11,12,13,14,15,32,33,34,35,36,37,38,39,40,41,42..., dimensions={0} | all-to-all | bytes 1572864 | tf_op jit(solution)/shard_map/all_to_all | solution.py:743
  161.6 3.6 %collective-permute-start.19 = (bf16[384,8,128]{2,1,0:T(8,128)(2,1)S(1)}, bf16[384,8,128]{2,1,0:T(8,128)(2,1)S(1)}, u32[]{:S(2)}, u32[]{:S(2)}) collective-permute-start(bf16[384,8,128]{2,1,0:T(8,128)(2,1)S(1)} %bitcast.64), channel_id=1, source_target_pairs={{0,16},{16,0},{32,48},{48,32},{64,80},{80,64},{96,112},{112,96},{1... | collective-permute-start | bytes 2359304 | tf_op jit(solution)/shard_map/ppermute | solution.py:747
  165.2 0.7 copy.20
  165.9 0.7 copy.21
  166.5 0.5 collective-permute-done.19
  167.1 0.1 broadcast_select_fusion.1
  167.4 0.8 shard_map.171
  168.3 0.1 concatenate.44
  168.4 0.8 convert_element_type.41
  169.2 0.1 pad_maximum_fusion.1
  169.3 0.1 concatenate.41
  169.4 0.6 convert_element_type.39
  170.0 0.4 concatenate.43
  170.4 1.2 convert_element_type.40
  (68 shorter events, 0.6 us)
Async XLA Ops:
  0.6 7.2 %copy-start.17 = (bf16[8,1728]{1,0:T(8,128)(2,1)S(1)}, bf16[8,1728]{1,0:T(8,128)(2,1)}, u32[]{:S(2)}) copy-start(bf16[8,1728]{1,0:T(8,128)(2,1)} %param.14) | copy-start | bytes 82948
  1.5 0.8 copy-start.6
  2.5 9.2 %collective-permute-start.1 = (bf16[10,32,128]{2,1,0:T(8,128)(2,1)S(1)}, bf16[10,32,128]{2,1,0:T(8,128)(2,1)S(1)}, u32[]{:S(2)}, u32[]{:S(2)}) collective-permute-start(bf16[10,32,128]{2,1,0:T(8,128)(2,1)S(1)} %get-tuple-element.33), channel_id=1, source_target_pairs={{0,1},{1,2},{2,3},{3,4},{4,5},{5,6},{6,7},{7,8},{8,9},{9,10},{10,1... | collective-permute-start | bytes 245768 | tf_op jit(solution)/shard_map/ppermute | solution.py:500
  6.5 5.2 %collective-permute-start = (bf16[10,32,128]{2,1,0:T(8,128)(2,1)S(1)}, bf16[10,32,128]{2,1,0:T(8,128)(2,1)S(1)}, u32[]{:S(2)}, u32[]{:S(2)}) collective-permute-start(bf16[10,32,128]{2,1,0:T(8,128)(2,1)S(1)} %get-tuple-element.32.own), channel_id=1, source_target_pairs={{1,0},{2,1},{3,2},{4,3},{5,4},{6,5},{7,6},{8,7},{9,8},{10,9},{11,1... | collective-permute-start | bytes 245768 | tf_op jit(solution)/shard_map/ppermute | solution.py:500
  7.8 28.3 %copy-start = (bf16[64,5184]{1,0:T(8,128)(2,1)S(1)}, bf16[64,5184]{1,0:T(8,128)(2,1)}, u32[]{:S(2)}) copy-start(bf16[64,5184]{1,0:T(8,128)(2,1)} %refs_1_.1) | copy-start | bytes 1990660
  7.8 28.3 %copy-start.1 = (bf16[32,2592]{1,0:T(8,128)(2,1)S(1)}, bf16[32,2592]{1,0:T(8,128)(2,1)}, u32[]{:S(2)}) copy-start(bf16[32,2592]{1,0:T(8,128)(2,1)} %refs_2_.1) | copy-start | bytes 497668
  7.8 28.3 %copy-start.2 = (bf16[64,864]{1,0:T(8,128)(2,1)S(1)}, bf16[64,864]{1,0:T(8,128)(2,1)}, u32[]{:S(2)}) copy-start(bf16[64,864]{1,0:T(8,128)(2,1)} %refs_0_.1) | copy-start | bytes 331780
  7.8 6.1 %collective-permute-start.6 = (bf16[4,32,128]{2,1,0:T(8,128)(2,1)S(1)}, bf16[4,32,128]{2,1,0:T(8,128)(2,1)S(1)}, u32[]{:S(2)}, u32[]{:S(2)}) collective-permute-start(bf16[4,32,128]{2,1,0:T(8,128)(2,1)S(1)} %bitcast.69), channel_id=1, source_target_pairs={{0,96},{16,112},{32,0},{48,16},{64,32},{80,48},{96,64},{112,80},{1... | collective-permute-start | bytes 98312 | tf_op jit(solution)/shard_map/ppermute | solution.py:561
  10.7 4.3 %collective-permute-start.5 = (bf16[4,32,128]{2,1,0:T(8,128)(2,1)S(1)}, bf16[4,32,128]{2,1,0:T(8,128)(2,1)S(1)}, u32[]{:S(2)}, u32[]{:S(2)}) collective-permute-start(bf16[4,32,128]{2,1,0:T(8,128)(2,1)S(1)} %bitcast.70), channel_id=1, source_target_pairs={{0,64},{16,80},{32,96},{48,112},{64,0},{80,16},{96,32},{112,48},{1... | collective-permute-start | bytes 98312 | tf_op jit(solution)/shard_map/ppermute | solution.py:561
  11.0 4.3 %collective-permute-start.4 = (bf16[4,32,128]{2,1,0:T(8,128)(2,1)S(1)}, bf16[4,32,128]{2,1,0:T(8,128)(2,1)S(1)}, u32[]{:S(2)}, u32[]{:S(2)}) collective-permute-start(bf16[4,32,128]{2,1,0:T(8,128)(2,1)S(1)} %bitcast.71), channel_id=1, source_target_pairs={{0,32},{16,48},{32,64},{48,80},{64,96},{80,112},{96,0},{112,16},{1... | collective-permute-start | bytes 98312 | tf_op jit(solution)/shard_map/ppermute | solution.py:561
  11.8 12.2 %collective-permute-start.2 = (bf16[28,32,128]{2,1,0:T(8,128)(2,1)S(1)}, bf16[28,32,128]{2,1,0:T(8,128)(2,1)S(1)}, u32[]{:S(2)}, u32[]{:S(2)}) collective-permute-start(bf16[28,32,128]{2,1,0:T(8,128)(2,1)S(1)} %shard_map.164.refs_1_), channel_id=1, source_target_pairs={{0,16},{16,0},{32,48},{48,32},{64,80},{80,64},{96,112},{112,96},{1... | collective-permute-start | bytes 688136 | tf_op jit(solution)/shard_map/ppermute | solution.py:574
  15.3 15.0 %collective-permute-start.7 = (bf16[16,32,128]{2,1,0:T(8,128)(2,1)S(1)}, bf16[16,32,128]{2,1,0:T(8,128)(2,1)S(1)}, u32[]{:S(2)}, u32[]{:S(2)}) collective-permute-start(bf16[16,32,128]{2,1,0:T(8,128)(2,1)S(1)} %pad_maximum_fusion.3), channel_id=1, source_target_pairs={{0,140},{1,141},{2,142},{3,143},{4,136},{5,137},{6,138},{7,139},{8... | collective-permute-start | bytes 393224 | tf_op jit(solution)/shard_map/ppermute | solution.py:563
  24.0 6.4 %collective-permute-start.3 = (bf16[32,32,128]{2,1,0:T(8,128)(2,1)S(1)}, bf16[32,32,128]{2,1,0:T(8,128)(2,1)S(1)}, u32[]{:S(2)}, u32[]{:S(2)}) collective-permute-start(bf16[32,32,128]{2,1,0:T(8,128)(2,1)S(1)} %pad_maximum_fusion.2), channel_id=1, source_target_pairs={{16,48},{32,0},{48,80},{64,32},{80,112},{96,64},{112,144},{128,96}... | collective-permute-start | bytes 786440 | tf_op jit(solution)/shard_map/ppermute | solution.py:505
  26.9 12.4 %collective-permute-start.9 = (bf16[8,32,128]{2,1,0:T(8,128)(2,1)}, bf16[8,32,128]{2,1,0:T(8,128)(2,1)S(1)}, u32[]{:S(2)}, u32[]{:S(2)}) collective-permute-start(bf16[8,32,128]{2,1,0:T(8,128)(2,1)} %pad_maximum_fusion.5), channel_id=1, source_target_pairs={{16,80},{48,112},{64,0},{80,144},{96,32},{112,176},{128,64},{144,2... | collective-permute-start | bytes 196616 | tf_op jit(solution)/shard_map/ppermute | solution.py:505
  30.4 10.5 %collective-permute-start.11 = (bf16[32,32,128]{2,1,0:T(8,128)(2,1)S(1)}, bf16[32,32,128]{2,1,0:T(8,128)(2,1)S(1)}, u32[]{:S(2)}, u32[]{:S(2)}) collective-permute-start(bf16[32,32,128]{2,1,0:T(8,128)(2,1)S(1)} %constant_dynamic-update-slice_fusion.refs_7_), channel_id=1, source_target_pairs={{0,16},{16,0},{32,48},{48,32},{64,80},{80,64},{96,112},{112,96},{1... | collective-permute-start | bytes 786440 | tf_op jit(solution)/shard_map/ppermute | solution.py:579
  36.0 4.8 %collective-permute-start.8 = (bf16[32,32,128]{2,1,0:T(8,128)(2,1)S(1)}, bf16[32,32,128]{2,1,0:T(8,128)(2,1)S(1)}, u32[]{:S(2)}, u32[]{:S(2)}) collective-permute-start(bf16[32,32,128]{2,1,0:T(8,128)(2,1)S(1)} %collective-permute-done.3.refs_3_), channel_id=1, source_target_pairs={{0,16},{16,0},{32,48},{48,32},{64,80},{80,64},{96,112},{112,96},{1... | collective-permute-start | bytes 786440 | tf_op jit(solution)/shard_map/ppermute | solution.py:580
  37.0 0.8 copy-start.9
  37.9 0.7 copy-start.11
  38.5 0.7 copy-start.13
  39.2 3.2 %copy-start.3 = (bf16[128,384]{1,0:T(8,128)(2,1)S(1)}, bf16[128,384]{1,0:T(8,128)(2,1)}, u32[]{:S(2)}) copy-start(bf16[128,384]{1,0:T(8,128)(2,1)} %constant.53.clone.refs_12_.refs_11_) | copy-start | bytes 294916
  39.2 3.2 %copy-start.4 = (bf16[384,128]{1,0:T(8,128)(2,1)S(1)}, bf16[384,128]{1,0:T(8,128)(2,1)}, u32[]{:S(2)}) copy-start(bf16[384,128]{1,0:T(8,128)(2,1)} %constant.54.clone.refs_13_) | copy-start | bytes 294916
  39.2 3.2 %copy-start.5 = (bf16[256,128]{1,0:T(8,128)(2,1)S(1)}, bf16[256,128]{1,0:T(8,128)(2,1)}, u32[]{:S(2)}) copy-start(bf16[256,128]{1,0:T(8,128)(2,1)} %constant.55.clone.refs_14_) | copy-start | bytes 196612
  39.2 3.3 %copy-start.7 = (bf16[128,128]{1,0:T(8,128)(2,1)S(1)}, bf16[128,128]{1,0:T(8,128)(2,1)}, u32[]{:S(2)}) copy-start(bf16[128,128]{1,0:T(8,128)(2,1)} %constant.51.clone.refs_10_) | copy-start | bytes 98308
  39.2 3.3 %copy-start.8 = (bf16[128,128]{1,0:T(8,128)(2,1)S(1)}, bf16[128,128]{1,0:T(8,128)(2,1)}, u32[]{:S(2)}) copy-start(bf16[128,128]{1,0:T(8,128)(2,1)} %constant.52.clone.refs_11_) | copy-start | bytes 98308
  39.2 3.2 %copy-start.10 = (bf16[192,1728]{1,0:T(8,128)(2,1)S(1)}, bf16[192,1728]{1,0:T(8,128)(2,1)}, u32[]{:S(2)}) copy-start(bf16[192,1728]{1,0:T(8,128)(2,1)} %copy-done.9) | copy-start | bytes 1990660
  39.2 3.2 %copy-start.12 = (bf16[96,864]{1,0:T(8,128)(2,1)S(1)}, bf16[96,864]{1,0:T(8,128)(2,1)}, u32[]{:S(2)}) copy-start(bf16[96,864]{1,0:T(8,128)(2,1)} %copy-done.11) | copy-start | bytes 497668
  39.3 3.2 %copy-start.14 = (bf16[192,288]{1,0:T(8,128)(2,1)S(1)}, bf16[192,288]{1,0:T(8,128)(2,1)}, u32[]{:S(2)}) copy-start(bf16[192,288]{1,0:T(8,128)(2,1)} %copy-done.13) | copy-start | bytes 331780
  39.3 1.6 collective-permute-start.10
  60.0 1.1 copy-start.15
  60.1 16.8 %collective-permute-start.17 = (bf16[330,8,128]{2,1,0:T(8,128)(2,1)S(1)}, bf16[330,8,128]{2,1,0:T(8,128)(2,1)}, u32[]{:S(2)}, u32[]{:S(2)}) collective-permute-start(bf16[330,8,128]{2,1,0:T(8,128)(2,1)S(1)} %constant_dynamic-slice_fusion.1), channel_id=1, source_target_pairs={{0,16},{16,0},{32,48},{48,32},{64,80},{80,64},{96,112},{112,96},{1... | collective-permute-start | bytes 2027528 | tf_op jit(solution)/shard_map/ppermute | solution.py:689
  61.1 5.3 %collective-permute-start.13 = (bf16[192,128]{1,0:T(8,128)(2,1)S(1)}, bf16[192,128]{1,0:T(8,128)(2,1)S(1)}, u32[]{:S(2)}, u32[]{:S(2)}) collective-permute-start(bf16[192,128]{1,0:T(8,128)(2,1)S(1)} %get-tuple-element.45.own), channel_id=1, source_target_pairs={{1,0},{2,1},{3,2},{4,3},{5,4},{6,5},{7,6},{8,7},{9,8},{10,9},{11,1... | collective-permute-start | bytes 147464 | tf_op jit(solution)/shard_map/ppermute | solution.py:500
  62.4 5.2 %collective-permute-start.12 = (bf16[192,128]{1,0:T(8,128)(2,1)S(1)}, bf16[192,128]{1,0:T(8,128)(2,1)S(1)}, u32[]{:S(2)}, u32[]{:S(2)}) collective-permute-start(bf16[192,128]{1,0:T(8,128)(2,1)S(1)} %get-tuple-element.45.own), channel_id=1, source_target_pairs={{0,1},{1,2},{2,3},{3,4},{4,5},{5,6},{6,7},{7,8},{8,9},{9,10},{10,1... | collective-permute-start | bytes 147464 | tf_op jit(solution)/shard_map/ppermute | solution.py:500
  67.7 2.5 %collective-permute-start.14 = (bf16[256,128]{1,0:T(8,128)(2,1)S(1)}, bf16[256,128]{1,0:T(8,128)(2,1)S(1)}, u32[]{:S(2)}, u32[]{:S(2)}) collective-permute-start(bf16[256,128]{1,0:T(8,128)(2,1)S(1)} %shard_map.168.refs_1_), channel_id=1, source_target_pairs={{0,16},{16,0},{32,48},{48,32},{64,80},{80,64},{96,112},{112,96},{1... | collective-permute-start | bytes 196616 | tf_op jit(solution)/shard_map/ppermute | solution.py:703
  70.1 2.8 %collective-permute-start.15 = (bf16[320,128]{1,0:T(8,128)(2,1)S(1)}, bf16[320,128]{1,0:T(8,128)(2,1)S(1)}, u32[]{:S(2)}, u32[]{:S(2)}) collective-permute-start(bf16[320,128]{1,0:T(8,128)(2,1)S(1)} %pad_maximum_fusion.4), channel_id=1, source_target_pairs={{16,48},{32,0},{48,80},{64,32},{80,112},{96,64},{112,144},{128,96}... | collective-permute-start | bytes 245768 | tf_op jit(solution)/shard_map/ppermute | solution.py:505
  71.5 5.4 %copy-start.16 = (bf16[660,8,128]{2,1,0:T(8,128)(2,1)S(1)}, bf16[660,8,128]{2,1,0:T(8,128)(2,1)}, u32[]{:S(2)}) copy-start(bf16[660,8,128]{2,1,0:T(8,128)(2,1)} %copy-done.15) | copy-start | bytes 4055044
  72.9 5.3 %collective-permute-start.16 = (bf16[320,128]{1,0:T(8,128)(2,1)S(1)}, bf16[320,128]{1,0:T(8,128)(2,1)S(1)}, u32[]{:S(2)}, u32[]{:S(2)}) collective-permute-start(bf16[320,128]{1,0:T(8,128)(2,1)S(1)} %collective-permute-done.15.refs_3_), channel_id=1, source_target_pairs={{0,16},{16,0},{32,48},{48,32},{64,80},{80,64},{96,112},{112,96},{1... | collective-permute-start | bytes 245768 | tf_op jit(solution)/shard_map/ppermute | solution.py:706
  80.3 1.3 collective-permute-start.18
  161.6 5.5 %collective-permute-start.19 = (bf16[384,8,128]{2,1,0:T(8,128)(2,1)S(1)}, bf16[384,8,128]{2,1,0:T(8,128)(2,1)S(1)}, u32[]{:S(2)}, u32[]{:S(2)}) collective-permute-start(bf16[384,8,128]{2,1,0:T(8,128)(2,1)S(1)} %bitcast.64), channel_id=1, source_target_pairs={{0,16},{16,0},{32,48},{48,32},{64,80},{80,64},{96,112},{112,96},{1... | collective-permute-start | bytes 2359304 | tf_op jit(solution)/shard_map/ppermute | solution.py:747

commit v10 on v9

--- a/solution.py
+++ b/solution.py
@@ -275,7 +275,7 @@
         value = silu(row_sum(sum_a, k, 64)) * (wide_in * row_ok(gx * 2 + k - 6, rows_mid))
         act_a[k] = value.astype(BF)
 
-    loop(14, enc_act, 2)
+    loop(14, enc_act, 7)
     for m in range(4):
         pre = row_sum(sum_a, m + 5, 64)
         pre_one[m] = jnp.where(lane(128) < 96, pre[:, 0:128], pre[:, 128:256])
@@ -305,7 +305,7 @@
         put_taps(taps_c, k, 128, 192, narrow, 8)
         sum_c[k] = dot(w_mid[...], taps_c[k])
 
-    loop(8, mid_taps, 2)
+    loop(8, mid_taps, 4)
 
     def mid_act(k):
         pre = row_sum(sum_c, k, 64)
@@ -328,7 +328,7 @@
             put_taps(taps_d, 2 * j + half, 0, 96, act_c[j], 16)
             sum_d[2 * j + half] = dot(w_top[...], taps_d[2 * j + half])
 
-    loop(6, top_taps, 2)
+    loop(6, top_taps, 3)
     for k in range(10):
         pre = row_sum(sum_d, k, 32)
         s = sigmoid(pre)
@@ -341,7 +341,7 @@
         put_taps(taps_e, k, 0, 32, err_d[k], 16)
         sum_e[k] = dot(t_top[...], taps_e[k])
 
-    loop(10, top_back, 2)
+    loop(10, top_back, 5)
 
     total = None
     for k in range(6):
@@ -369,7 +369,7 @@
         put_taps(taps_f, m, 0, 64, err_c[m], 8)
         sum_f[m] = dot(t_mid[...], taps_f[m])
 
-    loop(4, mid_back, 2)
+    loop(4, mid_back, 4)
     own_mid = jnp.where(lax.broadcasted_iota(jnp.int32, (64, 128), 1) < 64, 1.0, 0.0).astype(BF)
     for k in range(4):
         for a in range(3):

time: 172 us -> 170 us (0.988)
  Pallas kernels: 23.6 us -> 21.4 us
    pallas_call x9, Pallas kernels: 23.6 us -> 21.4 us  [call(): pl.pallas_call(kernel, out_shape=[jax.ShapeDtypeStruct(s, d) for s, d in...]
where the time goes in v10:
time: 170 us; the launch traced here: 169 us
  blocking collectives  79.4 us (47%)
  starting transfers between devices  48.1 us (28%)
  Pallas kernels  21.4 us (13%)
  local copies, waits for them, and re-layouts  7.09 us (4%)
  waiting for transfers between devices  6.87 us (4%)
  other arithmetic  5.11 us (3%)
    all_to_all x1, blocking collectives, step(): lax.all_to_all(parts, AXES, split_axis=0, concat_axis=0, axis_index_group...  49.4 us
    all_to_all x1, blocking collectives, step(): lax.all_to_all(spread, AXES, split_axis=0, concat_axis=0, axis_index_grou...  30 us
    pallas_call x9, Pallas kernels, call(): pl.pallas_call(kernel, out_shape=[jax.ShapeDtypeStruct(s, d) for s, d in...  21.4 us
    ppermute x4, starting transfers between devices, shift(): lax.ppermute(value, axis, [(i, i + step) for i in range(count) if 0 <= i...  10.5 us
    ppermute x1, starting transfers between devices, step(): lax.ppermute(w_line, AXES, [(i, mirrored(i)) for i in range(devices)])  8.64 us
    ppermute x3, starting transfers between devices, outward(): lax.ppermute(value, 'gx', [(i, j) for i, j in pairs if 0 <= j < count])  6.94 us
    ppermute x1, starting transfers between devices, step(): w_mate = lax.ppermute(w_mine, 'gx', swap)  5.64 us
    unnamed x42, local copies, waits for them, and re-layouts  5.08 us
  transfers between devices with their start and end apart: 20, of which 8 were waited for; matrix products, arithmetic and copies ran while one was open for 2% of the time, Pallas kernels for 1%

profile of v10, /device:TPU:1, one launch (start us, length us, event | category | flops | bytes accessed | tf_op | source)
XLA Modules:
  0.0 169.1 jit_solution(15625098421997265761)
XLA Ops:
  0.6 0.9 copy_bitcast_fusion
  1.5 0.0 copy-start.6
  1.6 0.8 copy-done.6
  2.4 0.2 shard_map.163
  2.5 3.9 %collective-permute-start.1 = (bf16[10,32,128]{2,1,0:T(8,128)(2,1)S(1)}, bf16[10,32,128]{2,1,0:T(8,128)(2,1)S(1)}, u32[]{:S(2)}, u32[]{:S(2)}) collective-permute-start(bf16[10,32,128]{2,1,0:T(8,128)(2,1)S(1)} %get-tuple-element.33), channel_id=1, source_target_pairs={{0,1},{1,2},{2,3},{3,4},{4,5},{5,6},{6,7},{7,8},{8,9},{9,10},{10,1... | collective-permute-start | bytes 245768 | tf_op jit(solution)/shard_map/ppermute | solution.py:500
  6.5 1.3 collective-permute-start
  7.8 2.8 %collective-permute-start.6 = (bf16[4,32,128]{2,1,0:T(8,128)(2,1)S(1)}, bf16[4,32,128]{2,1,0:T(8,128)(2,1)S(1)}, u32[]{:S(2)}, u32[]{:S(2)}) collective-permute-start(bf16[4,32,128]{2,1,0:T(8,128)(2,1)S(1)} %bitcast.69), channel_id=1, source_target_pairs={{0,96},{16,112},{32,0},{48,16},{64,32},{80,48},{96,64},{112,80},{1... | collective-permute-start | bytes 98312 | tf_op jit(solution)/shard_map/ppermute | solution.py:561
  10.7 0.3 collective-permute-start.5
  11.0 0.7 collective-permute-start.4
  11.8 2.2 %collective-permute-start.2 = (bf16[28,32,128]{2,1,0:T(8,128)(2,1)S(1)}, bf16[28,32,128]{2,1,0:T(8,128)(2,1)S(1)}, u32[]{:S(2)}, u32[]{:S(2)}) collective-permute-start(bf16[28,32,128]{2,1,0:T(8,128)(2,1)S(1)} %shard_map.164.refs_1_), channel_id=1, source_target_pairs={{0,16},{16,0},{32,48},{48,32},{64,80},{80,64},{96,112},{112,96},{1... | collective-permute-start | bytes 688136 | tf_op jit(solution)/shard_map/ppermute | solution.py:574
  13.9 1.0 collective-permute-done.5
  15.0 0.3 collective-permute-done.4
  15.3 8.6 %collective-permute-start.7 = (bf16[16,32,128]{2,1,0:T(8,128)(2,1)S(1)}, bf16[16,32,128]{2,1,0:T(8,128)(2,1)S(1)}, u32[]{:S(2)}, u32[]{:S(2)}) collective-permute-start(bf16[16,32,128]{2,1,0:T(8,128)(2,1)S(1)} %pad_maximum_fusion.3), channel_id=1, source_target_pairs={{0,140},{1,141},{2,142},{3,143},{4,136},{5,137},{6,138},{7,139},{8... | collective-permute-start | bytes 393224 | tf_op jit(solution)/shard_map/ppermute | solution.py:563
  24.0 2.2 %collective-permute-start.3 = (bf16[32,32,128]{2,1,0:T(8,128)(2,1)S(1)}, bf16[32,32,128]{2,1,0:T(8,128)(2,1)S(1)}, u32[]{:S(2)}, u32[]{:S(2)}) collective-permute-start(bf16[32,32,128]{2,1,0:T(8,128)(2,1)S(1)} %pad_maximum_fusion.2), channel_id=1, source_target_pairs={{16,48},{32,0},{48,80},{64,32},{80,112},{96,64},{112,144},{128,96}... | collective-permute-start | bytes 786440 | tf_op jit(solution)/shard_map/ppermute | solution.py:505
  26.2 0.6 pad_maximum_fusion.5
  26.9 3.4 %collective-permute-start.9 = (bf16[8,32,128]{2,1,0:T(8,128)(2,1)}, bf16[8,32,128]{2,1,0:T(8,128)(2,1)S(1)}, u32[]{:S(2)}, u32[]{:S(2)}) collective-permute-start(bf16[8,32,128]{2,1,0:T(8,128)(2,1)} %pad_maximum_fusion.5), channel_id=1, source_target_pairs={{16,80},{48,112},{64,0},{80,144},{96,32},{112,176},{128,64},{144,2... | collective-permute-start | bytes 196616 | tf_op jit(solution)/shard_map/ppermute | solution.py:505
  30.4 5.6 %collective-permute-start.11 = (bf16[32,32,128]{2,1,0:T(8,128)(2,1)S(1)}, bf16[32,32,128]{2,1,0:T(8,128)(2,1)S(1)}, u32[]{:S(2)}, u32[]{:S(2)}) collective-permute-start(bf16[32,32,128]{2,1,0:T(8,128)(2,1)S(1)} %constant_dynamic-update-slice_fusion.refs_7_), channel_id=1, source_target_pairs={{0,16},{16,0},{32,48},{48,32},{64,80},{80,64},{96,112},{112,96},{1... | collective-permute-start | bytes 786440 | tf_op jit(solution)/shard_map/ppermute | solution.py:579
  36.0 0.1 collective-permute-start.8
  36.1 0.9 shard_map.166
  37.0 0.8 copy-done.9
  37.9 0.7 copy-done.11
  38.5 0.7 copy-done.13
  39.2 0.0 copy-start.8
  39.3 0.7 collective-permute-start.10
  39.9 0.1 pad_add_fusion.refs_0_
  40.0 0.8 collective-permute-done.10.refs_6_
  40.9 1.6 shard_map.165
  42.5 15.1 %shard_map.167 = (bf16[4,32,256]{2,1,0:T(8,128)(2,1)S(1)}, f32[4,32,256]{2,1,0:T(8,128)S(1)}, bf16[192,128]{1,0:T(8,128)(2,1)S(1)}, f32[4,64,128]{2,1,0:T(8,128)...) custom-call(s32[2]{0:T(128)S(1)} %pad_add_fusion.refs_0_, ...), custom_call_target="tpu_custom_call" | custom-call | flops 10000000000 | bytes 20000000 | tf_op jit(solution)/shard_map/pallas_call | solution.py:486
  57.6 0.1 pad_maximum_fusion
  57.8 0.1 constant_dynamic-slice_fusion.1
  57.8 0.4 collective-permute-start.17
  58.3 0.6 copy-done.15
  58.9 1.3 collective-permute-start.13
  60.2 4.0 %collective-permute-start.12 = (bf16[192,128]{1,0:T(8,128)(2,1)S(1)}, bf16[192,128]{1,0:T(8,128)(2,1)S(1)}, u32[]{:S(2)}, u32[]{:S(2)}) collective-permute-start(bf16[192,128]{1,0:T(8,128)(2,1)S(1)} %get-tuple-element.45.own), channel_id=1, source_target_pairs={{0,1},{1,2},{2,3},{3,4},{4,5},{5,6},{6,7},{7,8},{8,9},{9,10},{10,1... | collective-permute-start | bytes 147464 | tf_op jit(solution)/shard_map/ppermute | solution.py:500
  64.2 1.1 collective-permute-done.12.left
  65.3 0.1 shard_map.168.refs_1_
  65.4 1.6 collective-permute-start.14
  67.0 0.9 collective-permute-done.14.refs_2_
  67.9 1.3 collective-permute-start.15
  69.2 0.6 shard_map.169.refs_8_
  69.8 0.9 collective-permute-done.15.refs_3_
  70.7 3.9 %collective-permute-start.16 = (bf16[320,128]{1,0:T(8,128)(2,1)S(1)}, bf16[320,128]{1,0:T(8,128)(2,1)S(1)}, u32[]{:S(2)}, u32[]{:S(2)}) collective-permute-start(bf16[320,128]{1,0:T(8,128)(2,1)S(1)} %collective-permute-done.15.refs_3_), channel_id=1, source_target_pairs={{0,16},{16,0},{32,48},{48,32},{64,80},{80,64},{96,112},{112,96},{1... | collective-permute-start | bytes 245768 | tf_op jit(solution)/shard_map/ppermute | solution.py:706
  74.6 1.3 add_convert_fusion
  75.9 0.1 pad.9
  76.0 2.1 %shard_map.170 = (bf16[4,32,256]{2,1,0:T(8,128)(2,1)S(1)}, bf16[432,128]{1,0:T(8,128)(2,1)S(1)}) custom-call(s32[2]{0:T(128)S(1)} %pad_add_fusion.refs_0_, bf16[256,128]{1,0:T(8,128)(2,1)S(1)} %shard_map.168.refs_1_, bf16[256,128]{1,0:T(8,128)(2,1)S(1)} %collective-permute-done.14.refs_2_, bf16[320,128]{1,0:T(8,128)(2,1)S(1)} %collective-permute-done.15.refs_3_, ...), custom_call_target="tpu_custom_call" | custom-call | flops 2000000000 | bytes 4000000 | tf_op jit(solution)/shard_map/pallas_call | solution.py:486
  78.1 0.1 collective-permute-start.18
  78.2 1.2 collective-permute-done.18
  79.5 49.4 %all_to_all.10 = bf16[128,24,128]{2,1,0:T(8,128)(2,1)S(1)} all-to-all(bf16[128,24,128]{2,1,0:T(8,128)(2,1)S(1)} %bitcast.63), channel_id=1, replica_groups={{0,1,2,3,4,5,6,7,8,9,10,11,12,13,14,15,32,33,34,35,36,37,38,39,40,41,42..., dimensions={0} | all-to-all | bytes 1572864 | tf_op jit(solution)/shard_map/all_to_all | solution.py:738
  128.9 0.2 reduce_sum.12
  129.0 0.1 broadcast_in_dim.2
  129.2 30.0 %all_to_all.11 = bf16[128,24,128]{2,1,0:T(8,128)(2,1)S(1)} all-to-all(bf16[128,24,128]{2,1,0:T(8,128)(2,1)S(1)} %broadcast_in_dim.2), channel_id=1, replica_groups={{0,1,2,3,4,5,6,7,8,9,10,11,12,13,14,15,32,33,34,35,36,37,38,39,40,41,42..., dimensions={0} | all-to-all | bytes 1572864 | tf_op jit(solution)/shard_map/all_to_all | solution.py:743
  159.1 3.6 %collective-permute-start.19 = (bf16[384,8,128]{2,1,0:T(8,128)(2,1)S(1)}, bf16[384,8,128]{2,1,0:T(8,128)(2,1)S(1)}, u32[]{:S(2)}, u32[]{:S(2)}) collective-permute-start(bf16[384,8,128]{2,1,0:T(8,128)(2,1)S(1)} %bitcast.64), channel_id=1, source_target_pairs={{0,16},{16,0},{32,48},{48,32},{64,80},{80,64},{96,112},{112,96},{1... | collective-permute-start | bytes 2359304 | tf_op jit(solution)/shard_map/ppermute | solution.py:747
  162.7 0.7 copy.20
  163.4 0.7 copy.21
  164.1 0.5 collective-permute-done.19
  164.6 0.1 broadcast_select_fusion.1
  165.0 0.8 shard_map.171
  165.8 0.1 concatenate.44
  166.0 0.8 convert_element_type.41
  166.7 0.1 pad_maximum_fusion.1
  166.9 0.1 concatenate.41
  166.9 0.6 convert_element_type.39
  167.6 0.4 concatenate.43
  168.0 1.2 convert_element_type.40
  (68 shorter events, 0.6 us)
Async XLA Ops:
  0.6 7.2 %copy-start.17 = (bf16[8,1728]{1,0:T(8,128)(2,1)S(1)}, bf16[8,1728]{1,0:T(8,128)(2,1)}, u32[]{:S(2)}) copy-start(bf16[8,1728]{1,0:T(8,128)(2,1)} %param.14) | copy-start | bytes 82948
  1.5 0.8 copy-start.6
  2.5 9.2 %collective-permute-start.1 = (bf16[10,32,128]{2,1,0:T(8,128)(2,1)S(1)}, bf16[10,32,128]{2,1,0:T(8,128)(2,1)S(1)}, u32[]{:S(2)}, u32[]{:S(2)}) collective-permute-start(bf16[10,32,128]{2,1,0:T(8,128)(2,1)S(1)} %get-tuple-element.33), channel_id=1, source_target_pairs={{0,1},{1,2},{2,3},{3,4},{4,5},{5,6},{6,7},{7,8},{8,9},{9,10},{10,1... | collective-permute-start | bytes 245768 | tf_op jit(solution)/shard_map/ppermute | solution.py:500
  6.5 5.2 %collective-permute-start = (bf16[10,32,128]{2,1,0:T(8,128)(2,1)S(1)}, bf16[10,32,128]{2,1,0:T(8,128)(2,1)S(1)}, u32[]{:S(2)}, u32[]{:S(2)}) collective-permute-start(bf16[10,32,128]{2,1,0:T(8,128)(2,1)S(1)} %get-tuple-element.32.own), channel_id=1, source_target_pairs={{1,0},{2,1},{3,2},{4,3},{5,4},{6,5},{7,6},{8,7},{9,8},{10,9},{11,1... | collective-permute-start | bytes 245768 | tf_op jit(solution)/shard_map/ppermute | solution.py:500
  7.8 28.3 %copy-start = (bf16[64,5184]{1,0:T(8,128)(2,1)S(1)}, bf16[64,5184]{1,0:T(8,128)(2,1)}, u32[]{:S(2)}) copy-start(bf16[64,5184]{1,0:T(8,128)(2,1)} %refs_1_.1) | copy-start | bytes 1990660
  7.8 28.3 %copy-start.1 = (bf16[32,2592]{1,0:T(8,128)(2,1)S(1)}, bf16[32,2592]{1,0:T(8,128)(2,1)}, u32[]{:S(2)}) copy-start(bf16[32,2592]{1,0:T(8,128)(2,1)} %refs_2_.1) | copy-start | bytes 497668
  7.8 28.3 %copy-start.2 = (bf16[64,864]{1,0:T(8,128)(2,1)S(1)}, bf16[64,864]{1,0:T(8,128)(2,1)}, u32[]{:S(2)}) copy-start(bf16[64,864]{1,0:T(8,128)(2,1)} %refs_0_.1) | copy-start | bytes 331780
  7.8 6.1 %collective-permute-start.6 = (bf16[4,32,128]{2,1,0:T(8,128)(2,1)S(1)}, bf16[4,32,128]{2,1,0:T(8,128)(2,1)S(1)}, u32[]{:S(2)}, u32[]{:S(2)}) collective-permute-start(bf16[4,32,128]{2,1,0:T(8,128)(2,1)S(1)} %bitcast.69), channel_id=1, source_target_pairs={{0,96},{16,112},{32,0},{48,16},{64,32},{80,48},{96,64},{112,80},{1... | collective-permute-start | bytes 98312 | tf_op jit(solution)/shard_map/ppermute | solution.py:561
  10.7 4.3 %collective-permute-start.5 = (bf16[4,32,128]{2,1,0:T(8,128)(2,1)S(1)}, bf16[4,32,128]{2,1,0:T(8,128)(2,1)S(1)}, u32[]{:S(2)}, u32[]{:S(2)}) collective-permute-start(bf16[4,32,128]{2,1,0:T(8,128)(2,1)S(1)} %bitcast.70), channel_id=1, source_target_pairs={{0,64},{16,80},{32,96},{48,112},{64,0},{80,16},{96,32},{112,48},{1... | collective-permute-start | bytes 98312 | tf_op jit(solution)/shard_map/ppermute | solution.py:561
  11.0 4.3 %collective-permute-start.4 = (bf16[4,32,128]{2,1,0:T(8,128)(2,1)S(1)}, bf16[4,32,128]{2,1,0:T(8,128)(2,1)S(1)}, u32[]{:S(2)}, u32[]{:S(2)}) collective-permute-start(bf16[4,32,128]{2,1,0:T(8,128)(2,1)S(1)} %bitcast.71), channel_id=1, source_target_pairs={{0,32},{16,48},{32,64},{48,80},{64,96},{80,112},{96,0},{112,16},{1... | collective-permute-start | bytes 98312 | tf_op jit(solution)/shard_map/ppermute | solution.py:561
  11.8 12.2 %collective-permute-start.2 = (bf16[28,32,128]{2,1,0:T(8,128)(2,1)S(1)}, bf16[28,32,128]{2,1,0:T(8,128)(2,1)S(1)}, u32[]{:S(2)}, u32[]{:S(2)}) collective-permute-start(bf16[28,32,128]{2,1,0:T(8,128)(2,1)S(1)} %shard_map.164.refs_1_), channel_id=1, source_target_pairs={{0,16},{16,0},{32,48},{48,32},{64,80},{80,64},{96,112},{112,96},{1... | collective-permute-start | bytes 688136 | tf_op jit(solution)/shard_map/ppermute | solution.py:574
  15.3 15.0 %collective-permute-start.7 = (bf16[16,32,128]{2,1,0:T(8,128)(2,1)S(1)}, bf16[16,32,128]{2,1,0:T(8,128)(2,1)S(1)}, u32[]{:S(2)}, u32[]{:S(2)}) collective-permute-start(bf16[16,32,128]{2,1,0:T(8,128)(2,1)S(1)} %pad_maximum_fusion.3), channel_id=1, source_target_pairs={{0,140},{1,141},{2,142},{3,143},{4,136},{5,137},{6,138},{7,139},{8... | collective-permute-start | bytes 393224 | tf_op jit(solution)/shard_map/ppermute | solution.py:563
  24.0 6.4 %collective-permute-start.3 = (bf16[32,32,128]{2,1,0:T(8,128)(2,1)S(1)}, bf16[32,32,128]{2,1,0:T(8,128)(2,1)S(1)}, u32[]{:S(2)}, u32[]{:S(2)}) collective-permute-start(bf16[32,32,128]{2,1,0:T(8,128)(2,1)S(1)} %pad_maximum_fusion.2), channel_id=1, source_target_pairs={{16,48},{32,0},{48,80},{64,32},{80,112},{96,64},{112,144},{128,96}... | collective-permute-start | bytes 786440 | tf_op jit(solution)/shard_map/ppermute | solution.py:505
  26.9 12.4 %collective-permute-start.9 = (bf16[8,32,128]{2,1,0:T(8,128)(2,1)}, bf16[8,32,128]{2,1,0:T(8,128)(2,1)S(1)}, u32[]{:S(2)}, u32[]{:S(2)}) collective-permute-start(bf16[8,32,128]{2,1,0:T(8,128)(2,1)} %pad_maximum_fusion.5), channel_id=1, source_target_pairs={{16,80},{48,112},{64,0},{80,144},{96,32},{112,176},{128,64},{144,2... | collective-permute-start | bytes 196616 | tf_op jit(solution)/shard_map/ppermute | solution.py:505
  30.4 10.5 %collective-permute-start.11 = (bf16[32,32,128]{2,1,0:T(8,128)(2,1)S(1)}, bf16[32,32,128]{2,1,0:T(8,128)(2,1)S(1)}, u32[]{:S(2)}, u32[]{:S(2)}) collective-permute-start(bf16[32,32,128]{2,1,0:T(8,128)(2,1)S(1)} %constant_dynamic-update-slice_fusion.refs_7_), channel_id=1, source_target_pairs={{0,16},{16,0},{32,48},{48,32},{64,80},{80,64},{96,112},{112,96},{1... | collective-permute-start | bytes 786440 | tf_op jit(solution)/shard_map/ppermute | solution.py:579
  36.0 4.8 %collective-permute-start.8 = (bf16[32,32,128]{2,1,0:T(8,128)(2,1)S(1)}, bf16[32,32,128]{2,1,0:T(8,128)(2,1)S(1)}, u32[]{:S(2)}, u32[]{:S(2)}) collective-permute-start(bf16[32,32,128]{2,1,0:T(8,128)(2,1)S(1)} %collective-permute-done.3.refs_3_), channel_id=1, source_target_pairs={{0,16},{16,0},{32,48},{48,32},{64,80},{80,64},{96,112},{112,96},{1... | collective-permute-start | bytes 786440 | tf_op jit(solution)/shard_map/ppermute | solution.py:580
  37.0 0.8 copy-start.9
  37.9 0.7 copy-start.11
  38.5 0.7 copy-start.13
  39.2 3.2 %copy-start.3 = (bf16[128,384]{1,0:T(8,128)(2,1)S(1)}, bf16[128,384]{1,0:T(8,128)(2,1)}, u32[]{:S(2)}) copy-start(bf16[128,384]{1,0:T(8,128)(2,1)} %constant.53.clone.refs_12_.refs_11_) | copy-start | bytes 294916
  39.2 3.2 %copy-start.4 = (bf16[384,128]{1,0:T(8,128)(2,1)S(1)}, bf16[384,128]{1,0:T(8,128)(2,1)}, u32[]{:S(2)}) copy-start(bf16[384,128]{1,0:T(8,128)(2,1)} %constant.54.clone.refs_13_) | copy-start | bytes 294916
  39.2 3.2 %copy-start.5 = (bf16[256,128]{1,0:T(8,128)(2,1)S(1)}, bf16[256,128]{1,0:T(8,128)(2,1)}, u32[]{:S(2)}) copy-start(bf16[256,128]{1,0:T(8,128)(2,1)} %constant.55.clone.refs_14_) | copy-start | bytes 196612
  39.2 3.3 %copy-start.7 = (bf16[128,128]{1,0:T(8,128)(2,1)S(1)}, bf16[128,128]{1,0:T(8,128)(2,1)}, u32[]{:S(2)}) copy-start(bf16[128,128]{1,0:T(8,128)(2,1)} %constant.51.clone.refs_10_) | copy-start | bytes 98308
  39.2 3.3 %copy-start.8 = (bf16[128,128]{1,0:T(8,128)(2,1)S(1)}, bf16[128,128]{1,0:T(8,128)(2,1)}, u32[]{:S(2)}) copy-start(bf16[128,128]{1,0:T(8,128)(2,1)} %constant.52.clone.refs_11_) | copy-start | bytes 98308
  39.2 3.2 %copy-start.10 = (bf16[192,1728]{1,0:T(8,128)(2,1)S(1)}, bf16[192,1728]{1,0:T(8,128)(2,1)}, u32[]{:S(2)}) copy-start(bf16[192,1728]{1,0:T(8,128)(2,1)} %copy-done.9) | copy-start | bytes 1990660
  39.2 3.2 %copy-start.12 = (bf16[96,864]{1,0:T(8,128)(2,1)S(1)}, bf16[96,864]{1,0:T(8,128)(2,1)}, u32[]{:S(2)}) copy-start(bf16[96,864]{1,0:T(8,128)(2,1)} %copy-done.11) | copy-start | bytes 497668
  39.3 3.2 %copy-start.14 = (bf16[192,288]{1,0:T(8,128)(2,1)S(1)}, bf16[192,288]{1,0:T(8,128)(2,1)}, u32[]{:S(2)}) copy-start(bf16[192,288]{1,0:T(8,128)(2,1)} %copy-done.13) | copy-start | bytes 331780
  39.3 1.6 collective-permute-start.10
  57.8 1.1 copy-start.15
  57.8 16.8 %collective-permute-start.17 = (bf16[330,8,128]{2,1,0:T(8,128)(2,1)S(1)}, bf16[330,8,128]{2,1,0:T(8,128)(2,1)}, u32[]{:S(2)}, u32[]{:S(2)}) collective-permute-start(bf16[330,8,128]{2,1,0:T(8,128)(2,1)S(1)} %constant_dynamic-slice_fusion.1), channel_id=1, source_target_pairs={{0,16},{16,0},{32,48},{48,32},{64,80},{80,64},{96,112},{112,96},{1... | collective-permute-start | bytes 2027528 | tf_op jit(solution)/shard_map/ppermute | solution.py:689
  58.9 5.3 %collective-permute-start.13 = (bf16[192,128]{1,0:T(8,128)(2,1)S(1)}, bf16[192,128]{1,0:T(8,128)(2,1)S(1)}, u32[]{:S(2)}, u32[]{:S(2)}) collective-permute-start(bf16[192,128]{1,0:T(8,128)(2,1)S(1)} %get-tuple-element.45.own), channel_id=1, source_target_pairs={{1,0},{2,1},{3,2},{4,3},{5,4},{6,5},{7,6},{8,7},{9,8},{10,9},{11,1... | collective-permute-start | bytes 147464 | tf_op jit(solution)/shard_map/ppermute | solution.py:500
  60.2 5.2 %collective-permute-start.12 = (bf16[192,128]{1,0:T(8,128)(2,1)S(1)}, bf16[192,128]{1,0:T(8,128)(2,1)S(1)}, u32[]{:S(2)}, u32[]{:S(2)}) collective-permute-start(bf16[192,128]{1,0:T(8,128)(2,1)S(1)} %get-tuple-element.45.own), channel_id=1, source_target_pairs={{0,1},{1,2},{2,3},{3,4},{4,5},{5,6},{6,7},{7,8},{8,9},{9,10},{10,1... | collective-permute-start | bytes 147464 | tf_op jit(solution)/shard_map/ppermute | solution.py:500
  65.4 2.5 %collective-permute-start.14 = (bf16[256,128]{1,0:T(8,128)(2,1)S(1)}, bf16[256,128]{1,0:T(8,128)(2,1)S(1)}, u32[]{:S(2)}, u32[]{:S(2)}) collective-permute-start(bf16[256,128]{1,0:T(8,128)(2,1)S(1)} %shard_map.168.refs_1_), channel_id=1, source_target_pairs={{0,16},{16,0},{32,48},{48,32},{64,80},{80,64},{96,112},{112,96},{1... | collective-permute-start | bytes 196616 | tf_op jit(solution)/shard_map/ppermute | solution.py:703
  67.9 2.8 %collective-permute-start.15 = (bf16[320,128]{1,0:T(8,128)(2,1)S(1)}, bf16[320,128]{1,0:T(8,128)(2,1)S(1)}, u32[]{:S(2)}, u32[]{:S(2)}) collective-permute-start(bf16[320,128]{1,0:T(8,128)(2,1)S(1)} %pad_maximum_fusion.4), channel_id=1, source_target_pairs={{16,48},{32,0},{48,80},{64,32},{80,112},{96,64},{112,144},{128,96}... | collective-permute-start | bytes 245768 | tf_op jit(solution)/shard_map/ppermute | solution.py:505
  69.2 5.4 %copy-start.16 = (bf16[660,8,128]{2,1,0:T(8,128)(2,1)S(1)}, bf16[660,8,128]{2,1,0:T(8,128)(2,1)}, u32[]{:S(2)}) copy-start(bf16[660,8,128]{2,1,0:T(8,128)(2,1)} %copy-done.15) | copy-start | bytes 4055044
  70.7 5.3 %collective-permute-start.16 = (bf16[320,128]{1,0:T(8,128)(2,1)S(1)}, bf16[320,128]{1,0:T(8,128)(2,1)S(1)}, u32[]{:S(2)}, u32[]{:S(2)}) collective-permute-start(bf16[320,128]{1,0:T(8,128)(2,1)S(1)} %collective-permute-done.15.refs_3_), channel_id=1, source_target_pairs={{0,16},{16,0},{32,48},{48,32},{64,80},{80,64},{96,112},{112,96},{1... | collective-permute-start | bytes 245768 | tf_op jit(solution)/shard_map/ppermute | solution.py:706
  78.1 1.3 collective-permute-start.18
  159.1 5.5 %collective-permute-start.19 = (bf16[384,8,128]{2,1,0:T(8,128)(2,1)S(1)}, bf16[384,8,128]{2,1,0:T(8,128)(2,1)S(1)}, u32[]{:S(2)}, u32[]{:S(2)}) collective-permute-start(bf16[384,8,128]{2,1,0:T(8,128)(2,1)S(1)} %bitcast.64), channel_id=1, source_target_pairs={{0,16},{16,0},{32,48},{48,32},{64,80},{80,64},{96,112},{112,96},{1... | collective-permute-start | bytes 2359304 | tf_op jit(solution)/shard_map/ppermute | solution.py:747
